TPU v7x, 32 devices: a whole 2x2x4 slice. The times are simulated.
32 devices in a mesh: seg: 2 (over y), chan: 8 (over z, core), tm: 2 (over x).
Axes of the slice: x: 2, y: 2, z: 4, core: 2. Of those that a mesh axis runs over, the one named last changes fastest.
Arguments:
- traces: bfloat16 [1024, 12288], P(('seg', 'chan'), 'tm'), parts along dimension 0, may hold values from -14 to 14
- filter_taps: float32 [512, 33], P('chan'), may hold values from -1 to 1
- source_counts: int32 [8], replicated, may hold values from 1 to 36, 96 in all
- source_channel: int32 [8, 36], replicated, may hold values from 0 to 63
- block_sources: int32 [8, 12], P('chan'), may hold values from 0 to 95
Outputs:
- stacked: float32 [1024, 12, 1024], P(('seg', 'chan', 'tm')), parts along dimension 0
There are 2 independent parts, one for each index of `seg`. A program takes and returns all parts, laid end to end along the dimension named above; an argument that names none is the same for every part. Nothing has to cross between parts.
Inputs may be any that keep to these rules, and one draw needn't show every extreme that they name: `source_counts`: the entries sum to 96 and the largest is exactly 36. `source_channel`: only the first source_counts[h] entries of row h name virtual sources.
All inputs are finite; a program needn't handle non-finite values.
Results may differ from a plain program's by a relative error of at most 0.0072.
Values may be sent and summed in bfloat16 or wider, within the bound.
No kernel may reach another device: no remote copies, remote signals or barrier semaphores. Data moves between devices by JAX's collectives and lax.ppermute only.
A program may use at most 64 MiB of HBM per device.

v0:
```python
import functools

import jax
import jax.numpy as jnp
import ml_dtypes
import numpy as np
from jax import lax
from jax.experimental import pallas as pl
from jax.experimental.pallas import tpu as pltpu
from jax.sharding import PartitionSpec as P


NFFT = 4096
NF = 512
F0 = 8
PIECE = NFFT // 8
HALF = NFFT // 2
CHUNK = 256
F32 = jnp.float32
BF16 = jnp.bfloat16
LIMIT = 24 * 1024 * 1024


def piece_table():
    bins = F0 + np.arange(NF)
    angle = (bins * np.arange(PIECE)[:, None] % NFFT) * (2.0 * np.pi / NFFT)
    exact = np.concatenate([np.cos(angle), -np.sin(angle)], axis=1)
    high = exact.astype(ml_dtypes.bfloat16)
    low = (exact - high.astype(np.float64)).astype(ml_dtypes.bfloat16)
    return np.concatenate([high, low], axis=0)


def split_two(x):
    high = x.astype(BF16)
    low = (x - high.astype(F32)).astype(BF16)
    return high, low


def dot(a, b):
    return jnp.dot(a, b, preferred_element_type=F32)


def stacked_parts(x):
    high, low = split_two(x)
    high = high.astype(F32)
    return jnp.concatenate([high, low.astype(F32), high], axis=0)


def stacked_rows(table, rows, cols):
    first = table[:rows, cols]
    return jnp.concatenate([first, first, table[PIECE : PIECE + rows, cols]], axis=0)


class Turns:
    def __init__(self):
        lane = lax.broadcasted_iota(jnp.int32, (1, CHUNK), 1)
        turn = lane % 4
        self.odd = (turn % 2) == 1
        self.sign = jnp.where(self.odd, -1.0, 1.0)
        self.real = jnp.where(turn < 2, 1.0, -1.0)
        self.imag = jnp.where((turn == 0) | (turn == 3), 1.0, -1.0)
        eighth = lane % 8
        root = np.float32(np.sqrt(0.5))
        self.cos = jnp.where(turn % 4 == 0, 1.0, jnp.where(turn == 2, 0.0, root))
        self.cos = jnp.where((eighth > 2) & (eighth < 6), -self.cos, self.cos)
        self.sin = jnp.where(turn == 2, 1.0, jnp.where(turn == 0, 0.0, root))
        self.sin = jnp.where(eighth < 4, -self.sin, self.sin)

    def quarter(self, ar, ai, br, bi):
        return (
            ar + self.real * jnp.where(self.odd, bi, br),
            ai + self.imag * jnp.where(self.odd, br, bi),
        )

    def half(self, re, im):
        ar, ai = self.quarter(re[0], im[0], re[2], im[2])
        br, bi = self.quarter(re[1], im[1], re[3], im[3])
        return ar + (br * self.cos - bi * self.sin), ai + (br * self.sin + bi * self.cos)


def half_spectra(x, table, channels, halves, turns, f):
    re = slice(f, f + CHUNK)
    im = slice(NF + f, NF + f + CHUNK)
    both = jnp.concatenate([x, x], axis=1)
    dr = dot(both, table[:, re])
    di = dot(both, table[:, im])
    out = []
    for b in range(halves):
        rows = [slice((4 * b + e) * channels, (4 * b + e + 1) * channels) for e in range(4)]
        out.append(turns.half([dr[r] for r in rows], [di[r] for r in rows]))
    return out


def end_terms(taps_wide, shifted, tap_count, ends):
    lag = tap_count - 1
    apart = ends.T
    size = apart.shape[0]
    shifted[...] = jnp.zeros_like(shifted)
    shifted[:tap_count, :] = taps_wide
    total = jnp.zeros((lag, apart.shape[1]), F32)
    for j in range(1, tap_count):
        total = total + shifted[j : j + lag, :] * apart[size - j : size - j + 1, :]
    return stacked_parts(total).T.astype(BF16)


def whiten_rows(re, im):
    rows = re.shape[0]
    place = lax.broadcasted_iota(jnp.int32, (rows, NF), 1)
    power = re * re + im * im
    smooth = power
    for s in (1, 2):
        smooth = smooth + jnp.where(place >= s, pltpu.roll(power, s, 1), 0.0)
        smooth = smooth + jnp.where(place < NF - s, pltpu.roll(power, NF - s, 1), 0.0)
    total = jnp.sum(power, axis=1, keepdims=True)
    scaling = lax.rsqrt(smooth * 0.2 + (total * (0.1 / NF) + 1e-06))
    return (re * scaling).astype(BF16), (im * scaling).astype(BF16)


ROWS = 16


def whiten_all(spectra, white, count):
    def step(i, carry):
        rows = pl.ds(pl.multiple_of(i * ROWS, ROWS), ROWS)
        re, im = whiten_rows(spectra[rows, :NF], spectra[rows, NF:])
        white[rows, :NF] = re
        white[rows, NF:] = im
        return carry

    lax.fori_loop(0, count // ROWS, step, 0, unroll=2)


def head_kernel(traces_in, taps_in, table_in, tail, traces, taps, table, sems):
    start = traces.shape[1] - tail.shape[1]
    copies = [
        pltpu.make_async_copy(traces_in.at[:, start:], tail, sems.at[0]),
        pltpu.make_async_copy(traces_in, traces, sems.at[1]),
        pltpu.make_async_copy(taps_in, taps, sems.at[2]),
        pltpu.make_async_copy(table_in, table, sems.at[3]),
    ]
    for copy in copies:
        copy.start()
    for copy in copies:
        copy.wait()


def own_kernel(windows, traces, taps, table, part, white, response, ends, square, shifted, spectra):
    channels, samples = traces.shape
    tap_count = taps.shape[0]
    square[...] = jnp.zeros_like(square)
    high, low = split_two(taps[...])
    high = high.astype(F32)
    lines = square.shape[0] // 3
    for i, value in enumerate((high, low.astype(F32), high)):
        square[i * lines : i * lines + tap_count, :channels] = value
    filter_taps = square[...].T[:channels].astype(BF16)
    tile = 128
    last = windows - 1
    for b in range(1, windows):
        ends[:, (b - 1) * tile : b * tile] = traces[:, b * HALF - tile : b * HALF]
    start = (last - 1) * HALF
    apart = traces[:, start - tile : start].astype(F32) - traces[:, samples - tile :].astype(F32)
    edge = end_terms(taps[...], shifted, tap_count, apart)
    pieces = samples // PIECE
    x = jnp.concatenate([traces[:, q * PIECE : (q + 1) * PIECE] for q in range(pieces)], axis=0)
    turns = Turns()
    for f in range(0, NF, CHUNK):
        re = slice(f, f + CHUNK)
        im = slice(NF + f, NF + f + CHUNK)
        pr = dot(filter_taps, stacked_rows(table, lines, re))
        pi = dot(filter_taps, stacked_rows(table, lines, im))
        response[:, re] = pr
        response[:, im] = pi
        halves = half_spectra(x, table, channels, windows, turns, f)
        for w in range(windows):
            xr, xi = halves[w]
            xr, xi = turns.sign * xr, turns.sign * xi
            if w > 0:
                xr, xi = xr + halves[w - 1][0], xi + halves[w - 1][1]
            yr = xr * pr - xi * pi
            yi = xr * pi + xi * pr
            if w < last:
                rows = slice(w * channels, (w + 1) * channels)
                part[rows, re] = yr
                part[rows, im] = yi
            else:
                spectra[:, re] = yr + dot(edge, stacked_rows(table, tap_count - 1, re))
                spectra[:, im] = yi + dot(edge, stacked_rows(table, tap_count - 1, im))
    whiten_all(spectra, white, channels)


def part_rows(windows, pairs):
    return [-(-w * pairs // 8) * 8 for w in (windows - 1, 1)]


def picks_kernel(shape, where, counts, slots, *refs):
    channels, windows, pairs, chips = shape
    wanted, picks, chosen = refs[:-2], refs[-2], refs[-1]
    group = where[0]
    first = jnp.int32(0)
    for g in range(counts.shape[0]):
        first = first + jnp.where(g < group, counts[g], 0)
    owned = counts[group]
    width = windows * channels
    lane = lax.broadcasted_iota(jnp.int32, (1, width), 1)
    columns = [jnp.where(lane // channels == w, lane % channels, -2) for w in range(windows)]
    sizes = part_rows(windows, pairs)
    per = wanted[0].shape[0]
    chosen[...] = jnp.zeros_like(chosen)
    for core in range(2):
        for d in range(chips):
            base = (core * chips + d) * sum(sizes)
            tail = base + sizes[0]
            for p in range(pairs):
                slot = wanted[2 * d // per][(2 * d + core) % per, p] - first
                mine = (slot >= 0) & (slot < owned)
                channel = slots[group, jnp.where(mine, slot, 0)]
                channel = jnp.where(mine, channel, -1)
                for w in range(windows):
                    row = (base + w * pairs if w < windows - 1 else tail) + p
                    chosen[row : row + 1, :] = (columns[w] == channel).astype(F32)
    picks[...] = chosen[...].astype(BF16)


def rest_kernel(
    windows, times, where, halo, ends, taps, table, part, own_white, response, picks, *refs
):
    keep, send = refs[:2]
    blocks = refs[2 : 2 + times]
    shifted, spectra, white = refs[2 + times :]
    channels = response.shape[0]
    tap_count = taps.shape[0]
    tile = halo.shape[1] - HALF
    rest = windows - 1

    before = [halo[:, :tile], halo[:, HALF:]]
    before += [ends[:, (b - 1) * tile : b * tile] for b in range(1, windows - 2)]
    after = [ends[:, w * tile : (w + 1) * tile] for w in range(rest)]
    apart = jnp.concatenate([b.astype(F32) - a.astype(F32) for b, a in zip(before, after)], axis=0)
    taps_wide = jnp.concatenate([taps[...]] * rest, axis=1)
    edge = end_terms(taps_wide, shifted, tap_count, apart)
    x = jnp.concatenate(
        [halo[:, tile + q * PIECE : tile + (q + 1) * PIECE] for q in range(HALF // PIECE)],
        axis=0,
    )
    turns = Turns()
    for f in range(0, NF, CHUNK):
        re = slice(f, f + CHUNK)
        im = slice(NF + f, NF + f + CHUNK)
        xr, xi = half_spectra(x, table, channels, 1, turns, f)[0]
        pr, pi = response[:, re], response[:, im]
        er = dot(edge, stacked_rows(table, tap_count - 1, re))
        ei = dot(edge, stacked_rows(table, tap_count - 1, im))
        spectra[:channels, re] = part[:channels, re] + er[:channels] + (xr * pr - xi * pi)
        spectra[:channels, im] = part[:channels, im] + ei[:channels] + (xr * pi + xi * pr)
        spectra[channels:, re] = part[channels:, re] + er[channels:]
        spectra[channels:, im] = part[channels:, im] + ei[channels:]
    count = rest * channels
    whiten_all(spectra, white, count)
    white[count:, :] = own_white[...]
    base = keep.shape[0]
    size = channels // times
    choose = picks[...]
    for f in range(0, 2 * NF, CHUNK):
        cols = slice(f, f + CHUNK)
        out = dot(choose, white[:, cols]).astype(BF16)
        keep[:, cols] = out[:base]
        send[:, cols] = out[base:]
    for d in range(times):
        line = (where[1] ^ d) * size
        for w in range(windows):
            if size % ROWS == 0:
                at = pl.multiple_of(w * channels + line, ROWS)
                blocks[d][w * size : (w + 1) * size, :] = white[pl.ds(at, size), :]
            else:
                row = lax.broadcasted_iota(jnp.int32, (size, channels), 0)
                col = lax.broadcasted_iota(jnp.int32, (size, channels), 1)
                move = (col == row + line).astype(F32).astype(BF16)
                moved = dot(move, white[w * channels : (w + 1) * channels, :])
                blocks[d][w * size : (w + 1) * size, :] = moved.astype(BF16)


def correlate_kernel(windows, factor, count, *refs):
    receivers = refs[:count]
    sources = refs[count : 3 * count]
    last = len(refs) == 3 * count + 6
    total = refs[3 * count] if last else None
    out, line_r, line_s = refs[3 * count + last : 3 * count + last + 3]
    held, sems = refs[-2:] if last else (out, None)
    pairs, part = out.shape[0], out.shape[1]
    for d in range(count):
        for w in range(windows):
            at = d * windows + w
            line_r[at] = receivers[d][w].astype(F32) * factor
            if w < windows - 1:
                rows = sources[2 * d][w * pairs : (w + 1) * pairs, :].astype(F32)
            else:
                rows = sources[2 * d + 1][:pairs, :].astype(F32)
            for p in range(pairs):
                line_s[p, at : at + 1, :] = rows[p : p + 1, :]

    def copy(p):
        return pltpu.make_async_copy(held.at[p], out.at[p], sems.at[p])

    def one(p, carry):
        for f in range(0, NF, 128):
            re = slice(f, f + 128)
            im = slice(NF + f, NF + f + 128)
            if last:
                total_r, total_i = total[p, :, re], total[p, :, im]
            else:
                total_r = jnp.zeros((part, 128), F32)
                total_i = jnp.zeros((part, 128), F32)
            for at in range(count * windows):
                rr = line_r[at, :, re]
                ri = line_r[at, :, im]
                sr = line_s[p, at : at + 1, re]
                si = line_s[p, at : at + 1, im]
                total_r = total_r + (sr * rr + si * ri)
                total_i = total_i + (sr * ri - si * rr)
            held[p, :, re] = total_r
            held[p, :, im] = total_i
        if last:
            copy(p).start()
        return carry

    lax.fori_loop(0, pairs, one, 0)
    if last:
        for p in range(pairs):
            copy(p).wait()


def correlate(receivers, sources, total, pairs, factor):
    windows, part, width = receivers[0].shape
    count = len(receivers)
    vmem = pl.BlockSpec(memory_space=pltpu.VMEM)
    shape = (pairs, part, width)
    last = total is not None
    scratch = [
        pltpu.VMEM((count * windows, part, width), F32),
        pltpu.VMEM((pairs, -(-count * windows // 8) * 8, width), F32),
    ]
    if last:
        scratch += [pltpu.VMEM(shape, F32), pltpu.SemaphoreType.DMA((pairs,))]
    return pl.pallas_call(
        functools.partial(correlate_kernel, windows, factor, count),
        out_shape=jax.ShapeDtypeStruct(shape, F32),
        in_specs=[vmem] * (3 * count + last),
        out_specs=pl.BlockSpec(memory_space=pltpu.HBM) if last else vmem,
        scratch_shapes=scratch,
        compiler_params=pltpu.CompilerParams(vmem_limit_bytes=LIMIT),
        name="correlate",
    )(*receivers, *(part for both in sources for part in both), *([total] if last else []))


def shards(traces, filter_taps, source_counts, source_channel, block_sources):
    channels, samples = traces.shape
    tap_count = filter_taps.shape[1]
    pairs = block_sources.shape[1]
    windows = samples // HALF
    groups = lax.axis_size("chan")
    times = lax.axis_size("tm")
    chips = groups // 2
    part = channels // times
    sizes = part_rows(windows, pairs)
    rows_out = chips * sum(sizes)

    def across(x, axis, distance):
        size = lax.axis_size(axis)
        return lax.ppermute(x, axis, [(i, i ^ distance) for i in range(size)])

    smem = pl.BlockSpec(memory_space=pltpu.SMEM)
    vmem = pl.BlockSpec(memory_space=pltpu.VMEM)
    hbm = pl.BlockSpec(memory_space=pltpu.HBM)
    params = pltpu.CompilerParams(vmem_limit_bytes=LIMIT)
    bits = [1 << b for b in range(chips.bit_length() - 1)]

    other = across(block_sources, "chan", 1)
    inputs = (traces, filter_taps.T, jnp.asarray(piece_table()))
    tail, traces, taps, table = pl.pallas_call(
        head_kernel,
        out_shape=[jax.ShapeDtypeStruct((channels, HALF + 128), BF16)]
        + [jax.ShapeDtypeStruct(a.shape, a.dtype) for a in inputs],
        in_specs=[hbm] * 3,
        out_specs=[vmem] * 4,
        scratch_shapes=[pltpu.SemaphoreType.DMA((4,))],
        compiler_params=params,
        name="head",
    )(*(pltpu.with_memory_space_constraint(a, pltpu.HBM) for a in inputs))
    halo = lax.ppermute(tail, "tm", [(i - 1, i) for i in range(1, times)])
    wanted = [jnp.concatenate([block_sources, other], axis=0)]
    for bit in bits:
        known = jnp.concatenate(wanted, axis=0)
        wanted = [known, across(known, "chan", 2 * bit)]
    where = jnp.stack([lax.axis_index("chan"), lax.axis_index("tm")]).astype(jnp.int32)

    shape = (channels, windows, pairs, chips)
    width = windows * channels
    own = pl.pallas_call(
        functools.partial(own_kernel, windows),
        out_shape=[
            jax.ShapeDtypeStruct((width - channels, 2 * NF), F32),
            jax.ShapeDtypeStruct((channels, 2 * NF), BF16),
            jax.ShapeDtypeStruct((channels, 2 * NF), F32),
            jax.ShapeDtypeStruct((channels, (windows - 1) * 128), BF16),
        ],
        in_specs=[vmem] * 3,
        out_specs=[vmem] * 4,
        scratch_shapes=[
            pltpu.VMEM((3 * (-(-tap_count // 16) * 16), 128), F32),
            pltpu.VMEM((2 * tap_count + 6, channels), F32),
            pltpu.VMEM((channels, 2 * NF), F32),
        ],
        compiler_params=params,
        name="own",
    )(traces, taps, table)
    part_spectra, own_white, response, ends = own
    picks = pl.pallas_call(
        functools.partial(picks_kernel, shape),
        out_shape=jax.ShapeDtypeStruct((2 * rows_out, width), BF16),
        in_specs=[smem] * (3 + len(wanted)),
        out_specs=vmem,
        scratch_shapes=[pltpu.VMEM((2 * rows_out, width), F32)],
        compiler_params=params,
        name="picks",
    )(where, source_counts, source_channel, *wanted)
    outs = pl.pallas_call(
        functools.partial(rest_kernel, windows, times),
        out_shape=[jax.ShapeDtypeStruct((rows_out, 2 * NF), BF16)] * 2
        + [jax.ShapeDtypeStruct((windows * part, 2 * NF), BF16)] * times,
        in_specs=[smem] + [vmem] * 8,
        out_specs=[vmem] * (2 + times),
        scratch_shapes=[
            pltpu.VMEM((2 * tap_count + 6, width - channels), F32),
            pltpu.VMEM((width - channels, 2 * NF), F32),
            pltpu.VMEM((width, 2 * NF), BF16),
        ],
        compiler_params=params,
        name="rest",
    )(where, halo, ends, taps, table, part_spectra, own_white, response, picks)
    keep, send, blocks = outs[0], outs[1], outs[2:]
    gathered = keep + across(send, "chan", 1)
    rows = sum(sizes)
    pieces = [gathered[d * rows : (d + 1) * rows] for d in range(chips)]
    pieces = list(lax.optimization_barrier(tuple(pieces)))
    for bit in bits:
        onward = [d for d in range(2 * bit, chips) if d & (2 * bit - 1) == bit]
        if onward:
            block = jnp.concatenate([pieces[d] for d in onward], axis=0)
            block = across(block, "chan", 2 * bit)
            for i, d in enumerate(onward):
                pieces[d ^ bit] = pieces[d ^ bit] + block[i * rows : (i + 1) * rows]
    mine = pieces[0]
    for bit in bits[:-1]:
        mine = mine + across(pieces[bit], "chan", 2 * bit)
    mine = [mine[: sizes[0]], mine[sizes[0] :]]
    if bits:
        last = pieces[bits[-1]]
        for i, x in enumerate((last[: sizes[0]], last[sizes[0] :])):
            mine[i] = mine[i] + across(x, "chan", 2 * bits[-1])
    receivers = [blocks[0]]
    for d in range(1, times):
        receivers.append(across(blocks[d], "tm", d))
    receivers = [r.reshape(windows, part, 2 * NF) for r in receivers]
    sources = [mine]
    for d in range(1, times):
        both = []
        for x in mine:
            both.append(across(x, "tm", d))
        sources.append(both)

    factor = 1.0 / (windows * times)
    total = correlate(receivers[:1], sources[:1], None, pairs, factor)
    if times > 1:
        total = correlate(receivers[1:], sources[1:], total, pairs, factor)
    return total.transpose(1, 0, 2)


def solution(mesh):
    in_specs = (P(("seg", "chan"), "tm"), P("chan", None), P(), P(), P("chan", None))
    out_specs = P(("seg", "chan", "tm"), None, None)
    return jax.shard_map(shards, mesh=mesh, in_specs=in_specs, out_specs=out_specs, check_vma=False)
```

profile of v0, /device:TPU:0, one launch (start us, length us, event | category | flops | bytes accessed | tf_op | source)
XLA Modules:
  0.0 38.6 jit_solution(3414996535985718737)
XLA Ops:
  0.0 0.0 copy-start.2
  0.0 0.5 %collective-permute-start.1 = (s32[1,12]{1,0:T(1,128)}, s32[1,12]{1,0:T(1,128)S(1)}, u32[]{:S(2)}, u32[]{:S(2)}) collective-permute-start(s32[1,12]{1,0:T(1,128)} %param.10), channel_id=1, source_target_pairs={{0,2},{2,0},{4,6},{6,4},{8,10},{10,8},{12,14},{14,12},{1,3},{3,1},... | collective-permute-start | bytes 152 | tf_op jit(solution)/shard_map/ppermute | solution.py:370
  0.5 2.0 %head.1 = (bf16[64,2176]{1,0:T(8,128)(2,1)S(1)}, bf16[64,6144]{1,0:T(8,128)(2,1)S(1)}, f32[33,64]{1,0:T(8,128)S(1)}, bf16[1024,1024]{1,0:T(8,128)(2,1)S(1)}) custom-call(bf16[64,6144]{1,0:T(8,128)(2,1)} %traces_in.1, f32[33,64]{1,0:T(8,128)} %bitcast.8, bf16[1024,1024]{1,0:T(8,128)(2,1)} %constant.10.clone.table_in), custom_call_target="tpu_custom_call" | custom-call | tf_op jit(solution)/shard_map/head/pallas_call | solution.py:380
  2.5 0.0 copy-start
  2.5 0.0 copy-start.1
  2.5 4.4 %collective-permute-start = (bf16[64,2176]{1,0:T(8,128)(2,1)S(1)}, bf16[64,2176]{1,0:T(8,128)(2,1)S(1)}, u32[]{:S(2)}, u32[]{:S(2)}) collective-permute-start(bf16[64,2176]{1,0:T(8,128)(2,1)S(1)} %get-tuple-element.21), channel_id=1, source_target_pairs={{0,1},{2,3},{4,5},{6,7},{8,9},{10,11},{12,13},{14,15},{16,17},{18,... | collective-permute-start | bytes 835592 | tf_op jit(solution)/shard_map/ppermute | solution.py:390
  6.9 0.0 collective-permute-done.1
  6.9 0.0 copy-done.2
  7.0 1.6 %collective-permute-start.2 = (s32[2,12]{1,0:T(2,128)S(1)}, s32[2,12]{1,0:T(2,128)S(1)}, u32[]{:S(2)}, u32[]{:S(2)}) collective-permute-start(s32[2,12]{1,0:T(2,128)S(1)} %pad_add_fusion.1), channel_id=1, source_target_pairs={{0,4},{2,6},{4,0},{6,2},{8,12},{10,14},{12,8},{14,10},{1,5},{3,7},... | collective-permute-start | bytes 296 | tf_op jit(solution)/shard_map/ppermute | solution.py:370
  8.6 0.1 pad_add_fusion.2.where
  8.7 1.9 %collective-permute-done.2 = s32[2,12]{1,0:T(2,128)S(1)} collective-permute-done((s32[2,12]{1,0:T(2,128)S(1)}, s32[2,12]{1,0:T(2,128)S(1)}, u32[]{:S(2)}, u32[]{:S(2)}) %collective-permute-start.2) | collective-permute-done | bytes 128 | tf_op jit(solution)/shard_map/ppermute | solution.py:370
  10.6 2.7 %collective-permute-start.3 = (s32[4,12]{1,0:T(4,128)S(1)}, s32[4,12]{1,0:T(4,128)S(1)}, u32[]{:S(2)}, u32[]{:S(2)}) collective-permute-start(s32[4,12]{1,0:T(4,128)S(1)} %pad_add_fusion.refs_0_), channel_id=1, source_target_pairs={{0,8},{2,10},{4,12},{6,14},{8,0},{10,2},{12,4},{14,6},{1,9},{3,11}... | collective-permute-start | bytes 584 | tf_op jit(solution)/shard_map/ppermute | solution.py:370
  13.3 2.5 %own.1 = (f32[128,1024]{1,0:T(8,128)S(1)}, bf16[64,1024]{1,0:T(8,128)(2,1)S(1)}, f32[64,1024]{1,0:T(8,128)S(1)}, bf16[64,256]{1,0:T(8,128)(2,1)S(1)}) custom-call(bf16[64,6144]{1,0:T(8,128)(2,1)S(1)} %get-tuple-element.22.traces, f32[33,64]{1,0:T(8,128)S(1)} %get-tuple-element.23.taps, bf16[1024,1024]{1,0:T(8,128)(2,1)S(1)} %get-tuple-element.24.table), custom_call_target="tpu_custom_call" | custom-call | tf_op jit(solution)/shard_map/own/pallas_call | solution.py:399
  15.8 0.0 collective-permute-done.3.refs_1_
  15.8 0.0 copy-done
  15.8 0.0 copy-done.1
  15.8 1.1 %picks.1 = bf16[320,192]{1,0:T(8,128)(2,1)S(1)} custom-call(s32[2]{0:T(128)S(1)} %pad_add_fusion.2.where, s32[8]{0:T(128)S(1)} %copy-done.1, s32[8,36]{1,0:T(8,128)S(1)} %copy-done, s32[4,12]{1,0:T(4,128)S(1)} %pad_add_fusion.refs_0_, s32[4,12]{1,0:T(4,128)S(1)} %collective-permute-done.3.refs_1_), custom_call_target="tpu_custom_call" | custom-call | tf_op jit(solution)/shard_map/picks/pallas_call | solution.py:418
  16.8 0.0 collective-permute-done.halo
  16.9 2.6 %rest.1 = (bf16[160,1024]{1,0:T(8,128)(2,1)S(1)}, bf16[160,1024]{1,0:T(8,128)(2,1)S(1)}, bf16[96,1024]{1,0:T(8,128)(2,1)S(1)}, bf16[96,1024]{1,0:T(8,128)(2,1)S(1)}) custom-call(s32[2]{0:T(128)S(1)} %pad_add_fusion.2.where, bf16[64,2176]{1,0:T(8,128)(2,1)S(1)} %collective-permute-done.halo, bf16[64,256]{1,0:T(8,128)(2,1)S(1)} %get-tuple-element.25.ends, ...), custom_call_target="tpu_custom_call" | custom-call | tf_op jit(solution)/shard_map/rest/pallas_call | solution.py:427
  19.4 0.1 collective-permute-start.5
  19.5 1.6 %collective-permute-done.5 = bf16[160,1024]{1,0:T(8,128)(2,1)S(1)} collective-permute-done((bf16[160,1024]{1,0:T(8,128)(2,1)S(1)}, bf16[160,1024]{1,0:T(8,128)(2,1)S(1)}, u32[]{:S(2)}, u32[]{:S(2)}) %collective-permute-start.5) | collective-permute-done | bytes 327712 | tf_op jit(solution)/shard_map/ppermute | solution.py:370
  21.1 0.1 add.15
  21.3 1.6 %collective-permute-start.7 = (bf16[40,1024]{1,0:T(8,128)(2,1)S(1)}, bf16[40,1024]{1,0:T(8,128)(2,1)S(1)}, u32[]{:S(2)}, u32[]{:S(2)}) collective-permute-start(bf16[40,1024]{1,0:T(8,128)(2,1)S(1)} %get-tuple-element.35), channel_id=1, source_target_pairs={{0,4},{2,6},{4,0},{6,2},{8,12},{10,14},{12,8},{14,10},{1,5},{3,7},... | collective-permute-start | bytes 245768 | tf_op jit(solution)/shard_map/ppermute | solution.py:370
  22.9 0.5 %collective-permute-start.6 = (bf16[40,1024]{1,0:T(8,128)(2,1)S(1)}, bf16[40,1024]{1,0:T(8,128)(2,1)S(1)}, u32[]{:S(2)}, u32[]{:S(2)}) collective-permute-start(bf16[40,1024]{1,0:T(8,128)(2,1)S(1)} %get-tuple-element.33), channel_id=1, source_target_pairs={{0,4},{2,6},{4,0},{6,2},{8,12},{10,14},{12,8},{14,10},{1,5},{3,7},... | collective-permute-start | bytes 245768 | tf_op jit(solution)/shard_map/ppermute | solution.py:370
  23.3 2.9 %collective-permute-done.7 = bf16[40,1024]{1,0:T(8,128)(2,1)S(1)} collective-permute-done((bf16[40,1024]{1,0:T(8,128)(2,1)S(1)}, bf16[40,1024]{1,0:T(8,128)(2,1)S(1)}, u32[]{:S(2)}, u32[]{:S(2)}) %collective-permute-start.7) | collective-permute-done | bytes 81952 | tf_op jit(solution)/shard_map/ppermute | solution.py:370
  26.3 2.0 %collective-permute-start.8 = (bf16[24,1024]{1,0:T(8,128)(2,1)S(1)}, bf16[24,1024]{1,0:T(8,128)(2,1)S(1)}, u32[]{:S(2)}, u32[]{:S(2)}) collective-permute-start(bf16[24,1024]{1,0:T(8,128)(2,1)S(1)} %slice.37), channel_id=1, source_target_pairs={{0,8},{2,10},{4,12},{6,14},{8,0},{10,2},{12,4},{14,6},{1,9},{3,11}... | collective-permute-start | bytes 147464 | tf_op jit(solution)/shard_map/ppermute | solution.py:370
  28.3 0.0 collective-permute-start.4
  28.3 1.0 %collective-permute-start.10 = (bf16[16,1024]{1,0:T(8,128)(2,1)S(1)}, bf16[16,1024]{1,0:T(8,128)(2,1)S(1)}, u32[]{:S(2)}, u32[]{:S(2)}) collective-permute-start(bf16[16,1024]{1,0:T(8,128)(2,1)S(1)} %slice.39), channel_id=1, source_target_pairs={{0,8},{2,10},{4,12},{6,14},{8,0},{10,2},{12,4},{14,6},{1,9},{3,11}... | collective-permute-start | bytes 98312 | tf_op jit(solution)/shard_map/ppermute | solution.py:370
  29.3 0.0 collective-permute-done.6
  29.3 2.0 %collective-permute-done.8 = bf16[24,1024]{1,0:T(8,128)(2,1)S(1)} collective-permute-done((bf16[24,1024]{1,0:T(8,128)(2,1)S(1)}, bf16[24,1024]{1,0:T(8,128)(2,1)S(1)}, u32[]{:S(2)}, u32[]{:S(2)}) %collective-permute-start.8) | collective-permute-done | bytes 49184 | tf_op jit(solution)/shard_map/ppermute | solution.py:370
  31.4 0.1 collective-permute-start.9
  31.5 1.7 %collective-permute-done.10 = bf16[16,1024]{1,0:T(8,128)(2,1)S(1)} collective-permute-done((bf16[16,1024]{1,0:T(8,128)(2,1)S(1)}, bf16[16,1024]{1,0:T(8,128)(2,1)S(1)}, u32[]{:S(2)}, u32[]{:S(2)}) %collective-permute-start.10) | collective-permute-done | bytes 32800 | tf_op jit(solution)/shard_map/ppermute | solution.py:370
  33.2 2.0 %collective-permute-start.11 = (bf16[16,1024]{1,0:T(8,128)(2,1)S(1)}, bf16[16,1024]{1,0:T(8,128)(2,1)S(1)}, u32[]{:S(2)}, u32[]{:S(2)}) collective-permute-start(bf16[16,1024]{1,0:T(8,128)(2,1)S(1)} %slice_add_fusion.1.refs_2_), channel_id=1, source_target_pairs={{0,1},{1,0},{2,3},{3,2},{4,5},{5,4},{6,7},{7,6},{8,9},{9,8},{10,11... | collective-permute-start | bytes 98312 | tf_op jit(solution)/shard_map/ppermute | solution.py:370
  35.2 0.8 %correlate.2.refs_3_ = f32[12,32,1024]{2,1,0:T(8,128)S(1)} custom-call(bf16[3,32,1024]{2,1,0:T(8,128)(2,1)S(1)} %bitcast.6, bf16[24,1024]{1,0:T(8,128)(2,1)S(1)} %slice_add_fusion.refs_1_, bf16[16,1024]{1,0:T(8,128)(2,1)S(1)} %slice_add_fusion.1.refs_2_), custom_call_target="tpu_custom_call" | custom-call | tf_op jit(solution)/shard_map/correlate/pallas_call | solution.py:345
  35.9 0.0 collective-permute-done.4
  35.9 1.1 %collective-permute-done.11.refs_2_ = bf16[16,1024]{1,0:T(8,128)(2,1)S(1)} collective-permute-done((bf16[16,1024]{1,0:T(8,128)(2,1)S(1)}, bf16[16,1024]{1,0:T(8,128)(2,1)S(1)}, u32[]{:S(2)}, u32[]{:S(2)}) %collective-permute-start.11) | collective-permute-done | bytes 32800 | tf_op jit(solution)/shard_map/ppermute | solution.py:370
  37.1 0.0 collective-permute-done.9.refs_1_
  37.1 1.6 %correlate.3 = f32[12,32,1024]{2,1,0:T(8,128)} custom-call(bf16[3,32,1024]{2,1,0:T(8,128)(2,1)S(1)} %bitcast.7, bf16[24,1024]{1,0:T(8,128)(2,1)S(1)} %collective-permute-done.9.refs_1_, bf16[16,1024]{1,0:T(8,128)(2,1)S(1)} %collective-permute-done.11.refs_2_, f32[12,32,1024]{2,1,0:T(8,128)S(1)} %correlate.2.refs_3_), custom_call_target="tpu_custom_call" | custom-call | tf_op jit(solution)/shard_map/correlate/pallas_call | solution.py:345
  (9 shorter events, 0.1 us)
Async XLA Ops:
  0.0 6.9 %copy-start.2 = (s32[1,12]{1,0:T(1,128)S(1)}, s32[1,12]{1,0:T(1,128)}, u32[]{:S(2)}) copy-start(s32[1,12]{1,0:T(1,128)} %param.10) | copy-start | bytes 148
  0.0 6.9 %collective-permute-start.1 = (s32[1,12]{1,0:T(1,128)}, s32[1,12]{1,0:T(1,128)S(1)}, u32[]{:S(2)}, u32[]{:S(2)}) collective-permute-start(s32[1,12]{1,0:T(1,128)} %param.10), channel_id=1, source_target_pairs={{0,2},{2,0},{4,6},{6,4},{8,10},{10,8},{12,14},{14,12},{1,3},{3,1},... | collective-permute-start | bytes 152 | tf_op jit(solution)/shard_map/ppermute | solution.py:370
  2.5 13.3 %copy-start = (s32[8,36]{1,0:T(8,128)S(1)}, s32[8,36]{1,0:T(8,128)}, u32[]{:S(2)}) copy-start(s32[8,36]{1,0:T(8,128)} %slots.1) | copy-start | bytes 3460
  2.5 13.3 %copy-start.1 = (s32[8]{0:T(128)S(1)}, s32[8]{0:T(128)}, u32[]{:S(2)}) copy-start(s32[8]{0:T(128)} %counts.1) | copy-start | bytes 100
  2.5 14.3 %collective-permute-start = (bf16[64,2176]{1,0:T(8,128)(2,1)S(1)}, bf16[64,2176]{1,0:T(8,128)(2,1)S(1)}, u32[]{:S(2)}, u32[]{:S(2)}) collective-permute-start(bf16[64,2176]{1,0:T(8,128)(2,1)S(1)} %get-tuple-element.21), channel_id=1, source_target_pairs={{0,1},{2,3},{4,5},{6,7},{8,9},{10,11},{12,13},{14,15},{16,17},{18,... | collective-permute-start | bytes 835592 | tf_op jit(solution)/shard_map/ppermute | solution.py:390
  7.0 3.6 %collective-permute-start.2 = (s32[2,12]{1,0:T(2,128)S(1)}, s32[2,12]{1,0:T(2,128)S(1)}, u32[]{:S(2)}, u32[]{:S(2)}) collective-permute-start(s32[2,12]{1,0:T(2,128)S(1)} %pad_add_fusion.1), channel_id=1, source_target_pairs={{0,4},{2,6},{4,0},{6,2},{8,12},{10,14},{12,8},{14,10},{1,5},{3,7},... | collective-permute-start | bytes 296 | tf_op jit(solution)/shard_map/ppermute | solution.py:370
  10.6 5.1 %collective-permute-start.3 = (s32[4,12]{1,0:T(4,128)S(1)}, s32[4,12]{1,0:T(4,128)S(1)}, u32[]{:S(2)}, u32[]{:S(2)}) collective-permute-start(s32[4,12]{1,0:T(4,128)S(1)} %pad_add_fusion.refs_0_), channel_id=1, source_target_pairs={{0,8},{2,10},{4,12},{6,14},{8,0},{10,2},{12,4},{14,6},{1,9},{3,11}... | collective-permute-start | bytes 584 | tf_op jit(solution)/shard_map/ppermute | solution.py:370
  19.4 1.7 %collective-permute-start.5 = (bf16[160,1024]{1,0:T(8,128)(2,1)S(1)}, bf16[160,1024]{1,0:T(8,128)(2,1)S(1)}, u32[]{:S(2)}, u32[]{:S(2)}) collective-permute-start(bf16[160,1024]{1,0:T(8,128)(2,1)S(1)} %get-tuple-element.31), channel_id=1, source_target_pairs={{0,2},{2,0},{4,6},{6,4},{8,10},{10,8},{12,14},{14,12},{1,3},{3,1},... | collective-permute-start | bytes 983048 | tf_op jit(solution)/shard_map/ppermute | solution.py:370
  21.3 5.0 %collective-permute-start.7 = (bf16[40,1024]{1,0:T(8,128)(2,1)S(1)}, bf16[40,1024]{1,0:T(8,128)(2,1)S(1)}, u32[]{:S(2)}, u32[]{:S(2)}) collective-permute-start(bf16[40,1024]{1,0:T(8,128)(2,1)S(1)} %get-tuple-element.35), channel_id=1, source_target_pairs={{0,4},{2,6},{4,0},{6,2},{8,12},{10,14},{12,8},{14,10},{1,5},{3,7},... | collective-permute-start | bytes 245768 | tf_op jit(solution)/shard_map/ppermute | solution.py:370
  22.9 6.4 %collective-permute-start.6 = (bf16[40,1024]{1,0:T(8,128)(2,1)S(1)}, bf16[40,1024]{1,0:T(8,128)(2,1)S(1)}, u32[]{:S(2)}, u32[]{:S(2)}) collective-permute-start(bf16[40,1024]{1,0:T(8,128)(2,1)S(1)} %get-tuple-element.33), channel_id=1, source_target_pairs={{0,4},{2,6},{4,0},{6,2},{8,12},{10,14},{12,8},{14,10},{1,5},{3,7},... | collective-permute-start | bytes 245768 | tf_op jit(solution)/shard_map/ppermute | solution.py:370
  26.3 5.1 %collective-permute-start.8 = (bf16[24,1024]{1,0:T(8,128)(2,1)S(1)}, bf16[24,1024]{1,0:T(8,128)(2,1)S(1)}, u32[]{:S(2)}, u32[]{:S(2)}) collective-permute-start(bf16[24,1024]{1,0:T(8,128)(2,1)S(1)} %slice.37), channel_id=1, source_target_pairs={{0,8},{2,10},{4,12},{6,14},{8,0},{10,2},{12,4},{14,6},{1,9},{3,11}... | collective-permute-start | bytes 147464 | tf_op jit(solution)/shard_map/ppermute | solution.py:370
  28.3 7.6 %collective-permute-start.4 = (bf16[96,1024]{1,0:T(8,128)(2,1)S(1)}, bf16[96,1024]{1,0:T(8,128)(2,1)S(1)}, u32[]{:S(2)}, u32[]{:S(2)}) collective-permute-start(bf16[96,1024]{1,0:T(8,128)(2,1)S(1)} %get-tuple-element.29), channel_id=1, source_target_pairs={{0,1},{1,0},{2,3},{3,2},{4,5},{5,4},{6,7},{7,6},{8,9},{9,8},{10,11... | collective-permute-start | bytes 589832 | tf_op jit(solution)/shard_map/ppermute | solution.py:370
  28.3 4.8 %collective-permute-start.10 = (bf16[16,1024]{1,0:T(8,128)(2,1)S(1)}, bf16[16,1024]{1,0:T(8,128)(2,1)S(1)}, u32[]{:S(2)}, u32[]{:S(2)}) collective-permute-start(bf16[16,1024]{1,0:T(8,128)(2,1)S(1)} %slice.39), channel_id=1, source_target_pairs={{0,8},{2,10},{4,12},{6,14},{8,0},{10,2},{12,4},{14,6},{1,9},{3,11}... | collective-permute-start | bytes 98312 | tf_op jit(solution)/shard_map/ppermute | solution.py:370
  31.4 5.7 %collective-permute-start.9 = (bf16[24,1024]{1,0:T(8,128)(2,1)S(1)}, bf16[24,1024]{1,0:T(8,128)(2,1)S(1)}, u32[]{:S(2)}, u32[]{:S(2)}) collective-permute-start(bf16[24,1024]{1,0:T(8,128)(2,1)S(1)} %slice_add_fusion.refs_1_), channel_id=1, source_target_pairs={{0,1},{1,0},{2,3},{3,2},{4,5},{5,4},{6,7},{7,6},{8,9},{9,8},{10,11... | collective-permute-start | bytes 147464 | tf_op jit(solution)/shard_map/ppermute | solution.py:370
  33.2 3.9 %collective-permute-start.11 = (bf16[16,1024]{1,0:T(8,128)(2,1)S(1)}, bf16[16,1024]{1,0:T(8,128)(2,1)S(1)}, u32[]{:S(2)}, u32[]{:S(2)}) collective-permute-start(bf16[16,1024]{1,0:T(8,128)(2,1)S(1)} %slice_add_fusion.1.refs_2_), channel_id=1, source_target_pairs={{0,1},{1,0},{2,3},{3,2},{4,5},{5,4},{6,7},{7,6},{8,9},{9,8},{10,11... | collective-permute-start | bytes 98312 | tf_op jit(solution)/shard_map/ppermute | solution.py:370
where the time goes:
time: 38.8 us; the launch traced here: 38.6 us
  starting transfers between devices  16.5 us (43%)
  waiting for transfers between devices  11.3 us (29%)
  Pallas kernels  10.4 us (27%)
    ppermute x11, starting transfers between devices, across(): return lax.ppermute(x, axis, [(i, i ^ distance) for i in range(size)])  12 us
    ppermute x11, waiting for transfers between devices, across(): return lax.ppermute(x, axis, [(i, i ^ distance) for i in range(size)])  11.3 us
    ppermute x1, starting transfers between devices, shards(): halo = lax.ppermute(tail, 'tm', [(i - 1, i) for i in range(1, times)])  4.41 us
    pallas_call x1, Pallas kernels, shards(): pl.pallas_call(functools.partial(rest_kernel, windows, times), out_shape=...  2.56 us
    pallas_call x1, Pallas kernels, shards(): pl.pallas_call(functools.partial(own_kernel, windows), out_shape=[jax.Sha...  2.48 us
    pallas_call x2, Pallas kernels, correlate(): pl.pallas_call(functools.partial(correlate_kernel, windows, factor, count...  2.32 us
    pallas_call x1, Pallas kernels, shards(): pl.pallas_call(head_kernel, out_shape=[jax.ShapeDtypeStruct((channels, HA...  1.98 us
    pallas_call x1, Pallas kernels, shards(): pl.pallas_call(functools.partial(picks_kernel, shape), out_shape=jax.Shap...  1.05 us
  transfers between devices with their start and end apart: 12, of which 6 were waited for; matrix products, arithmetic and copies ran while one was open for 0% of the time, Pallas kernels for 16%

commit v1 on v0

--- a/solution.py
+++ b/solution.py
@@ -19,6 +19,7 @@
 F32 = jnp.float32
 BF16 = jnp.bfloat16
 LIMIT = 24 * 1024 * 1024
+HINT = 10**10
 
 
 def piece_table():
@@ -130,18 +131,21 @@
     lax.fori_loop(0, count // ROWS, step, 0, unroll=2)
 
 
-def head_kernel(traces_in, taps_in, table_in, tail, traces, taps, table, sems):
+def tail_kernel(traces, wanted, tail, ids, sems):
     start = traces.shape[1] - tail.shape[1]
     copies = [
-        pltpu.make_async_copy(traces_in.at[:, start:], tail, sems.at[0]),
-        pltpu.make_async_copy(traces_in, traces, sems.at[1]),
-        pltpu.make_async_copy(taps_in, taps, sems.at[2]),
-        pltpu.make_async_copy(table_in, table, sems.at[3]),
+        pltpu.make_async_copy(traces.at[:, start:], tail, sems.at[0]),
+        pltpu.make_async_copy(wanted, ids, sems.at[1]),
     ]
     for copy in copies:
         copy.start()
     for copy in copies:
         copy.wait()
+
+
+def pair_kernel(mine, other, out):
+    out[:1, :] = mine[...]
+    out[1:, :] = other[...]
 
 
 def own_kernel(windows, traces, taps, table, part, white, response, ends, square, shifted, spectra):
@@ -375,20 +379,36 @@
     params = pltpu.CompilerParams(vmem_limit_bytes=LIMIT)
     bits = [1 << b for b in range(chips.bit_length() - 1)]
 
-    other = across(block_sources, "chan", 1)
-    inputs = (traces, filter_taps.T, jnp.asarray(piece_table()))
-    tail, traces, taps, table = pl.pallas_call(
-        head_kernel,
-        out_shape=[jax.ShapeDtypeStruct((channels, HALF + 128), BF16)]
-        + [jax.ShapeDtypeStruct(a.shape, a.dtype) for a in inputs],
-        in_specs=[hbm] * 3,
-        out_specs=[vmem] * 4,
-        scratch_shapes=[pltpu.SemaphoreType.DMA((4,))],
+    tail, ids = pl.pallas_call(
+        tail_kernel,
+        out_shape=[
+            jax.ShapeDtypeStruct((channels, HALF + 128), BF16),
+            jax.ShapeDtypeStruct(block_sources.shape, jnp.int32),
+        ],
+        in_specs=[hbm] * 2,
+        out_specs=[vmem] * 2,
+        scratch_shapes=[pltpu.SemaphoreType.DMA((2,))],
         compiler_params=params,
-        name="head",
-    )(*(pltpu.with_memory_space_constraint(a, pltpu.HBM) for a in inputs))
+        name="tail",
+    )(*(pltpu.with_memory_space_constraint(a, pltpu.HBM) for a in (traces, block_sources)))
     halo = lax.ppermute(tail, "tm", [(i - 1, i) for i in range(1, times)])
-    wanted = [jnp.concatenate([block_sources, other], axis=0)]
+    other = across(ids, "chan", 1)
+    taps = filter_taps.T
+    traces, taps, table = (
+        pltpu.with_memory_space_constraint(a, pltpu.VMEM)
+        for a in (traces, taps, jnp.asarray(piece_table()))
+    )
+    wanted = [
+        pl.pallas_call(
+            pair_kernel,
+            out_shape=jax.ShapeDtypeStruct((2, pairs), jnp.int32),
+            in_specs=[vmem] * 2,
+            out_specs=vmem,
+            compiler_params=params,
+            cost_estimate=pl.CostEstimate(flops=HINT, bytes_accessed=8 * pairs, transcendentals=0),
+            name="pair",
+        )(ids, other)
+    ]
     for bit in bits:
         known = jnp.concatenate(wanted, axis=0)
         wanted = [known, across(known, "chan", 2 * bit)]

time: 38.8 us -> 37.9 us (0.977)
  Pallas kernels: 10.4 us -> 9.43 us
    pallas_call x1 -> x2, Pallas kernels: 1.98 us -> 0.98 us  [the longest x1 0.97 us: shards(): pl.pallas_call(tail_kernel, out_shape=[jax.ShapeDtypeStruct((channels, HA...]
  transfers between devices with their start and end apart: 12 -> 12, of which waited for: 6 -> 6; matrix products, arithmetic and copies ran while one was open for 0% -> 0% of each run, Pallas kernels for 16% -> 11%
where the time goes in v1:
time: 37.9 us; the launch traced here: 37.8 us
  starting transfers between devices  16.5 us (44%)
  waiting for transfers between devices  11.3 us (30%)
  Pallas kernels  9.43 us (25%)
    ppermute x11, starting transfers between devices, across(): return lax.ppermute(x, axis, [(i, i ^ distance) for i in range(size)])  12.1 us
    ppermute x11, waiting for transfers between devices, across(): return lax.ppermute(x, axis, [(i, i ^ distance) for i in range(size)])  11.3 us
    ppermute x1, starting transfers between devices, shards(): halo = lax.ppermute(tail, 'tm', [(i - 1, i) for i in range(1, times)])  4.41 us
    pallas_call x1, Pallas kernels, shards(): pl.pallas_call(functools.partial(rest_kernel, windows, times), out_shape=...  2.57 us
    pallas_call x1, Pallas kernels, shards(): pl.pallas_call(functools.partial(own_kernel, windows), out_shape=[jax.Sha...  2.5 us
    pallas_call x2, Pallas kernels, correlate(): pl.pallas_call(functools.partial(correlate_kernel, windows, factor, count...  2.32 us
    pallas_call x1, Pallas kernels, shards(): pl.pallas_call(functools.partial(picks_kernel, shape), out_shape=jax.Shap...  1.05 us
    pallas_call x1, Pallas kernels, shards(): pl.pallas_call(tail_kernel, out_shape=[jax.ShapeDtypeStruct((channels, HA...  0.97 us
  transfers between devices with their start and end apart: 12, of which 6 were waited for; matrix products, arithmetic and copies ran while one was open for 0% of the time, Pallas kernels for 11%

profile of v1, /device:TPU:0, one launch (start us, length us, event | category | flops | bytes accessed | tf_op | source)
XLA Modules:
  0.0 37.8 jit_solution(1553532107262918794)
XLA Ops:
  0.0 1.0 %tail.1 = (bf16[64,2176]{1,0:T(8,128)(2,1)S(1)}, s32[1,12]{1,0:T(1,128)S(1)}) custom-call(bf16[64,6144]{1,0:T(8,128)(2,1)} %traces.3, s32[1,12]{1,0:T(1,128)} %wanted.1), custom_call_target="tpu_custom_call" | custom-call | tf_op jit(solution)/shard_map/tail/pallas_call | solution.py:382
  1.0 0.6 %collective-permute-start.1 = (s32[1,12]{1,0:T(1,128)S(1)}, s32[1,12]{1,0:T(1,128)S(1)}, u32[]{:S(2)}, u32[]{:S(2)}) collective-permute-start(s32[1,12]{1,0:T(1,128)S(1)} %get-tuple-element.24.mine), channel_id=1, source_target_pairs={{0,2},{2,0},{4,6},{6,4},{8,10},{10,8},{12,14},{14,12},{1,3},{3,1},... | collective-permute-start | bytes 152 | tf_op jit(solution)/shard_map/ppermute | solution.py:374
  1.5 4.4 %collective-permute-start = (bf16[64,2176]{1,0:T(8,128)(2,1)S(1)}, bf16[64,2176]{1,0:T(8,128)(2,1)S(1)}, u32[]{:S(2)}, u32[]{:S(2)}) collective-permute-start(bf16[64,2176]{1,0:T(8,128)(2,1)S(1)} %get-tuple-element.19), channel_id=1, source_target_pairs={{0,1},{2,3},{4,5},{6,7},{8,9},{10,11},{12,13},{14,15},{16,17},{18,... | collective-permute-start | bytes 835592 | tf_op jit(solution)/shard_map/ppermute | solution.py:394
  6.0 0.0 copy-start
  6.0 0.0 copy-start.1
  6.0 0.0 copy-start.2
  6.0 0.0 collective-permute-done.1.other
  6.0 0.0 copy-start.3
  6.0 0.0 copy-start.4
  6.0 1.6 %collective-permute-start.2 = (s32[2,12]{1,0:T(2,128)S(1)}, s32[2,12]{1,0:T(2,128)S(1)}, u32[]{:S(2)}, u32[]{:S(2)}) collective-permute-start(s32[2,12]{1,0:T(2,128)S(1)} %pair.1), channel_id=1, source_target_pairs={{0,4},{2,6},{4,0},{6,2},{8,12},{10,14},{12,8},{14,10},{1,5},{3,7},... | collective-permute-start | bytes 296 | tf_op jit(solution)/shard_map/ppermute | solution.py:374
  7.7 0.1 pad_add_fusion.1.where
  7.8 1.9 %collective-permute-done.2 = s32[2,12]{1,0:T(2,128)S(1)} collective-permute-done((s32[2,12]{1,0:T(2,128)S(1)}, s32[2,12]{1,0:T(2,128)S(1)}, u32[]{:S(2)}, u32[]{:S(2)}) %collective-permute-start.2) | collective-permute-done | bytes 128 | tf_op jit(solution)/shard_map/ppermute | solution.py:374
  9.7 2.6 %collective-permute-start.3 = (s32[4,12]{1,0:T(4,128)S(1)}, s32[4,12]{1,0:T(4,128)S(1)}, u32[]{:S(2)}, u32[]{:S(2)}) collective-permute-start(s32[4,12]{1,0:T(4,128)S(1)} %pad_add_fusion.refs_0_), channel_id=1, source_target_pairs={{0,8},{2,10},{4,12},{6,14},{8,0},{10,2},{12,4},{14,6},{1,9},{3,11}... | collective-permute-start | bytes 584 | tf_op jit(solution)/shard_map/ppermute | solution.py:374
  12.3 0.0 copy-done
  12.3 0.0 copy-done.1
  12.3 0.0 copy-done.2
  12.4 2.5 %own.1 = (f32[128,1024]{1,0:T(8,128)S(1)}, bf16[64,1024]{1,0:T(8,128)(2,1)S(1)}, f32[64,1024]{1,0:T(8,128)S(1)}, bf16[64,256]{1,0:T(8,128)(2,1)S(1)}) custom-call(bf16[64,6144]{1,0:T(8,128)(2,1)S(1)} %copy-done.1, f32[33,64]{1,0:T(8,128)S(1)} %bitcast.8, bf16[1024,1024]{1,0:T(8,128)(2,1)S(1)} %copy-done), custom_call_target="tpu_custom_call" | custom-call | tf_op jit(solution)/shard_map/own/pallas_call | solution.py:419
  14.9 0.0 collective-permute-done.3.refs_1_
  14.9 0.0 copy-done.3
  14.9 0.0 copy-done.4
  14.9 1.1 %picks.1 = bf16[320,192]{1,0:T(8,128)(2,1)S(1)} custom-call(s32[2]{0:T(128)S(1)} %pad_add_fusion.1.where, s32[8]{0:T(128)S(1)} %copy-done.4, s32[8,36]{1,0:T(8,128)S(1)} %copy-done.3, s32[4,12]{1,0:T(4,128)S(1)} %pad_add_fusion.refs_0_, s32[4,12]{1,0:T(4,128)S(1)} %collective-permute-done.3.refs_1_), custom_call_target="tpu_custom_call" | custom-call | tf_op jit(solution)/shard_map/picks/pallas_call | solution.py:438
  15.9 0.0 collective-permute-done.halo
  16.0 2.6 %rest.1 = (bf16[160,1024]{1,0:T(8,128)(2,1)S(1)}, bf16[160,1024]{1,0:T(8,128)(2,1)S(1)}, bf16[96,1024]{1,0:T(8,128)(2,1)S(1)}, bf16[96,1024]{1,0:T(8,128)(2,1)S(1)}) custom-call(s32[2]{0:T(128)S(1)} %pad_add_fusion.1.where, bf16[64,2176]{1,0:T(8,128)(2,1)S(1)} %collective-permute-done.halo, bf16[64,256]{1,0:T(8,128)(2,1)S(1)} %get-tuple-element.20.ends, ...), custom_call_target="tpu_custom_call" | custom-call | tf_op jit(solution)/shard_map/rest/pallas_call | solution.py:447
  18.5 0.1 collective-permute-start.5
  18.6 1.6 %collective-permute-done.5 = bf16[160,1024]{1,0:T(8,128)(2,1)S(1)} collective-permute-done((bf16[160,1024]{1,0:T(8,128)(2,1)S(1)}, bf16[160,1024]{1,0:T(8,128)(2,1)S(1)}, u32[]{:S(2)}, u32[]{:S(2)}) %collective-permute-start.5) | collective-permute-done | bytes 327712 | tf_op jit(solution)/shard_map/ppermute | solution.py:374
  20.2 0.1 add.15
  20.4 1.6 %collective-permute-start.7 = (bf16[40,1024]{1,0:T(8,128)(2,1)S(1)}, bf16[40,1024]{1,0:T(8,128)(2,1)S(1)}, u32[]{:S(2)}, u32[]{:S(2)}) collective-permute-start(bf16[40,1024]{1,0:T(8,128)(2,1)S(1)} %get-tuple-element.31), channel_id=1, source_target_pairs={{0,4},{2,6},{4,0},{6,2},{8,12},{10,14},{12,8},{14,10},{1,5},{3,7},... | collective-permute-start | bytes 245768 | tf_op jit(solution)/shard_map/ppermute | solution.py:374
  22.0 0.4 %collective-permute-start.6 = (bf16[40,1024]{1,0:T(8,128)(2,1)S(1)}, bf16[40,1024]{1,0:T(8,128)(2,1)S(1)}, u32[]{:S(2)}, u32[]{:S(2)}) collective-permute-start(bf16[40,1024]{1,0:T(8,128)(2,1)S(1)} %get-tuple-element.29), channel_id=1, source_target_pairs={{0,4},{2,6},{4,0},{6,2},{8,12},{10,14},{12,8},{14,10},{1,5},{3,7},... | collective-permute-start | bytes 245768 | tf_op jit(solution)/shard_map/ppermute | solution.py:374
  22.5 2.9 %collective-permute-done.7 = bf16[40,1024]{1,0:T(8,128)(2,1)S(1)} collective-permute-done((bf16[40,1024]{1,0:T(8,128)(2,1)S(1)}, bf16[40,1024]{1,0:T(8,128)(2,1)S(1)}, u32[]{:S(2)}, u32[]{:S(2)}) %collective-permute-start.7) | collective-permute-done | bytes 81952 | tf_op jit(solution)/shard_map/ppermute | solution.py:374
  25.4 2.0 %collective-permute-start.8 = (bf16[24,1024]{1,0:T(8,128)(2,1)S(1)}, bf16[24,1024]{1,0:T(8,128)(2,1)S(1)}, u32[]{:S(2)}, u32[]{:S(2)}) collective-permute-start(bf16[24,1024]{1,0:T(8,128)(2,1)S(1)} %slice.37), channel_id=1, source_target_pairs={{0,8},{2,10},{4,12},{6,14},{8,0},{10,2},{12,4},{14,6},{1,9},{3,11}... | collective-permute-start | bytes 147464 | tf_op jit(solution)/shard_map/ppermute | solution.py:374
  27.4 0.0 collective-permute-start.4
  27.4 1.0 %collective-permute-start.10 = (bf16[16,1024]{1,0:T(8,128)(2,1)S(1)}, bf16[16,1024]{1,0:T(8,128)(2,1)S(1)}, u32[]{:S(2)}, u32[]{:S(2)}) collective-permute-start(bf16[16,1024]{1,0:T(8,128)(2,1)S(1)} %slice.39), channel_id=1, source_target_pairs={{0,8},{2,10},{4,12},{6,14},{8,0},{10,2},{12,4},{14,6},{1,9},{3,11}... | collective-permute-start | bytes 98312 | tf_op jit(solution)/shard_map/ppermute | solution.py:374
  28.4 0.0 collective-permute-done.6
  28.4 2.0 %collective-permute-done.8 = bf16[24,1024]{1,0:T(8,128)(2,1)S(1)} collective-permute-done((bf16[24,1024]{1,0:T(8,128)(2,1)S(1)}, bf16[24,1024]{1,0:T(8,128)(2,1)S(1)}, u32[]{:S(2)}, u32[]{:S(2)}) %collective-permute-start.8) | collective-permute-done | bytes 49184 | tf_op jit(solution)/shard_map/ppermute | solution.py:374
  30.5 0.1 collective-permute-start.9
  30.6 1.7 %collective-permute-done.10 = bf16[16,1024]{1,0:T(8,128)(2,1)S(1)} collective-permute-done((bf16[16,1024]{1,0:T(8,128)(2,1)S(1)}, bf16[16,1024]{1,0:T(8,128)(2,1)S(1)}, u32[]{:S(2)}, u32[]{:S(2)}) %collective-permute-start.10) | collective-permute-done | bytes 32800 | tf_op jit(solution)/shard_map/ppermute | solution.py:374
  32.3 2.0 %collective-permute-start.11 = (bf16[16,1024]{1,0:T(8,128)(2,1)S(1)}, bf16[16,1024]{1,0:T(8,128)(2,1)S(1)}, u32[]{:S(2)}, u32[]{:S(2)}) collective-permute-start(bf16[16,1024]{1,0:T(8,128)(2,1)S(1)} %slice_add_fusion.1.refs_2_), channel_id=1, source_target_pairs={{0,1},{1,0},{2,3},{3,2},{4,5},{5,4},{6,7},{7,6},{8,9},{9,8},{10,11... | collective-permute-start | bytes 98312 | tf_op jit(solution)/shard_map/ppermute | solution.py:374
  34.3 0.8 %correlate.2.refs_3_ = f32[12,32,1024]{2,1,0:T(8,128)S(1)} custom-call(bf16[3,32,1024]{2,1,0:T(8,128)(2,1)S(1)} %bitcast.6, bf16[24,1024]{1,0:T(8,128)(2,1)S(1)} %slice_add_fusion.refs_1_, bf16[16,1024]{1,0:T(8,128)(2,1)S(1)} %slice_add_fusion.1.refs_2_), custom_call_target="tpu_custom_call" | custom-call | tf_op jit(solution)/shard_map/correlate/pallas_call | solution.py:349
  35.1 0.0 collective-permute-done.4
  35.1 1.1 %collective-permute-done.11.refs_2_ = bf16[16,1024]{1,0:T(8,128)(2,1)S(1)} collective-permute-done((bf16[16,1024]{1,0:T(8,128)(2,1)S(1)}, bf16[16,1024]{1,0:T(8,128)(2,1)S(1)}, u32[]{:S(2)}, u32[]{:S(2)}) %collective-permute-start.11) | collective-permute-done | bytes 32800 | tf_op jit(solution)/shard_map/ppermute | solution.py:374
  36.2 0.0 collective-permute-done.9.refs_1_
  36.2 1.6 %correlate.3 = f32[12,32,1024]{2,1,0:T(8,128)} custom-call(bf16[3,32,1024]{2,1,0:T(8,128)(2,1)S(1)} %bitcast.7, bf16[24,1024]{1,0:T(8,128)(2,1)S(1)} %collective-permute-done.9.refs_1_, bf16[16,1024]{1,0:T(8,128)(2,1)S(1)} %collective-permute-done.11.refs_2_, f32[12,32,1024]{2,1,0:T(8,128)S(1)} %correlate.2.refs_3_), custom_call_target="tpu_custom_call" | custom-call | tf_op jit(solution)/shard_map/correlate/pallas_call | solution.py:349
  (9 shorter events, 0.1 us)
Async XLA Ops:
  1.0 5.0 %collective-permute-start.1 = (s32[1,12]{1,0:T(1,128)S(1)}, s32[1,12]{1,0:T(1,128)S(1)}, u32[]{:S(2)}, u32[]{:S(2)}) collective-permute-start(s32[1,12]{1,0:T(1,128)S(1)} %get-tuple-element.24.mine), channel_id=1, source_target_pairs={{0,2},{2,0},{4,6},{6,4},{8,10},{10,8},{12,14},{14,12},{1,3},{3,1},... | collective-permute-start | bytes 152 | tf_op jit(solution)/shard_map/ppermute | solution.py:374
  1.5 14.4 %collective-permute-start = (bf16[64,2176]{1,0:T(8,128)(2,1)S(1)}, bf16[64,2176]{1,0:T(8,128)(2,1)S(1)}, u32[]{:S(2)}, u32[]{:S(2)}) collective-permute-start(bf16[64,2176]{1,0:T(8,128)(2,1)S(1)} %get-tuple-element.19), channel_id=1, source_target_pairs={{0,1},{2,3},{4,5},{6,7},{8,9},{10,11},{12,13},{14,15},{16,17},{18,... | collective-permute-start | bytes 835592 | tf_op jit(solution)/shard_map/ppermute | solution.py:394
  6.0 6.4 %copy-start = (bf16[1024,1024]{1,0:T(8,128)(2,1)S(1)}, bf16[1024,1024]{1,0:T(8,128)(2,1)}, u32[]{:S(2)}) copy-start(bf16[1024,1024]{1,0:T(8,128)(2,1)} %constant.10.clone.table) | copy-start | bytes 6291460
  6.0 6.4 %copy-start.1 = (bf16[64,6144]{1,0:T(8,128)(2,1)S(1)}, bf16[64,6144]{1,0:T(8,128)(2,1)}, u32[]{:S(2)}) copy-start(bf16[64,6144]{1,0:T(8,128)(2,1)} %traces.3) | copy-start | bytes 2359300
  6.0 6.4 %copy-start.2 = (f32[64,33]{0,1:T(8,128)S(1)}, f32[64,33]{0,1:T(8,128)}, u32[]{:S(2)}) copy-start(f32[64,33]{0,1:T(8,128)} %param.7) | copy-start | bytes 25348
  6.0 8.8 %copy-start.3 = (s32[8,36]{1,0:T(8,128)S(1)}, s32[8,36]{1,0:T(8,128)}, u32[]{:S(2)}) copy-start(s32[8,36]{1,0:T(8,128)} %slots.1) | copy-start | bytes 3460
  6.0 8.8 %copy-start.4 = (s32[8]{0:T(128)S(1)}, s32[8]{0:T(128)}, u32[]{:S(2)}) copy-start(s32[8]{0:T(128)} %counts.1) | copy-start | bytes 100
  6.0 3.6 %collective-permute-start.2 = (s32[2,12]{1,0:T(2,128)S(1)}, s32[2,12]{1,0:T(2,128)S(1)}, u32[]{:S(2)}, u32[]{:S(2)}) collective-permute-start(s32[2,12]{1,0:T(2,128)S(1)} %pair.1), channel_id=1, source_target_pairs={{0,4},{2,6},{4,0},{6,2},{8,12},{10,14},{12,8},{14,10},{1,5},{3,7},... | collective-permute-start | bytes 296 | tf_op jit(solution)/shard_map/ppermute | solution.py:374
  9.7 5.2 %collective-permute-start.3 = (s32[4,12]{1,0:T(4,128)S(1)}, s32[4,12]{1,0:T(4,128)S(1)}, u32[]{:S(2)}, u32[]{:S(2)}) collective-permute-start(s32[4,12]{1,0:T(4,128)S(1)} %pad_add_fusion.refs_0_), channel_id=1, source_target_pairs={{0,8},{2,10},{4,12},{6,14},{8,0},{10,2},{12,4},{14,6},{1,9},{3,11}... | collective-permute-start | bytes 584 | tf_op jit(solution)/shard_map/ppermute | solution.py:374
  18.5 1.7 %collective-permute-start.5 = (bf16[160,1024]{1,0:T(8,128)(2,1)S(1)}, bf16[160,1024]{1,0:T(8,128)(2,1)S(1)}, u32[]{:S(2)}, u32[]{:S(2)}) collective-permute-start(bf16[160,1024]{1,0:T(8,128)(2,1)S(1)} %get-tuple-element.27), channel_id=1, source_target_pairs={{0,2},{2,0},{4,6},{6,4},{8,10},{10,8},{12,14},{14,12},{1,3},{3,1},... | collective-permute-start | bytes 983048 | tf_op jit(solution)/shard_map/ppermute | solution.py:374
  20.4 5.0 %collective-permute-start.7 = (bf16[40,1024]{1,0:T(8,128)(2,1)S(1)}, bf16[40,1024]{1,0:T(8,128)(2,1)S(1)}, u32[]{:S(2)}, u32[]{:S(2)}) collective-permute-start(bf16[40,1024]{1,0:T(8,128)(2,1)S(1)} %get-tuple-element.31), channel_id=1, source_target_pairs={{0,4},{2,6},{4,0},{6,2},{8,12},{10,14},{12,8},{14,10},{1,5},{3,7},... | collective-permute-start | bytes 245768 | tf_op jit(solution)/shard_map/ppermute | solution.py:374
  22.0 6.4 %collective-permute-start.6 = (bf16[40,1024]{1,0:T(8,128)(2,1)S(1)}, bf16[40,1024]{1,0:T(8,128)(2,1)S(1)}, u32[]{:S(2)}, u32[]{:S(2)}) collective-permute-start(bf16[40,1024]{1,0:T(8,128)(2,1)S(1)} %get-tuple-element.29), channel_id=1, source_target_pairs={{0,4},{2,6},{4,0},{6,2},{8,12},{10,14},{12,8},{14,10},{1,5},{3,7},... | collective-permute-start | bytes 245768 | tf_op jit(solution)/shard_map/ppermute | solution.py:374
  25.4 5.1 %collective-permute-start.8 = (bf16[24,1024]{1,0:T(8,128)(2,1)S(1)}, bf16[24,1024]{1,0:T(8,128)(2,1)S(1)}, u32[]{:S(2)}, u32[]{:S(2)}) collective-permute-start(bf16[24,1024]{1,0:T(8,128)(2,1)S(1)} %slice.37), channel_id=1, source_target_pairs={{0,8},{2,10},{4,12},{6,14},{8,0},{10,2},{12,4},{14,6},{1,9},{3,11}... | collective-permute-start | bytes 147464 | tf_op jit(solution)/shard_map/ppermute | solution.py:374
  27.4 7.6 %collective-permute-start.4 = (bf16[96,1024]{1,0:T(8,128)(2,1)S(1)}, bf16[96,1024]{1,0:T(8,128)(2,1)S(1)}, u32[]{:S(2)}, u32[]{:S(2)}) collective-permute-start(bf16[96,1024]{1,0:T(8,128)(2,1)S(1)} %get-tuple-element.25), channel_id=1, source_target_pairs={{0,1},{1,0},{2,3},{3,2},{4,5},{5,4},{6,7},{7,6},{8,9},{9,8},{10,11... | collective-permute-start | bytes 589832 | tf_op jit(solution)/shard_map/ppermute | solution.py:374
  27.4 4.8 %collective-permute-start.10 = (bf16[16,1024]{1,0:T(8,128)(2,1)S(1)}, bf16[16,1024]{1,0:T(8,128)(2,1)S(1)}, u32[]{:S(2)}, u32[]{:S(2)}) collective-permute-start(bf16[16,1024]{1,0:T(8,128)(2,1)S(1)} %slice.39), channel_id=1, source_target_pairs={{0,8},{2,10},{4,12},{6,14},{8,0},{10,2},{12,4},{14,6},{1,9},{3,11}... | collective-permute-start | bytes 98312 | tf_op jit(solution)/shard_map/ppermute | solution.py:374
  30.5 5.7 %collective-permute-start.9 = (bf16[24,1024]{1,0:T(8,128)(2,1)S(1)}, bf16[24,1024]{1,0:T(8,128)(2,1)S(1)}, u32[]{:S(2)}, u32[]{:S(2)}) collective-permute-start(bf16[24,1024]{1,0:T(8,128)(2,1)S(1)} %slice_add_fusion.refs_1_), channel_id=1, source_target_pairs={{0,1},{1,0},{2,3},{3,2},{4,5},{5,4},{6,7},{7,6},{8,9},{9,8},{10,11... | collective-permute-start | bytes 147464 | tf_op jit(solution)/shard_map/ppermute | solution.py:374
  32.3 3.9 %collective-permute-start.11 = (bf16[16,1024]{1,0:T(8,128)(2,1)S(1)}, bf16[16,1024]{1,0:T(8,128)(2,1)S(1)}, u32[]{:S(2)}, u32[]{:S(2)}) collective-permute-start(bf16[16,1024]{1,0:T(8,128)(2,1)S(1)} %slice_add_fusion.1.refs_2_), channel_id=1, source_target_pairs={{0,1},{1,0},{2,3},{3,2},{4,5},{5,4},{6,7},{7,6},{8,9},{9,8},{10,11... | collective-permute-start | bytes 98312 | tf_op jit(solution)/shard_map/ppermute | solution.py:374

commit v2 on v1

--- a/solution.py
+++ b/solution.py
@@ -148,49 +148,65 @@
     out[1:, :] = other[...]
 
 
-def own_kernel(windows, traces, taps, table, part, white, response, ends, square, shifted, spectra):
+def own_chunk(windows, f, traces, table, lines, edge, part, response, last):
+    channels, samples = traces.shape
+    size = lines.shape[1] // 3
+    lag = edge.shape[1] // 3
+    pieces = samples // PIECE
+    x = jnp.concatenate([traces[:, q * PIECE : (q + 1) * PIECE] for q in range(pieces)], axis=0)
+    turns = Turns()
+    re = slice(f, f + CHUNK)
+    im = slice(NF + f, NF + f + CHUNK)
+    pr = dot(lines[...], stacked_rows(table, size, re))
+    pi = dot(lines[...], stacked_rows(table, size, im))
+    response[:, :CHUNK] = pr
+    response[:, CHUNK:] = pi
+    halves = half_spectra(x, table, channels, windows, turns, f)
+    for w in range(windows):
+        xr, xi = halves[w]
+        xr, xi = turns.sign * xr, turns.sign * xi
+        if w > 0:
+            xr, xi = xr + halves[w - 1][0], xi + halves[w - 1][1]
+        yr = xr * pr - xi * pi
+        yi = xr * pi + xi * pr
+        if w < windows - 1:
+            rows = slice(w * channels, (w + 1) * channels)
+            part[rows, :CHUNK] = yr
+            part[rows, CHUNK:] = yi
+        else:
+            last[:, :CHUNK] = yr + dot(edge[...], stacked_rows(table, lag, re))
+            last[:, CHUNK:] = yi + dot(edge[...], stacked_rows(table, lag, im))
+
+
+def first_kernel(
+    windows, traces, taps, table, part, response, last, ends, edge, lines, square, shifted
+):
     channels, samples = traces.shape
     tap_count = taps.shape[0]
     square[...] = jnp.zeros_like(square)
     high, low = split_two(taps[...])
     high = high.astype(F32)
-    lines = square.shape[0] // 3
+    size = square.shape[0] // 3
     for i, value in enumerate((high, low.astype(F32), high)):
-        square[i * lines : i * lines + tap_count, :channels] = value
-    filter_taps = square[...].T[:channels].astype(BF16)
+        square[i * size : i * size + tap_count, :channels] = value
+    lines[...] = square[...].T[:channels].astype(BF16)
     tile = 128
-    last = windows - 1
     for b in range(1, windows):
         ends[:, (b - 1) * tile : b * tile] = traces[:, b * HALF - tile : b * HALF]
-    start = (last - 1) * HALF
+    start = (windows - 2) * HALF
     apart = traces[:, start - tile : start].astype(F32) - traces[:, samples - tile :].astype(F32)
-    edge = end_terms(taps[...], shifted, tap_count, apart)
-    pieces = samples // PIECE
-    x = jnp.concatenate([traces[:, q * PIECE : (q + 1) * PIECE] for q in range(pieces)], axis=0)
-    turns = Turns()
-    for f in range(0, NF, CHUNK):
-        re = slice(f, f + CHUNK)
-        im = slice(NF + f, NF + f + CHUNK)
-        pr = dot(filter_taps, stacked_rows(table, lines, re))
-        pi = dot(filter_taps, stacked_rows(table, lines, im))
-        response[:, re] = pr
-        response[:, im] = pi
-        halves = half_spectra(x, table, channels, windows, turns, f)
-        for w in range(windows):
-            xr, xi = halves[w]
-            xr, xi = turns.sign * xr, turns.sign * xi
-            if w > 0:
-                xr, xi = xr + halves[w - 1][0], xi + halves[w - 1][1]
-            yr = xr * pr - xi * pi
-            yi = xr * pi + xi * pr
-            if w < last:
-                rows = slice(w * channels, (w + 1) * channels)
-                part[rows, re] = yr
-                part[rows, im] = yi
-            else:
-                spectra[:, re] = yr + dot(edge, stacked_rows(table, tap_count - 1, re))
-                spectra[:, im] = yi + dot(edge, stacked_rows(table, tap_count - 1, im))
-    whiten_all(spectra, white, channels)
+    edge[...] = end_terms(taps[...], shifted, tap_count, apart)
+    own_chunk(windows, 0, traces, table, lines, edge, part, response, last)
+
+
+def second_kernel(
+    windows, traces, table, lines, edge, first, part, response, white, second, spectra
+):
+    own_chunk(windows, CHUNK, traces, table, lines, edge, part, response, second)
+    for i, half in enumerate((first, second)):
+        spectra[:, i * CHUNK : (i + 1) * CHUNK] = half[:, :CHUNK]
+        spectra[:, NF + i * CHUNK : NF + (i + 1) * CHUNK] = half[:, CHUNK:]
+    whiten_all(spectra, white, white.shape[0])
 
 
 def part_rows(windows, pairs):
@@ -227,12 +243,12 @@
 
 
 def rest_kernel(
-    windows, times, where, halo, ends, taps, table, part, own_white, response, picks, *refs
+    windows, times, where, halo, ends, taps, table, part_a, part_b, response_a, response_b, *refs
 ):
-    keep, send = refs[:2]
-    blocks = refs[2 : 2 + times]
-    shifted, spectra, white = refs[2 + times :]
-    channels = response.shape[0]
+    own_white, picks, keep, send = refs[:4]
+    blocks = refs[4 : 4 + times]
+    shifted, spectra, white = refs[4 + times :]
+    channels = response_a.shape[0]
     tap_count = taps.shape[0]
     tile = halo.shape[1] - HALF
     rest = windows - 1
@@ -252,13 +268,14 @@
         re = slice(f, f + CHUNK)
         im = slice(NF + f, NF + f + CHUNK)
         xr, xi = half_spectra(x, table, channels, 1, turns, f)[0]
-        pr, pi = response[:, re], response[:, im]
+        part, response = (part_b, response_b) if f else (part_a, response_a)
+        pr, pi = response[:, :CHUNK], response[:, CHUNK:]
         er = dot(edge, stacked_rows(table, tap_count - 1, re))
         ei = dot(edge, stacked_rows(table, tap_count - 1, im))
-        spectra[:channels, re] = part[:channels, re] + er[:channels] + (xr * pr - xi * pi)
-        spectra[:channels, im] = part[:channels, im] + ei[:channels] + (xr * pi + xi * pr)
-        spectra[channels:, re] = part[channels:, re] + er[channels:]
-        spectra[channels:, im] = part[channels:, im] + ei[channels:]
+        spectra[:channels, re] = part[:channels, :CHUNK] + er[:channels] + (xr * pr - xi * pi)
+        spectra[:channels, im] = part[:channels, CHUNK:] + ei[:channels] + (xr * pi + xi * pr)
+        spectra[channels:, re] = part[channels:, :CHUNK] + er[channels:]
+        spectra[channels:, im] = part[channels:, CHUNK:] + ei[channels:]
     count = rest * channels
     whiten_all(spectra, white, count)
     white[count:, :] = own_white[...]
@@ -379,6 +396,7 @@
     params = pltpu.CompilerParams(vmem_limit_bytes=LIMIT)
     bits = [1 << b for b in range(chips.bit_length() - 1)]
 
+    other = across(block_sources, "chan", 1)
     tail, ids = pl.pallas_call(
         tail_kernel,
         out_shape=[
@@ -392,7 +410,6 @@
         name="tail",
     )(*(pltpu.with_memory_space_constraint(a, pltpu.HBM) for a in (traces, block_sources)))
     halo = lax.ppermute(tail, "tm", [(i - 1, i) for i in range(1, times)])
-    other = across(ids, "chan", 1)
     taps = filter_taps.T
     traces, taps, table = (
         pltpu.with_memory_space_constraint(a, pltpu.VMEM)
@@ -416,25 +433,41 @@
 
     shape = (channels, windows, pairs, chips)
     width = windows * channels
-    own = pl.pallas_call(
-        functools.partial(own_kernel, windows),
-        out_shape=[
-            jax.ShapeDtypeStruct((width - channels, 2 * NF), F32),
-            jax.ShapeDtypeStruct((channels, 2 * NF), BF16),
-            jax.ShapeDtypeStruct((channels, 2 * NF), F32),
+    chunk_shapes = [
+        jax.ShapeDtypeStruct((width - channels, 2 * CHUNK), F32),
+        jax.ShapeDtypeStruct((channels, 2 * CHUNK), F32),
+    ]
+    size = -(-tap_count // 16) * 16
+    part_a, response_a, last, ends, edge, lines = pl.pallas_call(
+        functools.partial(first_kernel, windows),
+        out_shape=chunk_shapes
+        + [
+            chunk_shapes[1],
             jax.ShapeDtypeStruct((channels, (windows - 1) * 128), BF16),
+            jax.ShapeDtypeStruct((channels, 3 * (tap_count - 1)), BF16),
+            jax.ShapeDtypeStruct((channels, 3 * size), BF16),
         ],
         in_specs=[vmem] * 3,
-        out_specs=[vmem] * 4,
+        out_specs=[vmem] * 6,
         scratch_shapes=[
-            pltpu.VMEM((3 * (-(-tap_count // 16) * 16), 128), F32),
+            pltpu.VMEM((3 * size, 128), F32),
             pltpu.VMEM((2 * tap_count + 6, channels), F32),
+        ],
+        compiler_params=params,
+        name="first",
+    )(traces, taps, table)
+    part_b, response_b, own_white = pl.pallas_call(
+        functools.partial(second_kernel, windows),
+        out_shape=chunk_shapes + [jax.ShapeDtypeStruct((channels, 2 * NF), BF16)],
+        in_specs=[vmem] * 5,
+        out_specs=[vmem] * 3,
+        scratch_shapes=[
+            pltpu.VMEM((channels, 2 * CHUNK), F32),
             pltpu.VMEM((channels, 2 * NF), F32),
         ],
         compiler_params=params,
-        name="own",
-    )(traces, taps, table)
-    part_spectra, own_white, response, ends = own
+        name="second",
+    )(traces, table, lines, edge, last)
     picks = pl.pallas_call(
         functools.partial(picks_kernel, shape),
         out_shape=jax.ShapeDtypeStruct((2 * rows_out, width), BF16),
@@ -448,7 +481,7 @@
         functools.partial(rest_kernel, windows, times),
         out_shape=[jax.ShapeDtypeStruct((rows_out, 2 * NF), BF16)] * 2
         + [jax.ShapeDtypeStruct((windows * part, 2 * NF), BF16)] * times,
-        in_specs=[smem] + [vmem] * 8,
+        in_specs=[smem] + [vmem] * 10,
         out_specs=[vmem] * (2 + times),
         scratch_shapes=[
             pltpu.VMEM((2 * tap_count + 6, width - channels), F32),
@@ -457,7 +490,19 @@
         ],
         compiler_params=params,
         name="rest",
-    )(where, halo, ends, taps, table, part_spectra, own_white, response, picks)
+    )(
+        where,
+        halo,
+        ends,
+        taps,
+        table,
+        part_a,
+        part_b,
+        response_a,
+        response_b,
+        own_white,
+        picks,
+    )
     keep, send, blocks = outs[0], outs[1], outs[2:]
     gathered = keep + across(send, "chan", 1)
     rows = sum(sizes)

time: 37.9 us -> 37.9 us (level)
    pallas_call x1 -> x2, Pallas kernels: 2.5 us -> 2.63 us  [the longest x1 1.49 us: shards(): pl.pallas_call(functools.partial(second_kernel, windows), out_shape=chunk...]
  transfers between devices with their start and end apart: 12 -> 12, of which waited for: 6 -> 7; matrix products, arithmetic and copies ran while one was open for 0% -> 0% of each run, Pallas kernels for 11% -> 14%
where the time goes in v2:
time: 37.9 us; the launch traced here: 37.7 us
  starting transfers between devices  16.4 us (43%)
  waiting for transfers between devices  11.2 us (30%)
  Pallas kernels  9.55 us (25%)
    ppermute x11, starting transfers between devices, across(): return lax.ppermute(x, axis, [(i, i ^ distance) for i in range(size)])  12 us
    ppermute x11, waiting for transfers between devices, across(): return lax.ppermute(x, axis, [(i, i ^ distance) for i in range(size)])  11.2 us
    ppermute x1, starting transfers between devices, shards(): halo = lax.ppermute(tail, 'tm', [(i - 1, i) for i in range(1, times)])  4.4 us
    pallas_call x1, Pallas kernels, shards(): pl.pallas_call(functools.partial(rest_kernel, windows, times), out_shape=...  2.56 us
    pallas_call x2, Pallas kernels, correlate(): pl.pallas_call(functools.partial(correlate_kernel, windows, factor, count...  2.32 us
    pallas_call x1, Pallas kernels, shards(): pl.pallas_call(functools.partial(second_kernel, windows), out_shape=chunk...  1.49 us
    pallas_call x1, Pallas kernels, shards(): pl.pallas_call(functools.partial(first_kernel, windows), out_shape=chunk_...  1.14 us
    pallas_call x1, Pallas kernels, shards(): pl.pallas_call(functools.partial(picks_kernel, shape), out_shape=jax.Shap...  1.05 us
  transfers between devices with their start and end apart: 12, of which 7 were waited for; matrix products, arithmetic and copies ran while one was open for 0% of the time, Pallas kernels for 14%

profile of v2, /device:TPU:0, one launch (start us, length us, event | category | flops | bytes accessed | tf_op | source)
XLA Modules:
  0.0 37.7 jit_solution(8560506901718507797)
XLA Ops:
  0.0 0.5 %collective-permute-start.1 = (s32[1,12]{1,0:T(1,128)}, s32[1,12]{1,0:T(1,128)S(1)}, u32[]{:S(2)}, u32[]{:S(2)}) collective-permute-start(s32[1,12]{1,0:T(1,128)} %wanted.1), channel_id=1, source_target_pairs={{0,2},{2,0},{4,6},{6,4},{8,10},{10,8},{12,14},{14,12},{1,3},{3,1},... | collective-permute-start | bytes 152 | tf_op jit(solution)/shard_map/ppermute | solution.py:391
  0.5 1.0 %tail.1 = (bf16[64,2176]{1,0:T(8,128)(2,1)S(1)}, s32[1,12]{1,0:T(1,128)S(1)}) custom-call(bf16[64,6144]{1,0:T(8,128)(2,1)} %traces.5, s32[1,12]{1,0:T(1,128)} %wanted.1), custom_call_target="tpu_custom_call" | custom-call | tf_op jit(solution)/shard_map/tail/pallas_call | solution.py:400
  1.5 4.4 %collective-permute-start = (bf16[64,2176]{1,0:T(8,128)(2,1)S(1)}, bf16[64,2176]{1,0:T(8,128)(2,1)S(1)}, u32[]{:S(2)}, u32[]{:S(2)}) collective-permute-start(bf16[64,2176]{1,0:T(8,128)(2,1)S(1)} %get-tuple-element.24), channel_id=1, source_target_pairs={{0,1},{2,3},{4,5},{6,7},{8,9},{10,11},{12,13},{14,15},{16,17},{18,... | collective-permute-start | bytes 835592 | tf_op jit(solution)/shard_map/ppermute | solution.py:412
  5.9 0.1 pad_add_fusion.1.where
  6.0 0.0 collective-permute-done.1.other
  6.0 0.0 copy-start
  6.0 0.0 copy-start.1
  6.0 0.0 copy-start.2
  6.0 1.6 %collective-permute-start.2 = (s32[2,12]{1,0:T(2,128)S(1)}, s32[2,12]{1,0:T(2,128)S(1)}, u32[]{:S(2)}, u32[]{:S(2)}) collective-permute-start(s32[2,12]{1,0:T(2,128)S(1)} %pair.1), channel_id=1, source_target_pairs={{0,4},{2,6},{4,0},{6,2},{8,12},{10,14},{12,8},{14,10},{1,5},{3,7},... | collective-permute-start | bytes 296 | tf_op jit(solution)/shard_map/ppermute | solution.py:391
  7.6 0.0 copy-done
  7.6 0.1 copy-done.1
  7.7 0.0 copy-done.2
  7.7 1.1 %first.1 = (f32[128,512]{1,0:T(8,128)S(1)}, f32[64,512]{1,0:T(8,128)S(1)}, f32[64,512]{1,0:T(8,128)S(1)}, bf16[64,256]{1,0:T(8,128)(2,1)S(1)}, bf16[64,96]{1,0:T(8,128)(2,1)S(1)}, /*index=5*/bf16[64,144]{1,0:T(8,128)(2,1)S(1)}) custom-call(bf16[64,6144]{1,0:T(8,128)(2,1)S(1)} %copy-done.1, f32[33,64]{1,0:T(8,128)S(1)} %bitcast.8, bf16[1024,1024]{1,0:T(8,128)(2,1)S(1)} %copy-done), custom_call_target="tpu_custom_call" | custom-call | tf_op jit(solution)/shard_map/first/pallas_call | solution.py:441
  8.9 0.0 copy-start.3
  8.9 0.0 copy-start.4
  8.9 0.7 %collective-permute-done.2 = s32[2,12]{1,0:T(2,128)S(1)} collective-permute-done((s32[2,12]{1,0:T(2,128)S(1)}, s32[2,12]{1,0:T(2,128)S(1)}, u32[]{:S(2)}, u32[]{:S(2)}) %collective-permute-start.2) | collective-permute-done | bytes 128 | tf_op jit(solution)/shard_map/ppermute | solution.py:391
  9.6 2.6 %collective-permute-start.3 = (s32[4,12]{1,0:T(4,128)S(1)}, s32[4,12]{1,0:T(4,128)S(1)}, u32[]{:S(2)}, u32[]{:S(2)}) collective-permute-start(s32[4,12]{1,0:T(4,128)S(1)} %pad_add_fusion.refs_0_), channel_id=1, source_target_pairs={{0,8},{2,10},{4,12},{6,14},{8,0},{10,2},{12,4},{14,6},{1,9},{3,11}... | collective-permute-start | bytes 584 | tf_op jit(solution)/shard_map/ppermute | solution.py:391
  12.3 1.5 %second.1 = (f32[128,512]{1,0:T(8,128)S(1)}, f32[64,512]{1,0:T(8,128)S(1)}, bf16[64,1024]{1,0:T(8,128)(2,1)S(1)}) custom-call(bf16[64,6144]{1,0:T(8,128)(2,1)S(1)} %copy-done.1, bf16[1024,1024]{1,0:T(8,128)(2,1)S(1)} %copy-done, bf16[64,144]{1,0:T(8,128)(2,1)S(1)} %get-tuple-element.27.lines, bf16[64,96]{1,0:T(8,128)(2,1)S(1)} %get-tuple-element.28.edge, ...), custom_call_target="tpu_custom_call" | custom-call | tf_op jit(solution)/shard_map/second/pallas_call | solution.py:459
  13.8 0.4 %collective-permute-done.3.refs_1_ = s32[4,12]{1,0:T(4,128)S(1)} collective-permute-done((s32[4,12]{1,0:T(4,128)S(1)}, s32[4,12]{1,0:T(4,128)S(1)}, u32[]{:S(2)}, u32[]{:S(2)}) %collective-permute-start.3) | collective-permute-done | bytes 224 | tf_op jit(solution)/shard_map/ppermute | solution.py:391
  14.2 0.0 copy-done.3
  14.2 0.0 copy-done.4
  14.2 1.1 %picks.1.refs_1_ = bf16[320,192]{1,0:T(8,128)(2,1)S(1)} custom-call(s32[2]{0:T(128)S(1)} %pad_add_fusion.1.where, s32[8]{0:T(128)S(1)} %copy-done.4, s32[8,36]{1,0:T(8,128)S(1)} %copy-done.3, s32[4,12]{1,0:T(4,128)S(1)} %pad_add_fusion.refs_0_, s32[4,12]{1,0:T(4,128)S(1)} %collective-permute-done.3.refs_1_), custom_call_target="tpu_custom_call" | custom-call | tf_op jit(solution)/shard_map/picks/pallas_call | solution.py:471
  15.2 0.0 collective-permute-done.halo
  15.3 2.6 %rest.1 = (bf16[160,1024]{1,0:T(8,128)(2,1)S(1)}, bf16[160,1024]{1,0:T(8,128)(2,1)S(1)}, bf16[96,1024]{1,0:T(8,128)(2,1)S(1)}, bf16[96,1024]{1,0:T(8,128)(2,1)S(1)}) custom-call(s32[2]{0:T(128)S(1)} %pad_add_fusion.1.where, bf16[64,2176]{1,0:T(8,128)(2,1)S(1)} %collective-permute-done.halo, bf16[64,256]{1,0:T(8,128)(2,1)S(1)} %get-tuple-element.25.ends, ...), custom_call_target="tpu_custom_call" | custom-call | tf_op jit(solution)/shard_map/rest/pallas_call | solution.py:480
  17.8 0.1 collective-permute-start.5
  17.9 1.6 %collective-permute-done.5 = bf16[160,1024]{1,0:T(8,128)(2,1)S(1)} collective-permute-done((bf16[160,1024]{1,0:T(8,128)(2,1)S(1)}, bf16[160,1024]{1,0:T(8,128)(2,1)S(1)}, u32[]{:S(2)}, u32[]{:S(2)}) %collective-permute-start.5) | collective-permute-done | bytes 327712 | tf_op jit(solution)/shard_map/ppermute | solution.py:391
  19.5 0.1 add.15
  19.7 1.6 %collective-permute-start.7 = (bf16[40,1024]{1,0:T(8,128)(2,1)S(1)}, bf16[40,1024]{1,0:T(8,128)(2,1)S(1)}, u32[]{:S(2)}, u32[]{:S(2)}) collective-permute-start(bf16[40,1024]{1,0:T(8,128)(2,1)S(1)} %get-tuple-element.41), channel_id=1, source_target_pairs={{0,4},{2,6},{4,0},{6,2},{8,12},{10,14},{12,8},{14,10},{1,5},{3,7},... | collective-permute-start | bytes 245768 | tf_op jit(solution)/shard_map/ppermute | solution.py:391
  21.3 0.4 %collective-permute-start.6 = (bf16[40,1024]{1,0:T(8,128)(2,1)S(1)}, bf16[40,1024]{1,0:T(8,128)(2,1)S(1)}, u32[]{:S(2)}, u32[]{:S(2)}) collective-permute-start(bf16[40,1024]{1,0:T(8,128)(2,1)S(1)} %get-tuple-element.39), channel_id=1, source_target_pairs={{0,4},{2,6},{4,0},{6,2},{8,12},{10,14},{12,8},{14,10},{1,5},{3,7},... | collective-permute-start | bytes 245768 | tf_op jit(solution)/shard_map/ppermute | solution.py:391
  21.7 2.9 %collective-permute-done.7 = bf16[40,1024]{1,0:T(8,128)(2,1)S(1)} collective-permute-done((bf16[40,1024]{1,0:T(8,128)(2,1)S(1)}, bf16[40,1024]{1,0:T(8,128)(2,1)S(1)}, u32[]{:S(2)}, u32[]{:S(2)}) %collective-permute-start.7) | collective-permute-done | bytes 81952 | tf_op jit(solution)/shard_map/ppermute | solution.py:391
  24.7 2.7 %collective-permute-start.8 = (bf16[24,1024]{1,0:T(8,128)(2,1)S(1)}, bf16[24,1024]{1,0:T(8,128)(2,1)S(1)}, u32[]{:S(2)}, u32[]{:S(2)}) collective-permute-start(bf16[24,1024]{1,0:T(8,128)(2,1)S(1)} %slice.37), channel_id=1, source_target_pairs={{0,8},{2,10},{4,12},{6,14},{8,0},{10,2},{12,4},{14,6},{1,9},{3,11}... | collective-permute-start | bytes 147464 | tf_op jit(solution)/shard_map/ppermute | solution.py:391
  27.4 0.0 collective-permute-start.4
  27.4 0.3 collective-permute-start.10
  27.7 0.0 collective-permute-done.6
  27.7 2.4 %collective-permute-done.8 = bf16[24,1024]{1,0:T(8,128)(2,1)S(1)} collective-permute-done((bf16[24,1024]{1,0:T(8,128)(2,1)S(1)}, bf16[24,1024]{1,0:T(8,128)(2,1)S(1)}, u32[]{:S(2)}, u32[]{:S(2)}) %collective-permute-start.8) | collective-permute-done | bytes 49184 | tf_op jit(solution)/shard_map/ppermute | solution.py:391
  30.1 0.1 collective-permute-start.9
  30.2 2.0 %collective-permute-done.10 = bf16[16,1024]{1,0:T(8,128)(2,1)S(1)} collective-permute-done((bf16[16,1024]{1,0:T(8,128)(2,1)S(1)}, bf16[16,1024]{1,0:T(8,128)(2,1)S(1)}, u32[]{:S(2)}, u32[]{:S(2)}) %collective-permute-start.10) | collective-permute-done | bytes 32800 | tf_op jit(solution)/shard_map/ppermute | solution.py:391
  32.2 2.0 %collective-permute-start.11 = (bf16[16,1024]{1,0:T(8,128)(2,1)S(1)}, bf16[16,1024]{1,0:T(8,128)(2,1)S(1)}, u32[]{:S(2)}, u32[]{:S(2)}) collective-permute-start(bf16[16,1024]{1,0:T(8,128)(2,1)S(1)} %slice_add_fusion.1.refs_2_), channel_id=1, source_target_pairs={{0,1},{1,0},{2,3},{3,2},{4,5},{5,4},{6,7},{7,6},{8,9},{9,8},{10,11... | collective-permute-start | bytes 98312 | tf_op jit(solution)/shard_map/ppermute | solution.py:391
  34.2 0.8 %correlate.2.refs_3_ = f32[12,32,1024]{2,1,0:T(8,128)S(1)} custom-call(bf16[3,32,1024]{2,1,0:T(8,128)(2,1)S(1)} %bitcast.6, bf16[24,1024]{1,0:T(8,128)(2,1)S(1)} %slice_add_fusion.refs_1_, bf16[16,1024]{1,0:T(8,128)(2,1)S(1)} %slice_add_fusion.1.refs_2_), custom_call_target="tpu_custom_call" | custom-call | tf_op jit(solution)/shard_map/correlate/pallas_call | solution.py:366
  35.0 0.0 collective-permute-done.4
  35.0 1.1 %collective-permute-done.11.refs_2_ = bf16[16,1024]{1,0:T(8,128)(2,1)S(1)} collective-permute-done((bf16[16,1024]{1,0:T(8,128)(2,1)S(1)}, bf16[16,1024]{1,0:T(8,128)(2,1)S(1)}, u32[]{:S(2)}, u32[]{:S(2)}) %collective-permute-start.11) | collective-permute-done | bytes 32800 | tf_op jit(solution)/shard_map/ppermute | solution.py:391
  36.1 0.0 collective-permute-done.9.refs_1_
  36.1 1.6 %correlate.3 = f32[12,32,1024]{2,1,0:T(8,128)} custom-call(bf16[3,32,1024]{2,1,0:T(8,128)(2,1)S(1)} %bitcast.7, bf16[24,1024]{1,0:T(8,128)(2,1)S(1)} %collective-permute-done.9.refs_1_, bf16[16,1024]{1,0:T(8,128)(2,1)S(1)} %collective-permute-done.11.refs_2_, f32[12,32,1024]{2,1,0:T(8,128)S(1)} %correlate.2.refs_3_), custom_call_target="tpu_custom_call" | custom-call | tf_op jit(solution)/shard_map/correlate/pallas_call | solution.py:366
  (9 shorter events, 0.1 us)
Async XLA Ops:
  0.0 6.0 %collective-permute-start.1 = (s32[1,12]{1,0:T(1,128)}, s32[1,12]{1,0:T(1,128)S(1)}, u32[]{:S(2)}, u32[]{:S(2)}) collective-permute-start(s32[1,12]{1,0:T(1,128)} %wanted.1), channel_id=1, source_target_pairs={{0,2},{2,0},{4,6},{6,4},{8,10},{10,8},{12,14},{14,12},{1,3},{3,1},... | collective-permute-start | bytes 152 | tf_op jit(solution)/shard_map/ppermute | solution.py:391
  1.5 13.8 %collective-permute-start = (bf16[64,2176]{1,0:T(8,128)(2,1)S(1)}, bf16[64,2176]{1,0:T(8,128)(2,1)S(1)}, u32[]{:S(2)}, u32[]{:S(2)}) collective-permute-start(bf16[64,2176]{1,0:T(8,128)(2,1)S(1)} %get-tuple-element.24), channel_id=1, source_target_pairs={{0,1},{2,3},{4,5},{6,7},{8,9},{10,11},{12,13},{14,15},{16,17},{18,... | collective-permute-start | bytes 835592 | tf_op jit(solution)/shard_map/ppermute | solution.py:412
  6.0 1.7 %copy-start = (bf16[1024,1024]{1,0:T(8,128)(2,1)S(1)}, bf16[1024,1024]{1,0:T(8,128)(2,1)}, u32[]{:S(2)}) copy-start(bf16[1024,1024]{1,0:T(8,128)(2,1)} %constant.10.clone.table) | copy-start | bytes 6291460
  6.0 1.8 %copy-start.1 = (bf16[64,6144]{1,0:T(8,128)(2,1)S(1)}, bf16[64,6144]{1,0:T(8,128)(2,1)}, u32[]{:S(2)}) copy-start(bf16[64,6144]{1,0:T(8,128)(2,1)} %traces.5) | copy-start | bytes 2359300
  6.0 1.8 %copy-start.2 = (f32[64,33]{0,1:T(8,128)S(1)}, f32[64,33]{0,1:T(8,128)}, u32[]{:S(2)}) copy-start(f32[64,33]{0,1:T(8,128)} %param.7) | copy-start | bytes 25348
  6.0 3.6 %collective-permute-start.2 = (s32[2,12]{1,0:T(2,128)S(1)}, s32[2,12]{1,0:T(2,128)S(1)}, u32[]{:S(2)}, u32[]{:S(2)}) collective-permute-start(s32[2,12]{1,0:T(2,128)S(1)} %pair.1), channel_id=1, source_target_pairs={{0,4},{2,6},{4,0},{6,2},{8,12},{10,14},{12,8},{14,10},{1,5},{3,7},... | collective-permute-start | bytes 296 | tf_op jit(solution)/shard_map/ppermute | solution.py:391
  8.9 5.3 %copy-start.3 = (s32[8,36]{1,0:T(8,128)S(1)}, s32[8,36]{1,0:T(8,128)}, u32[]{:S(2)}) copy-start(s32[8,36]{1,0:T(8,128)} %slots.1) | copy-start | bytes 3460
  8.9 5.3 %copy-start.4 = (s32[8]{0:T(128)S(1)}, s32[8]{0:T(128)}, u32[]{:S(2)}) copy-start(s32[8]{0:T(128)} %counts.1) | copy-start | bytes 100
  9.6 4.5 %collective-permute-start.3 = (s32[4,12]{1,0:T(4,128)S(1)}, s32[4,12]{1,0:T(4,128)S(1)}, u32[]{:S(2)}, u32[]{:S(2)}) collective-permute-start(s32[4,12]{1,0:T(4,128)S(1)} %pad_add_fusion.refs_0_), channel_id=1, source_target_pairs={{0,8},{2,10},{4,12},{6,14},{8,0},{10,2},{12,4},{14,6},{1,9},{3,11}... | collective-permute-start | bytes 584 | tf_op jit(solution)/shard_map/ppermute | solution.py:391
  17.8 1.7 %collective-permute-start.5 = (bf16[160,1024]{1,0:T(8,128)(2,1)S(1)}, bf16[160,1024]{1,0:T(8,128)(2,1)S(1)}, u32[]{:S(2)}, u32[]{:S(2)}) collective-permute-start(bf16[160,1024]{1,0:T(8,128)(2,1)S(1)} %get-tuple-element.37), channel_id=1, source_target_pairs={{0,2},{2,0},{4,6},{6,4},{8,10},{10,8},{12,14},{14,12},{1,3},{3,1},... | collective-permute-start | bytes 983048 | tf_op jit(solution)/shard_map/ppermute | solution.py:391
  19.7 5.0 %collective-permute-start.7 = (bf16[40,1024]{1,0:T(8,128)(2,1)S(1)}, bf16[40,1024]{1,0:T(8,128)(2,1)S(1)}, u32[]{:S(2)}, u32[]{:S(2)}) collective-permute-start(bf16[40,1024]{1,0:T(8,128)(2,1)S(1)} %get-tuple-element.41), channel_id=1, source_target_pairs={{0,4},{2,6},{4,0},{6,2},{8,12},{10,14},{12,8},{14,10},{1,5},{3,7},... | collective-permute-start | bytes 245768 | tf_op jit(solution)/shard_map/ppermute | solution.py:391
  21.3 6.4 %collective-permute-start.6 = (bf16[40,1024]{1,0:T(8,128)(2,1)S(1)}, bf16[40,1024]{1,0:T(8,128)(2,1)S(1)}, u32[]{:S(2)}, u32[]{:S(2)}) collective-permute-start(bf16[40,1024]{1,0:T(8,128)(2,1)S(1)} %get-tuple-element.39), channel_id=1, source_target_pairs={{0,4},{2,6},{4,0},{6,2},{8,12},{10,14},{12,8},{14,10},{1,5},{3,7},... | collective-permute-start | bytes 245768 | tf_op jit(solution)/shard_map/ppermute | solution.py:391
  24.7 5.4 %collective-permute-start.8 = (bf16[24,1024]{1,0:T(8,128)(2,1)S(1)}, bf16[24,1024]{1,0:T(8,128)(2,1)S(1)}, u32[]{:S(2)}, u32[]{:S(2)}) collective-permute-start(bf16[24,1024]{1,0:T(8,128)(2,1)S(1)} %slice.37), channel_id=1, source_target_pairs={{0,8},{2,10},{4,12},{6,14},{8,0},{10,2},{12,4},{14,6},{1,9},{3,11}... | collective-permute-start | bytes 147464 | tf_op jit(solution)/shard_map/ppermute | solution.py:391
  27.4 7.6 %collective-permute-start.4 = (bf16[96,1024]{1,0:T(8,128)(2,1)S(1)}, bf16[96,1024]{1,0:T(8,128)(2,1)S(1)}, u32[]{:S(2)}, u32[]{:S(2)}) collective-permute-start(bf16[96,1024]{1,0:T(8,128)(2,1)S(1)} %get-tuple-element.35), channel_id=1, source_target_pairs={{0,1},{1,0},{2,3},{3,2},{4,5},{5,4},{6,7},{7,6},{8,9},{9,8},{10,11... | collective-permute-start | bytes 589832 | tf_op jit(solution)/shard_map/ppermute | solution.py:391
  27.4 4.8 %collective-permute-start.10 = (bf16[16,1024]{1,0:T(8,128)(2,1)S(1)}, bf16[16,1024]{1,0:T(8,128)(2,1)S(1)}, u32[]{:S(2)}, u32[]{:S(2)}) collective-permute-start(bf16[16,1024]{1,0:T(8,128)(2,1)S(1)} %slice.39), channel_id=1, source_target_pairs={{0,8},{2,10},{4,12},{6,14},{8,0},{10,2},{12,4},{14,6},{1,9},{3,11}... | collective-permute-start | bytes 98312 | tf_op jit(solution)/shard_map/ppermute | solution.py:391
  30.1 6.0 %collective-permute-start.9 = (bf16[24,1024]{1,0:T(8,128)(2,1)S(1)}, bf16[24,1024]{1,0:T(8,128)(2,1)S(1)}, u32[]{:S(2)}, u32[]{:S(2)}) collective-permute-start(bf16[24,1024]{1,0:T(8,128)(2,1)S(1)} %slice_add_fusion.refs_1_), channel_id=1, source_target_pairs={{0,1},{1,0},{2,3},{3,2},{4,5},{5,4},{6,7},{7,6},{8,9},{9,8},{10,11... | collective-permute-start | bytes 147464 | tf_op jit(solution)/shard_map/ppermute | solution.py:391
  32.2 3.9 %collective-permute-start.11 = (bf16[16,1024]{1,0:T(8,128)(2,1)S(1)}, bf16[16,1024]{1,0:T(8,128)(2,1)S(1)}, u32[]{:S(2)}, u32[]{:S(2)}) collective-permute-start(bf16[16,1024]{1,0:T(8,128)(2,1)S(1)} %slice_add_fusion.1.refs_2_), channel_id=1, source_target_pairs={{0,1},{1,0},{2,3},{3,2},{4,5},{5,4},{6,7},{7,6},{8,9},{9,8},{10,11... | collective-permute-start | bytes 98312 | tf_op jit(solution)/shard_map/ppermute | solution.py:391

commit v3 on v2

--- a/solution.py
+++ b/solution.py
@@ -409,7 +409,6 @@
         compiler_params=params,
         name="tail",
     )(*(pltpu.with_memory_space_constraint(a, pltpu.HBM) for a in (traces, block_sources)))
-    halo = lax.ppermute(tail, "tm", [(i - 1, i) for i in range(1, times)])
     taps = filter_taps.T
     traces, taps, table = (
         pltpu.with_memory_space_constraint(a, pltpu.VMEM)
@@ -426,9 +425,11 @@
             name="pair",
         )(ids, other)
     ]
-    for bit in bits:
-        known = jnp.concatenate(wanted, axis=0)
-        wanted = [known, across(known, "chan", 2 * bit)]
+    tail, pair = lax.optimization_barrier((tail, wanted[0]))
+    wanted = [pair]
+    halo = lax.ppermute(tail, "tm", [(i - 1, i) for i in range(1, times)])
+    for d in range(1, chips):
+        wanted.append(across(pair, "chan", 2 * d))
     where = jnp.stack([lax.axis_index("chan"), lax.axis_index("tm")]).astype(jnp.int32)
 
     shape = (channels, windows, pairs, chips)

time: 37.9 us -> 40.7 us (1.074)
  waiting for transfers between devices: 11.2 us -> 13.5 us
  starting transfers between devices: 16.4 us -> 17 us
    ppermute x11 -> x12, waiting for transfers between devices: 11.2 us -> 13.5 us  [across(): return lax.ppermute(x, axis, [(i, i ^ distance) for i in range(size)])]
    ppermute x1, starting transfers between devices: 4.4 us -> 4.93 us  [shards(): halo = lax.ppermute(tail, 'tm', [(i - 1, i) for i in range(1, times)])]
    ppermute x11 -> x12, starting transfers between devices: 12 us -> 12.1 us  [across(): return lax.ppermute(x, axis, [(i, i ^ distance) for i in range(size)])]
  transfers between devices with their start and end apart: 12 -> 13, of which waited for: 7 -> 7; matrix products, arithmetic and copies ran while one was open for 0% -> 0% of each run, Pallas kernels for 14% -> 13%
where the time goes in v3:
time: 40.7 us; the launch traced here: 40.6 us
  starting transfers between devices  17 us (42%)
  waiting for transfers between devices  13.5 us (33%)
  Pallas kernels  9.52 us (23%)
    ppermute x12, waiting for transfers between devices, across(): return lax.ppermute(x, axis, [(i, i ^ distance) for i in range(size)])  13.5 us
    ppermute x12, starting transfers between devices, across(): return lax.ppermute(x, axis, [(i, i ^ distance) for i in range(size)])  12.1 us
    ppermute x1, starting transfers between devices, shards(): halo = lax.ppermute(tail, 'tm', [(i - 1, i) for i in range(1, times)])  4.93 us
    pallas_call x1, Pallas kernels, shards(): pl.pallas_call(functools.partial(rest_kernel, windows, times), out_shape=...  2.55 us
    pallas_call x2, Pallas kernels, correlate(): pl.pallas_call(functools.partial(correlate_kernel, windows, factor, count...  2.32 us
    pallas_call x1, Pallas kernels, shards(): pl.pallas_call(functools.partial(second_kernel, windows), out_shape=chunk...  1.47 us
    pallas_call x1, Pallas kernels, shards(): pl.pallas_call(functools.partial(first_kernel, windows), out_shape=chunk_...  1.14 us
    pallas_call x1, Pallas kernels, shards(): pl.pallas_call(functools.partial(picks_kernel, shape), out_shape=jax.Shap...  1.05 us
  transfers between devices with their start and end apart: 13, of which 7 were waited for; matrix products, arithmetic and copies ran while one was open for 0% of the time, Pallas kernels for 13%

profile of v3, /device:TPU:0, one launch (start us, length us, event | category | flops | bytes accessed | tf_op | source)
XLA Modules:
  0.0 40.6 jit_solution(16105243233373159703)
XLA Ops:
  0.0 0.5 %collective-permute-start = (s32[1,12]{1,0:T(1,128)}, s32[1,12]{1,0:T(1,128)S(1)}, u32[]{:S(2)}, u32[]{:S(2)}) collective-permute-start(s32[1,12]{1,0:T(1,128)} %wanted.1), channel_id=1, source_target_pairs={{0,2},{2,0},{4,6},{6,4},{8,10},{10,8},{12,14},{14,12},{1,3},{3,1},... | collective-permute-start | bytes 152 | tf_op jit(solution)/shard_map/ppermute | solution.py:391
  0.5 1.0 %tail.1 = (bf16[64,2176]{1,0:T(8,128)(2,1)S(1)}, s32[1,12]{1,0:T(1,128)S(1)}) custom-call(bf16[64,6144]{1,0:T(8,128)(2,1)} %traces.5, s32[1,12]{1,0:T(1,128)} %wanted.1), custom_call_target="tpu_custom_call" | custom-call | tf_op jit(solution)/shard_map/tail/pallas_call | solution.py:400
  1.5 0.0 collective-permute-done.other
  1.5 0.0 copy-start
  1.5 0.0 copy-start.1
  1.5 0.0 copy-start.2
  1.5 4.9 %collective-permute-start.1 = (bf16[64,2176]{1,0:T(8,128)(2,1)S(1)}, bf16[64,2176]{1,0:T(8,128)(2,1)S(1)}, u32[]{:S(2)}, u32[]{:S(2)}) collective-permute-start(bf16[64,2176]{1,0:T(8,128)(2,1)S(1)} %get-tuple-element.28), channel_id=1, source_target_pairs={{0,1},{2,3},{4,5},{6,7},{8,9},{10,11},{12,13},{14,15},{16,17},{18,... | collective-permute-start | bytes 835592 | tf_op jit(solution)/shard_map/ppermute | solution.py:430
  6.5 0.0 copy-done
  6.5 0.0 copy-done.1
  6.5 0.0 copy-done.2
  6.5 1.1 %first.1 = (f32[128,512]{1,0:T(8,128)S(1)}, f32[64,512]{1,0:T(8,128)S(1)}, f32[64,512]{1,0:T(8,128)S(1)}, bf16[64,256]{1,0:T(8,128)(2,1)S(1)}, bf16[64,96]{1,0:T(8,128)(2,1)S(1)}, /*index=5*/bf16[64,144]{1,0:T(8,128)(2,1)S(1)}) custom-call(bf16[64,6144]{1,0:T(8,128)(2,1)S(1)} %copy-done.1, f32[33,64]{1,0:T(8,128)S(1)} %bitcast.8, bf16[1024,1024]{1,0:T(8,128)(2,1)S(1)} %copy-done), custom_call_target="tpu_custom_call" | custom-call | tf_op jit(solution)/shard_map/first/pallas_call | solution.py:442
  7.7 0.0 copy-start.3
  7.7 0.0 copy-start.4
  7.7 1.5 %second.1 = (f32[128,512]{1,0:T(8,128)S(1)}, f32[64,512]{1,0:T(8,128)S(1)}, bf16[64,1024]{1,0:T(8,128)(2,1)S(1)}) custom-call(bf16[64,6144]{1,0:T(8,128)(2,1)S(1)} %copy-done.1, bf16[1024,1024]{1,0:T(8,128)(2,1)S(1)} %copy-done, bf16[64,144]{1,0:T(8,128)(2,1)S(1)} %get-tuple-element.31.lines, bf16[64,96]{1,0:T(8,128)(2,1)S(1)} %get-tuple-element.32.edge, ...), custom_call_target="tpu_custom_call" | custom-call | tf_op jit(solution)/shard_map/second/pallas_call | solution.py:460
  9.2 0.1 pad_add_fusion.where
  9.2 3.6 %collective-permute-start.4 = (s32[2,12]{1,0:T(2,128)S(1)}, s32[2,12]{1,0:T(2,128)S(1)}, u32[]{:S(2)}, u32[]{:S(2)}) collective-permute-start(s32[2,12]{1,0:T(2,128)S(1)} %pair.1.refs_0_), channel_id=1, source_target_pairs={{0,12},{2,14},{4,8},{6,10},{8,4},{10,6},{12,0},{14,2},{1,13},{3,15... | collective-permute-start | bytes 296 | tf_op jit(solution)/shard_map/ppermute | solution.py:391
  12.8 0.0 collective-permute-start.3
  12.8 0.8 %collective-permute-start.2 = (s32[2,12]{1,0:T(2,128)S(1)}, s32[2,12]{1,0:T(2,128)S(1)}, u32[]{:S(2)}, u32[]{:S(2)}) collective-permute-start(s32[2,12]{1,0:T(2,128)S(1)} %pair.1.refs_0_), channel_id=1, source_target_pairs={{0,4},{2,6},{4,0},{6,2},{8,12},{10,14},{12,8},{14,10},{1,5},{3,7},... | collective-permute-start | bytes 296 | tf_op jit(solution)/shard_map/ppermute | solution.py:391
  13.6 1.0 %collective-permute-done.4.refs_3_ = s32[2,12]{1,0:T(2,128)S(1)} collective-permute-done((s32[2,12]{1,0:T(2,128)S(1)}, s32[2,12]{1,0:T(2,128)S(1)}, u32[]{:S(2)}, u32[]{:S(2)}) %collective-permute-start.4) | collective-permute-done | bytes 128 | tf_op jit(solution)/shard_map/ppermute | solution.py:391
  14.6 2.7 %collective-permute-done.3.refs_2_ = s32[2,12]{1,0:T(2,128)S(1)} collective-permute-done((s32[2,12]{1,0:T(2,128)S(1)}, s32[2,12]{1,0:T(2,128)S(1)}, u32[]{:S(2)}, u32[]{:S(2)}) %collective-permute-start.3) | collective-permute-done | bytes 128 | tf_op jit(solution)/shard_map/ppermute | solution.py:391
  17.3 0.0 collective-permute-done.2.refs_1_
  17.3 0.0 copy-done.3
  17.3 0.0 copy-done.4
  17.3 1.1 %picks.1.refs_1_ = bf16[320,192]{1,0:T(8,128)(2,1)S(1)} custom-call(s32[2]{0:T(128)S(1)} %pad_add_fusion.where, s32[8]{0:T(128)S(1)} %copy-done.4, s32[8,36]{1,0:T(8,128)S(1)} %copy-done.3, s32[2,12]{1,0:T(2,128)S(1)} %pair.1.refs_0_, s32[2,12]{1,0:T(2,128)S(1)} %collective-permute-done.2.refs_1_, s32[2,12]{1,0:T(2,128)S(1)} %collective-permute-done.3.refs_2_, ...), custom_call_target="tpu_custom_call" | custom-call | tf_op jit(solution)/shard_map/picks/pallas_call | solution.py:472
  18.4 0.0 collective-permute-done.1.halo
  18.4 2.5 %rest.1 = (bf16[160,1024]{1,0:T(8,128)(2,1)S(1)}, bf16[160,1024]{1,0:T(8,128)(2,1)S(1)}, bf16[96,1024]{1,0:T(8,128)(2,1)S(1)}, bf16[96,1024]{1,0:T(8,128)(2,1)S(1)}) custom-call(s32[2]{0:T(128)S(1)} %pad_add_fusion.where, bf16[64,2176]{1,0:T(8,128)(2,1)S(1)} %collective-permute-done.1.halo, bf16[64,256]{1,0:T(8,128)(2,1)S(1)} %get-tuple-element.29.ends, ...), custom_call_target="tpu_custom_call" | custom-call | tf_op jit(solution)/shard_map/rest/pallas_call | solution.py:481
  20.9 0.1 collective-permute-start.6
  21.0 1.6 %collective-permute-done.6 = bf16[160,1024]{1,0:T(8,128)(2,1)S(1)} collective-permute-done((bf16[160,1024]{1,0:T(8,128)(2,1)S(1)}, bf16[160,1024]{1,0:T(8,128)(2,1)S(1)}, u32[]{:S(2)}, u32[]{:S(2)}) %collective-permute-start.6) | collective-permute-done | bytes 327712 | tf_op jit(solution)/shard_map/ppermute | solution.py:391
  22.6 0.1 add.15
  22.8 0.1 collective-permute-start.8
  22.9 2.0 %collective-permute-start.7 = (bf16[40,1024]{1,0:T(8,128)(2,1)S(1)}, bf16[40,1024]{1,0:T(8,128)(2,1)S(1)}, u32[]{:S(2)}, u32[]{:S(2)}) collective-permute-start(bf16[40,1024]{1,0:T(8,128)(2,1)S(1)} %get-tuple-element.43), channel_id=1, source_target_pairs={{0,4},{2,6},{4,0},{6,2},{8,12},{10,14},{12,8},{14,10},{1,5},{3,7},... | collective-permute-start | bytes 245768 | tf_op jit(solution)/shard_map/ppermute | solution.py:391
  24.9 3.3 %collective-permute-done.8 = bf16[40,1024]{1,0:T(8,128)(2,1)S(1)} collective-permute-done((bf16[40,1024]{1,0:T(8,128)(2,1)S(1)}, bf16[40,1024]{1,0:T(8,128)(2,1)S(1)}, u32[]{:S(2)}, u32[]{:S(2)}) %collective-permute-start.8) | collective-permute-done | bytes 81952 | tf_op jit(solution)/shard_map/ppermute | solution.py:391
  28.2 2.1 %collective-permute-start.9 = (bf16[24,1024]{1,0:T(8,128)(2,1)S(1)}, bf16[24,1024]{1,0:T(8,128)(2,1)S(1)}, u32[]{:S(2)}, u32[]{:S(2)}) collective-permute-start(bf16[24,1024]{1,0:T(8,128)(2,1)S(1)} %slice.37), channel_id=1, source_target_pairs={{0,8},{2,10},{4,12},{6,14},{8,0},{10,2},{12,4},{14,6},{1,9},{3,11}... | collective-permute-start | bytes 147464 | tf_op jit(solution)/shard_map/ppermute | solution.py:391
  30.3 0.0 collective-permute-start.5
  30.3 0.9 %collective-permute-start.11 = (bf16[16,1024]{1,0:T(8,128)(2,1)S(1)}, bf16[16,1024]{1,0:T(8,128)(2,1)S(1)}, u32[]{:S(2)}, u32[]{:S(2)}) collective-permute-start(bf16[16,1024]{1,0:T(8,128)(2,1)S(1)} %slice.39), channel_id=1, source_target_pairs={{0,8},{2,10},{4,12},{6,14},{8,0},{10,2},{12,4},{14,6},{1,9},{3,11}... | collective-permute-start | bytes 98312 | tf_op jit(solution)/shard_map/ppermute | solution.py:391
  31.2 0.0 collective-permute-done.7
  31.2 2.4 %collective-permute-done.9 = bf16[24,1024]{1,0:T(8,128)(2,1)S(1)} collective-permute-done((bf16[24,1024]{1,0:T(8,128)(2,1)S(1)}, bf16[24,1024]{1,0:T(8,128)(2,1)S(1)}, u32[]{:S(2)}, u32[]{:S(2)}) %collective-permute-start.9) | collective-permute-done | bytes 49184 | tf_op jit(solution)/shard_map/ppermute | solution.py:391
  33.7 0.1 collective-permute-start.10
  33.7 1.4 %collective-permute-done.11 = bf16[16,1024]{1,0:T(8,128)(2,1)S(1)} collective-permute-done((bf16[16,1024]{1,0:T(8,128)(2,1)S(1)}, bf16[16,1024]{1,0:T(8,128)(2,1)S(1)}, u32[]{:S(2)}, u32[]{:S(2)}) %collective-permute-start.11) | collective-permute-done | bytes 32800 | tf_op jit(solution)/shard_map/ppermute | solution.py:391
  35.1 2.0 %collective-permute-start.12 = (bf16[16,1024]{1,0:T(8,128)(2,1)S(1)}, bf16[16,1024]{1,0:T(8,128)(2,1)S(1)}, u32[]{:S(2)}, u32[]{:S(2)}) collective-permute-start(bf16[16,1024]{1,0:T(8,128)(2,1)S(1)} %slice_add_fusion.1.refs_2_), channel_id=1, source_target_pairs={{0,1},{1,0},{2,3},{3,2},{4,5},{5,4},{6,7},{7,6},{8,9},{9,8},{10,11... | collective-permute-start | bytes 98312 | tf_op jit(solution)/shard_map/ppermute | solution.py:391
  37.1 0.8 %correlate.2.refs_3_ = f32[12,32,1024]{2,1,0:T(8,128)S(1)} custom-call(bf16[3,32,1024]{2,1,0:T(8,128)(2,1)S(1)} %bitcast.6, bf16[24,1024]{1,0:T(8,128)(2,1)S(1)} %slice_add_fusion.refs_1_, bf16[16,1024]{1,0:T(8,128)(2,1)S(1)} %slice_add_fusion.1.refs_2_), custom_call_target="tpu_custom_call" | custom-call | tf_op jit(solution)/shard_map/correlate/pallas_call | solution.py:366
  37.9 0.0 collective-permute-done.5
  37.9 1.1 %collective-permute-done.12.refs_2_ = bf16[16,1024]{1,0:T(8,128)(2,1)S(1)} collective-permute-done((bf16[16,1024]{1,0:T(8,128)(2,1)S(1)}, bf16[16,1024]{1,0:T(8,128)(2,1)S(1)}, u32[]{:S(2)}, u32[]{:S(2)}) %collective-permute-start.12) | collective-permute-done | bytes 32800 | tf_op jit(solution)/shard_map/ppermute | solution.py:391
  39.0 0.0 collective-permute-done.10.refs_1_
  39.0 1.6 %correlate.3 = f32[12,32,1024]{2,1,0:T(8,128)} custom-call(bf16[3,32,1024]{2,1,0:T(8,128)(2,1)S(1)} %bitcast.7, bf16[24,1024]{1,0:T(8,128)(2,1)S(1)} %collective-permute-done.10.refs_1_, bf16[16,1024]{1,0:T(8,128)(2,1)S(1)} %collective-permute-done.12.refs_2_, f32[12,32,1024]{2,1,0:T(8,128)S(1)} %correlate.2.refs_3_), custom_call_target="tpu_custom_call" | custom-call | tf_op jit(solution)/shard_map/correlate/pallas_call | solution.py:366
  (8 shorter events, 0.1 us)
Async XLA Ops:
  0.0 1.5 %collective-permute-start = (s32[1,12]{1,0:T(1,128)}, s32[1,12]{1,0:T(1,128)S(1)}, u32[]{:S(2)}, u32[]{:S(2)}) collective-permute-start(s32[1,12]{1,0:T(1,128)} %wanted.1), channel_id=1, source_target_pairs={{0,2},{2,0},{4,6},{6,4},{8,10},{10,8},{12,14},{14,12},{1,3},{3,1},... | collective-permute-start | bytes 152 | tf_op jit(solution)/shard_map/ppermute | solution.py:391
  1.5 5.0 %copy-start = (bf16[1024,1024]{1,0:T(8,128)(2,1)S(1)}, bf16[1024,1024]{1,0:T(8,128)(2,1)}, u32[]{:S(2)}) copy-start(bf16[1024,1024]{1,0:T(8,128)(2,1)} %constant.10.clone.table) | copy-start | bytes 6291460
  1.5 5.0 %copy-start.1 = (bf16[64,6144]{1,0:T(8,128)(2,1)S(1)}, bf16[64,6144]{1,0:T(8,128)(2,1)}, u32[]{:S(2)}) copy-start(bf16[64,6144]{1,0:T(8,128)(2,1)} %traces.5) | copy-start | bytes 2359300
  1.5 5.0 %copy-start.2 = (f32[64,33]{0,1:T(8,128)S(1)}, f32[64,33]{0,1:T(8,128)}, u32[]{:S(2)}) copy-start(f32[64,33]{0,1:T(8,128)} %param.7) | copy-start | bytes 25348
  1.5 16.8 %collective-permute-start.1 = (bf16[64,2176]{1,0:T(8,128)(2,1)S(1)}, bf16[64,2176]{1,0:T(8,128)(2,1)S(1)}, u32[]{:S(2)}, u32[]{:S(2)}) collective-permute-start(bf16[64,2176]{1,0:T(8,128)(2,1)S(1)} %get-tuple-element.28), channel_id=1, source_target_pairs={{0,1},{2,3},{4,5},{6,7},{8,9},{10,11},{12,13},{14,15},{16,17},{18,... | collective-permute-start | bytes 835592 | tf_op jit(solution)/shard_map/ppermute | solution.py:430
  7.7 9.7 %copy-start.3 = (s32[8,36]{1,0:T(8,128)S(1)}, s32[8,36]{1,0:T(8,128)}, u32[]{:S(2)}) copy-start(s32[8,36]{1,0:T(8,128)} %slots.1) | copy-start | bytes 3460
  7.7 9.7 %copy-start.4 = (s32[8]{0:T(128)S(1)}, s32[8]{0:T(128)}, u32[]{:S(2)}) copy-start(s32[8]{0:T(128)} %counts.1) | copy-start | bytes 100
  9.2 5.4 %collective-permute-start.4 = (s32[2,12]{1,0:T(2,128)S(1)}, s32[2,12]{1,0:T(2,128)S(1)}, u32[]{:S(2)}, u32[]{:S(2)}) collective-permute-start(s32[2,12]{1,0:T(2,128)S(1)} %pair.1.refs_0_), channel_id=1, source_target_pairs={{0,12},{2,14},{4,8},{6,10},{8,4},{10,6},{12,0},{14,2},{1,13},{3,15... | collective-permute-start | bytes 296 | tf_op jit(solution)/shard_map/ppermute | solution.py:391
  12.8 4.5 %collective-permute-start.3 = (s32[2,12]{1,0:T(2,128)S(1)}, s32[2,12]{1,0:T(2,128)S(1)}, u32[]{:S(2)}, u32[]{:S(2)}) collective-permute-start(s32[2,12]{1,0:T(2,128)S(1)} %pair.1.refs_0_), channel_id=1, source_target_pairs={{0,8},{2,10},{4,12},{6,14},{8,0},{10,2},{12,4},{14,6},{1,9},{3,11}... | collective-permute-start | bytes 296 | tf_op jit(solution)/shard_map/ppermute | solution.py:391
  12.8 4.5 %collective-permute-start.2 = (s32[2,12]{1,0:T(2,128)S(1)}, s32[2,12]{1,0:T(2,128)S(1)}, u32[]{:S(2)}, u32[]{:S(2)}) collective-permute-start(s32[2,12]{1,0:T(2,128)S(1)} %pair.1.refs_0_), channel_id=1, source_target_pairs={{0,4},{2,6},{4,0},{6,2},{8,12},{10,14},{12,8},{14,10},{1,5},{3,7},... | collective-permute-start | bytes 296 | tf_op jit(solution)/shard_map/ppermute | solution.py:391
  20.9 1.7 %collective-permute-start.6 = (bf16[160,1024]{1,0:T(8,128)(2,1)S(1)}, bf16[160,1024]{1,0:T(8,128)(2,1)S(1)}, u32[]{:S(2)}, u32[]{:S(2)}) collective-permute-start(bf16[160,1024]{1,0:T(8,128)(2,1)S(1)} %get-tuple-element.41), channel_id=1, source_target_pairs={{0,2},{2,0},{4,6},{6,4},{8,10},{10,8},{12,14},{14,12},{1,3},{3,1},... | collective-permute-start | bytes 983048 | tf_op jit(solution)/shard_map/ppermute | solution.py:391
  22.8 5.4 %collective-permute-start.8 = (bf16[40,1024]{1,0:T(8,128)(2,1)S(1)}, bf16[40,1024]{1,0:T(8,128)(2,1)S(1)}, u32[]{:S(2)}, u32[]{:S(2)}) collective-permute-start(bf16[40,1024]{1,0:T(8,128)(2,1)S(1)} %get-tuple-element.45), channel_id=1, source_target_pairs={{0,4},{2,6},{4,0},{6,2},{8,12},{10,14},{12,8},{14,10},{1,5},{3,7},... | collective-permute-start | bytes 245768 | tf_op jit(solution)/shard_map/ppermute | solution.py:391
  22.9 8.3 %collective-permute-start.7 = (bf16[40,1024]{1,0:T(8,128)(2,1)S(1)}, bf16[40,1024]{1,0:T(8,128)(2,1)S(1)}, u32[]{:S(2)}, u32[]{:S(2)}) collective-permute-start(bf16[40,1024]{1,0:T(8,128)(2,1)S(1)} %get-tuple-element.43), channel_id=1, source_target_pairs={{0,4},{2,6},{4,0},{6,2},{8,12},{10,14},{12,8},{14,10},{1,5},{3,7},... | collective-permute-start | bytes 245768 | tf_op jit(solution)/shard_map/ppermute | solution.py:391
  28.2 5.5 %collective-permute-start.9 = (bf16[24,1024]{1,0:T(8,128)(2,1)S(1)}, bf16[24,1024]{1,0:T(8,128)(2,1)S(1)}, u32[]{:S(2)}, u32[]{:S(2)}) collective-permute-start(bf16[24,1024]{1,0:T(8,128)(2,1)S(1)} %slice.37), channel_id=1, source_target_pairs={{0,8},{2,10},{4,12},{6,14},{8,0},{10,2},{12,4},{14,6},{1,9},{3,11}... | collective-permute-start | bytes 147464 | tf_op jit(solution)/shard_map/ppermute | solution.py:391
  30.3 7.6 %collective-permute-start.5 = (bf16[96,1024]{1,0:T(8,128)(2,1)S(1)}, bf16[96,1024]{1,0:T(8,128)(2,1)S(1)}, u32[]{:S(2)}, u32[]{:S(2)}) collective-permute-start(bf16[96,1024]{1,0:T(8,128)(2,1)S(1)} %get-tuple-element.39), channel_id=1, source_target_pairs={{0,1},{1,0},{2,3},{3,2},{4,5},{5,4},{6,7},{7,6},{8,9},{9,8},{10,11... | collective-permute-start | bytes 589832 | tf_op jit(solution)/shard_map/ppermute | solution.py:391
  30.3 4.8 %collective-permute-start.11 = (bf16[16,1024]{1,0:T(8,128)(2,1)S(1)}, bf16[16,1024]{1,0:T(8,128)(2,1)S(1)}, u32[]{:S(2)}, u32[]{:S(2)}) collective-permute-start(bf16[16,1024]{1,0:T(8,128)(2,1)S(1)} %slice.39), channel_id=1, source_target_pairs={{0,8},{2,10},{4,12},{6,14},{8,0},{10,2},{12,4},{14,6},{1,9},{3,11}... | collective-permute-start | bytes 98312 | tf_op jit(solution)/shard_map/ppermute | solution.py:391
  33.7 5.4 %collective-permute-start.10 = (bf16[24,1024]{1,0:T(8,128)(2,1)S(1)}, bf16[24,1024]{1,0:T(8,128)(2,1)S(1)}, u32[]{:S(2)}, u32[]{:S(2)}) collective-permute-start(bf16[24,1024]{1,0:T(8,128)(2,1)S(1)} %slice_add_fusion.refs_1_), channel_id=1, source_target_pairs={{0,1},{1,0},{2,3},{3,2},{4,5},{5,4},{6,7},{7,6},{8,9},{9,8},{10,11... | collective-permute-start | bytes 147464 | tf_op jit(solution)/shard_map/ppermute | solution.py:391
  35.1 3.9 %collective-permute-start.12 = (bf16[16,1024]{1,0:T(8,128)(2,1)S(1)}, bf16[16,1024]{1,0:T(8,128)(2,1)S(1)}, u32[]{:S(2)}, u32[]{:S(2)}) collective-permute-start(bf16[16,1024]{1,0:T(8,128)(2,1)S(1)} %slice_add_fusion.1.refs_2_), channel_id=1, source_target_pairs={{0,1},{1,0},{2,3},{3,2},{4,5},{5,4},{6,7},{7,6},{8,9},{9,8},{10,11... | collective-permute-start | bytes 98312 | tf_op jit(solution)/shard_map/ppermute | solution.py:391

commit v4 on v2

--- a/solution.py
+++ b/solution.py
@@ -215,30 +215,37 @@
 
 def picks_kernel(shape, where, counts, slots, *refs):
     channels, windows, pairs, chips = shape
-    wanted, picks, chosen = refs[:-2], refs[-2], refs[-1]
+    wanted, (picks, chosen, lines) = refs[:-3], refs[-3:]
     group = where[0]
     first = jnp.int32(0)
     for g in range(counts.shape[0]):
         first = first + jnp.where(g < group, counts[g], 0)
     owned = counts[group]
+    lines[...] = jnp.zeros_like(lines)
+    at = 0
+    for w in wanted:
+        lines[at : at + w.shape[0], :pairs] = w[...]
+        at += w.shape[0]
+    slot = lines[...] - first
+    channel = jnp.full(slot.shape, -1, jnp.int32)
+    for s in range(slots.shape[1]):
+        channel = jnp.where(slot == s, slots[group, s], channel)
+    channel = jnp.where((slot >= 0) & (slot < owned), channel, -1)
+    turned = channel.astype(F32).T
     width = windows * channels
     lane = lax.broadcasted_iota(jnp.int32, (1, width), 1)
-    columns = [jnp.where(lane // channels == w, lane % channels, -2) for w in range(windows)]
+    columns = [
+        jnp.where(lane // channels == w, lane % channels, -2).astype(F32) for w in range(windows)
+    ]
     sizes = part_rows(windows, pairs)
-    per = wanted[0].shape[0]
     chosen[...] = jnp.zeros_like(chosen)
     for core in range(2):
         for d in range(chips):
             base = (core * chips + d) * sum(sizes)
-            tail = base + sizes[0]
-            for p in range(pairs):
-                slot = wanted[2 * d // per][(2 * d + core) % per, p] - first
-                mine = (slot >= 0) & (slot < owned)
-                channel = slots[group, jnp.where(mine, slot, 0)]
-                channel = jnp.where(mine, channel, -1)
-                for w in range(windows):
-                    row = (base + w * pairs if w < windows - 1 else tail) + p
-                    chosen[row : row + 1, :] = (columns[w] == channel).astype(F32)
+            one = turned[:pairs, 2 * d + core : 2 * d + core + 1]
+            for w in range(windows):
+                row = base + (w * pairs if w < windows - 1 else sizes[0])
+                chosen[row : row + pairs, :] = (one == columns[w]).astype(F32)
     picks[...] = chosen[...].astype(BF16)
 
 
@@ -301,24 +308,21 @@
                 blocks[d][w * size : (w + 1) * size, :] = moved.astype(BF16)
 
 
-def correlate_kernel(windows, factor, count, *refs):
-    receivers = refs[:count]
-    sources = refs[count : 3 * count]
-    last = len(refs) == 3 * count + 6
-    total = refs[3 * count] if last else None
-    out, line_r, line_s = refs[3 * count + last : 3 * count + last + 3]
+def correlate_kernel(spans, pairs, factor, has_total, last, *refs):
+    count = len(spans)
+    receivers, sources = refs[:count], refs[count : 2 * count]
+    total = refs[2 * count] if has_total else None
+    out, line_r, line_s = refs[2 * count + has_total : 2 * count + has_total + 3]
     held, sems = refs[-2:] if last else (out, None)
-    pairs, part = out.shape[0], out.shape[1]
-    for d in range(count):
-        for w in range(windows):
-            at = d * windows + w
-            line_r[at] = receivers[d][w].astype(F32) * factor
-            if w < windows - 1:
-                rows = sources[2 * d][w * pairs : (w + 1) * pairs, :].astype(F32)
-            else:
-                rows = sources[2 * d + 1][:pairs, :].astype(F32)
+    part = out.shape[1]
+    windows = 0
+    for receiver, source, span in zip(receivers, sources, spans):
+        for i, w in enumerate(span):
+            line_r[windows] = receiver[w].astype(F32) * factor
+            rows = source[i * pairs : (i + 1) * pairs, :].astype(F32)
             for p in range(pairs):
-                line_s[p, at : at + 1, :] = rows[p : p + 1, :]
+                line_s[p, windows : windows + 1, :] = rows[p : p + 1, :]
+            windows += 1
 
     def copy(p):
         return pltpu.make_async_copy(held.at[p], out.at[p], sems.at[p])
@@ -327,12 +331,12 @@
         for f in range(0, NF, 128):
             re = slice(f, f + 128)
             im = slice(NF + f, NF + f + 128)
-            if last:
+            if has_total:
                 total_r, total_i = total[p, :, re], total[p, :, im]
             else:
                 total_r = jnp.zeros((part, 128), F32)
                 total_i = jnp.zeros((part, 128), F32)
-            for at in range(count * windows):
+            for at in range(windows):
                 rr = line_r[at, :, re]
                 ri = line_r[at, :, im]
                 sr = line_s[p, at : at + 1, re]
@@ -351,27 +355,27 @@
             copy(p).wait()
 
 
-def correlate(receivers, sources, total, pairs, factor):
-    windows, part, width = receivers[0].shape
-    count = len(receivers)
+def correlate(receivers, sources, spans, total, pairs, factor, last):
+    _, part, width = receivers[0].shape
+    windows = sum(len(span) for span in spans)
     vmem = pl.BlockSpec(memory_space=pltpu.VMEM)
     shape = (pairs, part, width)
-    last = total is not None
+    extra = [] if total is None else [total]
     scratch = [
-        pltpu.VMEM((count * windows, part, width), F32),
-        pltpu.VMEM((pairs, -(-count * windows // 8) * 8, width), F32),
+        pltpu.VMEM((windows, part, width), F32),
+        pltpu.VMEM((pairs, -(-windows // 8) * 8, width), F32),
     ]
     if last:
         scratch += [pltpu.VMEM(shape, F32), pltpu.SemaphoreType.DMA((pairs,))]
     return pl.pallas_call(
-        functools.partial(correlate_kernel, windows, factor, count),
+        functools.partial(correlate_kernel, spans, pairs, factor, len(extra), last),
         out_shape=jax.ShapeDtypeStruct(shape, F32),
-        in_specs=[vmem] * (3 * count + last),
+        in_specs=[vmem] * (2 * len(spans) + len(extra)),
         out_specs=pl.BlockSpec(memory_space=pltpu.HBM) if last else vmem,
         scratch_shapes=scratch,
         compiler_params=pltpu.CompilerParams(vmem_limit_bytes=LIMIT),
         name="correlate",
-    )(*receivers, *(part for both in sources for part in both), *([total] if last else []))
+    )(*receivers, *sources, *extra)
 
 
 def shards(traces, filter_taps, source_counts, source_channel, block_sources):
@@ -409,7 +413,6 @@
         compiler_params=params,
         name="tail",
     )(*(pltpu.with_memory_space_constraint(a, pltpu.HBM) for a in (traces, block_sources)))
-    halo = lax.ppermute(tail, "tm", [(i - 1, i) for i in range(1, times)])
     taps = filter_taps.T
     traces, taps, table = (
         pltpu.with_memory_space_constraint(a, pltpu.VMEM)
@@ -426,6 +429,9 @@
             name="pair",
         )(ids, other)
     ]
+    tail, pair = lax.optimization_barrier((tail, wanted[0]))
+    wanted = [pair]
+    halo = lax.ppermute(tail, "tm", [(i - 1, i) for i in range(1, times)])
     for bit in bits:
         known = jnp.concatenate(wanted, axis=0)
         wanted = [known, across(known, "chan", 2 * bit)]
@@ -471,9 +477,12 @@
     picks = pl.pallas_call(
         functools.partial(picks_kernel, shape),
         out_shape=jax.ShapeDtypeStruct((2 * rows_out, width), BF16),
-        in_specs=[smem] * (3 + len(wanted)),
+        in_specs=[smem] * 3 + [vmem] * len(wanted),
         out_specs=vmem,
-        scratch_shapes=[pltpu.VMEM((2 * rows_out, width), F32)],
+        scratch_shapes=[
+            pltpu.VMEM((2 * rows_out, width), F32),
+            pltpu.VMEM((2 * chips, 128), jnp.int32),
+        ],
         compiler_params=params,
         name="picks",
     )(where, source_counts, source_channel, *wanted)
@@ -535,9 +544,21 @@
         sources.append(both)
 
     factor = 1.0 / (windows * times)
-    total = correlate(receivers[:1], sources[:1], None, pairs, factor)
+    early, late = list(range(windows - 1)), [windows - 1]
+    total = correlate(
+        receivers[:1] * 2, sources[0], (early, late), None, pairs, factor, times == 1
+    )
     if times > 1:
-        total = correlate(receivers[1:], sources[1:], total, pairs, factor)
+        for i, span in enumerate((early, late)):
+            total = correlate(
+                receivers[1:],
+                [both[i] for both in sources[1:]],
+                (span,) * (times - 1),
+                total,
+                pairs,
+                factor,
+                i == 1,
+            )
     return total.transpose(1, 0, 2)
 
 

time: 37.9 us -> 37.8 us (level)
  starting transfers between devices: 16.4 us -> 16.9 us
  waiting for transfers between devices: 11.2 us -> 10.7 us
    ppermute x1, starting transfers between devices: 4.4 us -> 4.93 us  [shards(): halo = lax.ppermute(tail, 'tm', [(i - 1, i) for i in range(1, times)])]
    ppermute x11, waiting for transfers between devices: 11.2 us -> 10.7 us  [across(): return lax.ppermute(x, axis, [(i, i ^ distance) for i in range(size)])]
    pallas_call x2 -> x3, Pallas kernels: 2.32 us -> 2.59 us  [correlate(): pl.pallas_call(functools.partial(correlate_kernel, spans, pairs, factor,...]
  transfers between devices with their start and end apart: 12 -> 12, of which waited for: 7 -> 7; matrix products, arithmetic and copies ran while one was open for 0% -> 0% of each run, Pallas kernels for 14% -> 15%
where the time goes in v4:
time: 37.8 us; the launch traced here: 37.6 us
  starting transfers between devices  16.9 us (45%)
  waiting for transfers between devices  10.7 us (28%)
  Pallas kernels  9.57 us (25%)
    ppermute x11, starting transfers between devices, across(): return lax.ppermute(x, axis, [(i, i ^ distance) for i in range(size)])  12 us
    ppermute x11, waiting for transfers between devices, across(): return lax.ppermute(x, axis, [(i, i ^ distance) for i in range(size)])  10.7 us
    ppermute x1, starting transfers between devices, shards(): halo = lax.ppermute(tail, 'tm', [(i - 1, i) for i in range(1, times)])  4.93 us
    pallas_call x3, Pallas kernels, correlate(): pl.pallas_call(functools.partial(correlate_kernel, spans, pairs, factor,...  2.59 us
    pallas_call x1, Pallas kernels, shards(): pl.pallas_call(functools.partial(rest_kernel, windows, times), out_shape=...  2.55 us
    pallas_call x1, Pallas kernels, shards(): pl.pallas_call(functools.partial(second_kernel, windows), out_shape=chunk...  1.48 us
    pallas_call x1, Pallas kernels, shards(): pl.pallas_call(functools.partial(first_kernel, windows), out_shape=chunk_...  1.14 us
    pallas_call x1, Pallas kernels, shards(): pl.pallas_call(tail_kernel, out_shape=[jax.ShapeDtypeStruct((channels, HA...  0.97 us
  transfers between devices with their start and end apart: 12, of which 7 were waited for; matrix products, arithmetic and copies ran while one was open for 0% of the time, Pallas kernels for 15%

profile of v4, /device:TPU:0, one launch (start us, length us, event | category | flops | bytes accessed | tf_op | source)
XLA Modules:
  0.0 37.6 jit_solution(15695130878503400788)
XLA Ops:
  0.0 0.5 %collective-permute-start = (s32[1,12]{1,0:T(1,128)}, s32[1,12]{1,0:T(1,128)S(1)}, u32[]{:S(2)}, u32[]{:S(2)}) collective-permute-start(s32[1,12]{1,0:T(1,128)} %wanted.1), channel_id=1, source_target_pairs={{0,2},{2,0},{4,6},{6,4},{8,10},{10,8},{12,14},{14,12},{1,3},{3,1},... | collective-permute-start | bytes 152 | tf_op jit(solution)/shard_map/ppermute | solution.py:395
  0.5 1.0 %tail.1 = (bf16[64,2176]{1,0:T(8,128)(2,1)S(1)}, s32[1,12]{1,0:T(1,128)S(1)}) custom-call(bf16[64,6144]{1,0:T(8,128)(2,1)} %traces.5, s32[1,12]{1,0:T(1,128)} %wanted.1), custom_call_target="tpu_custom_call" | custom-call | tf_op jit(solution)/shard_map/tail/pallas_call | solution.py:404
  1.5 0.0 collective-permute-done.other
  1.5 0.0 copy-start
  1.5 0.0 copy-start.1
  1.5 0.0 copy-start.2
  1.5 4.9 %collective-permute-start.1 = (bf16[64,2176]{1,0:T(8,128)(2,1)S(1)}, bf16[64,2176]{1,0:T(8,128)(2,1)S(1)}, u32[]{:S(2)}, u32[]{:S(2)}) collective-permute-start(bf16[64,2176]{1,0:T(8,128)(2,1)S(1)} %get-tuple-element.28), channel_id=1, source_target_pairs={{0,1},{2,3},{4,5},{6,7},{8,9},{10,11},{12,13},{14,15},{16,17},{18,... | collective-permute-start | bytes 835592 | tf_op jit(solution)/shard_map/ppermute | solution.py:434
  6.5 0.1 pad_add_fusion.1.where
  6.5 1.6 %collective-permute-start.2 = (s32[2,12]{1,0:T(2,128)S(1)}, s32[2,12]{1,0:T(2,128)S(1)}, u32[]{:S(2)}, u32[]{:S(2)}) collective-permute-start(s32[2,12]{1,0:T(2,128)S(1)} %pair.1), channel_id=1, source_target_pairs={{0,4},{2,6},{4,0},{6,2},{8,12},{10,14},{12,8},{14,10},{1,5},{3,7},... | collective-permute-start | bytes 296 | tf_op jit(solution)/shard_map/ppermute | solution.py:395
  8.1 0.0 copy-done
  8.1 0.0 copy-done.1
  8.1 0.0 copy-done.2
  8.1 1.1 %first.1 = (f32[128,512]{1,0:T(8,128)S(1)}, f32[64,512]{1,0:T(8,128)S(1)}, f32[64,512]{1,0:T(8,128)S(1)}, bf16[64,256]{1,0:T(8,128)(2,1)S(1)}, bf16[64,96]{1,0:T(8,128)(2,1)S(1)}, /*index=5*/bf16[64,144]{1,0:T(8,128)(2,1)S(1)}) custom-call(bf16[64,6144]{1,0:T(8,128)(2,1)S(1)} %copy-done.1, f32[33,64]{1,0:T(8,128)S(1)} %bitcast.10, bf16[1024,1024]{1,0:T(8,128)(2,1)S(1)} %copy-done), custom_call_target="tpu_custom_call" | custom-call | tf_op jit(solution)/shard_map/first/pallas_call | solution.py:447
  9.3 0.0 copy-start.3
  9.3 0.0 copy-start.4
  9.3 0.8 %collective-permute-done.2 = s32[2,12]{1,0:T(2,128)S(1)} collective-permute-done((s32[2,12]{1,0:T(2,128)S(1)}, s32[2,12]{1,0:T(2,128)S(1)}, u32[]{:S(2)}, u32[]{:S(2)}) %collective-permute-start.2) | collective-permute-done | bytes 128 | tf_op jit(solution)/shard_map/ppermute | solution.py:395
  10.1 2.6 %collective-permute-start.3 = (s32[4,12]{1,0:T(4,128)S(1)}, s32[4,12]{1,0:T(4,128)S(1)}, u32[]{:S(2)}, u32[]{:S(2)}) collective-permute-start(s32[4,12]{1,0:T(4,128)S(1)} %pad_add_fusion.refs_0_), channel_id=1, source_target_pairs={{0,8},{2,10},{4,12},{6,14},{8,0},{10,2},{12,4},{14,6},{1,9},{3,11}... | collective-permute-start | bytes 584 | tf_op jit(solution)/shard_map/ppermute | solution.py:395
  12.8 1.5 %second.1 = (f32[128,512]{1,0:T(8,128)S(1)}, f32[64,512]{1,0:T(8,128)S(1)}, bf16[64,1024]{1,0:T(8,128)(2,1)S(1)}) custom-call(bf16[64,6144]{1,0:T(8,128)(2,1)S(1)} %copy-done.1, bf16[1024,1024]{1,0:T(8,128)(2,1)S(1)} %copy-done, bf16[64,144]{1,0:T(8,128)(2,1)S(1)} %get-tuple-element.31.lines, bf16[64,96]{1,0:T(8,128)(2,1)S(1)} %get-tuple-element.32.edge, ...), custom_call_target="tpu_custom_call" | custom-call | tf_op jit(solution)/shard_map/second/pallas_call | solution.py:465
  14.3 0.4 %collective-permute-done.3.refs_1_ = s32[4,12]{1,0:T(4,128)S(1)} collective-permute-done((s32[4,12]{1,0:T(4,128)S(1)}, s32[4,12]{1,0:T(4,128)S(1)}, u32[]{:S(2)}, u32[]{:S(2)}) %collective-permute-start.3) | collective-permute-done | bytes 224 | tf_op jit(solution)/shard_map/ppermute | solution.py:395
  14.7 0.0 copy-done.3
  14.7 0.0 copy-done.4
  14.7 0.8 %picks.1.refs_1_ = bf16[320,192]{1,0:T(8,128)(2,1)S(1)} custom-call(s32[2]{0:T(128)S(1)} %pad_add_fusion.1.where, s32[8]{0:T(128)S(1)} %copy-done.4, s32[8,36]{1,0:T(8,128)S(1)} %copy-done.3, s32[4,12]{1,0:T(4,128)S(1)} %pad_add_fusion.refs_0_, s32[4,12]{1,0:T(4,128)S(1)} %collective-permute-done.3.refs_1_), custom_call_target="tpu_custom_call" | custom-call | tf_op jit(solution)/shard_map/picks/pallas_call | solution.py:477
  15.5 0.0 collective-permute-done.1.halo
  15.5 2.6 %rest.1 = (bf16[160,1024]{1,0:T(8,128)(2,1)S(1)}, bf16[160,1024]{1,0:T(8,128)(2,1)S(1)}, bf16[96,1024]{1,0:T(8,128)(2,1)S(1)}, bf16[96,1024]{1,0:T(8,128)(2,1)S(1)}) custom-call(s32[2]{0:T(128)S(1)} %pad_add_fusion.1.where, bf16[64,2176]{1,0:T(8,128)(2,1)S(1)} %collective-permute-done.1.halo, bf16[64,256]{1,0:T(8,128)(2,1)S(1)} %get-tuple-element.29.ends, ...), custom_call_target="tpu_custom_call" | custom-call | tf_op jit(solution)/shard_map/rest/pallas_call | solution.py:489
  18.1 0.1 collective-permute-start.5
  18.2 1.6 %collective-permute-done.5 = bf16[160,1024]{1,0:T(8,128)(2,1)S(1)} collective-permute-done((bf16[160,1024]{1,0:T(8,128)(2,1)S(1)}, bf16[160,1024]{1,0:T(8,128)(2,1)S(1)}, u32[]{:S(2)}, u32[]{:S(2)}) %collective-permute-start.5) | collective-permute-done | bytes 327712 | tf_op jit(solution)/shard_map/ppermute | solution.py:395
  19.8 0.1 add.15
  19.9 1.6 %collective-permute-start.7 = (bf16[40,1024]{1,0:T(8,128)(2,1)S(1)}, bf16[40,1024]{1,0:T(8,128)(2,1)S(1)}, u32[]{:S(2)}, u32[]{:S(2)}) collective-permute-start(bf16[40,1024]{1,0:T(8,128)(2,1)S(1)} %get-tuple-element.45), channel_id=1, source_target_pairs={{0,4},{2,6},{4,0},{6,2},{8,12},{10,14},{12,8},{14,10},{1,5},{3,7},... | collective-permute-start | bytes 245768 | tf_op jit(solution)/shard_map/ppermute | solution.py:395
  21.6 0.4 %collective-permute-start.6 = (bf16[40,1024]{1,0:T(8,128)(2,1)S(1)}, bf16[40,1024]{1,0:T(8,128)(2,1)S(1)}, u32[]{:S(2)}, u32[]{:S(2)}) collective-permute-start(bf16[40,1024]{1,0:T(8,128)(2,1)S(1)} %get-tuple-element.43), channel_id=1, source_target_pairs={{0,4},{2,6},{4,0},{6,2},{8,12},{10,14},{12,8},{14,10},{1,5},{3,7},... | collective-permute-start | bytes 245768 | tf_op jit(solution)/shard_map/ppermute | solution.py:395
  22.0 2.9 %collective-permute-done.7 = bf16[40,1024]{1,0:T(8,128)(2,1)S(1)} collective-permute-done((bf16[40,1024]{1,0:T(8,128)(2,1)S(1)}, bf16[40,1024]{1,0:T(8,128)(2,1)S(1)}, u32[]{:S(2)}, u32[]{:S(2)}) %collective-permute-start.7) | collective-permute-done | bytes 81952 | tf_op jit(solution)/shard_map/ppermute | solution.py:395
  25.0 2.6 %collective-permute-start.10 = (bf16[24,1024]{1,0:T(8,128)(2,1)S(1)}, bf16[24,1024]{1,0:T(8,128)(2,1)S(1)}, u32[]{:S(2)}, u32[]{:S(2)}) collective-permute-start(bf16[24,1024]{1,0:T(8,128)(2,1)S(1)} %slice.39), channel_id=1, source_target_pairs={{0,8},{2,10},{4,12},{6,14},{8,0},{10,2},{12,4},{14,6},{1,9},{3,11}... | collective-permute-start | bytes 147464 | tf_op jit(solution)/shard_map/ppermute | solution.py:395
  27.6 0.0 collective-permute-start.4
  27.6 0.3 collective-permute-start.8
  28.0 0.0 collective-permute-done.6
  28.0 2.4 %collective-permute-done.10 = bf16[24,1024]{1,0:T(8,128)(2,1)S(1)} collective-permute-done((bf16[24,1024]{1,0:T(8,128)(2,1)S(1)}, bf16[24,1024]{1,0:T(8,128)(2,1)S(1)}, u32[]{:S(2)}, u32[]{:S(2)}) %collective-permute-start.10) | collective-permute-done | bytes 49184 | tf_op jit(solution)/shard_map/ppermute | solution.py:395
  30.4 0.1 collective-permute-start.11
  30.5 2.0 %collective-permute-done.8 = bf16[16,1024]{1,0:T(8,128)(2,1)S(1)} collective-permute-done((bf16[16,1024]{1,0:T(8,128)(2,1)S(1)}, bf16[16,1024]{1,0:T(8,128)(2,1)S(1)}, u32[]{:S(2)}, u32[]{:S(2)}) %collective-permute-start.8) | collective-permute-done | bytes 32800 | tf_op jit(solution)/shard_map/ppermute | solution.py:395
  32.4 2.0 %collective-permute-start.9 = (bf16[16,1024]{1,0:T(8,128)(2,1)S(1)}, bf16[16,1024]{1,0:T(8,128)(2,1)S(1)}, u32[]{:S(2)}, u32[]{:S(2)}) collective-permute-start(bf16[16,1024]{1,0:T(8,128)(2,1)S(1)} %slice_add_fusion.1.refs_3_), channel_id=1, source_target_pairs={{0,1},{1,0},{2,3},{3,2},{4,5},{5,4},{6,7},{7,6},{8,9},{9,8},{10,11... | collective-permute-start | bytes 98312 | tf_op jit(solution)/shard_map/ppermute | solution.py:395
  34.5 0.8 %correlate.3.refs_2_ = f32[12,32,1024]{2,1,0:T(8,128)S(1)} custom-call(bf16[3,32,1024]{2,1,0:T(8,128)(2,1)S(1)} %bitcast.8, bf16[3,32,1024]{2,1,0:T(8,128)(2,1)S(1)} %bitcast.9, bf16[24,1024]{1,0:T(8,128)(2,1)S(1)} %slice_add_fusion.refs_2_, bf16[16,1024]{1,0:T(8,128)(2,1)S(1)} %slice_add_fusion.1.refs_3_), custom_call_target="tpu_custom_call" | custom-call | tf_op jit(solution)/shard_map/correlate/pallas_call | solution.py:370
  35.2 0.0 collective-permute-done.4
  35.2 0.0 collective-permute-done.11.refs_1_
  35.3 0.6 %correlate.4.refs_2_ = f32[12,32,1024]{2,1,0:T(8,128)S(1)} custom-call(bf16[3,32,1024]{2,1,0:T(8,128)(2,1)S(1)} %bitcast.6, bf16[24,1024]{1,0:T(8,128)(2,1)S(1)} %collective-permute-done.11.refs_1_, f32[12,32,1024]{2,1,0:T(8,128)S(1)} %correlate.3.refs_2_), custom_call_target="tpu_custom_call" | custom-call | tf_op jit(solution)/shard_map/correlate/pallas_call | solution.py:370
  35.8 0.5 %collective-permute-done.9.refs_1_ = bf16[16,1024]{1,0:T(8,128)(2,1)S(1)} collective-permute-done((bf16[16,1024]{1,0:T(8,128)(2,1)S(1)}, bf16[16,1024]{1,0:T(8,128)(2,1)S(1)}, u32[]{:S(2)}, u32[]{:S(2)}) %collective-permute-start.9) | collective-permute-done | bytes 32800 | tf_op jit(solution)/shard_map/ppermute | solution.py:395
  36.4 1.3 %correlate.5 = f32[12,32,1024]{2,1,0:T(8,128)} custom-call(bf16[3,32,1024]{2,1,0:T(8,128)(2,1)S(1)} %bitcast.7, bf16[16,1024]{1,0:T(8,128)(2,1)S(1)} %collective-permute-done.9.refs_1_, f32[12,32,1024]{2,1,0:T(8,128)S(1)} %correlate.4.refs_2_), custom_call_target="tpu_custom_call" | custom-call | tf_op jit(solution)/shard_map/correlate/pallas_call | solution.py:370
  (9 shorter events, 0.1 us)
Async XLA Ops:
  0.0 1.5 %collective-permute-start = (s32[1,12]{1,0:T(1,128)}, s32[1,12]{1,0:T(1,128)S(1)}, u32[]{:S(2)}, u32[]{:S(2)}) collective-permute-start(s32[1,12]{1,0:T(1,128)} %wanted.1), channel_id=1, source_target_pairs={{0,2},{2,0},{4,6},{6,4},{8,10},{10,8},{12,14},{14,12},{1,3},{3,1},... | collective-permute-start | bytes 152 | tf_op jit(solution)/shard_map/ppermute | solution.py:395
  1.5 6.6 %copy-start = (bf16[1024,1024]{1,0:T(8,128)(2,1)S(1)}, bf16[1024,1024]{1,0:T(8,128)(2,1)}, u32[]{:S(2)}) copy-start(bf16[1024,1024]{1,0:T(8,128)(2,1)} %constant.10.clone.table) | copy-start | bytes 6291460
  1.5 6.6 %copy-start.1 = (bf16[64,6144]{1,0:T(8,128)(2,1)S(1)}, bf16[64,6144]{1,0:T(8,128)(2,1)}, u32[]{:S(2)}) copy-start(bf16[64,6144]{1,0:T(8,128)(2,1)} %traces.5) | copy-start | bytes 2359300
  1.5 6.6 %copy-start.2 = (f32[64,33]{0,1:T(8,128)S(1)}, f32[64,33]{0,1:T(8,128)}, u32[]{:S(2)}) copy-start(f32[64,33]{0,1:T(8,128)} %param.7) | copy-start | bytes 25348
  1.5 14.0 %collective-permute-start.1 = (bf16[64,2176]{1,0:T(8,128)(2,1)S(1)}, bf16[64,2176]{1,0:T(8,128)(2,1)S(1)}, u32[]{:S(2)}, u32[]{:S(2)}) collective-permute-start(bf16[64,2176]{1,0:T(8,128)(2,1)S(1)} %get-tuple-element.28), channel_id=1, source_target_pairs={{0,1},{2,3},{4,5},{6,7},{8,9},{10,11},{12,13},{14,15},{16,17},{18,... | collective-permute-start | bytes 835592 | tf_op jit(solution)/shard_map/ppermute | solution.py:434
  6.5 3.6 %collective-permute-start.2 = (s32[2,12]{1,0:T(2,128)S(1)}, s32[2,12]{1,0:T(2,128)S(1)}, u32[]{:S(2)}, u32[]{:S(2)}) collective-permute-start(s32[2,12]{1,0:T(2,128)S(1)} %pair.1), channel_id=1, source_target_pairs={{0,4},{2,6},{4,0},{6,2},{8,12},{10,14},{12,8},{14,10},{1,5},{3,7},... | collective-permute-start | bytes 296 | tf_op jit(solution)/shard_map/ppermute | solution.py:395
  9.3 5.4 %copy-start.3 = (s32[8,36]{1,0:T(8,128)S(1)}, s32[8,36]{1,0:T(8,128)}, u32[]{:S(2)}) copy-start(s32[8,36]{1,0:T(8,128)} %slots.1) | copy-start | bytes 3460
  9.3 5.4 %copy-start.4 = (s32[8]{0:T(128)S(1)}, s32[8]{0:T(128)}, u32[]{:S(2)}) copy-start(s32[8]{0:T(128)} %counts.1) | copy-start | bytes 100
  10.1 4.5 %collective-permute-start.3 = (s32[4,12]{1,0:T(4,128)S(1)}, s32[4,12]{1,0:T(4,128)S(1)}, u32[]{:S(2)}, u32[]{:S(2)}) collective-permute-start(s32[4,12]{1,0:T(4,128)S(1)} %pad_add_fusion.refs_0_), channel_id=1, source_target_pairs={{0,8},{2,10},{4,12},{6,14},{8,0},{10,2},{12,4},{14,6},{1,9},{3,11}... | collective-permute-start | bytes 584 | tf_op jit(solution)/shard_map/ppermute | solution.py:395
  18.1 1.7 %collective-permute-start.5 = (bf16[160,1024]{1,0:T(8,128)(2,1)S(1)}, bf16[160,1024]{1,0:T(8,128)(2,1)S(1)}, u32[]{:S(2)}, u32[]{:S(2)}) collective-permute-start(bf16[160,1024]{1,0:T(8,128)(2,1)S(1)} %get-tuple-element.41), channel_id=1, source_target_pairs={{0,2},{2,0},{4,6},{6,4},{8,10},{10,8},{12,14},{14,12},{1,3},{3,1},... | collective-permute-start | bytes 983048 | tf_op jit(solution)/shard_map/ppermute | solution.py:395
  19.9 5.0 %collective-permute-start.7 = (bf16[40,1024]{1,0:T(8,128)(2,1)S(1)}, bf16[40,1024]{1,0:T(8,128)(2,1)S(1)}, u32[]{:S(2)}, u32[]{:S(2)}) collective-permute-start(bf16[40,1024]{1,0:T(8,128)(2,1)S(1)} %get-tuple-element.45), channel_id=1, source_target_pairs={{0,4},{2,6},{4,0},{6,2},{8,12},{10,14},{12,8},{14,10},{1,5},{3,7},... | collective-permute-start | bytes 245768 | tf_op jit(solution)/shard_map/ppermute | solution.py:395
  21.6 6.4 %collective-permute-start.6 = (bf16[40,1024]{1,0:T(8,128)(2,1)S(1)}, bf16[40,1024]{1,0:T(8,128)(2,1)S(1)}, u32[]{:S(2)}, u32[]{:S(2)}) collective-permute-start(bf16[40,1024]{1,0:T(8,128)(2,1)S(1)} %get-tuple-element.43), channel_id=1, source_target_pairs={{0,4},{2,6},{4,0},{6,2},{8,12},{10,14},{12,8},{14,10},{1,5},{3,7},... | collective-permute-start | bytes 245768 | tf_op jit(solution)/shard_map/ppermute | solution.py:395
  25.0 5.4 %collective-permute-start.10 = (bf16[24,1024]{1,0:T(8,128)(2,1)S(1)}, bf16[24,1024]{1,0:T(8,128)(2,1)S(1)}, u32[]{:S(2)}, u32[]{:S(2)}) collective-permute-start(bf16[24,1024]{1,0:T(8,128)(2,1)S(1)} %slice.39), channel_id=1, source_target_pairs={{0,8},{2,10},{4,12},{6,14},{8,0},{10,2},{12,4},{14,6},{1,9},{3,11}... | collective-permute-start | bytes 147464 | tf_op jit(solution)/shard_map/ppermute | solution.py:395
  27.6 7.6 %collective-permute-start.4 = (bf16[96,1024]{1,0:T(8,128)(2,1)S(1)}, bf16[96,1024]{1,0:T(8,128)(2,1)S(1)}, u32[]{:S(2)}, u32[]{:S(2)}) collective-permute-start(bf16[96,1024]{1,0:T(8,128)(2,1)S(1)} %get-tuple-element.39), channel_id=1, source_target_pairs={{0,1},{1,0},{2,3},{3,2},{4,5},{5,4},{6,7},{7,6},{8,9},{9,8},{10,11... | collective-permute-start | bytes 589832 | tf_op jit(solution)/shard_map/ppermute | solution.py:395
  27.6 4.8 %collective-permute-start.8 = (bf16[16,1024]{1,0:T(8,128)(2,1)S(1)}, bf16[16,1024]{1,0:T(8,128)(2,1)S(1)}, u32[]{:S(2)}, u32[]{:S(2)}) collective-permute-start(bf16[16,1024]{1,0:T(8,128)(2,1)S(1)} %slice.37), channel_id=1, source_target_pairs={{0,8},{2,10},{4,12},{6,14},{8,0},{10,2},{12,4},{14,6},{1,9},{3,11}... | collective-permute-start | bytes 98312 | tf_op jit(solution)/shard_map/ppermute | solution.py:395
  30.4 4.9 %collective-permute-start.11 = (bf16[24,1024]{1,0:T(8,128)(2,1)S(1)}, bf16[24,1024]{1,0:T(8,128)(2,1)S(1)}, u32[]{:S(2)}, u32[]{:S(2)}) collective-permute-start(bf16[24,1024]{1,0:T(8,128)(2,1)S(1)} %slice_add_fusion.refs_2_), channel_id=1, source_target_pairs={{0,1},{1,0},{2,3},{3,2},{4,5},{5,4},{6,7},{7,6},{8,9},{9,8},{10,11... | collective-permute-start | bytes 147464 | tf_op jit(solution)/shard_map/ppermute | solution.py:395
  32.4 3.9 %collective-permute-start.9 = (bf16[16,1024]{1,0:T(8,128)(2,1)S(1)}, bf16[16,1024]{1,0:T(8,128)(2,1)S(1)}, u32[]{:S(2)}, u32[]{:S(2)}) collective-permute-start(bf16[16,1024]{1,0:T(8,128)(2,1)S(1)} %slice_add_fusion.1.refs_3_), channel_id=1, source_target_pairs={{0,1},{1,0},{2,3},{3,2},{4,5},{5,4},{6,7},{7,6},{8,9},{9,8},{10,11... | collective-permute-start | bytes 98312 | tf_op jit(solution)/shard_map/ppermute | solution.py:395

commit v5 on v4

--- a/solution.py
+++ b/solution.py
@@ -128,7 +128,7 @@
         white[rows, NF:] = im
         return carry
 
-    lax.fori_loop(0, count // ROWS, step, 0, unroll=2)
+    lax.fori_loop(0, count // ROWS, step, 0, unroll=4)
 
 
 def tail_kernel(traces, wanted, tail, ids, sems):
@@ -213,25 +213,28 @@
     return [-(-w * pairs // 8) * 8 for w in (windows - 1, 1)]
 
 
-def picks_kernel(shape, where, counts, slots, *refs):
+def picks_kernel(shape, counts, slots, *refs):
     channels, windows, pairs, chips = shape
     wanted, (picks, chosen, lines) = refs[:-3], refs[-3:]
-    group = where[0]
-    first = jnp.int32(0)
-    for g in range(counts.shape[0]):
-        first = first + jnp.where(g < group, counts[g], 0)
-    owned = counts[group]
+    group = lax.axis_index("chan")
+    place = lax.broadcasted_iota(jnp.int32, counts.shape, 1)
+    held = counts[...].astype(F32)
+    first = jnp.sum(jnp.where(place < group, held, 0.0), axis=1, keepdims=True)
+    owned = jnp.sum(jnp.where(place == group, held, 0.0), axis=1, keepdims=True)
+    row = lax.broadcasted_iota(jnp.int32, slots.shape, 0)
+    own_slots = jnp.where(row == group, slots[...], 0).astype(F32)
+    own_slots = jnp.sum(own_slots, axis=0, keepdims=True)
     lines[...] = jnp.zeros_like(lines)
     at = 0
     for w in wanted:
-        lines[at : at + w.shape[0], :pairs] = w[...]
+        lines[at : at + w.shape[0], :pairs] = w[...].astype(F32)
         at += w.shape[0]
     slot = lines[...] - first
-    channel = jnp.full(slot.shape, -1, jnp.int32)
+    channel = jnp.full(slot.shape, -1.0, F32)
     for s in range(slots.shape[1]):
-        channel = jnp.where(slot == s, slots[group, s], channel)
-    channel = jnp.where((slot >= 0) & (slot < owned), channel, -1)
-    turned = channel.astype(F32).T
+        channel = jnp.where(slot == s, own_slots[:, s : s + 1], channel)
+    channel = jnp.where((slot >= 0) & (slot < owned), channel, -1.0)
+    turned = channel.T
     width = windows * channels
     lane = lax.broadcasted_iota(jnp.int32, (1, width), 1)
     columns = [
@@ -250,7 +253,7 @@
 
 
 def rest_kernel(
-    windows, times, where, halo, ends, taps, table, part_a, part_b, response_a, response_b, *refs
+    windows, times, halo, ends, taps, table, part_a, part_b, response_a, response_b, *refs
 ):
     own_white, picks, keep, send = refs[:4]
     blocks = refs[4 : 4 + times]
@@ -295,7 +298,7 @@
         keep[:, cols] = out[:base]
         send[:, cols] = out[base:]
     for d in range(times):
-        line = (where[1] ^ d) * size
+        line = (lax.axis_index("tm") ^ d) * size
         for w in range(windows):
             if size % ROWS == 0:
                 at = pl.multiple_of(w * channels + line, ROWS)
@@ -394,7 +397,6 @@
         size = lax.axis_size(axis)
         return lax.ppermute(x, axis, [(i, i ^ distance) for i in range(size)])
 
-    smem = pl.BlockSpec(memory_space=pltpu.SMEM)
     vmem = pl.BlockSpec(memory_space=pltpu.VMEM)
     hbm = pl.BlockSpec(memory_space=pltpu.HBM)
     params = pltpu.CompilerParams(vmem_limit_bytes=LIMIT)
@@ -435,7 +437,6 @@
     for bit in bits:
         known = jnp.concatenate(wanted, axis=0)
         wanted = [known, across(known, "chan", 2 * bit)]
-    where = jnp.stack([lax.axis_index("chan"), lax.axis_index("tm")]).astype(jnp.int32)
 
     shape = (channels, windows, pairs, chips)
     width = windows * channels
@@ -477,20 +478,17 @@
     picks = pl.pallas_call(
         functools.partial(picks_kernel, shape),
         out_shape=jax.ShapeDtypeStruct((2 * rows_out, width), BF16),
-        in_specs=[smem] * 3 + [vmem] * len(wanted),
+        in_specs=[vmem] * (2 + len(wanted)),
         out_specs=vmem,
-        scratch_shapes=[
-            pltpu.VMEM((2 * rows_out, width), F32),
-            pltpu.VMEM((2 * chips, 128), jnp.int32),
-        ],
+        scratch_shapes=[pltpu.VMEM((2 * rows_out, width), F32), pltpu.VMEM((2 * chips, 128), F32)],
         compiler_params=params,
         name="picks",
-    )(where, source_counts, source_channel, *wanted)
+    )(source_counts[None], source_channel, *wanted)
     outs = pl.pallas_call(
         functools.partial(rest_kernel, windows, times),
         out_shape=[jax.ShapeDtypeStruct((rows_out, 2 * NF), BF16)] * 2
         + [jax.ShapeDtypeStruct((windows * part, 2 * NF), BF16)] * times,
-        in_specs=[smem] + [vmem] * 10,
+        in_specs=[vmem] * 10,
         out_specs=[vmem] * (2 + times),
         scratch_shapes=[
             pltpu.VMEM((2 * tap_count + 6, width - channels), F32),
@@ -500,7 +498,6 @@
         compiler_params=params,
         name="rest",
     )(
-        where,
         halo,
         ends,
         taps,

time: 37.8 us -> 36.8 us (0.974)
  Pallas kernels: 9.57 us -> 8.2 us
    pallas_call x1, Pallas kernels: 2.55 us -> 1.83 us  [shards(): pl.pallas_call(functools.partial(rest_kernel, windows, times), out_shape=...]
    pallas_call x1, Pallas kernels: 0.83 us -> 0.35 us  [shards(): pl.pallas_call(functools.partial(picks_kernel, shape), out_shape=jax.Shap...]
  transfers between devices with their start and end apart: 12 -> 12, of which waited for: 7 -> 7; matrix products, arithmetic and copies ran while one was open for 0% -> 0% of each run, Pallas kernels for 15% -> 14%
where the time goes in v5:
time: 36.8 us; the launch traced here: 36.6 us
  starting transfers between devices  17 us (46%)
  waiting for transfers between devices  11 us (30%)
  Pallas kernels  8.2 us (22%)
    ppermute x11, starting transfers between devices, across(): return lax.ppermute(x, axis, [(i, i ^ distance) for i in range(size)])  12 us
    ppermute x11, waiting for transfers between devices, across(): return lax.ppermute(x, axis, [(i, i ^ distance) for i in range(size)])  11 us
    ppermute x1, starting transfers between devices, shards(): halo = lax.ppermute(tail, 'tm', [(i - 1, i) for i in range(1, times)])  4.93 us
    pallas_call x3, Pallas kernels, correlate(): pl.pallas_call(functools.partial(correlate_kernel, spans, pairs, factor,...  2.59 us
    pallas_call x1, Pallas kernels, shards(): pl.pallas_call(functools.partial(rest_kernel, windows, times), out_shape=...  1.83 us
    pallas_call x1, Pallas kernels, shards(): pl.pallas_call(functools.partial(second_kernel, windows), out_shape=chunk...  1.3 us
    pallas_call x1, Pallas kernels, shards(): pl.pallas_call(functools.partial(first_kernel, windows), out_shape=chunk_...  1.15 us
    pallas_call x1, Pallas kernels, shards(): pl.pallas_call(tail_kernel, out_shape=[jax.ShapeDtypeStruct((channels, HA...  0.97 us
  transfers between devices with their start and end apart: 12, of which 7 were waited for; matrix products, arithmetic and copies ran while one was open for 0% of the time, Pallas kernels for 14%

profile of v5, /device:TPU:0, one launch (start us, length us, event | category | flops | bytes accessed | tf_op | source)
XLA Modules:
  0.0 36.6 jit_solution(6887701893516033620)
XLA Ops:
  0.0 0.5 %collective-permute-start = (s32[1,12]{1,0:T(1,128)}, s32[1,12]{1,0:T(1,128)S(1)}, u32[]{:S(2)}, u32[]{:S(2)}) collective-permute-start(s32[1,12]{1,0:T(1,128)} %wanted.1), channel_id=1, source_target_pairs={{0,2},{2,0},{4,6},{6,4},{8,10},{10,8},{12,14},{14,12},{1,3},{3,1},... | collective-permute-start | bytes 152 | tf_op jit(solution)/shard_map/ppermute | solution.py:398
  0.5 1.0 %tail.1 = (bf16[64,2176]{1,0:T(8,128)(2,1)S(1)}, s32[1,12]{1,0:T(1,128)S(1)}) custom-call(bf16[64,6144]{1,0:T(8,128)(2,1)} %traces.5, s32[1,12]{1,0:T(1,128)} %wanted.1), custom_call_target="tpu_custom_call" | custom-call | tf_op jit(solution)/shard_map/tail/pallas_call | solution.py:406
  1.5 0.0 collective-permute-done.other
  1.5 0.0 copy-start
  1.5 0.0 copy-start.1
  1.5 0.0 copy-start.2
  1.5 4.9 %collective-permute-start.1 = (bf16[64,2176]{1,0:T(8,128)(2,1)S(1)}, bf16[64,2176]{1,0:T(8,128)(2,1)S(1)}, u32[]{:S(2)}, u32[]{:S(2)}) collective-permute-start(bf16[64,2176]{1,0:T(8,128)(2,1)S(1)} %get-tuple-element.28), channel_id=1, source_target_pairs={{0,1},{2,3},{4,5},{6,7},{8,9},{10,11},{12,13},{14,15},{16,17},{18,... | collective-permute-start | bytes 835592 | tf_op jit(solution)/shard_map/ppermute | solution.py:436
  6.5 1.6 %collective-permute-start.2 = (s32[2,12]{1,0:T(2,128)S(1)}, s32[2,12]{1,0:T(2,128)S(1)}, u32[]{:S(2)}, u32[]{:S(2)}) collective-permute-start(s32[2,12]{1,0:T(2,128)S(1)} %pair.1), channel_id=1, source_target_pairs={{0,4},{2,6},{4,0},{6,2},{8,12},{10,14},{12,8},{14,10},{1,5},{3,7},... | collective-permute-start | bytes 296 | tf_op jit(solution)/shard_map/ppermute | solution.py:398
  8.1 0.0 copy-done
  8.1 0.0 copy-done.1
  8.1 0.0 copy-done.2
  8.1 1.1 %first.1 = (f32[128,512]{1,0:T(8,128)S(1)}, f32[64,512]{1,0:T(8,128)S(1)}, f32[64,512]{1,0:T(8,128)S(1)}, bf16[64,256]{1,0:T(8,128)(2,1)S(1)}, bf16[64,96]{1,0:T(8,128)(2,1)S(1)}, /*index=5*/bf16[64,144]{1,0:T(8,128)(2,1)S(1)}) custom-call(bf16[64,6144]{1,0:T(8,128)(2,1)S(1)} %copy-done.1, f32[33,64]{1,0:T(8,128)S(1)} %bitcast.9, bf16[1024,1024]{1,0:T(8,128)(2,1)S(1)} %copy-done), custom_call_target="tpu_custom_call" | custom-call | tf_op jit(solution)/shard_map/first/pallas_call | solution.py:448
  9.3 0.0 copy-start.3
  9.3 0.0 copy-start.4
  9.3 0.8 %collective-permute-done.2 = s32[2,12]{1,0:T(2,128)S(1)} collective-permute-done((s32[2,12]{1,0:T(2,128)S(1)}, s32[2,12]{1,0:T(2,128)S(1)}, u32[]{:S(2)}, u32[]{:S(2)}) %collective-permute-start.2) | collective-permute-done | bytes 128 | tf_op jit(solution)/shard_map/ppermute | solution.py:398
  10.1 2.6 %collective-permute-start.3 = (s32[4,12]{1,0:T(4,128)S(1)}, s32[4,12]{1,0:T(4,128)S(1)}, u32[]{:S(2)}, u32[]{:S(2)}) collective-permute-start(s32[4,12]{1,0:T(4,128)S(1)} %pad_add_fusion.refs_0_), channel_id=1, source_target_pairs={{0,8},{2,10},{4,12},{6,14},{8,0},{10,2},{12,4},{14,6},{1,9},{3,11}... | collective-permute-start | bytes 584 | tf_op jit(solution)/shard_map/ppermute | solution.py:398
  12.8 1.3 %second.1 = (f32[128,512]{1,0:T(8,128)S(1)}, f32[64,512]{1,0:T(8,128)S(1)}, bf16[64,1024]{1,0:T(8,128)(2,1)S(1)}) custom-call(bf16[64,6144]{1,0:T(8,128)(2,1)S(1)} %copy-done.1, bf16[1024,1024]{1,0:T(8,128)(2,1)S(1)} %copy-done, bf16[64,144]{1,0:T(8,128)(2,1)S(1)} %get-tuple-element.31.lines, bf16[64,96]{1,0:T(8,128)(2,1)S(1)} %get-tuple-element.32.edge, ...), custom_call_target="tpu_custom_call" | custom-call | tf_op jit(solution)/shard_map/second/pallas_call | solution.py:466
  14.1 0.6 %collective-permute-done.3.refs_1_ = s32[4,12]{1,0:T(4,128)S(1)} collective-permute-done((s32[4,12]{1,0:T(4,128)S(1)}, s32[4,12]{1,0:T(4,128)S(1)}, u32[]{:S(2)}, u32[]{:S(2)}) %collective-permute-start.3) | collective-permute-done | bytes 224 | tf_op jit(solution)/shard_map/ppermute | solution.py:398
  14.7 0.0 copy-done.3
  14.7 0.0 copy-done.4
  14.7 0.3 picks.1.refs_1_
  15.0 0.0 collective-permute-done.1.halo
  15.0 1.8 %rest.1 = (bf16[160,1024]{1,0:T(8,128)(2,1)S(1)}, bf16[160,1024]{1,0:T(8,128)(2,1)S(1)}, bf16[96,1024]{1,0:T(8,128)(2,1)S(1)}, bf16[96,1024]{1,0:T(8,128)(2,1)S(1)}) custom-call(bf16[64,2176]{1,0:T(8,128)(2,1)S(1)} %collective-permute-done.1.halo, bf16[64,256]{1,0:T(8,128)(2,1)S(1)} %get-tuple-element.29.ends, f32[33,64]{1,0:T(8,128)S(1)} %bitcast.10, ...), custom_call_target="tpu_custom_call" | custom-call | tf_op jit(solution)/shard_map/rest/pallas_call | solution.py:487
  16.9 0.1 collective-permute-start.5
  17.0 1.6 %collective-permute-done.5 = bf16[160,1024]{1,0:T(8,128)(2,1)S(1)} collective-permute-done((bf16[160,1024]{1,0:T(8,128)(2,1)S(1)}, bf16[160,1024]{1,0:T(8,128)(2,1)S(1)}, u32[]{:S(2)}, u32[]{:S(2)}) %collective-permute-start.5) | collective-permute-done | bytes 327712 | tf_op jit(solution)/shard_map/ppermute | solution.py:398
  18.6 0.1 add.15
  18.7 1.6 %collective-permute-start.7 = (bf16[40,1024]{1,0:T(8,128)(2,1)S(1)}, bf16[40,1024]{1,0:T(8,128)(2,1)S(1)}, u32[]{:S(2)}, u32[]{:S(2)}) collective-permute-start(bf16[40,1024]{1,0:T(8,128)(2,1)S(1)} %get-tuple-element.45), channel_id=1, source_target_pairs={{0,4},{2,6},{4,0},{6,2},{8,12},{10,14},{12,8},{14,10},{1,5},{3,7},... | collective-permute-start | bytes 245768 | tf_op jit(solution)/shard_map/ppermute | solution.py:398
  20.3 0.4 %collective-permute-start.6 = (bf16[40,1024]{1,0:T(8,128)(2,1)S(1)}, bf16[40,1024]{1,0:T(8,128)(2,1)S(1)}, u32[]{:S(2)}, u32[]{:S(2)}) collective-permute-start(bf16[40,1024]{1,0:T(8,128)(2,1)S(1)} %get-tuple-element.43), channel_id=1, source_target_pairs={{0,4},{2,6},{4,0},{6,2},{8,12},{10,14},{12,8},{14,10},{1,5},{3,7},... | collective-permute-start | bytes 245768 | tf_op jit(solution)/shard_map/ppermute | solution.py:398
  20.8 2.9 %collective-permute-done.7 = bf16[40,1024]{1,0:T(8,128)(2,1)S(1)} collective-permute-done((bf16[40,1024]{1,0:T(8,128)(2,1)S(1)}, bf16[40,1024]{1,0:T(8,128)(2,1)S(1)}, u32[]{:S(2)}, u32[]{:S(2)}) %collective-permute-start.7) | collective-permute-done | bytes 81952 | tf_op jit(solution)/shard_map/ppermute | solution.py:398
  23.8 2.7 %collective-permute-start.10 = (bf16[24,1024]{1,0:T(8,128)(2,1)S(1)}, bf16[24,1024]{1,0:T(8,128)(2,1)S(1)}, u32[]{:S(2)}, u32[]{:S(2)}) collective-permute-start(bf16[24,1024]{1,0:T(8,128)(2,1)S(1)} %slice.39), channel_id=1, source_target_pairs={{0,8},{2,10},{4,12},{6,14},{8,0},{10,2},{12,4},{14,6},{1,9},{3,11}... | collective-permute-start | bytes 147464 | tf_op jit(solution)/shard_map/ppermute | solution.py:398
  26.4 0.2 collective-permute-start.4
  26.6 0.3 collective-permute-start.8
  27.0 0.0 collective-permute-done.6
  27.0 2.2 %collective-permute-done.10 = bf16[24,1024]{1,0:T(8,128)(2,1)S(1)} collective-permute-done((bf16[24,1024]{1,0:T(8,128)(2,1)S(1)}, bf16[24,1024]{1,0:T(8,128)(2,1)S(1)}, u32[]{:S(2)}, u32[]{:S(2)}) %collective-permute-start.10) | collective-permute-done | bytes 49184 | tf_op jit(solution)/shard_map/ppermute | solution.py:398
  29.2 0.1 collective-permute-start.11
  29.2 2.2 %collective-permute-done.8 = bf16[16,1024]{1,0:T(8,128)(2,1)S(1)} collective-permute-done((bf16[16,1024]{1,0:T(8,128)(2,1)S(1)}, bf16[16,1024]{1,0:T(8,128)(2,1)S(1)}, u32[]{:S(2)}, u32[]{:S(2)}) %collective-permute-start.8) | collective-permute-done | bytes 32800 | tf_op jit(solution)/shard_map/ppermute | solution.py:398
  31.4 1.8 %collective-permute-start.9 = (bf16[16,1024]{1,0:T(8,128)(2,1)S(1)}, bf16[16,1024]{1,0:T(8,128)(2,1)S(1)}, u32[]{:S(2)}, u32[]{:S(2)}) collective-permute-start(bf16[16,1024]{1,0:T(8,128)(2,1)S(1)} %slice_add_fusion.1.refs_3_), channel_id=1, source_target_pairs={{0,1},{1,0},{2,3},{3,2},{4,5},{5,4},{6,7},{7,6},{8,9},{9,8},{10,11... | collective-permute-start | bytes 98312 | tf_op jit(solution)/shard_map/ppermute | solution.py:398
  33.3 0.8 %correlate.3.refs_2_ = f32[12,32,1024]{2,1,0:T(8,128)S(1)} custom-call(bf16[3,32,1024]{2,1,0:T(8,128)(2,1)S(1)} %bitcast.7, bf16[3,32,1024]{2,1,0:T(8,128)(2,1)S(1)} %bitcast.8, bf16[24,1024]{1,0:T(8,128)(2,1)S(1)} %slice_add_fusion.refs_2_, bf16[16,1024]{1,0:T(8,128)(2,1)S(1)} %slice_add_fusion.1.refs_3_), custom_call_target="tpu_custom_call" | custom-call | tf_op jit(solution)/shard_map/correlate/pallas_call | solution.py:373
  34.0 0.0 collective-permute-done.4
  34.0 0.0 collective-permute-done.11.refs_1_
  34.0 0.6 %correlate.4.refs_2_ = f32[12,32,1024]{2,1,0:T(8,128)S(1)} custom-call(bf16[3,32,1024]{2,1,0:T(8,128)(2,1)S(1)} %bitcast.5, bf16[24,1024]{1,0:T(8,128)(2,1)S(1)} %collective-permute-done.11.refs_1_, f32[12,32,1024]{2,1,0:T(8,128)S(1)} %correlate.3.refs_2_), custom_call_target="tpu_custom_call" | custom-call | tf_op jit(solution)/shard_map/correlate/pallas_call | solution.py:373
  34.6 0.7 %collective-permute-done.9.refs_1_ = bf16[16,1024]{1,0:T(8,128)(2,1)S(1)} collective-permute-done((bf16[16,1024]{1,0:T(8,128)(2,1)S(1)}, bf16[16,1024]{1,0:T(8,128)(2,1)S(1)}, u32[]{:S(2)}, u32[]{:S(2)}) %collective-permute-start.9) | collective-permute-done | bytes 32800 | tf_op jit(solution)/shard_map/ppermute | solution.py:398
  35.3 1.3 %correlate.5 = f32[12,32,1024]{2,1,0:T(8,128)} custom-call(bf16[3,32,1024]{2,1,0:T(8,128)(2,1)S(1)} %bitcast.6, bf16[16,1024]{1,0:T(8,128)(2,1)S(1)} %collective-permute-done.9.refs_1_, f32[12,32,1024]{2,1,0:T(8,128)S(1)} %correlate.4.refs_2_), custom_call_target="tpu_custom_call" | custom-call | tf_op jit(solution)/shard_map/correlate/pallas_call | solution.py:373
  (9 shorter events, 0.1 us)
Async XLA Ops:
  0.0 1.5 %collective-permute-start = (s32[1,12]{1,0:T(1,128)}, s32[1,12]{1,0:T(1,128)S(1)}, u32[]{:S(2)}, u32[]{:S(2)}) collective-permute-start(s32[1,12]{1,0:T(1,128)} %wanted.1), channel_id=1, source_target_pairs={{0,2},{2,0},{4,6},{6,4},{8,10},{10,8},{12,14},{14,12},{1,3},{3,1},... | collective-permute-start | bytes 152 | tf_op jit(solution)/shard_map/ppermute | solution.py:398
  1.5 6.6 %copy-start = (bf16[1024,1024]{1,0:T(8,128)(2,1)S(1)}, bf16[1024,1024]{1,0:T(8,128)(2,1)}, u32[]{:S(2)}) copy-start(bf16[1024,1024]{1,0:T(8,128)(2,1)} %constant.2.clone.table) | copy-start | bytes 6291460
  1.5 6.6 %copy-start.1 = (bf16[64,6144]{1,0:T(8,128)(2,1)S(1)}, bf16[64,6144]{1,0:T(8,128)(2,1)}, u32[]{:S(2)}) copy-start(bf16[64,6144]{1,0:T(8,128)(2,1)} %traces.5) | copy-start | bytes 2359300
  1.5 6.6 %copy-start.2 = (f32[64,33]{0,1:T(8,128)S(1)}, f32[64,33]{0,1:T(8,128)}, u32[]{:S(2)}) copy-start(f32[64,33]{0,1:T(8,128)} %param.7) | copy-start | bytes 25348
  1.5 13.5 %collective-permute-start.1 = (bf16[64,2176]{1,0:T(8,128)(2,1)S(1)}, bf16[64,2176]{1,0:T(8,128)(2,1)S(1)}, u32[]{:S(2)}, u32[]{:S(2)}) collective-permute-start(bf16[64,2176]{1,0:T(8,128)(2,1)S(1)} %get-tuple-element.28), channel_id=1, source_target_pairs={{0,1},{2,3},{4,5},{6,7},{8,9},{10,11},{12,13},{14,15},{16,17},{18,... | collective-permute-start | bytes 835592 | tf_op jit(solution)/shard_map/ppermute | solution.py:436
  6.5 3.6 %collective-permute-start.2 = (s32[2,12]{1,0:T(2,128)S(1)}, s32[2,12]{1,0:T(2,128)S(1)}, u32[]{:S(2)}, u32[]{:S(2)}) collective-permute-start(s32[2,12]{1,0:T(2,128)S(1)} %pair.1), channel_id=1, source_target_pairs={{0,4},{2,6},{4,0},{6,2},{8,12},{10,14},{12,8},{14,10},{1,5},{3,7},... | collective-permute-start | bytes 296 | tf_op jit(solution)/shard_map/ppermute | solution.py:398
  9.3 5.4 %copy-start.3 = (s32[8,36]{1,0:T(8,128)S(1)}, s32[8,36]{1,0:T(8,128)}, u32[]{:S(2)}) copy-start(s32[8,36]{1,0:T(8,128)} %slots.1) | copy-start | bytes 3460
  9.3 5.4 %copy-start.4 = (s32[8]{0:T(128)S(1)}, s32[8]{0:T(128)}, u32[]{:S(2)}) copy-start(s32[8]{0:T(128)} %param.8) | copy-start | bytes 100
  10.1 4.5 %collective-permute-start.3 = (s32[4,12]{1,0:T(4,128)S(1)}, s32[4,12]{1,0:T(4,128)S(1)}, u32[]{:S(2)}, u32[]{:S(2)}) collective-permute-start(s32[4,12]{1,0:T(4,128)S(1)} %pad_add_fusion.refs_0_), channel_id=1, source_target_pairs={{0,8},{2,10},{4,12},{6,14},{8,0},{10,2},{12,4},{14,6},{1,9},{3,11}... | collective-permute-start | bytes 584 | tf_op jit(solution)/shard_map/ppermute | solution.py:398
  16.9 1.7 %collective-permute-start.5 = (bf16[160,1024]{1,0:T(8,128)(2,1)S(1)}, bf16[160,1024]{1,0:T(8,128)(2,1)S(1)}, u32[]{:S(2)}, u32[]{:S(2)}) collective-permute-start(bf16[160,1024]{1,0:T(8,128)(2,1)S(1)} %get-tuple-element.41), channel_id=1, source_target_pairs={{0,2},{2,0},{4,6},{6,4},{8,10},{10,8},{12,14},{14,12},{1,3},{3,1},... | collective-permute-start | bytes 983048 | tf_op jit(solution)/shard_map/ppermute | solution.py:398
  18.7 5.0 %collective-permute-start.7 = (bf16[40,1024]{1,0:T(8,128)(2,1)S(1)}, bf16[40,1024]{1,0:T(8,128)(2,1)S(1)}, u32[]{:S(2)}, u32[]{:S(2)}) collective-permute-start(bf16[40,1024]{1,0:T(8,128)(2,1)S(1)} %get-tuple-element.45), channel_id=1, source_target_pairs={{0,4},{2,6},{4,0},{6,2},{8,12},{10,14},{12,8},{14,10},{1,5},{3,7},... | collective-permute-start | bytes 245768 | tf_op jit(solution)/shard_map/ppermute | solution.py:398
  20.3 6.6 %collective-permute-start.6 = (bf16[40,1024]{1,0:T(8,128)(2,1)S(1)}, bf16[40,1024]{1,0:T(8,128)(2,1)S(1)}, u32[]{:S(2)}, u32[]{:S(2)}) collective-permute-start(bf16[40,1024]{1,0:T(8,128)(2,1)S(1)} %get-tuple-element.43), channel_id=1, source_target_pairs={{0,4},{2,6},{4,0},{6,2},{8,12},{10,14},{12,8},{14,10},{1,5},{3,7},... | collective-permute-start | bytes 245768 | tf_op jit(solution)/shard_map/ppermute | solution.py:398
  23.8 5.4 %collective-permute-start.10 = (bf16[24,1024]{1,0:T(8,128)(2,1)S(1)}, bf16[24,1024]{1,0:T(8,128)(2,1)S(1)}, u32[]{:S(2)}, u32[]{:S(2)}) collective-permute-start(bf16[24,1024]{1,0:T(8,128)(2,1)S(1)} %slice.39), channel_id=1, source_target_pairs={{0,8},{2,10},{4,12},{6,14},{8,0},{10,2},{12,4},{14,6},{1,9},{3,11}... | collective-permute-start | bytes 147464 | tf_op jit(solution)/shard_map/ppermute | solution.py:398
  26.4 7.6 %collective-permute-start.4 = (bf16[96,1024]{1,0:T(8,128)(2,1)S(1)}, bf16[96,1024]{1,0:T(8,128)(2,1)S(1)}, u32[]{:S(2)}, u32[]{:S(2)}) collective-permute-start(bf16[96,1024]{1,0:T(8,128)(2,1)S(1)} %get-tuple-element.39), channel_id=1, source_target_pairs={{0,1},{1,0},{2,3},{3,2},{4,5},{5,4},{6,7},{7,6},{8,9},{9,8},{10,11... | collective-permute-start | bytes 589832 | tf_op jit(solution)/shard_map/ppermute | solution.py:398
  26.6 4.8 %collective-permute-start.8 = (bf16[16,1024]{1,0:T(8,128)(2,1)S(1)}, bf16[16,1024]{1,0:T(8,128)(2,1)S(1)}, u32[]{:S(2)}, u32[]{:S(2)}) collective-permute-start(bf16[16,1024]{1,0:T(8,128)(2,1)S(1)} %slice.37), channel_id=1, source_target_pairs={{0,8},{2,10},{4,12},{6,14},{8,0},{10,2},{12,4},{14,6},{1,9},{3,11}... | collective-permute-start | bytes 98312 | tf_op jit(solution)/shard_map/ppermute | solution.py:398
  29.2 4.9 %collective-permute-start.11 = (bf16[24,1024]{1,0:T(8,128)(2,1)S(1)}, bf16[24,1024]{1,0:T(8,128)(2,1)S(1)}, u32[]{:S(2)}, u32[]{:S(2)}) collective-permute-start(bf16[24,1024]{1,0:T(8,128)(2,1)S(1)} %slice_add_fusion.refs_2_), channel_id=1, source_target_pairs={{0,1},{1,0},{2,3},{3,2},{4,5},{5,4},{6,7},{7,6},{8,9},{9,8},{10,11... | collective-permute-start | bytes 147464 | tf_op jit(solution)/shard_map/ppermute | solution.py:398
  31.4 3.9 %collective-permute-start.9 = (bf16[16,1024]{1,0:T(8,128)(2,1)S(1)}, bf16[16,1024]{1,0:T(8,128)(2,1)S(1)}, u32[]{:S(2)}, u32[]{:S(2)}) collective-permute-start(bf16[16,1024]{1,0:T(8,128)(2,1)S(1)} %slice_add_fusion.1.refs_3_), channel_id=1, source_target_pairs={{0,1},{1,0},{2,3},{3,2},{4,5},{5,4},{6,7},{7,6},{8,9},{9,8},{10,11... | collective-permute-start | bytes 98312 | tf_op jit(solution)/shard_map/ppermute | solution.py:398

commit v6 on v5

--- a/solution.py
+++ b/solution.py
@@ -541,21 +541,21 @@
         sources.append(both)
 
     factor = 1.0 / (windows * times)
-    early, late = list(range(windows - 1)), [windows - 1]
-    total = correlate(
-        receivers[:1] * 2, sources[0], (early, late), None, pairs, factor, times == 1
-    )
-    if times > 1:
+    early, late = tuple(range(windows - 1)), (windows - 1,)
+    total = None
+    for which in ([0], list(range(1, times))):
         for i, span in enumerate((early, late)):
-            total = correlate(
-                receivers[1:],
-                [both[i] for both in sources[1:]],
-                (span,) * (times - 1),
-                total,
-                pairs,
-                factor,
-                i == 1,
-            )
+            if which:
+                last = i == 1 and which[-1] == times - 1
+                total = correlate(
+                    [receivers[d] for d in which],
+                    [sources[d][i] for d in which],
+                    (span,) * len(which),
+                    total,
+                    pairs,
+                    factor,
+                    last,
+                )
     return total.transpose(1, 0, 2)
 
 

time: 36.8 us -> 36.8 us (level)
    pallas_call x3 -> x4, Pallas kernels: 2.59 us -> 2.67 us  [correlate(): pl.pallas_call(functools.partial(correlate_kernel, spans, pairs, factor,...]
where the time goes in v6:
time: 36.8 us; the launch traced here: 36.6 us
  starting transfers between devices  16.9 us (46%)
  waiting for transfers between devices  11 us (30%)
  Pallas kernels  8.29 us (23%)
    ppermute x11, starting transfers between devices, across(): return lax.ppermute(x, axis, [(i, i ^ distance) for i in range(size)])  12 us
    ppermute x11, waiting for transfers between devices, across(): return lax.ppermute(x, axis, [(i, i ^ distance) for i in range(size)])  11 us
    ppermute x1, starting transfers between devices, shards(): halo = lax.ppermute(tail, 'tm', [(i - 1, i) for i in range(1, times)])  4.93 us
    pallas_call x4, Pallas kernels, correlate(): pl.pallas_call(functools.partial(correlate_kernel, spans, pairs, factor,...  2.67 us
    pallas_call x1, Pallas kernels, shards(): pl.pallas_call(functools.partial(rest_kernel, windows, times), out_shape=...  1.85 us
    pallas_call x1, Pallas kernels, shards(): pl.pallas_call(functools.partial(second_kernel, windows), out_shape=chunk...  1.3 us
    pallas_call x1, Pallas kernels, shards(): pl.pallas_call(functools.partial(first_kernel, windows), out_shape=chunk_...  1.15 us
    pallas_call x1, Pallas kernels, shards(): pl.pallas_call(tail_kernel, out_shape=[jax.ShapeDtypeStruct((channels, HA...  0.97 us
  transfers between devices with their start and end apart: 12, of which 7 were waited for; matrix products, arithmetic and copies ran while one was open for 0% of the time, Pallas kernels for 14%

profile of v6, /device:TPU:0, one launch (start us, length us, event | category | flops | bytes accessed | tf_op | source)
XLA Modules:
  0.0 36.6 jit_solution(6610804017963848797)
XLA Ops:
  0.0 0.5 %collective-permute-start = (s32[1,12]{1,0:T(1,128)}, s32[1,12]{1,0:T(1,128)S(1)}, u32[]{:S(2)}, u32[]{:S(2)}) collective-permute-start(s32[1,12]{1,0:T(1,128)} %wanted.1), channel_id=1, source_target_pairs={{0,2},{2,0},{4,6},{6,4},{8,10},{10,8},{12,14},{14,12},{1,3},{3,1},... | collective-permute-start | bytes 152 | tf_op jit(solution)/shard_map/ppermute | solution.py:398
  0.5 1.0 %tail.1 = (bf16[64,2176]{1,0:T(8,128)(2,1)S(1)}, s32[1,12]{1,0:T(1,128)S(1)}) custom-call(bf16[64,6144]{1,0:T(8,128)(2,1)} %traces.5, s32[1,12]{1,0:T(1,128)} %wanted.1), custom_call_target="tpu_custom_call" | custom-call | tf_op jit(solution)/shard_map/tail/pallas_call | solution.py:406
  1.5 0.0 collective-permute-done.other
  1.5 0.0 copy-start
  1.5 0.0 copy-start.1
  1.5 0.0 copy-start.2
  1.5 4.9 %collective-permute-start.1 = (bf16[64,2176]{1,0:T(8,128)(2,1)S(1)}, bf16[64,2176]{1,0:T(8,128)(2,1)S(1)}, u32[]{:S(2)}, u32[]{:S(2)}) collective-permute-start(bf16[64,2176]{1,0:T(8,128)(2,1)S(1)} %get-tuple-element.28), channel_id=1, source_target_pairs={{0,1},{2,3},{4,5},{6,7},{8,9},{10,11},{12,13},{14,15},{16,17},{18,... | collective-permute-start | bytes 835592 | tf_op jit(solution)/shard_map/ppermute | solution.py:436
  6.5 1.6 %collective-permute-start.2 = (s32[2,12]{1,0:T(2,128)S(1)}, s32[2,12]{1,0:T(2,128)S(1)}, u32[]{:S(2)}, u32[]{:S(2)}) collective-permute-start(s32[2,12]{1,0:T(2,128)S(1)} %pair.1), channel_id=1, source_target_pairs={{0,4},{2,6},{4,0},{6,2},{8,12},{10,14},{12,8},{14,10},{1,5},{3,7},... | collective-permute-start | bytes 296 | tf_op jit(solution)/shard_map/ppermute | solution.py:398
  8.1 0.0 copy-done
  8.1 0.0 copy-done.1
  8.1 0.0 copy-done.2
  8.1 1.1 %first.1 = (f32[128,512]{1,0:T(8,128)S(1)}, f32[64,512]{1,0:T(8,128)S(1)}, f32[64,512]{1,0:T(8,128)S(1)}, bf16[64,256]{1,0:T(8,128)(2,1)S(1)}, bf16[64,96]{1,0:T(8,128)(2,1)S(1)}, /*index=5*/bf16[64,144]{1,0:T(8,128)(2,1)S(1)}) custom-call(bf16[64,6144]{1,0:T(8,128)(2,1)S(1)} %copy-done.1, f32[33,64]{1,0:T(8,128)S(1)} %bitcast.9, bf16[1024,1024]{1,0:T(8,128)(2,1)S(1)} %copy-done), custom_call_target="tpu_custom_call" | custom-call | tf_op jit(solution)/shard_map/first/pallas_call | solution.py:448
  9.3 0.0 copy-start.3
  9.3 0.0 copy-start.4
  9.3 0.8 %collective-permute-done.2 = s32[2,12]{1,0:T(2,128)S(1)} collective-permute-done((s32[2,12]{1,0:T(2,128)S(1)}, s32[2,12]{1,0:T(2,128)S(1)}, u32[]{:S(2)}, u32[]{:S(2)}) %collective-permute-start.2) | collective-permute-done | bytes 128 | tf_op jit(solution)/shard_map/ppermute | solution.py:398
  10.1 2.6 %collective-permute-start.3 = (s32[4,12]{1,0:T(4,128)S(1)}, s32[4,12]{1,0:T(4,128)S(1)}, u32[]{:S(2)}, u32[]{:S(2)}) collective-permute-start(s32[4,12]{1,0:T(4,128)S(1)} %pad_add_fusion.refs_0_), channel_id=1, source_target_pairs={{0,8},{2,10},{4,12},{6,14},{8,0},{10,2},{12,4},{14,6},{1,9},{3,11}... | collective-permute-start | bytes 584 | tf_op jit(solution)/shard_map/ppermute | solution.py:398
  12.8 1.3 %second.1 = (f32[128,512]{1,0:T(8,128)S(1)}, f32[64,512]{1,0:T(8,128)S(1)}, bf16[64,1024]{1,0:T(8,128)(2,1)S(1)}) custom-call(bf16[64,6144]{1,0:T(8,128)(2,1)S(1)} %copy-done.1, bf16[1024,1024]{1,0:T(8,128)(2,1)S(1)} %copy-done, bf16[64,144]{1,0:T(8,128)(2,1)S(1)} %get-tuple-element.31.lines, bf16[64,96]{1,0:T(8,128)(2,1)S(1)} %get-tuple-element.32.edge, ...), custom_call_target="tpu_custom_call" | custom-call | tf_op jit(solution)/shard_map/second/pallas_call | solution.py:466
  14.1 0.6 %collective-permute-done.3.refs_1_ = s32[4,12]{1,0:T(4,128)S(1)} collective-permute-done((s32[4,12]{1,0:T(4,128)S(1)}, s32[4,12]{1,0:T(4,128)S(1)}, u32[]{:S(2)}, u32[]{:S(2)}) %collective-permute-start.3) | collective-permute-done | bytes 224 | tf_op jit(solution)/shard_map/ppermute | solution.py:398
  14.7 0.0 copy-done.3
  14.7 0.0 copy-done.4
  14.7 0.3 picks.1.refs_1_
  15.0 0.0 collective-permute-done.1.halo
  15.0 1.9 %rest.1 = (bf16[160,1024]{1,0:T(8,128)(2,1)S(1)}, bf16[160,1024]{1,0:T(8,128)(2,1)S(1)}, bf16[96,1024]{1,0:T(8,128)(2,1)S(1)}, bf16[96,1024]{1,0:T(8,128)(2,1)S(1)}) custom-call(bf16[64,2176]{1,0:T(8,128)(2,1)S(1)} %collective-permute-done.1.halo, bf16[64,256]{1,0:T(8,128)(2,1)S(1)} %get-tuple-element.29.ends, f32[33,64]{1,0:T(8,128)S(1)} %bitcast.10, ...), custom_call_target="tpu_custom_call" | custom-call | tf_op jit(solution)/shard_map/rest/pallas_call | solution.py:487
  16.9 0.1 collective-permute-start.5
  17.0 1.6 %collective-permute-done.5 = bf16[160,1024]{1,0:T(8,128)(2,1)S(1)} collective-permute-done((bf16[160,1024]{1,0:T(8,128)(2,1)S(1)}, bf16[160,1024]{1,0:T(8,128)(2,1)S(1)}, u32[]{:S(2)}, u32[]{:S(2)}) %collective-permute-start.5) | collective-permute-done | bytes 327712 | tf_op jit(solution)/shard_map/ppermute | solution.py:398
  18.6 0.1 add.15
  18.7 1.6 %collective-permute-start.7 = (bf16[40,1024]{1,0:T(8,128)(2,1)S(1)}, bf16[40,1024]{1,0:T(8,128)(2,1)S(1)}, u32[]{:S(2)}, u32[]{:S(2)}) collective-permute-start(bf16[40,1024]{1,0:T(8,128)(2,1)S(1)} %get-tuple-element.45), channel_id=1, source_target_pairs={{0,4},{2,6},{4,0},{6,2},{8,12},{10,14},{12,8},{14,10},{1,5},{3,7},... | collective-permute-start | bytes 245768 | tf_op jit(solution)/shard_map/ppermute | solution.py:398
  20.4 0.4 %collective-permute-start.6 = (bf16[40,1024]{1,0:T(8,128)(2,1)S(1)}, bf16[40,1024]{1,0:T(8,128)(2,1)S(1)}, u32[]{:S(2)}, u32[]{:S(2)}) collective-permute-start(bf16[40,1024]{1,0:T(8,128)(2,1)S(1)} %get-tuple-element.43), channel_id=1, source_target_pairs={{0,4},{2,6},{4,0},{6,2},{8,12},{10,14},{12,8},{14,10},{1,5},{3,7},... | collective-permute-start | bytes 245768 | tf_op jit(solution)/shard_map/ppermute | solution.py:398
  20.8 2.9 %collective-permute-done.7 = bf16[40,1024]{1,0:T(8,128)(2,1)S(1)} collective-permute-done((bf16[40,1024]{1,0:T(8,128)(2,1)S(1)}, bf16[40,1024]{1,0:T(8,128)(2,1)S(1)}, u32[]{:S(2)}, u32[]{:S(2)}) %collective-permute-start.7) | collective-permute-done | bytes 81952 | tf_op jit(solution)/shard_map/ppermute | solution.py:398
  23.8 2.6 %collective-permute-start.10 = (bf16[24,1024]{1,0:T(8,128)(2,1)S(1)}, bf16[24,1024]{1,0:T(8,128)(2,1)S(1)}, u32[]{:S(2)}, u32[]{:S(2)}) collective-permute-start(bf16[24,1024]{1,0:T(8,128)(2,1)S(1)} %slice.39), channel_id=1, source_target_pairs={{0,8},{2,10},{4,12},{6,14},{8,0},{10,2},{12,4},{14,6},{1,9},{3,11}... | collective-permute-start | bytes 147464 | tf_op jit(solution)/shard_map/ppermute | solution.py:398
  26.4 0.2 collective-permute-start.4
  26.6 0.3 collective-permute-start.8
  27.0 0.0 collective-permute-done.6
  27.0 2.2 %collective-permute-done.10 = bf16[24,1024]{1,0:T(8,128)(2,1)S(1)} collective-permute-done((bf16[24,1024]{1,0:T(8,128)(2,1)S(1)}, bf16[24,1024]{1,0:T(8,128)(2,1)S(1)}, u32[]{:S(2)}, u32[]{:S(2)}) %collective-permute-start.10) | collective-permute-done | bytes 49184 | tf_op jit(solution)/shard_map/ppermute | solution.py:398
  29.2 0.1 collective-permute-start.11
  29.3 2.2 %collective-permute-done.8 = bf16[16,1024]{1,0:T(8,128)(2,1)S(1)} collective-permute-done((bf16[16,1024]{1,0:T(8,128)(2,1)S(1)}, bf16[16,1024]{1,0:T(8,128)(2,1)S(1)}, u32[]{:S(2)}, u32[]{:S(2)}) %collective-permute-start.8) | collective-permute-done | bytes 32800 | tf_op jit(solution)/shard_map/ppermute | solution.py:398
  31.4 1.8 %collective-permute-start.9 = (bf16[16,1024]{1,0:T(8,128)(2,1)S(1)}, bf16[16,1024]{1,0:T(8,128)(2,1)S(1)}, u32[]{:S(2)}, u32[]{:S(2)}) collective-permute-start(bf16[16,1024]{1,0:T(8,128)(2,1)S(1)} %slice_add_fusion.1.refs_1_), channel_id=1, source_target_pairs={{0,1},{1,0},{2,3},{3,2},{4,5},{5,4},{6,7},{7,6},{8,9},{9,8},{10,11... | collective-permute-start | bytes 98312 | tf_op jit(solution)/shard_map/ppermute | solution.py:398
  33.3 0.5 %correlate.4.refs_2_ = f32[12,32,1024]{2,1,0:T(8,128)S(1)} custom-call(bf16[3,32,1024]{2,1,0:T(8,128)(2,1)S(1)} %bitcast.5, bf16[24,1024]{1,0:T(8,128)(2,1)S(1)} %slice_add_fusion.refs_1_), custom_call_target="tpu_custom_call" | custom-call | tf_op jit(solution)/shard_map/correlate/pallas_call | solution.py:373
  33.8 0.3 correlate.5.refs_2_
  34.1 0.0 collective-permute-done.4
  34.1 0.0 collective-permute-done.11.refs_1_
  34.1 0.6 %correlate.6.refs_2_ = f32[12,32,1024]{2,1,0:T(8,128)S(1)} custom-call(bf16[3,32,1024]{2,1,0:T(8,128)(2,1)S(1)} %bitcast.7, bf16[24,1024]{1,0:T(8,128)(2,1)S(1)} %collective-permute-done.11.refs_1_, f32[12,32,1024]{2,1,0:T(8,128)S(1)} %correlate.5.refs_2_), custom_call_target="tpu_custom_call" | custom-call | tf_op jit(solution)/shard_map/correlate/pallas_call | solution.py:373
  34.7 0.7 %collective-permute-done.9.refs_1_ = bf16[16,1024]{1,0:T(8,128)(2,1)S(1)} collective-permute-done((bf16[16,1024]{1,0:T(8,128)(2,1)S(1)}, bf16[16,1024]{1,0:T(8,128)(2,1)S(1)}, u32[]{:S(2)}, u32[]{:S(2)}) %collective-permute-start.9) | collective-permute-done | bytes 32800 | tf_op jit(solution)/shard_map/ppermute | solution.py:398
  35.4 1.3 %correlate.7 = f32[12,32,1024]{2,1,0:T(8,128)} custom-call(bf16[3,32,1024]{2,1,0:T(8,128)(2,1)S(1)} %bitcast.8, bf16[16,1024]{1,0:T(8,128)(2,1)S(1)} %collective-permute-done.9.refs_1_, f32[12,32,1024]{2,1,0:T(8,128)S(1)} %correlate.6.refs_2_), custom_call_target="tpu_custom_call" | custom-call | tf_op jit(solution)/shard_map/correlate/pallas_call | solution.py:373
  (9 shorter events, 0.1 us)
Async XLA Ops:
  0.0 1.5 %collective-permute-start = (s32[1,12]{1,0:T(1,128)}, s32[1,12]{1,0:T(1,128)S(1)}, u32[]{:S(2)}, u32[]{:S(2)}) collective-permute-start(s32[1,12]{1,0:T(1,128)} %wanted.1), channel_id=1, source_target_pairs={{0,2},{2,0},{4,6},{6,4},{8,10},{10,8},{12,14},{14,12},{1,3},{3,1},... | collective-permute-start | bytes 152 | tf_op jit(solution)/shard_map/ppermute | solution.py:398
  1.5 6.6 %copy-start = (bf16[1024,1024]{1,0:T(8,128)(2,1)S(1)}, bf16[1024,1024]{1,0:T(8,128)(2,1)}, u32[]{:S(2)}) copy-start(bf16[1024,1024]{1,0:T(8,128)(2,1)} %constant.2.clone.table) | copy-start | bytes 6291460
  1.5 6.6 %copy-start.1 = (bf16[64,6144]{1,0:T(8,128)(2,1)S(1)}, bf16[64,6144]{1,0:T(8,128)(2,1)}, u32[]{:S(2)}) copy-start(bf16[64,6144]{1,0:T(8,128)(2,1)} %traces.5) | copy-start | bytes 2359300
  1.5 6.6 %copy-start.2 = (f32[64,33]{0,1:T(8,128)S(1)}, f32[64,33]{0,1:T(8,128)}, u32[]{:S(2)}) copy-start(f32[64,33]{0,1:T(8,128)} %param.7) | copy-start | bytes 25348
  1.5 13.5 %collective-permute-start.1 = (bf16[64,2176]{1,0:T(8,128)(2,1)S(1)}, bf16[64,2176]{1,0:T(8,128)(2,1)S(1)}, u32[]{:S(2)}, u32[]{:S(2)}) collective-permute-start(bf16[64,2176]{1,0:T(8,128)(2,1)S(1)} %get-tuple-element.28), channel_id=1, source_target_pairs={{0,1},{2,3},{4,5},{6,7},{8,9},{10,11},{12,13},{14,15},{16,17},{18,... | collective-permute-start | bytes 835592 | tf_op jit(solution)/shard_map/ppermute | solution.py:436
  6.5 3.6 %collective-permute-start.2 = (s32[2,12]{1,0:T(2,128)S(1)}, s32[2,12]{1,0:T(2,128)S(1)}, u32[]{:S(2)}, u32[]{:S(2)}) collective-permute-start(s32[2,12]{1,0:T(2,128)S(1)} %pair.1), channel_id=1, source_target_pairs={{0,4},{2,6},{4,0},{6,2},{8,12},{10,14},{12,8},{14,10},{1,5},{3,7},... | collective-permute-start | bytes 296 | tf_op jit(solution)/shard_map/ppermute | solution.py:398
  9.3 5.4 %copy-start.3 = (s32[8,36]{1,0:T(8,128)S(1)}, s32[8,36]{1,0:T(8,128)}, u32[]{:S(2)}) copy-start(s32[8,36]{1,0:T(8,128)} %slots.1) | copy-start | bytes 3460
  9.3 5.4 %copy-start.4 = (s32[8]{0:T(128)S(1)}, s32[8]{0:T(128)}, u32[]{:S(2)}) copy-start(s32[8]{0:T(128)} %param.8) | copy-start | bytes 100
  10.1 4.5 %collective-permute-start.3 = (s32[4,12]{1,0:T(4,128)S(1)}, s32[4,12]{1,0:T(4,128)S(1)}, u32[]{:S(2)}, u32[]{:S(2)}) collective-permute-start(s32[4,12]{1,0:T(4,128)S(1)} %pad_add_fusion.refs_0_), channel_id=1, source_target_pairs={{0,8},{2,10},{4,12},{6,14},{8,0},{10,2},{12,4},{14,6},{1,9},{3,11}... | collective-permute-start | bytes 584 | tf_op jit(solution)/shard_map/ppermute | solution.py:398
  16.9 1.7 %collective-permute-start.5 = (bf16[160,1024]{1,0:T(8,128)(2,1)S(1)}, bf16[160,1024]{1,0:T(8,128)(2,1)S(1)}, u32[]{:S(2)}, u32[]{:S(2)}) collective-permute-start(bf16[160,1024]{1,0:T(8,128)(2,1)S(1)} %get-tuple-element.41), channel_id=1, source_target_pairs={{0,2},{2,0},{4,6},{6,4},{8,10},{10,8},{12,14},{14,12},{1,3},{3,1},... | collective-permute-start | bytes 983048 | tf_op jit(solution)/shard_map/ppermute | solution.py:398
  18.7 5.0 %collective-permute-start.7 = (bf16[40,1024]{1,0:T(8,128)(2,1)S(1)}, bf16[40,1024]{1,0:T(8,128)(2,1)S(1)}, u32[]{:S(2)}, u32[]{:S(2)}) collective-permute-start(bf16[40,1024]{1,0:T(8,128)(2,1)S(1)} %get-tuple-element.45), channel_id=1, source_target_pairs={{0,4},{2,6},{4,0},{6,2},{8,12},{10,14},{12,8},{14,10},{1,5},{3,7},... | collective-permute-start | bytes 245768 | tf_op jit(solution)/shard_map/ppermute | solution.py:398
  20.4 6.6 %collective-permute-start.6 = (bf16[40,1024]{1,0:T(8,128)(2,1)S(1)}, bf16[40,1024]{1,0:T(8,128)(2,1)S(1)}, u32[]{:S(2)}, u32[]{:S(2)}) collective-permute-start(bf16[40,1024]{1,0:T(8,128)(2,1)S(1)} %get-tuple-element.43), channel_id=1, source_target_pairs={{0,4},{2,6},{4,0},{6,2},{8,12},{10,14},{12,8},{14,10},{1,5},{3,7},... | collective-permute-start | bytes 245768 | tf_op jit(solution)/shard_map/ppermute | solution.py:398
  23.8 5.4 %collective-permute-start.10 = (bf16[24,1024]{1,0:T(8,128)(2,1)S(1)}, bf16[24,1024]{1,0:T(8,128)(2,1)S(1)}, u32[]{:S(2)}, u32[]{:S(2)}) collective-permute-start(bf16[24,1024]{1,0:T(8,128)(2,1)S(1)} %slice.39), channel_id=1, source_target_pairs={{0,8},{2,10},{4,12},{6,14},{8,0},{10,2},{12,4},{14,6},{1,9},{3,11}... | collective-permute-start | bytes 147464 | tf_op jit(solution)/shard_map/ppermute | solution.py:398
  26.4 7.7 %collective-permute-start.4 = (bf16[96,1024]{1,0:T(8,128)(2,1)S(1)}, bf16[96,1024]{1,0:T(8,128)(2,1)S(1)}, u32[]{:S(2)}, u32[]{:S(2)}) collective-permute-start(bf16[96,1024]{1,0:T(8,128)(2,1)S(1)} %get-tuple-element.39), channel_id=1, source_target_pairs={{0,1},{1,0},{2,3},{3,2},{4,5},{5,4},{6,7},{7,6},{8,9},{9,8},{10,11... | collective-permute-start | bytes 589832 | tf_op jit(solution)/shard_map/ppermute | solution.py:398
  26.6 4.8 %collective-permute-start.8 = (bf16[16,1024]{1,0:T(8,128)(2,1)S(1)}, bf16[16,1024]{1,0:T(8,128)(2,1)S(1)}, u32[]{:S(2)}, u32[]{:S(2)}) collective-permute-start(bf16[16,1024]{1,0:T(8,128)(2,1)S(1)} %slice.37), channel_id=1, source_target_pairs={{0,8},{2,10},{4,12},{6,14},{8,0},{10,2},{12,4},{14,6},{1,9},{3,11}... | collective-permute-start | bytes 98312 | tf_op jit(solution)/shard_map/ppermute | solution.py:398
  29.2 4.9 %collective-permute-start.11 = (bf16[24,1024]{1,0:T(8,128)(2,1)S(1)}, bf16[24,1024]{1,0:T(8,128)(2,1)S(1)}, u32[]{:S(2)}, u32[]{:S(2)}) collective-permute-start(bf16[24,1024]{1,0:T(8,128)(2,1)S(1)} %slice_add_fusion.refs_1_), channel_id=1, source_target_pairs={{0,1},{1,0},{2,3},{3,2},{4,5},{5,4},{6,7},{7,6},{8,9},{9,8},{10,11... | collective-permute-start | bytes 147464 | tf_op jit(solution)/shard_map/ppermute | solution.py:398
  31.4 3.9 %collective-permute-start.9 = (bf16[16,1024]{1,0:T(8,128)(2,1)S(1)}, bf16[16,1024]{1,0:T(8,128)(2,1)S(1)}, u32[]{:S(2)}, u32[]{:S(2)}) collective-permute-start(bf16[16,1024]{1,0:T(8,128)(2,1)S(1)} %slice_add_fusion.1.refs_1_), channel_id=1, source_target_pairs={{0,1},{1,0},{2,3},{3,2},{4,5},{5,4},{6,7},{7,6},{8,9},{9,8},{10,11... | collective-permute-start | bytes 98312 | tf_op jit(solution)/shard_map/ppermute | solution.py:398

commit v7 on v6

--- a/solution.py
+++ b/solution.py
@@ -19,7 +19,6 @@
 F32 = jnp.float32
 BF16 = jnp.bfloat16
 LIMIT = 24 * 1024 * 1024
-HINT = 10**10
 
 
 def piece_table():
@@ -131,15 +130,43 @@
     lax.fori_loop(0, count // ROWS, step, 0, unroll=4)
 
 
-def tail_kernel(traces, wanted, tail, ids, sems):
-    start = traces.shape[1] - tail.shape[1]
-    copies = [
-        pltpu.make_async_copy(traces.at[:, start:], tail, sems.at[0]),
-        pltpu.make_async_copy(wanted, ids, sems.at[1]),
+def load_kernel(
+    traces_in, taps_in, table_in, ids_in, message, last_half, traces, taps, table, ids, sems
+):
+    channels, samples = traces.shape
+    begin = samples - HALF - 128
+    copies = [pltpu.make_async_copy(traces_in.at[:, begin:], traces.at[:, begin:], sems.at[0])]
+    order = [c for f in range(0, NF, CHUNK) for c in (f, NF + f)]
+    for i, c in enumerate(order):
+        cols = slice(c, c + CHUNK)
+        copies.append(
+            pltpu.make_async_copy(table_in.at[:, cols], table.at[:, cols], sems.at[1 + i])
+        )
+    at = 1 + len(order)
+    copies += [
+        pltpu.make_async_copy(traces_in.at[:, :begin], traces.at[:, :begin], sems.at[at]),
+        pltpu.make_async_copy(taps_in, taps, sems.at[at + 1]),
+        pltpu.make_async_copy(ids_in, ids, sems.at[at + 2]),
     ]
     for copy in copies:
         copy.start()
-    for copy in copies:
+    copies[0].wait()
+    message[:, 2 * NF : 2 * NF + 128] = traces[:, begin : begin + 128]
+    message[:, 2 * NF + 128 :] = traces[:, samples - 128 :]
+    pieces = [samples - HALF + q * PIECE for q in range(HALF // PIECE)]
+    x = jnp.concatenate([traces[:, p : p + PIECE] for p in pieces], axis=0)
+    turns = Turns()
+    for i, f in enumerate(range(0, NF, CHUNK)):
+        re = slice(f, f + CHUNK)
+        im = slice(NF + f, NF + f + CHUNK)
+        copies[1 + 2 * i].wait()
+        copies[2 + 2 * i].wait()
+        xr, xi = half_spectra(x, table, channels, 1, turns, f)[0]
+        last_half[:, re] = xr
+        last_half[:, im] = xi
+        message[:, re] = xr.astype(BF16)
+        message[:, im] = xi.astype(BF16)
+    for copy in copies[at:]:
         copy.wait()
 
 
@@ -148,11 +175,11 @@
     out[1:, :] = other[...]
 
 
-def own_chunk(windows, f, traces, table, lines, edge, part, response, last):
+def own_chunk(windows, f, traces, table, last_half, lines, edge, part, response, last):
     channels, samples = traces.shape
     size = lines.shape[1] // 3
     lag = edge.shape[1] // 3
-    pieces = samples // PIECE
+    pieces = (samples - HALF) // PIECE
     x = jnp.concatenate([traces[:, q * PIECE : (q + 1) * PIECE] for q in range(pieces)], axis=0)
     turns = Turns()
     re = slice(f, f + CHUNK)
@@ -161,7 +188,8 @@
     pi = dot(lines[...], stacked_rows(table, size, im))
     response[:, :CHUNK] = pr
     response[:, CHUNK:] = pi
-    halves = half_spectra(x, table, channels, windows, turns, f)
+    halves = half_spectra(x, table, channels, windows - 1, turns, f)
+    halves.append((last_half[:, re], last_half[:, im]))
     for w in range(windows):
         xr, xi = halves[w]
         xr, xi = turns.sign * xr, turns.sign * xi
@@ -179,7 +207,7 @@
 
 
 def first_kernel(
-    windows, traces, taps, table, part, response, last, ends, edge, lines, square, shifted
+    windows, traces, taps, table, last_half, part, response, last, ends, edge, lines, square, shifted
 ):
     channels, samples = traces.shape
     tap_count = taps.shape[0]
@@ -196,13 +224,13 @@
     start = (windows - 2) * HALF
     apart = traces[:, start - tile : start].astype(F32) - traces[:, samples - tile :].astype(F32)
     edge[...] = end_terms(taps[...], shifted, tap_count, apart)
-    own_chunk(windows, 0, traces, table, lines, edge, part, response, last)
+    own_chunk(windows, 0, traces, table, last_half, lines, edge, part, response, last)
 
 
 def second_kernel(
-    windows, traces, table, lines, edge, first, part, response, white, second, spectra
+    windows, traces, table, last_half, lines, edge, first, part, response, white, second, spectra
 ):
-    own_chunk(windows, CHUNK, traces, table, lines, edge, part, response, second)
+    own_chunk(windows, CHUNK, traces, table, last_half, lines, edge, part, response, second)
     for i, half in enumerate((first, second)):
         spectra[:, i * CHUNK : (i + 1) * CHUNK] = half[:, :CHUNK]
         spectra[:, NF + i * CHUNK : NF + (i + 1) * CHUNK] = half[:, CHUNK:]
@@ -260,24 +288,19 @@
     shifted, spectra, white = refs[4 + times :]
     channels = response_a.shape[0]
     tap_count = taps.shape[0]
-    tile = halo.shape[1] - HALF
+    tile = 128
     rest = windows - 1
 
-    before = [halo[:, :tile], halo[:, HALF:]]
+    before = [halo[:, 2 * NF : 2 * NF + tile], halo[:, 2 * NF + tile :]]
     before += [ends[:, (b - 1) * tile : b * tile] for b in range(1, windows - 2)]
     after = [ends[:, w * tile : (w + 1) * tile] for w in range(rest)]
     apart = jnp.concatenate([b.astype(F32) - a.astype(F32) for b, a in zip(before, after)], axis=0)
     taps_wide = jnp.concatenate([taps[...]] * rest, axis=1)
     edge = end_terms(taps_wide, shifted, tap_count, apart)
-    x = jnp.concatenate(
-        [halo[:, tile + q * PIECE : tile + (q + 1) * PIECE] for q in range(HALF // PIECE)],
-        axis=0,
-    )
-    turns = Turns()
     for f in range(0, NF, CHUNK):
         re = slice(f, f + CHUNK)
         im = slice(NF + f, NF + f + CHUNK)
-        xr, xi = half_spectra(x, table, channels, 1, turns, f)[0]
+        xr, xi = halo[:, re].astype(F32), halo[:, im].astype(F32)
         part, response = (part_b, response_b) if f else (part_a, response_a)
         pr, pi = response[:, :CHUNK], response[:, CHUNK:]
         er = dot(edge, stacked_rows(table, tap_count - 1, re))
@@ -403,23 +426,20 @@
     bits = [1 << b for b in range(chips.bit_length() - 1)]
 
     other = across(block_sources, "chan", 1)
-    tail, ids = pl.pallas_call(
-        tail_kernel,
+    inputs = (traces, filter_taps.T, jnp.asarray(piece_table()), block_sources)
+    message, last_half, traces, taps, table, ids = pl.pallas_call(
+        load_kernel,
         out_shape=[
-            jax.ShapeDtypeStruct((channels, HALF + 128), BF16),
-            jax.ShapeDtypeStruct(block_sources.shape, jnp.int32),
-        ],
-        in_specs=[hbm] * 2,
-        out_specs=[vmem] * 2,
-        scratch_shapes=[pltpu.SemaphoreType.DMA((2,))],
+            jax.ShapeDtypeStruct((channels, 2 * NF + 256), BF16),
+            jax.ShapeDtypeStruct((channels, 2 * NF), F32),
+        ]
+        + [jax.ShapeDtypeStruct(a.shape, a.dtype) for a in inputs],
+        in_specs=[hbm] * 4,
+        out_specs=[vmem] * 6,
+        scratch_shapes=[pltpu.SemaphoreType.DMA((4 + 2 * NF // CHUNK,))],
         compiler_params=params,
-        name="tail",
-    )(*(pltpu.with_memory_space_constraint(a, pltpu.HBM) for a in (traces, block_sources)))
-    taps = filter_taps.T
-    traces, taps, table = (
-        pltpu.with_memory_space_constraint(a, pltpu.VMEM)
-        for a in (traces, taps, jnp.asarray(piece_table()))
-    )
+        name="load",
+    )(*(pltpu.with_memory_space_constraint(a, pltpu.HBM) for a in inputs))
     wanted = [
         pl.pallas_call(
             pair_kernel,
@@ -427,13 +447,10 @@
             in_specs=[vmem] * 2,
             out_specs=vmem,
             compiler_params=params,
-            cost_estimate=pl.CostEstimate(flops=HINT, bytes_accessed=8 * pairs, transcendentals=0),
             name="pair",
         )(ids, other)
     ]
-    tail, pair = lax.optimization_barrier((tail, wanted[0]))
-    wanted = [pair]
-    halo = lax.ppermute(tail, "tm", [(i - 1, i) for i in range(1, times)])
+    halo = lax.ppermute(message, "tm", [(i - 1, i) for i in range(1, times)])
     for bit in bits:
         known = jnp.concatenate(wanted, axis=0)
         wanted = [known, across(known, "chan", 2 * bit)]
@@ -454,7 +471,7 @@
             jax.ShapeDtypeStruct((channels, 3 * (tap_count - 1)), BF16),
             jax.ShapeDtypeStruct((channels, 3 * size), BF16),
         ],
-        in_specs=[vmem] * 3,
+        in_specs=[vmem] * 4,
         out_specs=[vmem] * 6,
         scratch_shapes=[
             pltpu.VMEM((3 * size, 128), F32),
@@ -462,11 +479,11 @@
         ],
         compiler_params=params,
         name="first",
-    )(traces, taps, table)
+    )(traces, taps, table, last_half)
     part_b, response_b, own_white = pl.pallas_call(
         functools.partial(second_kernel, windows),
         out_shape=chunk_shapes + [jax.ShapeDtypeStruct((channels, 2 * NF), BF16)],
-        in_specs=[vmem] * 5,
+        in_specs=[vmem] * 6,
         out_specs=[vmem] * 3,
         scratch_shapes=[
             pltpu.VMEM((channels, 2 * CHUNK), F32),
@@ -474,7 +491,7 @@
         ],
         compiler_params=params,
         name="second",
-    )(traces, table, lines, edge, last)
+    )(traces, table, last_half, lines, edge, last)
     picks = pl.pallas_call(
         functools.partial(picks_kernel, shape),
         out_shape=jax.ShapeDtypeStruct((2 * rows_out, width), BF16),

time: 36.8 us -> 38.1 us (1.035)
  waiting for transfers between devices: 11 us -> 12.5 us
  starting transfers between devices: 16.9 us -> 16.4 us
    ppermute x11, waiting for transfers between devices: 11 us -> 12.5 us  [across(): return lax.ppermute(x, axis, [(i, i ^ distance) for i in range(size)])]
    pallas_call x1, Pallas kernels: 0.97 us -> 2.32 us  [shards(): pl.pallas_call(load_kernel, out_shape=[jax.ShapeDtypeStruct((channels, 2...]
    ppermute x11, starting transfers between devices: 12 us -> 11.5 us  [across(): return lax.ppermute(x, axis, [(i, i ^ distance) for i in range(size)])]
    pallas_call x1, Pallas kernels: 1.85 us -> 1.41 us  [shards(): pl.pallas_call(functools.partial(rest_kernel, windows, times), out_shape=...]
  transfers between devices with their start and end apart: 12 -> 12, of which waited for: 7 -> 8; matrix products, arithmetic and copies ran while one was open for 0% -> 0% of each run, Pallas kernels for 14% -> 10%
where the time goes in v7:
time: 38.1 us; the launch traced here: 37.9 us
  starting transfers between devices  16.4 us (43%)
  waiting for transfers between devices  12.5 us (33%)
  Pallas kernels  8.66 us (23%)
    ppermute x11, waiting for transfers between devices, across(): return lax.ppermute(x, axis, [(i, i ^ distance) for i in range(size)])  12.5 us
    ppermute x11, starting transfers between devices, across(): return lax.ppermute(x, axis, [(i, i ^ distance) for i in range(size)])  11.5 us
    ppermute x1, starting transfers between devices, shards(): halo = lax.ppermute(message, 'tm', [(i - 1, i) for i in range(1, times)])  4.88 us
    pallas_call x4, Pallas kernels, correlate(): pl.pallas_call(functools.partial(correlate_kernel, spans, pairs, factor,...  2.67 us
    pallas_call x1, Pallas kernels, shards(): pl.pallas_call(load_kernel, out_shape=[jax.ShapeDtypeStruct((channels, 2...  2.32 us
    pallas_call x1, Pallas kernels, shards(): pl.pallas_call(functools.partial(rest_kernel, windows, times), out_shape=...  1.41 us
    pallas_call x1, Pallas kernels, shards(): pl.pallas_call(functools.partial(second_kernel, windows), out_shape=chunk...  1.03 us
    pallas_call x1, Pallas kernels, shards(): pl.pallas_call(functools.partial(first_kernel, windows), out_shape=chunk_...  0.88 us
  transfers between devices with their start and end apart: 12, of which 8 were waited for; matrix products, arithmetic and copies ran while one was open for 0% of the time, Pallas kernels for 10%

profile of v7, /device:TPU:0, one launch (start us, length us, event | category | flops | bytes accessed | tf_op | source)
XLA Modules:
  0.0 37.9 jit_solution(11045934828623266751)
XLA Ops:
  0.0 0.0 copy-start.2
  0.0 2.3 %load.1 = (bf16[64,1280]{1,0:T(8,128)(2,1)S(1)}, f32[64,1024]{1,0:T(8,128)S(1)}, bf16[64,6144]{1,0:T(8,128)(2,1)S(1)}, f32[33,64]{1,0:T(8,128)S(1)}, bf16[1024,1...) custom-call(bf16[64,6144]{1,0:T(8,128)(2,1)} %traces_in.1, f32[33,64]{1,0:T(8,128)} %bitcast.10, ...), custom_call_target="tpu_custom_call" | custom-call | tf_op jit(solution)/shard_map/load/pallas_call | solution.py:430
  2.3 4.9 %collective-permute-start = (bf16[64,1280]{1,0:T(8,128)(2,1)S(1)}, bf16[64,1280]{1,0:T(8,128)(2,1)S(1)}, u32[]{:S(2)}, u32[]{:S(2)}) collective-permute-start(bf16[64,1280]{1,0:T(8,128)(2,1)S(1)} %get-tuple-element.28), channel_id=1, source_target_pairs={{0,1},{2,3},{4,5},{6,7},{8,9},{10,11},{12,13},{14,15},{16,17},{18,... | collective-permute-start | bytes 491528 | tf_op jit(solution)/shard_map/ppermute | solution.py:453
  7.2 0.0 copy-done.2
  7.2 0.1 collective-permute-start.1
  7.3 1.1 %collective-permute-done.1.other = s32[1,12]{1,0:T(1,128)S(1)} collective-permute-done((s32[1,12]{1,0:T(1,128)S(1)}, s32[1,12]{1,0:T(1,128)S(1)}, u32[]{:S(2)}, u32[]{:S(2)}) %collective-permute-start.1) | collective-permute-done | bytes 80 | tf_op jit(solution)/shard_map/ppermute | solution.py:421
  8.4 1.6 %collective-permute-start.2 = (s32[2,12]{1,0:T(2,128)S(1)}, s32[2,12]{1,0:T(2,128)S(1)}, u32[]{:S(2)}, u32[]{:S(2)}) collective-permute-start(s32[2,12]{1,0:T(2,128)S(1)} %pair.1), channel_id=1, source_target_pairs={{0,4},{2,6},{4,0},{6,2},{8,12},{10,14},{12,8},{14,10},{1,5},{3,7},... | collective-permute-start | bytes 296 | tf_op jit(solution)/shard_map/ppermute | solution.py:421
  10.0 0.9 %first.1 = (f32[128,512]{1,0:T(8,128)S(1)}, f32[64,512]{1,0:T(8,128)S(1)}, f32[64,512]{1,0:T(8,128)S(1)}, bf16[64,256]{1,0:T(8,128)(2,1)S(1)}, bf16[64,96]{1,0:T(8,128)(2,1)S(1)}, /*index=5*/bf16[64,144]{1,0:T(8,128)(2,1)S(1)}) custom-call(bf16[64,6144]{1,0:T(8,128)(2,1)S(1)} %get-tuple-element.29.traces, f32[33,64]{1,0:T(8,128)S(1)} %get-tuple-element.30.taps, ...), custom_call_target="tpu_custom_call" | custom-call | tf_op jit(solution)/shard_map/first/pallas_call | solution.py:465
  10.9 1.1 %collective-permute-done.2 = s32[2,12]{1,0:T(2,128)S(1)} collective-permute-done((s32[2,12]{1,0:T(2,128)S(1)}, s32[2,12]{1,0:T(2,128)S(1)}, u32[]{:S(2)}, u32[]{:S(2)}) %collective-permute-start.2) | collective-permute-done | bytes 128 | tf_op jit(solution)/shard_map/ppermute | solution.py:421
  12.0 2.6 %collective-permute-start.3 = (s32[4,12]{1,0:T(4,128)S(1)}, s32[4,12]{1,0:T(4,128)S(1)}, u32[]{:S(2)}, u32[]{:S(2)}) collective-permute-start(s32[4,12]{1,0:T(4,128)S(1)} %pad_add_fusion.refs_0_), channel_id=1, source_target_pairs={{0,8},{2,10},{4,12},{6,14},{8,0},{10,2},{12,4},{14,6},{1,9},{3,11}... | collective-permute-start | bytes 584 | tf_op jit(solution)/shard_map/ppermute | solution.py:421
  14.7 0.0 copy-start
  14.7 0.0 copy-start.1
  14.7 1.0 %second.1 = (f32[128,512]{1,0:T(8,128)S(1)}, f32[64,512]{1,0:T(8,128)S(1)}, bf16[64,1024]{1,0:T(8,128)(2,1)S(1)}) custom-call(bf16[64,6144]{1,0:T(8,128)(2,1)S(1)} %get-tuple-element.29.traces, bf16[1024,1024]{1,0:T(8,128)(2,1)S(1)} %get-tuple-element.31.table, f32[64,1024]{1,0:T(8,128)S(1)} %get-tuple-element.32.last_half, ...), custom_call_target="tpu_custom_call" | custom-call | tf_op jit(solution)/shard_map/second/pallas_call | solution.py:483
  15.7 0.9 %collective-permute-done.3.refs_1_ = s32[4,12]{1,0:T(4,128)S(1)} collective-permute-done((s32[4,12]{1,0:T(4,128)S(1)}, s32[4,12]{1,0:T(4,128)S(1)}, u32[]{:S(2)}, u32[]{:S(2)}) %collective-permute-start.3) | collective-permute-done | bytes 224 | tf_op jit(solution)/shard_map/ppermute | solution.py:421
  16.6 0.0 copy-done
  16.6 0.0 copy-done.1
  16.6 0.3 picks.1.refs_1_
  16.9 0.0 collective-permute-done.halo
  16.9 1.4 %rest.1 = (bf16[160,1024]{1,0:T(8,128)(2,1)S(1)}, bf16[160,1024]{1,0:T(8,128)(2,1)S(1)}, bf16[96,1024]{1,0:T(8,128)(2,1)S(1)}, bf16[96,1024]{1,0:T(8,128)(2,1)S(1)}) custom-call(bf16[64,1280]{1,0:T(8,128)(2,1)S(1)} %collective-permute-done.halo, bf16[64,256]{1,0:T(8,128)(2,1)S(1)} %get-tuple-element.33.ends, f32[33,64]{1,0:T(8,128)S(1)} %get-tuple-element.30.taps, ...), custom_call_target="tpu_custom_call" | custom-call | tf_op jit(solution)/shard_map/rest/pallas_call | solution.py:504
  18.4 0.1 collective-permute-start.5
  18.4 1.6 %collective-permute-done.5 = bf16[160,1024]{1,0:T(8,128)(2,1)S(1)} collective-permute-done((bf16[160,1024]{1,0:T(8,128)(2,1)S(1)}, bf16[160,1024]{1,0:T(8,128)(2,1)S(1)}, u32[]{:S(2)}, u32[]{:S(2)}) %collective-permute-start.5) | collective-permute-done | bytes 327712 | tf_op jit(solution)/shard_map/ppermute | solution.py:421
  20.1 0.1 add.15
  20.2 1.6 %collective-permute-start.7 = (bf16[40,1024]{1,0:T(8,128)(2,1)S(1)}, bf16[40,1024]{1,0:T(8,128)(2,1)S(1)}, u32[]{:S(2)}, u32[]{:S(2)}) collective-permute-start(bf16[40,1024]{1,0:T(8,128)(2,1)S(1)} %get-tuple-element.49), channel_id=1, source_target_pairs={{0,4},{2,6},{4,0},{6,2},{8,12},{10,14},{12,8},{14,10},{1,5},{3,7},... | collective-permute-start | bytes 245768 | tf_op jit(solution)/shard_map/ppermute | solution.py:421
  21.8 0.4 %collective-permute-start.6 = (bf16[40,1024]{1,0:T(8,128)(2,1)S(1)}, bf16[40,1024]{1,0:T(8,128)(2,1)S(1)}, u32[]{:S(2)}, u32[]{:S(2)}) collective-permute-start(bf16[40,1024]{1,0:T(8,128)(2,1)S(1)} %get-tuple-element.47), channel_id=1, source_target_pairs={{0,4},{2,6},{4,0},{6,2},{8,12},{10,14},{12,8},{14,10},{1,5},{3,7},... | collective-permute-start | bytes 245768 | tf_op jit(solution)/shard_map/ppermute | solution.py:421
  22.3 2.9 %collective-permute-done.7 = bf16[40,1024]{1,0:T(8,128)(2,1)S(1)} collective-permute-done((bf16[40,1024]{1,0:T(8,128)(2,1)S(1)}, bf16[40,1024]{1,0:T(8,128)(2,1)S(1)}, u32[]{:S(2)}, u32[]{:S(2)}) %collective-permute-start.7) | collective-permute-done | bytes 81952 | tf_op jit(solution)/shard_map/ppermute | solution.py:421
  25.2 2.7 %collective-permute-start.10 = (bf16[24,1024]{1,0:T(8,128)(2,1)S(1)}, bf16[24,1024]{1,0:T(8,128)(2,1)S(1)}, u32[]{:S(2)}, u32[]{:S(2)}) collective-permute-start(bf16[24,1024]{1,0:T(8,128)(2,1)S(1)} %slice.39), channel_id=1, source_target_pairs={{0,8},{2,10},{4,12},{6,14},{8,0},{10,2},{12,4},{14,6},{1,9},{3,11}... | collective-permute-start | bytes 147464 | tf_op jit(solution)/shard_map/ppermute | solution.py:421
  27.9 0.0 collective-permute-start.4
  27.9 0.3 collective-permute-start.8
  28.2 0.0 collective-permute-done.6
  28.3 2.4 %collective-permute-done.10 = bf16[24,1024]{1,0:T(8,128)(2,1)S(1)} collective-permute-done((bf16[24,1024]{1,0:T(8,128)(2,1)S(1)}, bf16[24,1024]{1,0:T(8,128)(2,1)S(1)}, u32[]{:S(2)}, u32[]{:S(2)}) %collective-permute-start.10) | collective-permute-done | bytes 49184 | tf_op jit(solution)/shard_map/ppermute | solution.py:421
  30.6 0.1 collective-permute-start.11
  30.7 2.0 %collective-permute-done.8 = bf16[16,1024]{1,0:T(8,128)(2,1)S(1)} collective-permute-done((bf16[16,1024]{1,0:T(8,128)(2,1)S(1)}, bf16[16,1024]{1,0:T(8,128)(2,1)S(1)}, u32[]{:S(2)}, u32[]{:S(2)}) %collective-permute-start.8) | collective-permute-done | bytes 32800 | tf_op jit(solution)/shard_map/ppermute | solution.py:421
  32.7 2.0 %collective-permute-start.9 = (bf16[16,1024]{1,0:T(8,128)(2,1)S(1)}, bf16[16,1024]{1,0:T(8,128)(2,1)S(1)}, u32[]{:S(2)}, u32[]{:S(2)}) collective-permute-start(bf16[16,1024]{1,0:T(8,128)(2,1)S(1)} %slice_add_fusion.1.refs_1_), channel_id=1, source_target_pairs={{0,1},{1,0},{2,3},{3,2},{4,5},{5,4},{6,7},{7,6},{8,9},{9,8},{10,11... | collective-permute-start | bytes 98312 | tf_op jit(solution)/shard_map/ppermute | solution.py:421
  34.7 0.5 %correlate.4.refs_2_ = f32[12,32,1024]{2,1,0:T(8,128)S(1)} custom-call(bf16[3,32,1024]{2,1,0:T(8,128)(2,1)S(1)} %bitcast.5, bf16[24,1024]{1,0:T(8,128)(2,1)S(1)} %slice_add_fusion.refs_1_), custom_call_target="tpu_custom_call" | custom-call | tf_op jit(solution)/shard_map/correlate/pallas_call | solution.py:396
  35.3 0.3 correlate.5.refs_2_
  35.6 0.0 collective-permute-done.4
  35.6 0.0 collective-permute-done.11.refs_1_
  35.6 0.6 %correlate.6.refs_2_ = f32[12,32,1024]{2,1,0:T(8,128)S(1)} custom-call(bf16[3,32,1024]{2,1,0:T(8,128)(2,1)S(1)} %bitcast.7, bf16[24,1024]{1,0:T(8,128)(2,1)S(1)} %collective-permute-done.11.refs_1_, f32[12,32,1024]{2,1,0:T(8,128)S(1)} %correlate.5.refs_2_), custom_call_target="tpu_custom_call" | custom-call | tf_op jit(solution)/shard_map/correlate/pallas_call | solution.py:396
  36.2 0.5 %collective-permute-done.9.refs_1_ = bf16[16,1024]{1,0:T(8,128)(2,1)S(1)} collective-permute-done((bf16[16,1024]{1,0:T(8,128)(2,1)S(1)}, bf16[16,1024]{1,0:T(8,128)(2,1)S(1)}, u32[]{:S(2)}, u32[]{:S(2)}) %collective-permute-start.9) | collective-permute-done | bytes 32800 | tf_op jit(solution)/shard_map/ppermute | solution.py:421
  36.6 1.3 %correlate.7 = f32[12,32,1024]{2,1,0:T(8,128)} custom-call(bf16[3,32,1024]{2,1,0:T(8,128)(2,1)S(1)} %bitcast.8, bf16[16,1024]{1,0:T(8,128)(2,1)S(1)} %collective-permute-done.9.refs_1_, f32[12,32,1024]{2,1,0:T(8,128)S(1)} %correlate.6.refs_2_), custom_call_target="tpu_custom_call" | custom-call | tf_op jit(solution)/shard_map/correlate/pallas_call | solution.py:396
  (9 shorter events, 0.1 us)
Async XLA Ops:
  0.0 7.2 %copy-start.2 = (s32[1,12]{1,0:T(1,128)S(1)}, s32[1,12]{1,0:T(1,128)}, u32[]{:S(2)}) copy-start(s32[1,12]{1,0:T(1,128)} %ids_in.1) | copy-start | bytes 148
  2.3 14.6 %collective-permute-start = (bf16[64,1280]{1,0:T(8,128)(2,1)S(1)}, bf16[64,1280]{1,0:T(8,128)(2,1)S(1)}, u32[]{:S(2)}, u32[]{:S(2)}) collective-permute-start(bf16[64,1280]{1,0:T(8,128)(2,1)S(1)} %get-tuple-element.28), channel_id=1, source_target_pairs={{0,1},{2,3},{4,5},{6,7},{8,9},{10,11},{12,13},{14,15},{16,17},{18,... | collective-permute-start | bytes 491528 | tf_op jit(solution)/shard_map/ppermute | solution.py:453
  7.2 1.2 %collective-permute-start.1 = (s32[1,12]{1,0:T(1,128)S(1)}, s32[1,12]{1,0:T(1,128)S(1)}, u32[]{:S(2)}, u32[]{:S(2)}) collective-permute-start(s32[1,12]{1,0:T(1,128)S(1)} %copy-done.2), channel_id=1, source_target_pairs={{0,2},{2,0},{4,6},{6,4},{8,10},{10,8},{12,14},{14,12},{1,3},{3,1},... | collective-permute-start | bytes 152 | tf_op jit(solution)/shard_map/ppermute | solution.py:421
  8.4 3.6 %collective-permute-start.2 = (s32[2,12]{1,0:T(2,128)S(1)}, s32[2,12]{1,0:T(2,128)S(1)}, u32[]{:S(2)}, u32[]{:S(2)}) collective-permute-start(s32[2,12]{1,0:T(2,128)S(1)} %pair.1), channel_id=1, source_target_pairs={{0,4},{2,6},{4,0},{6,2},{8,12},{10,14},{12,8},{14,10},{1,5},{3,7},... | collective-permute-start | bytes 296 | tf_op jit(solution)/shard_map/ppermute | solution.py:421
  12.0 4.5 %collective-permute-start.3 = (s32[4,12]{1,0:T(4,128)S(1)}, s32[4,12]{1,0:T(4,128)S(1)}, u32[]{:S(2)}, u32[]{:S(2)}) collective-permute-start(s32[4,12]{1,0:T(4,128)S(1)} %pad_add_fusion.refs_0_), channel_id=1, source_target_pairs={{0,8},{2,10},{4,12},{6,14},{8,0},{10,2},{12,4},{14,6},{1,9},{3,11}... | collective-permute-start | bytes 584 | tf_op jit(solution)/shard_map/ppermute | solution.py:421
  14.7 1.9 %copy-start = (s32[8,36]{1,0:T(8,128)S(1)}, s32[8,36]{1,0:T(8,128)}, u32[]{:S(2)}) copy-start(s32[8,36]{1,0:T(8,128)} %slots.1) | copy-start | bytes 3460
  14.7 1.9 %copy-start.1 = (s32[8]{0:T(128)S(1)}, s32[8]{0:T(128)}, u32[]{:S(2)}) copy-start(s32[8]{0:T(128)} %param.8) | copy-start | bytes 100
  18.4 1.7 %collective-permute-start.5 = (bf16[160,1024]{1,0:T(8,128)(2,1)S(1)}, bf16[160,1024]{1,0:T(8,128)(2,1)S(1)}, u32[]{:S(2)}, u32[]{:S(2)}) collective-permute-start(bf16[160,1024]{1,0:T(8,128)(2,1)S(1)} %get-tuple-element.45), channel_id=1, source_target_pairs={{0,2},{2,0},{4,6},{6,4},{8,10},{10,8},{12,14},{14,12},{1,3},{3,1},... | collective-permute-start | bytes 983048 | tf_op jit(solution)/shard_map/ppermute | solution.py:421
  20.2 5.0 %collective-permute-start.7 = (bf16[40,1024]{1,0:T(8,128)(2,1)S(1)}, bf16[40,1024]{1,0:T(8,128)(2,1)S(1)}, u32[]{:S(2)}, u32[]{:S(2)}) collective-permute-start(bf16[40,1024]{1,0:T(8,128)(2,1)S(1)} %get-tuple-element.49), channel_id=1, source_target_pairs={{0,4},{2,6},{4,0},{6,2},{8,12},{10,14},{12,8},{14,10},{1,5},{3,7},... | collective-permute-start | bytes 245768 | tf_op jit(solution)/shard_map/ppermute | solution.py:421
  21.8 6.4 %collective-permute-start.6 = (bf16[40,1024]{1,0:T(8,128)(2,1)S(1)}, bf16[40,1024]{1,0:T(8,128)(2,1)S(1)}, u32[]{:S(2)}, u32[]{:S(2)}) collective-permute-start(bf16[40,1024]{1,0:T(8,128)(2,1)S(1)} %get-tuple-element.47), channel_id=1, source_target_pairs={{0,4},{2,6},{4,0},{6,2},{8,12},{10,14},{12,8},{14,10},{1,5},{3,7},... | collective-permute-start | bytes 245768 | tf_op jit(solution)/shard_map/ppermute | solution.py:421
  25.2 5.4 %collective-permute-start.10 = (bf16[24,1024]{1,0:T(8,128)(2,1)S(1)}, bf16[24,1024]{1,0:T(8,128)(2,1)S(1)}, u32[]{:S(2)}, u32[]{:S(2)}) collective-permute-start(bf16[24,1024]{1,0:T(8,128)(2,1)S(1)} %slice.39), channel_id=1, source_target_pairs={{0,8},{2,10},{4,12},{6,14},{8,0},{10,2},{12,4},{14,6},{1,9},{3,11}... | collective-permute-start | bytes 147464 | tf_op jit(solution)/shard_map/ppermute | solution.py:421
  27.9 7.7 %collective-permute-start.4 = (bf16[96,1024]{1,0:T(8,128)(2,1)S(1)}, bf16[96,1024]{1,0:T(8,128)(2,1)S(1)}, u32[]{:S(2)}, u32[]{:S(2)}) collective-permute-start(bf16[96,1024]{1,0:T(8,128)(2,1)S(1)} %get-tuple-element.43), channel_id=1, source_target_pairs={{0,1},{1,0},{2,3},{3,2},{4,5},{5,4},{6,7},{7,6},{8,9},{9,8},{10,11... | collective-permute-start | bytes 589832 | tf_op jit(solution)/shard_map/ppermute | solution.py:421
  27.9 4.8 %collective-permute-start.8 = (bf16[16,1024]{1,0:T(8,128)(2,1)S(1)}, bf16[16,1024]{1,0:T(8,128)(2,1)S(1)}, u32[]{:S(2)}, u32[]{:S(2)}) collective-permute-start(bf16[16,1024]{1,0:T(8,128)(2,1)S(1)} %slice.37), channel_id=1, source_target_pairs={{0,8},{2,10},{4,12},{6,14},{8,0},{10,2},{12,4},{14,6},{1,9},{3,11}... | collective-permute-start | bytes 98312 | tf_op jit(solution)/shard_map/ppermute | solution.py:421
  30.6 5.0 %collective-permute-start.11 = (bf16[24,1024]{1,0:T(8,128)(2,1)S(1)}, bf16[24,1024]{1,0:T(8,128)(2,1)S(1)}, u32[]{:S(2)}, u32[]{:S(2)}) collective-permute-start(bf16[24,1024]{1,0:T(8,128)(2,1)S(1)} %slice_add_fusion.refs_1_), channel_id=1, source_target_pairs={{0,1},{1,0},{2,3},{3,2},{4,5},{5,4},{6,7},{7,6},{8,9},{9,8},{10,11... | collective-permute-start | bytes 147464 | tf_op jit(solution)/shard_map/ppermute | solution.py:421
  32.7 3.9 %collective-permute-start.9 = (bf16[16,1024]{1,0:T(8,128)(2,1)S(1)}, bf16[16,1024]{1,0:T(8,128)(2,1)S(1)}, u32[]{:S(2)}, u32[]{:S(2)}) collective-permute-start(bf16[16,1024]{1,0:T(8,128)(2,1)S(1)} %slice_add_fusion.1.refs_1_), channel_id=1, source_target_pairs={{0,1},{1,0},{2,3},{3,2},{4,5},{5,4},{6,7},{7,6},{8,9},{9,8},{10,11... | collective-permute-start | bytes 98312 | tf_op jit(solution)/shard_map/ppermute | solution.py:421

commit v8 on v7

--- a/solution.py
+++ b/solution.py
@@ -19,6 +19,7 @@
 F32 = jnp.float32
 BF16 = jnp.bfloat16
 LIMIT = 24 * 1024 * 1024
+HINT = 10**10
 
 
 def piece_table():
@@ -130,12 +131,10 @@
     lax.fori_loop(0, count // ROWS, step, 0, unroll=4)
 
 
-def load_kernel(
-    traces_in, taps_in, table_in, ids_in, message, last_half, traces, taps, table, ids, sems
-):
+def load_kernel(end, traces_in, table_in, ids_in, message, last_half, table, ids, traces, sems):
     channels, samples = traces.shape
-    begin = samples - HALF - 128
-    copies = [pltpu.make_async_copy(traces_in.at[:, begin:], traces.at[:, begin:], sems.at[0])]
+    begin = traces_in.shape[1] - samples
+    copies = [pltpu.make_async_copy(traces_in.at[:, begin:], traces, sems.at[0])]
     order = [c for f in range(0, NF, CHUNK) for c in (f, NF + f)]
     for i, c in enumerate(order):
         cols = slice(c, c + CHUNK)
@@ -143,16 +142,14 @@
             pltpu.make_async_copy(table_in.at[:, cols], table.at[:, cols], sems.at[1 + i])
         )
     at = 1 + len(order)
-    copies += [
-        pltpu.make_async_copy(traces_in.at[:, :begin], traces.at[:, :begin], sems.at[at]),
-        pltpu.make_async_copy(taps_in, taps, sems.at[at + 1]),
-        pltpu.make_async_copy(ids_in, ids, sems.at[at + 2]),
-    ]
+    copies.append(pltpu.make_async_copy(ids_in, ids, sems.at[at]))
     for copy in copies:
         copy.start()
     copies[0].wait()
-    message[:, 2 * NF : 2 * NF + 128] = traces[:, begin : begin + 128]
-    message[:, 2 * NF + 128 :] = traces[:, samples - 128 :]
+    lane = lax.broadcasted_iota(jnp.int32, (channels, 128), 1)
+    final = pltpu.roll(traces[:, samples - 128 :].astype(F32), 128 - end, 1)
+    tile = jnp.where(lane < 128 - end, final, traces[:, :128].astype(F32))
+    message[:, 2 * NF :] = tile.astype(BF16)
     pieces = [samples - HALF + q * PIECE for q in range(HALF // PIECE)]
     x = jnp.concatenate([traces[:, p : p + PIECE] for p in pieces], axis=0)
     turns = Turns()
@@ -291,7 +288,8 @@
     tile = 128
     rest = windows - 1
 
-    before = [halo[:, 2 * NF : 2 * NF + tile], halo[:, 2 * NF + tile :]]
+    arrived = halo[:, 2 * NF :].astype(F32)
+    before = [arrived, pltpu.roll(arrived, tap_count - 1, 1)]
     before += [ends[:, (b - 1) * tile : b * tile] for b in range(1, windows - 2)]
     after = [ends[:, w * tile : (w + 1) * tile] for w in range(rest)]
     apart = jnp.concatenate([b.astype(F32) - a.astype(F32) for b, a in zip(before, after)], axis=0)
@@ -426,20 +424,26 @@
     bits = [1 << b for b in range(chips.bit_length() - 1)]
 
     other = across(block_sources, "chan", 1)
-    inputs = (traces, filter_taps.T, jnp.asarray(piece_table()), block_sources)
-    message, last_half, traces, taps, table, ids = pl.pallas_call(
-        load_kernel,
+    inputs = (traces, jnp.asarray(piece_table()), block_sources)
+    message, last_half, table, ids = pl.pallas_call(
+        functools.partial(load_kernel, tap_count - 1),
         out_shape=[
-            jax.ShapeDtypeStruct((channels, 2 * NF + 256), BF16),
+            jax.ShapeDtypeStruct((channels, 2 * NF + 128), BF16),
             jax.ShapeDtypeStruct((channels, 2 * NF), F32),
         ]
-        + [jax.ShapeDtypeStruct(a.shape, a.dtype) for a in inputs],
-        in_specs=[hbm] * 4,
-        out_specs=[vmem] * 6,
-        scratch_shapes=[pltpu.SemaphoreType.DMA((4 + 2 * NF // CHUNK,))],
+        + [jax.ShapeDtypeStruct(a.shape, a.dtype) for a in inputs[1:]],
+        in_specs=[hbm] * 3,
+        out_specs=[vmem] * 4,
+        scratch_shapes=[
+            pltpu.VMEM((channels, HALF + 128), BF16),
+            pltpu.SemaphoreType.DMA((2 + 2 * NF // CHUNK,)),
+        ],
         compiler_params=params,
         name="load",
     )(*(pltpu.with_memory_space_constraint(a, pltpu.HBM) for a in inputs))
+    traces, taps = (
+        pltpu.with_memory_space_constraint(a, pltpu.VMEM) for a in (traces, filter_taps.T)
+    )
     wanted = [
         pl.pallas_call(
             pair_kernel,
@@ -447,6 +451,7 @@
             in_specs=[vmem] * 2,
             out_specs=vmem,
             compiler_params=params,
+            cost_estimate=pl.CostEstimate(flops=HINT, bytes_accessed=8 * pairs, transcendentals=0),
             name="pair",
         )(ids, other)
     ]

time: 38.1 us -> 36.9 us (0.969)
  waiting for transfers between devices: 12.5 us -> 11.3 us
    ppermute x11, waiting for transfers between devices: 12.5 us -> 11.3 us  [across(): return lax.ppermute(x, axis, [(i, i ^ distance) for i in range(size)])]
    ppermute x11, starting transfers between devices: 11.5 us -> 12 us  [across(): return lax.ppermute(x, axis, [(i, i ^ distance) for i in range(size)])]
    ppermute x1, starting transfers between devices: 4.88 us -> 4.39 us  [shards(): halo = lax.ppermute(message, 'tm', [(i - 1, i) for i in range(1, times)])]
  transfers between devices with their start and end apart: 12 -> 12, of which waited for: 8 -> 7; matrix products, arithmetic and copies ran while one was open for 0% -> 0% of each run, Pallas kernels for 10% -> 16%
where the time goes in v8:
time: 36.9 us; the launch traced here: 36.8 us
  starting transfers between devices  16.4 us (44%)
  waiting for transfers between devices  11.3 us (31%)
  Pallas kernels  8.66 us (23%)
    ppermute x11, starting transfers between devices, across(): return lax.ppermute(x, axis, [(i, i ^ distance) for i in range(size)])  12 us
    ppermute x11, waiting for transfers between devices, across(): return lax.ppermute(x, axis, [(i, i ^ distance) for i in range(size)])  11.3 us
    ppermute x1, starting transfers between devices, shards(): halo = lax.ppermute(message, 'tm', [(i - 1, i) for i in range(1, times)])  4.39 us
    pallas_call x4, Pallas kernels, correlate(): pl.pallas_call(functools.partial(correlate_kernel, spans, pairs, factor,...  2.67 us
    pallas_call x1, Pallas kernels, shards(): pl.pallas_call(functools.partial(load_kernel, tap_count - 1), out_shape=[...  2.27 us
    pallas_call x1, Pallas kernels, shards(): pl.pallas_call(functools.partial(rest_kernel, windows, times), out_shape=...  1.45 us
    pallas_call x1, Pallas kernels, shards(): pl.pallas_call(functools.partial(second_kernel, windows), out_shape=chunk...  1.03 us
    pallas_call x1, Pallas kernels, shards(): pl.pallas_call(functools.partial(first_kernel, windows), out_shape=chunk_...  0.89 us
  transfers between devices with their start and end apart: 12, of which 7 were waited for; matrix products, arithmetic and copies ran while one was open for 0% of the time, Pallas kernels for 16%

profile of v8, /device:TPU:0, one launch (start us, length us, event | category | flops | bytes accessed | tf_op | source)
XLA Modules:
  0.0 36.8 jit_solution(10806582945923105621)
XLA Ops:
  0.0 0.5 %collective-permute-start.1 = (s32[1,12]{1,0:T(1,128)}, s32[1,12]{1,0:T(1,128)S(1)}, u32[]{:S(2)}, u32[]{:S(2)}) collective-permute-start(s32[1,12]{1,0:T(1,128)} %ids_in.1), channel_id=1, source_target_pairs={{0,2},{2,0},{4,6},{6,4},{8,10},{10,8},{12,14},{14,12},{1,3},{3,1},... | collective-permute-start | bytes 152 | tf_op jit(solution)/shard_map/ppermute | solution.py:419
  0.5 2.3 %load.1 = (bf16[64,1152]{1,0:T(8,128)(2,1)S(1)}, f32[64,1024]{1,0:T(8,128)S(1)}, bf16[1024,1024]{1,0:T(8,128)(2,1)S(1)}, s32[1,12]{1,0:T(1,128)S(1)}) custom-call(bf16[64,6144]{1,0:T(8,128)(2,1)} %traces.3, bf16[1024,1024]{1,0:T(8,128)(2,1)} %constant.2.clone.table_in, s32[1,12]{1,0:T(1,128)} %ids_in.1), custom_call_target="tpu_custom_call" | custom-call | tf_op jit(solution)/shard_map/load/pallas_call | solution.py:428
  2.8 4.4 %collective-permute-start = (bf16[64,1152]{1,0:T(8,128)(2,1)S(1)}, bf16[64,1152]{1,0:T(8,128)(2,1)S(1)}, u32[]{:S(2)}, u32[]{:S(2)}) collective-permute-start(bf16[64,1152]{1,0:T(8,128)(2,1)S(1)} %get-tuple-element.26), channel_id=1, source_target_pairs={{0,1},{2,3},{4,5},{6,7},{8,9},{10,11},{12,13},{14,15},{16,17},{18,... | collective-permute-start | bytes 442376 | tf_op jit(solution)/shard_map/ppermute | solution.py:458
  7.2 0.0 collective-permute-done.1.other
  7.2 0.0 copy-start
  7.2 0.0 copy-start.1
  7.2 1.6 %collective-permute-start.2 = (s32[2,12]{1,0:T(2,128)S(1)}, s32[2,12]{1,0:T(2,128)S(1)}, u32[]{:S(2)}, u32[]{:S(2)}) collective-permute-start(s32[2,12]{1,0:T(2,128)S(1)} %pair.1), channel_id=1, source_target_pairs={{0,4},{2,6},{4,0},{6,2},{8,12},{10,14},{12,8},{14,10},{1,5},{3,7},... | collective-permute-start | bytes 296 | tf_op jit(solution)/shard_map/ppermute | solution.py:419
  8.9 0.0 copy-done
  8.9 0.0 copy-done.1
  8.9 0.9 %first.1 = (f32[128,512]{1,0:T(8,128)S(1)}, f32[64,512]{1,0:T(8,128)S(1)}, f32[64,512]{1,0:T(8,128)S(1)}, bf16[64,256]{1,0:T(8,128)(2,1)S(1)}, bf16[64,96]{1,0:T(8,128)(2,1)S(1)}, /*index=5*/bf16[64,144]{1,0:T(8,128)(2,1)S(1)}) custom-call(bf16[64,6144]{1,0:T(8,128)(2,1)S(1)} %copy-done, f32[33,64]{1,0:T(8,128)S(1)} %bitcast.9, ...), custom_call_target="tpu_custom_call" | custom-call | tf_op jit(solution)/shard_map/first/pallas_call | solution.py:470
  9.8 1.1 %collective-permute-done.2 = s32[2,12]{1,0:T(2,128)S(1)} collective-permute-done((s32[2,12]{1,0:T(2,128)S(1)}, s32[2,12]{1,0:T(2,128)S(1)}, u32[]{:S(2)}, u32[]{:S(2)}) %collective-permute-start.2) | collective-permute-done | bytes 128 | tf_op jit(solution)/shard_map/ppermute | solution.py:419
  10.9 2.6 %collective-permute-start.3 = (s32[4,12]{1,0:T(4,128)S(1)}, s32[4,12]{1,0:T(4,128)S(1)}, u32[]{:S(2)}, u32[]{:S(2)}) collective-permute-start(s32[4,12]{1,0:T(4,128)S(1)} %pad_add_fusion.refs_0_), channel_id=1, source_target_pairs={{0,8},{2,10},{4,12},{6,14},{8,0},{10,2},{12,4},{14,6},{1,9},{3,11}... | collective-permute-start | bytes 584 | tf_op jit(solution)/shard_map/ppermute | solution.py:419
  13.5 0.0 copy-start.2
  13.5 0.0 copy-start.3
  13.5 1.0 %second.1 = (f32[128,512]{1,0:T(8,128)S(1)}, f32[64,512]{1,0:T(8,128)S(1)}, bf16[64,1024]{1,0:T(8,128)(2,1)S(1)}) custom-call(bf16[64,6144]{1,0:T(8,128)(2,1)S(1)} %copy-done, bf16[1024,1024]{1,0:T(8,128)(2,1)S(1)} %get-tuple-element.27.table, f32[64,1024]{1,0:T(8,128)S(1)} %get-tuple-element.28.last_half, bf16[64,144]{1,0:T(8,128)(2,1)S(1)} %get-tuple-element.31.lines, ...), custom_call_target="tpu_custom_call" | custom-call | tf_op jit(solution)/shard_map/second/pallas_call | solution.py:488
  14.6 0.9 %collective-permute-done.3.refs_1_ = s32[4,12]{1,0:T(4,128)S(1)} collective-permute-done((s32[4,12]{1,0:T(4,128)S(1)}, s32[4,12]{1,0:T(4,128)S(1)}, u32[]{:S(2)}, u32[]{:S(2)}) %collective-permute-start.3) | collective-permute-done | bytes 224 | tf_op jit(solution)/shard_map/ppermute | solution.py:419
  15.4 0.0 copy-done.2
  15.4 0.0 copy-done.3
  15.4 0.3 picks.1.refs_1_
  15.8 0.0 collective-permute-done.halo
  15.8 1.4 %rest.1 = (bf16[160,1024]{1,0:T(8,128)(2,1)S(1)}, bf16[160,1024]{1,0:T(8,128)(2,1)S(1)}, bf16[96,1024]{1,0:T(8,128)(2,1)S(1)}, bf16[96,1024]{1,0:T(8,128)(2,1)S(1)}) custom-call(bf16[64,1152]{1,0:T(8,128)(2,1)S(1)} %collective-permute-done.halo, bf16[64,256]{1,0:T(8,128)(2,1)S(1)} %get-tuple-element.29.ends, f32[33,64]{1,0:T(8,128)S(1)} %bitcast.10, ...), custom_call_target="tpu_custom_call" | custom-call | tf_op jit(solution)/shard_map/rest/pallas_call | solution.py:509
  17.2 0.1 collective-permute-start.5
  17.3 1.6 %collective-permute-done.5 = bf16[160,1024]{1,0:T(8,128)(2,1)S(1)} collective-permute-done((bf16[160,1024]{1,0:T(8,128)(2,1)S(1)}, bf16[160,1024]{1,0:T(8,128)(2,1)S(1)}, u32[]{:S(2)}, u32[]{:S(2)}) %collective-permute-start.5) | collective-permute-done | bytes 327712 | tf_op jit(solution)/shard_map/ppermute | solution.py:419
  18.9 0.1 add.15
  19.1 1.6 %collective-permute-start.7 = (bf16[40,1024]{1,0:T(8,128)(2,1)S(1)}, bf16[40,1024]{1,0:T(8,128)(2,1)S(1)}, u32[]{:S(2)}, u32[]{:S(2)}) collective-permute-start(bf16[40,1024]{1,0:T(8,128)(2,1)S(1)} %get-tuple-element.45), channel_id=1, source_target_pairs={{0,4},{2,6},{4,0},{6,2},{8,12},{10,14},{12,8},{14,10},{1,5},{3,7},... | collective-permute-start | bytes 245768 | tf_op jit(solution)/shard_map/ppermute | solution.py:419
  20.7 0.5 %collective-permute-start.6 = (bf16[40,1024]{1,0:T(8,128)(2,1)S(1)}, bf16[40,1024]{1,0:T(8,128)(2,1)S(1)}, u32[]{:S(2)}, u32[]{:S(2)}) collective-permute-start(bf16[40,1024]{1,0:T(8,128)(2,1)S(1)} %get-tuple-element.43), channel_id=1, source_target_pairs={{0,4},{2,6},{4,0},{6,2},{8,12},{10,14},{12,8},{14,10},{1,5},{3,7},... | collective-permute-start | bytes 245768 | tf_op jit(solution)/shard_map/ppermute | solution.py:419
  21.2 2.9 %collective-permute-done.7 = bf16[40,1024]{1,0:T(8,128)(2,1)S(1)} collective-permute-done((bf16[40,1024]{1,0:T(8,128)(2,1)S(1)}, bf16[40,1024]{1,0:T(8,128)(2,1)S(1)}, u32[]{:S(2)}, u32[]{:S(2)}) %collective-permute-start.7) | collective-permute-done | bytes 81952 | tf_op jit(solution)/shard_map/ppermute | solution.py:419
  24.1 2.6 %collective-permute-start.10 = (bf16[24,1024]{1,0:T(8,128)(2,1)S(1)}, bf16[24,1024]{1,0:T(8,128)(2,1)S(1)}, u32[]{:S(2)}, u32[]{:S(2)}) collective-permute-start(bf16[24,1024]{1,0:T(8,128)(2,1)S(1)} %slice.39), channel_id=1, source_target_pairs={{0,8},{2,10},{4,12},{6,14},{8,0},{10,2},{12,4},{14,6},{1,9},{3,11}... | collective-permute-start | bytes 147464 | tf_op jit(solution)/shard_map/ppermute | solution.py:419
  26.8 0.0 collective-permute-start.4
  26.8 0.4 collective-permute-start.8
  27.1 0.0 collective-permute-done.6
  27.2 2.4 %collective-permute-done.10 = bf16[24,1024]{1,0:T(8,128)(2,1)S(1)} collective-permute-done((bf16[24,1024]{1,0:T(8,128)(2,1)S(1)}, bf16[24,1024]{1,0:T(8,128)(2,1)S(1)}, u32[]{:S(2)}, u32[]{:S(2)}) %collective-permute-start.10) | collective-permute-done | bytes 49184 | tf_op jit(solution)/shard_map/ppermute | solution.py:419
  29.5 0.1 collective-permute-start.11
  29.6 2.0 %collective-permute-done.8 = bf16[16,1024]{1,0:T(8,128)(2,1)S(1)} collective-permute-done((bf16[16,1024]{1,0:T(8,128)(2,1)S(1)}, bf16[16,1024]{1,0:T(8,128)(2,1)S(1)}, u32[]{:S(2)}, u32[]{:S(2)}) %collective-permute-start.8) | collective-permute-done | bytes 32800 | tf_op jit(solution)/shard_map/ppermute | solution.py:419
  31.6 2.0 %collective-permute-start.9 = (bf16[16,1024]{1,0:T(8,128)(2,1)S(1)}, bf16[16,1024]{1,0:T(8,128)(2,1)S(1)}, u32[]{:S(2)}, u32[]{:S(2)}) collective-permute-start(bf16[16,1024]{1,0:T(8,128)(2,1)S(1)} %slice_add_fusion.1.refs_1_), channel_id=1, source_target_pairs={{0,1},{1,0},{2,3},{3,2},{4,5},{5,4},{6,7},{7,6},{8,9},{9,8},{10,11... | collective-permute-start | bytes 98312 | tf_op jit(solution)/shard_map/ppermute | solution.py:419
  33.6 0.5 %correlate.4.refs_2_ = f32[12,32,1024]{2,1,0:T(8,128)S(1)} custom-call(bf16[3,32,1024]{2,1,0:T(8,128)(2,1)S(1)} %bitcast.5, bf16[24,1024]{1,0:T(8,128)(2,1)S(1)} %slice_add_fusion.refs_1_), custom_call_target="tpu_custom_call" | custom-call | tf_op jit(solution)/shard_map/correlate/pallas_call | solution.py:394
  34.1 0.3 correlate.5.refs_2_
  34.5 0.0 collective-permute-done.4
  34.5 0.0 collective-permute-done.11.refs_1_
  34.5 0.6 %correlate.6.refs_2_ = f32[12,32,1024]{2,1,0:T(8,128)S(1)} custom-call(bf16[3,32,1024]{2,1,0:T(8,128)(2,1)S(1)} %bitcast.7, bf16[24,1024]{1,0:T(8,128)(2,1)S(1)} %collective-permute-done.11.refs_1_, f32[12,32,1024]{2,1,0:T(8,128)S(1)} %correlate.5.refs_2_), custom_call_target="tpu_custom_call" | custom-call | tf_op jit(solution)/shard_map/correlate/pallas_call | solution.py:394
  35.0 0.5 %collective-permute-done.9.refs_1_ = bf16[16,1024]{1,0:T(8,128)(2,1)S(1)} collective-permute-done((bf16[16,1024]{1,0:T(8,128)(2,1)S(1)}, bf16[16,1024]{1,0:T(8,128)(2,1)S(1)}, u32[]{:S(2)}, u32[]{:S(2)}) %collective-permute-start.9) | collective-permute-done | bytes 32800 | tf_op jit(solution)/shard_map/ppermute | solution.py:419
  35.5 1.3 %correlate.7 = f32[12,32,1024]{2,1,0:T(8,128)} custom-call(bf16[3,32,1024]{2,1,0:T(8,128)(2,1)S(1)} %bitcast.8, bf16[16,1024]{1,0:T(8,128)(2,1)S(1)} %collective-permute-done.9.refs_1_, f32[12,32,1024]{2,1,0:T(8,128)S(1)} %correlate.6.refs_2_), custom_call_target="tpu_custom_call" | custom-call | tf_op jit(solution)/shard_map/correlate/pallas_call | solution.py:394
  (9 shorter events, 0.1 us)
Async XLA Ops:
  0.0 7.2 %collective-permute-start.1 = (s32[1,12]{1,0:T(1,128)}, s32[1,12]{1,0:T(1,128)S(1)}, u32[]{:S(2)}, u32[]{:S(2)}) collective-permute-start(s32[1,12]{1,0:T(1,128)} %ids_in.1), channel_id=1, source_target_pairs={{0,2},{2,0},{4,6},{6,4},{8,10},{10,8},{12,14},{14,12},{1,3},{3,1},... | collective-permute-start | bytes 152 | tf_op jit(solution)/shard_map/ppermute | solution.py:419
  2.8 13.0 %collective-permute-start = (bf16[64,1152]{1,0:T(8,128)(2,1)S(1)}, bf16[64,1152]{1,0:T(8,128)(2,1)S(1)}, u32[]{:S(2)}, u32[]{:S(2)}) collective-permute-start(bf16[64,1152]{1,0:T(8,128)(2,1)S(1)} %get-tuple-element.26), channel_id=1, source_target_pairs={{0,1},{2,3},{4,5},{6,7},{8,9},{10,11},{12,13},{14,15},{16,17},{18,... | collective-permute-start | bytes 442376 | tf_op jit(solution)/shard_map/ppermute | solution.py:458
  7.2 1.7 %copy-start = (bf16[64,6144]{1,0:T(8,128)(2,1)S(1)}, bf16[64,6144]{1,0:T(8,128)(2,1)}, u32[]{:S(2)}) copy-start(bf16[64,6144]{1,0:T(8,128)(2,1)} %traces.3) | copy-start | bytes 2359300
  7.2 1.7 %copy-start.1 = (f32[64,33]{0,1:T(8,128)S(1)}, f32[64,33]{0,1:T(8,128)}, u32[]{:S(2)}) copy-start(f32[64,33]{0,1:T(8,128)} %param.7) | copy-start | bytes 25348
  7.2 3.6 %collective-permute-start.2 = (s32[2,12]{1,0:T(2,128)S(1)}, s32[2,12]{1,0:T(2,128)S(1)}, u32[]{:S(2)}, u32[]{:S(2)}) collective-permute-start(s32[2,12]{1,0:T(2,128)S(1)} %pair.1), channel_id=1, source_target_pairs={{0,4},{2,6},{4,0},{6,2},{8,12},{10,14},{12,8},{14,10},{1,5},{3,7},... | collective-permute-start | bytes 296 | tf_op jit(solution)/shard_map/ppermute | solution.py:419
  10.9 4.5 %collective-permute-start.3 = (s32[4,12]{1,0:T(4,128)S(1)}, s32[4,12]{1,0:T(4,128)S(1)}, u32[]{:S(2)}, u32[]{:S(2)}) collective-permute-start(s32[4,12]{1,0:T(4,128)S(1)} %pad_add_fusion.refs_0_), channel_id=1, source_target_pairs={{0,8},{2,10},{4,12},{6,14},{8,0},{10,2},{12,4},{14,6},{1,9},{3,11}... | collective-permute-start | bytes 584 | tf_op jit(solution)/shard_map/ppermute | solution.py:419
  13.5 1.9 %copy-start.2 = (s32[8,36]{1,0:T(8,128)S(1)}, s32[8,36]{1,0:T(8,128)}, u32[]{:S(2)}) copy-start(s32[8,36]{1,0:T(8,128)} %slots.1) | copy-start | bytes 3460
  13.5 1.9 %copy-start.3 = (s32[8]{0:T(128)S(1)}, s32[8]{0:T(128)}, u32[]{:S(2)}) copy-start(s32[8]{0:T(128)} %param.8) | copy-start | bytes 100
  17.2 1.7 %collective-permute-start.5 = (bf16[160,1024]{1,0:T(8,128)(2,1)S(1)}, bf16[160,1024]{1,0:T(8,128)(2,1)S(1)}, u32[]{:S(2)}, u32[]{:S(2)}) collective-permute-start(bf16[160,1024]{1,0:T(8,128)(2,1)S(1)} %get-tuple-element.41), channel_id=1, source_target_pairs={{0,2},{2,0},{4,6},{6,4},{8,10},{10,8},{12,14},{14,12},{1,3},{3,1},... | collective-permute-start | bytes 983048 | tf_op jit(solution)/shard_map/ppermute | solution.py:419
  19.1 5.0 %collective-permute-start.7 = (bf16[40,1024]{1,0:T(8,128)(2,1)S(1)}, bf16[40,1024]{1,0:T(8,128)(2,1)S(1)}, u32[]{:S(2)}, u32[]{:S(2)}) collective-permute-start(bf16[40,1024]{1,0:T(8,128)(2,1)S(1)} %get-tuple-element.45), channel_id=1, source_target_pairs={{0,4},{2,6},{4,0},{6,2},{8,12},{10,14},{12,8},{14,10},{1,5},{3,7},... | collective-permute-start | bytes 245768 | tf_op jit(solution)/shard_map/ppermute | solution.py:419
  20.7 6.4 %collective-permute-start.6 = (bf16[40,1024]{1,0:T(8,128)(2,1)S(1)}, bf16[40,1024]{1,0:T(8,128)(2,1)S(1)}, u32[]{:S(2)}, u32[]{:S(2)}) collective-permute-start(bf16[40,1024]{1,0:T(8,128)(2,1)S(1)} %get-tuple-element.43), channel_id=1, source_target_pairs={{0,4},{2,6},{4,0},{6,2},{8,12},{10,14},{12,8},{14,10},{1,5},{3,7},... | collective-permute-start | bytes 245768 | tf_op jit(solution)/shard_map/ppermute | solution.py:419
  24.1 5.4 %collective-permute-start.10 = (bf16[24,1024]{1,0:T(8,128)(2,1)S(1)}, bf16[24,1024]{1,0:T(8,128)(2,1)S(1)}, u32[]{:S(2)}, u32[]{:S(2)}) collective-permute-start(bf16[24,1024]{1,0:T(8,128)(2,1)S(1)} %slice.39), channel_id=1, source_target_pairs={{0,8},{2,10},{4,12},{6,14},{8,0},{10,2},{12,4},{14,6},{1,9},{3,11}... | collective-permute-start | bytes 147464 | tf_op jit(solution)/shard_map/ppermute | solution.py:419
  26.8 7.7 %collective-permute-start.4 = (bf16[96,1024]{1,0:T(8,128)(2,1)S(1)}, bf16[96,1024]{1,0:T(8,128)(2,1)S(1)}, u32[]{:S(2)}, u32[]{:S(2)}) collective-permute-start(bf16[96,1024]{1,0:T(8,128)(2,1)S(1)} %get-tuple-element.39), channel_id=1, source_target_pairs={{0,1},{1,0},{2,3},{3,2},{4,5},{5,4},{6,7},{7,6},{8,9},{9,8},{10,11... | collective-permute-start | bytes 589832 | tf_op jit(solution)/shard_map/ppermute | solution.py:419
  26.8 4.8 %collective-permute-start.8 = (bf16[16,1024]{1,0:T(8,128)(2,1)S(1)}, bf16[16,1024]{1,0:T(8,128)(2,1)S(1)}, u32[]{:S(2)}, u32[]{:S(2)}) collective-permute-start(bf16[16,1024]{1,0:T(8,128)(2,1)S(1)} %slice.37), channel_id=1, source_target_pairs={{0,8},{2,10},{4,12},{6,14},{8,0},{10,2},{12,4},{14,6},{1,9},{3,11}... | collective-permute-start | bytes 98312 | tf_op jit(solution)/shard_map/ppermute | solution.py:419
  29.5 4.9 %collective-permute-start.11 = (bf16[24,1024]{1,0:T(8,128)(2,1)S(1)}, bf16[24,1024]{1,0:T(8,128)(2,1)S(1)}, u32[]{:S(2)}, u32[]{:S(2)}) collective-permute-start(bf16[24,1024]{1,0:T(8,128)(2,1)S(1)} %slice_add_fusion.refs_1_), channel_id=1, source_target_pairs={{0,1},{1,0},{2,3},{3,2},{4,5},{5,4},{6,7},{7,6},{8,9},{9,8},{10,11... | collective-permute-start | bytes 147464 | tf_op jit(solution)/shard_map/ppermute | solution.py:419
  31.6 3.9 %collective-permute-start.9 = (bf16[16,1024]{1,0:T(8,128)(2,1)S(1)}, bf16[16,1024]{1,0:T(8,128)(2,1)S(1)}, u32[]{:S(2)}, u32[]{:S(2)}) collective-permute-start(bf16[16,1024]{1,0:T(8,128)(2,1)S(1)} %slice_add_fusion.1.refs_1_), channel_id=1, source_target_pairs={{0,1},{1,0},{2,3},{3,2},{4,5},{5,4},{6,7},{7,6},{8,9},{9,8},{10,11... | collective-permute-start | bytes 98312 | tf_op jit(solution)/shard_map/ppermute | solution.py:419

commit v9 on v8

--- a/solution.py
+++ b/solution.py
@@ -28,7 +28,9 @@
     exact = np.concatenate([np.cos(angle), -np.sin(angle)], axis=1)
     high = exact.astype(ml_dtypes.bfloat16)
     low = (exact - high.astype(np.float64)).astype(ml_dtypes.bfloat16)
-    return np.concatenate([high, low], axis=0)
+    both = np.concatenate([high, low], axis=0)
+    starts = [c for f in range(0, NF, CHUNK) for c in (f, NF + f)]
+    return np.stack([both[:, c : c + CHUNK] for c in starts])
 
 
 def split_two(x):
@@ -47,9 +49,9 @@
     return jnp.concatenate([high, low.astype(F32), high], axis=0)
 
 
-def stacked_rows(table, rows, cols):
-    first = table[:rows, cols]
-    return jnp.concatenate([first, first, table[PIECE : PIECE + rows, cols]], axis=0)
+def stacked_rows(table, rows, at):
+    first = table[at, :rows, :]
+    return jnp.concatenate([first, first, table[at, PIECE : PIECE + rows, :]], axis=0)
 
 
 class Turns:
@@ -80,11 +82,10 @@
 
 
 def half_spectra(x, table, channels, halves, turns, f):
-    re = slice(f, f + CHUNK)
-    im = slice(NF + f, NF + f + CHUNK)
     both = jnp.concatenate([x, x], axis=1)
-    dr = dot(both, table[:, re])
-    di = dot(both, table[:, im])
+    at = 2 * (f // CHUNK)
+    dr = dot(both, table[at])
+    di = dot(both, table[at + 1])
     out = []
     for b in range(halves):
         rows = [slice((4 * b + e) * channels, (4 * b + e + 1) * channels) for e in range(4)]
@@ -135,13 +136,9 @@
     channels, samples = traces.shape
     begin = traces_in.shape[1] - samples
     copies = [pltpu.make_async_copy(traces_in.at[:, begin:], traces, sems.at[0])]
-    order = [c for f in range(0, NF, CHUNK) for c in (f, NF + f)]
-    for i, c in enumerate(order):
-        cols = slice(c, c + CHUNK)
-        copies.append(
-            pltpu.make_async_copy(table_in.at[:, cols], table.at[:, cols], sems.at[1 + i])
-        )
-    at = 1 + len(order)
+    at = 1 + table.shape[0]
+    for i in range(table.shape[0]):
+        copies.append(pltpu.make_async_copy(table_in.at[i], table.at[i], sems.at[1 + i]))
     copies.append(pltpu.make_async_copy(ids_in, ids, sems.at[at]))
     for copy in copies:
         copy.start()
@@ -181,8 +178,9 @@
     turns = Turns()
     re = slice(f, f + CHUNK)
     im = slice(NF + f, NF + f + CHUNK)
-    pr = dot(lines[...], stacked_rows(table, size, re))
-    pi = dot(lines[...], stacked_rows(table, size, im))
+    at = 2 * (f // CHUNK)
+    pr = dot(lines[...], stacked_rows(table, size, at))
+    pi = dot(lines[...], stacked_rows(table, size, at + 1))
     response[:, :CHUNK] = pr
     response[:, CHUNK:] = pi
     halves = half_spectra(x, table, channels, windows - 1, turns, f)
@@ -199,8 +197,8 @@
             part[rows, :CHUNK] = yr
             part[rows, CHUNK:] = yi
         else:
-            last[:, :CHUNK] = yr + dot(edge[...], stacked_rows(table, lag, re))
-            last[:, CHUNK:] = yi + dot(edge[...], stacked_rows(table, lag, im))
+            last[:, :CHUNK] = yr + dot(edge[...], stacked_rows(table, lag, at))
+            last[:, CHUNK:] = yi + dot(edge[...], stacked_rows(table, lag, at + 1))
 
 
 def first_kernel(
@@ -301,8 +299,9 @@
         xr, xi = halo[:, re].astype(F32), halo[:, im].astype(F32)
         part, response = (part_b, response_b) if f else (part_a, response_a)
         pr, pi = response[:, :CHUNK], response[:, CHUNK:]
-        er = dot(edge, stacked_rows(table, tap_count - 1, re))
-        ei = dot(edge, stacked_rows(table, tap_count - 1, im))
+        at = 2 * (f // CHUNK)
+        er = dot(edge, stacked_rows(table, tap_count - 1, at))
+        ei = dot(edge, stacked_rows(table, tap_count - 1, at + 1))
         spectra[:channels, re] = part[:channels, :CHUNK] + er[:channels] + (xr * pr - xi * pi)
         spectra[:channels, im] = part[:channels, CHUNK:] + ei[:channels] + (xr * pi + xi * pr)
         spectra[channels:, re] = part[channels:, :CHUNK] + er[channels:]
@@ -373,7 +372,7 @@
             copy(p).start()
         return carry
 
-    lax.fori_loop(0, pairs, one, 0)
+    lax.fori_loop(0, pairs, one, 0, unroll=2 if pairs % 2 == 0 else 1)
     if last:
         for p in range(pairs):
             copy(p).wait()

time: 36.9 us -> 36.9 us (level)
  no operation moved by 1% of the time
where the time goes in v9:
time: 36.9 us; the launch traced here: 36.8 us
  starting transfers between devices  16.4 us (44%)
  waiting for transfers between devices  11.4 us (31%)
  Pallas kernels  8.55 us (23%)
    ppermute x11, starting transfers between devices, across(): return lax.ppermute(x, axis, [(i, i ^ distance) for i in range(size)])  12 us
    ppermute x11, waiting for transfers between devices, across(): return lax.ppermute(x, axis, [(i, i ^ distance) for i in range(size)])  11.4 us
    ppermute x1, starting transfers between devices, shards(): halo = lax.ppermute(message, 'tm', [(i - 1, i) for i in range(1, times)])  4.39 us
    pallas_call x4, Pallas kernels, correlate(): pl.pallas_call(functools.partial(correlate_kernel, spans, pairs, factor,...  2.58 us
    pallas_call x1, Pallas kernels, shards(): pl.pallas_call(functools.partial(load_kernel, tap_count - 1), out_shape=[...  2.26 us
    pallas_call x1, Pallas kernels, shards(): pl.pallas_call(functools.partial(rest_kernel, windows, times), out_shape=...  1.44 us
    pallas_call x1, Pallas kernels, shards(): pl.pallas_call(functools.partial(second_kernel, windows), out_shape=chunk...  1.03 us
    pallas_call x1, Pallas kernels, shards(): pl.pallas_call(functools.partial(first_kernel, windows), out_shape=chunk_...  0.89 us
  transfers between devices with their start and end apart: 12, of which 7 were waited for; matrix products, arithmetic and copies ran while one was open for 0% of the time, Pallas kernels for 16%

profile of v9, /device:TPU:0, one launch (start us, length us, event | category | flops | bytes accessed | tf_op | source)
XLA Modules:
  0.0 36.8 jit_solution(17602633287370567000)
XLA Ops:
  0.0 0.5 %collective-permute-start.1 = (s32[1,12]{1,0:T(1,128)}, s32[1,12]{1,0:T(1,128)S(1)}, u32[]{:S(2)}, u32[]{:S(2)}) collective-permute-start(s32[1,12]{1,0:T(1,128)} %ids_in.1), channel_id=1, source_target_pairs={{0,2},{2,0},{4,6},{6,4},{8,10},{10,8},{12,14},{14,12},{1,3},{3,1},... | collective-permute-start | bytes 152 | tf_op jit(solution)/shard_map/ppermute | solution.py:418
  0.5 2.3 %load.1 = (bf16[64,1152]{1,0:T(8,128)(2,1)S(1)}, f32[64,1024]{1,0:T(8,128)S(1)}, bf16[4,1024,256]{2,1,0:T(8,128)(2,1)S(1)}, s32[1,12]{1,0:T(1,128)S(1)}) custom-call(bf16[64,6144]{1,0:T(8,128)(2,1)} %traces.3, bf16[4,1024,256]{2,1,0:T(8,128)(2,1)} %constant.2.clone.table_in, s32[1,12]{1,0:T(1,128)} %ids_in.1), custom_call_target="tpu_custom_call" | custom-call | tf_op jit(solution)/shard_map/load/pallas_call | solution.py:427
  2.8 4.4 %collective-permute-start = (bf16[64,1152]{1,0:T(8,128)(2,1)S(1)}, bf16[64,1152]{1,0:T(8,128)(2,1)S(1)}, u32[]{:S(2)}, u32[]{:S(2)}) collective-permute-start(bf16[64,1152]{1,0:T(8,128)(2,1)S(1)} %get-tuple-element.26), channel_id=1, source_target_pairs={{0,1},{2,3},{4,5},{6,7},{8,9},{10,11},{12,13},{14,15},{16,17},{18,... | collective-permute-start | bytes 442376 | tf_op jit(solution)/shard_map/ppermute | solution.py:457
  7.2 0.0 collective-permute-done.1.other
  7.2 0.0 copy-start
  7.2 0.0 copy-start.1
  7.2 1.6 %collective-permute-start.2 = (s32[2,12]{1,0:T(2,128)S(1)}, s32[2,12]{1,0:T(2,128)S(1)}, u32[]{:S(2)}, u32[]{:S(2)}) collective-permute-start(s32[2,12]{1,0:T(2,128)S(1)} %pair.1), channel_id=1, source_target_pairs={{0,4},{2,6},{4,0},{6,2},{8,12},{10,14},{12,8},{14,10},{1,5},{3,7},... | collective-permute-start | bytes 296 | tf_op jit(solution)/shard_map/ppermute | solution.py:418
  8.9 0.0 copy-done
  8.9 0.0 copy-done.1
  8.9 0.9 %first.1 = (f32[128,512]{1,0:T(8,128)S(1)}, f32[64,512]{1,0:T(8,128)S(1)}, f32[64,512]{1,0:T(8,128)S(1)}, bf16[64,256]{1,0:T(8,128)(2,1)S(1)}, bf16[64,96]{1,0:T(8,128)(2,1)S(1)}, /*index=5*/bf16[64,144]{1,0:T(8,128)(2,1)S(1)}) custom-call(bf16[64,6144]{1,0:T(8,128)(2,1)S(1)} %copy-done, f32[33,64]{1,0:T(8,128)S(1)} %bitcast.9, ...), custom_call_target="tpu_custom_call" | custom-call | tf_op jit(solution)/shard_map/first/pallas_call | solution.py:469
  9.8 1.1 %collective-permute-done.2 = s32[2,12]{1,0:T(2,128)S(1)} collective-permute-done((s32[2,12]{1,0:T(2,128)S(1)}, s32[2,12]{1,0:T(2,128)S(1)}, u32[]{:S(2)}, u32[]{:S(2)}) %collective-permute-start.2) | collective-permute-done | bytes 128 | tf_op jit(solution)/shard_map/ppermute | solution.py:418
  10.9 2.6 %collective-permute-start.3 = (s32[4,12]{1,0:T(4,128)S(1)}, s32[4,12]{1,0:T(4,128)S(1)}, u32[]{:S(2)}, u32[]{:S(2)}) collective-permute-start(s32[4,12]{1,0:T(4,128)S(1)} %pad_add_fusion.refs_0_), channel_id=1, source_target_pairs={{0,8},{2,10},{4,12},{6,14},{8,0},{10,2},{12,4},{14,6},{1,9},{3,11}... | collective-permute-start | bytes 584 | tf_op jit(solution)/shard_map/ppermute | solution.py:418
  13.5 0.0 copy-start.2
  13.5 0.0 copy-start.3
  13.5 1.0 %second.1 = (f32[128,512]{1,0:T(8,128)S(1)}, f32[64,512]{1,0:T(8,128)S(1)}, bf16[64,1024]{1,0:T(8,128)(2,1)S(1)}) custom-call(bf16[64,6144]{1,0:T(8,128)(2,1)S(1)} %copy-done, bf16[4,1024,256]{2,1,0:T(8,128)(2,1)S(1)} %get-tuple-element.27.table, f32[64,1024]{1,0:T(8,128)S(1)} %get-tuple-element.28.last_half, bf16[64,144]{1,0:T(8,128)(2,1)S(1)} %get-tuple-element.31.lines, ...), custom_call_target="tpu_custom_call" | custom-call | tf_op jit(solution)/shard_map/second/pallas_call | solution.py:487
  14.5 0.9 %collective-permute-done.3.refs_1_ = s32[4,12]{1,0:T(4,128)S(1)} collective-permute-done((s32[4,12]{1,0:T(4,128)S(1)}, s32[4,12]{1,0:T(4,128)S(1)}, u32[]{:S(2)}, u32[]{:S(2)}) %collective-permute-start.3) | collective-permute-done | bytes 224 | tf_op jit(solution)/shard_map/ppermute | solution.py:418
  15.4 0.0 copy-done.2
  15.4 0.0 copy-done.3
  15.4 0.3 picks.1.refs_1_
  15.8 0.0 collective-permute-done.halo
  15.8 1.4 %rest.1 = (bf16[160,1024]{1,0:T(8,128)(2,1)S(1)}, bf16[160,1024]{1,0:T(8,128)(2,1)S(1)}, bf16[96,1024]{1,0:T(8,128)(2,1)S(1)}, bf16[96,1024]{1,0:T(8,128)(2,1)S(1)}) custom-call(bf16[64,1152]{1,0:T(8,128)(2,1)S(1)} %collective-permute-done.halo, bf16[64,256]{1,0:T(8,128)(2,1)S(1)} %get-tuple-element.29.ends, f32[33,64]{1,0:T(8,128)S(1)} %bitcast.10, ...), custom_call_target="tpu_custom_call" | custom-call | tf_op jit(solution)/shard_map/rest/pallas_call | solution.py:508
  17.2 0.1 collective-permute-start.5
  17.3 1.6 %collective-permute-done.5 = bf16[160,1024]{1,0:T(8,128)(2,1)S(1)} collective-permute-done((bf16[160,1024]{1,0:T(8,128)(2,1)S(1)}, bf16[160,1024]{1,0:T(8,128)(2,1)S(1)}, u32[]{:S(2)}, u32[]{:S(2)}) %collective-permute-start.5) | collective-permute-done | bytes 327712 | tf_op jit(solution)/shard_map/ppermute | solution.py:418
  18.9 0.1 add.15
  19.1 1.6 %collective-permute-start.7 = (bf16[40,1024]{1,0:T(8,128)(2,1)S(1)}, bf16[40,1024]{1,0:T(8,128)(2,1)S(1)}, u32[]{:S(2)}, u32[]{:S(2)}) collective-permute-start(bf16[40,1024]{1,0:T(8,128)(2,1)S(1)} %get-tuple-element.45), channel_id=1, source_target_pairs={{0,4},{2,6},{4,0},{6,2},{8,12},{10,14},{12,8},{14,10},{1,5},{3,7},... | collective-permute-start | bytes 245768 | tf_op jit(solution)/shard_map/ppermute | solution.py:418
  20.7 0.4 %collective-permute-start.6 = (bf16[40,1024]{1,0:T(8,128)(2,1)S(1)}, bf16[40,1024]{1,0:T(8,128)(2,1)S(1)}, u32[]{:S(2)}, u32[]{:S(2)}) collective-permute-start(bf16[40,1024]{1,0:T(8,128)(2,1)S(1)} %get-tuple-element.43), channel_id=1, source_target_pairs={{0,4},{2,6},{4,0},{6,2},{8,12},{10,14},{12,8},{14,10},{1,5},{3,7},... | collective-permute-start | bytes 245768 | tf_op jit(solution)/shard_map/ppermute | solution.py:418
  21.1 2.9 %collective-permute-done.7 = bf16[40,1024]{1,0:T(8,128)(2,1)S(1)} collective-permute-done((bf16[40,1024]{1,0:T(8,128)(2,1)S(1)}, bf16[40,1024]{1,0:T(8,128)(2,1)S(1)}, u32[]{:S(2)}, u32[]{:S(2)}) %collective-permute-start.7) | collective-permute-done | bytes 81952 | tf_op jit(solution)/shard_map/ppermute | solution.py:418
  24.1 2.6 %collective-permute-start.10 = (bf16[24,1024]{1,0:T(8,128)(2,1)S(1)}, bf16[24,1024]{1,0:T(8,128)(2,1)S(1)}, u32[]{:S(2)}, u32[]{:S(2)}) collective-permute-start(bf16[24,1024]{1,0:T(8,128)(2,1)S(1)} %slice.39), channel_id=1, source_target_pairs={{0,8},{2,10},{4,12},{6,14},{8,0},{10,2},{12,4},{14,6},{1,9},{3,11}... | collective-permute-start | bytes 147464 | tf_op jit(solution)/shard_map/ppermute | solution.py:418
  26.7 0.0 collective-permute-start.4
  26.7 0.3 collective-permute-start.8
  27.1 0.0 collective-permute-done.6
  27.1 2.4 %collective-permute-done.10 = bf16[24,1024]{1,0:T(8,128)(2,1)S(1)} collective-permute-done((bf16[24,1024]{1,0:T(8,128)(2,1)S(1)}, bf16[24,1024]{1,0:T(8,128)(2,1)S(1)}, u32[]{:S(2)}, u32[]{:S(2)}) %collective-permute-start.10) | collective-permute-done | bytes 49184 | tf_op jit(solution)/shard_map/ppermute | solution.py:418
  29.5 0.1 collective-permute-start.11
  29.6 2.0 %collective-permute-done.8 = bf16[16,1024]{1,0:T(8,128)(2,1)S(1)} collective-permute-done((bf16[16,1024]{1,0:T(8,128)(2,1)S(1)}, bf16[16,1024]{1,0:T(8,128)(2,1)S(1)}, u32[]{:S(2)}, u32[]{:S(2)}) %collective-permute-start.8) | collective-permute-done | bytes 32800 | tf_op jit(solution)/shard_map/ppermute | solution.py:418
  31.6 2.0 %collective-permute-start.9 = (bf16[16,1024]{1,0:T(8,128)(2,1)S(1)}, bf16[16,1024]{1,0:T(8,128)(2,1)S(1)}, u32[]{:S(2)}, u32[]{:S(2)}) collective-permute-start(bf16[16,1024]{1,0:T(8,128)(2,1)S(1)} %slice_add_fusion.1.refs_1_), channel_id=1, source_target_pairs={{0,1},{1,0},{2,3},{3,2},{4,5},{5,4},{6,7},{7,6},{8,9},{9,8},{10,11... | collective-permute-start | bytes 98312 | tf_op jit(solution)/shard_map/ppermute | solution.py:418
  33.6 0.5 %correlate.4.refs_2_ = f32[12,32,1024]{2,1,0:T(8,128)S(1)} custom-call(bf16[3,32,1024]{2,1,0:T(8,128)(2,1)S(1)} %bitcast.5, bf16[24,1024]{1,0:T(8,128)(2,1)S(1)} %slice_add_fusion.refs_1_), custom_call_target="tpu_custom_call" | custom-call | tf_op jit(solution)/shard_map/correlate/pallas_call | solution.py:393
  34.1 0.3 correlate.5.refs_2_
  34.4 0.0 collective-permute-done.4
  34.4 0.0 collective-permute-done.11.refs_1_
  34.4 0.5 %correlate.6.refs_2_ = f32[12,32,1024]{2,1,0:T(8,128)S(1)} custom-call(bf16[3,32,1024]{2,1,0:T(8,128)(2,1)S(1)} %bitcast.7, bf16[24,1024]{1,0:T(8,128)(2,1)S(1)} %collective-permute-done.11.refs_1_, f32[12,32,1024]{2,1,0:T(8,128)S(1)} %correlate.5.refs_2_), custom_call_target="tpu_custom_call" | custom-call | tf_op jit(solution)/shard_map/correlate/pallas_call | solution.py:393
  34.9 0.6 %collective-permute-done.9.refs_1_ = bf16[16,1024]{1,0:T(8,128)(2,1)S(1)} collective-permute-done((bf16[16,1024]{1,0:T(8,128)(2,1)S(1)}, bf16[16,1024]{1,0:T(8,128)(2,1)S(1)}, u32[]{:S(2)}, u32[]{:S(2)}) %collective-permute-start.9) | collective-permute-done | bytes 32800 | tf_op jit(solution)/shard_map/ppermute | solution.py:418
  35.5 1.3 %correlate.7 = f32[12,32,1024]{2,1,0:T(8,128)} custom-call(bf16[3,32,1024]{2,1,0:T(8,128)(2,1)S(1)} %bitcast.8, bf16[16,1024]{1,0:T(8,128)(2,1)S(1)} %collective-permute-done.9.refs_1_, f32[12,32,1024]{2,1,0:T(8,128)S(1)} %correlate.6.refs_2_), custom_call_target="tpu_custom_call" | custom-call | tf_op jit(solution)/shard_map/correlate/pallas_call | solution.py:393
  (9 shorter events, 0.1 us)
Async XLA Ops:
  0.0 7.2 %collective-permute-start.1 = (s32[1,12]{1,0:T(1,128)}, s32[1,12]{1,0:T(1,128)S(1)}, u32[]{:S(2)}, u32[]{:S(2)}) collective-permute-start(s32[1,12]{1,0:T(1,128)} %ids_in.1), channel_id=1, source_target_pairs={{0,2},{2,0},{4,6},{6,4},{8,10},{10,8},{12,14},{14,12},{1,3},{3,1},... | collective-permute-start | bytes 152 | tf_op jit(solution)/shard_map/ppermute | solution.py:418
  2.8 13.0 %collective-permute-start = (bf16[64,1152]{1,0:T(8,128)(2,1)S(1)}, bf16[64,1152]{1,0:T(8,128)(2,1)S(1)}, u32[]{:S(2)}, u32[]{:S(2)}) collective-permute-start(bf16[64,1152]{1,0:T(8,128)(2,1)S(1)} %get-tuple-element.26), channel_id=1, source_target_pairs={{0,1},{2,3},{4,5},{6,7},{8,9},{10,11},{12,13},{14,15},{16,17},{18,... | collective-permute-start | bytes 442376 | tf_op jit(solution)/shard_map/ppermute | solution.py:457
  7.2 1.7 %copy-start = (bf16[64,6144]{1,0:T(8,128)(2,1)S(1)}, bf16[64,6144]{1,0:T(8,128)(2,1)}, u32[]{:S(2)}) copy-start(bf16[64,6144]{1,0:T(8,128)(2,1)} %traces.3) | copy-start | bytes 2359300
  7.2 1.7 %copy-start.1 = (f32[64,33]{0,1:T(8,128)S(1)}, f32[64,33]{0,1:T(8,128)}, u32[]{:S(2)}) copy-start(f32[64,33]{0,1:T(8,128)} %param.7) | copy-start | bytes 25348
  7.2 3.6 %collective-permute-start.2 = (s32[2,12]{1,0:T(2,128)S(1)}, s32[2,12]{1,0:T(2,128)S(1)}, u32[]{:S(2)}, u32[]{:S(2)}) collective-permute-start(s32[2,12]{1,0:T(2,128)S(1)} %pair.1), channel_id=1, source_target_pairs={{0,4},{2,6},{4,0},{6,2},{8,12},{10,14},{12,8},{14,10},{1,5},{3,7},... | collective-permute-start | bytes 296 | tf_op jit(solution)/shard_map/ppermute | solution.py:418
  10.9 4.5 %collective-permute-start.3 = (s32[4,12]{1,0:T(4,128)S(1)}, s32[4,12]{1,0:T(4,128)S(1)}, u32[]{:S(2)}, u32[]{:S(2)}) collective-permute-start(s32[4,12]{1,0:T(4,128)S(1)} %pad_add_fusion.refs_0_), channel_id=1, source_target_pairs={{0,8},{2,10},{4,12},{6,14},{8,0},{10,2},{12,4},{14,6},{1,9},{3,11}... | collective-permute-start | bytes 584 | tf_op jit(solution)/shard_map/ppermute | solution.py:418
  13.5 1.9 %copy-start.2 = (s32[8,36]{1,0:T(8,128)S(1)}, s32[8,36]{1,0:T(8,128)}, u32[]{:S(2)}) copy-start(s32[8,36]{1,0:T(8,128)} %slots.1) | copy-start | bytes 3460
  13.5 1.9 %copy-start.3 = (s32[8]{0:T(128)S(1)}, s32[8]{0:T(128)}, u32[]{:S(2)}) copy-start(s32[8]{0:T(128)} %param.8) | copy-start | bytes 100
  17.2 1.7 %collective-permute-start.5 = (bf16[160,1024]{1,0:T(8,128)(2,1)S(1)}, bf16[160,1024]{1,0:T(8,128)(2,1)S(1)}, u32[]{:S(2)}, u32[]{:S(2)}) collective-permute-start(bf16[160,1024]{1,0:T(8,128)(2,1)S(1)} %get-tuple-element.41), channel_id=1, source_target_pairs={{0,2},{2,0},{4,6},{6,4},{8,10},{10,8},{12,14},{14,12},{1,3},{3,1},... | collective-permute-start | bytes 983048 | tf_op jit(solution)/shard_map/ppermute | solution.py:418
  19.1 5.0 %collective-permute-start.7 = (bf16[40,1024]{1,0:T(8,128)(2,1)S(1)}, bf16[40,1024]{1,0:T(8,128)(2,1)S(1)}, u32[]{:S(2)}, u32[]{:S(2)}) collective-permute-start(bf16[40,1024]{1,0:T(8,128)(2,1)S(1)} %get-tuple-element.45), channel_id=1, source_target_pairs={{0,4},{2,6},{4,0},{6,2},{8,12},{10,14},{12,8},{14,10},{1,5},{3,7},... | collective-permute-start | bytes 245768 | tf_op jit(solution)/shard_map/ppermute | solution.py:418
  20.7 6.4 %collective-permute-start.6 = (bf16[40,1024]{1,0:T(8,128)(2,1)S(1)}, bf16[40,1024]{1,0:T(8,128)(2,1)S(1)}, u32[]{:S(2)}, u32[]{:S(2)}) collective-permute-start(bf16[40,1024]{1,0:T(8,128)(2,1)S(1)} %get-tuple-element.43), channel_id=1, source_target_pairs={{0,4},{2,6},{4,0},{6,2},{8,12},{10,14},{12,8},{14,10},{1,5},{3,7},... | collective-permute-start | bytes 245768 | tf_op jit(solution)/shard_map/ppermute | solution.py:418
  24.1 5.4 %collective-permute-start.10 = (bf16[24,1024]{1,0:T(8,128)(2,1)S(1)}, bf16[24,1024]{1,0:T(8,128)(2,1)S(1)}, u32[]{:S(2)}, u32[]{:S(2)}) collective-permute-start(bf16[24,1024]{1,0:T(8,128)(2,1)S(1)} %slice.39), channel_id=1, source_target_pairs={{0,8},{2,10},{4,12},{6,14},{8,0},{10,2},{12,4},{14,6},{1,9},{3,11}... | collective-permute-start | bytes 147464 | tf_op jit(solution)/shard_map/ppermute | solution.py:418
  26.7 7.6 %collective-permute-start.4 = (bf16[96,1024]{1,0:T(8,128)(2,1)S(1)}, bf16[96,1024]{1,0:T(8,128)(2,1)S(1)}, u32[]{:S(2)}, u32[]{:S(2)}) collective-permute-start(bf16[96,1024]{1,0:T(8,128)(2,1)S(1)} %get-tuple-element.39), channel_id=1, source_target_pairs={{0,1},{1,0},{2,3},{3,2},{4,5},{5,4},{6,7},{7,6},{8,9},{9,8},{10,11... | collective-permute-start | bytes 589832 | tf_op jit(solution)/shard_map/ppermute | solution.py:418
  26.7 4.8 %collective-permute-start.8 = (bf16[16,1024]{1,0:T(8,128)(2,1)S(1)}, bf16[16,1024]{1,0:T(8,128)(2,1)S(1)}, u32[]{:S(2)}, u32[]{:S(2)}) collective-permute-start(bf16[16,1024]{1,0:T(8,128)(2,1)S(1)} %slice.37), channel_id=1, source_target_pairs={{0,8},{2,10},{4,12},{6,14},{8,0},{10,2},{12,4},{14,6},{1,9},{3,11}... | collective-permute-start | bytes 98312 | tf_op jit(solution)/shard_map/ppermute | solution.py:418
  29.5 4.9 %collective-permute-start.11 = (bf16[24,1024]{1,0:T(8,128)(2,1)S(1)}, bf16[24,1024]{1,0:T(8,128)(2,1)S(1)}, u32[]{:S(2)}, u32[]{:S(2)}) collective-permute-start(bf16[24,1024]{1,0:T(8,128)(2,1)S(1)} %slice_add_fusion.refs_1_), channel_id=1, source_target_pairs={{0,1},{1,0},{2,3},{3,2},{4,5},{5,4},{6,7},{7,6},{8,9},{9,8},{10,11... | collective-permute-start | bytes 147464 | tf_op jit(solution)/shard_map/ppermute | solution.py:418
  31.6 3.9 %collective-permute-start.9 = (bf16[16,1024]{1,0:T(8,128)(2,1)S(1)}, bf16[16,1024]{1,0:T(8,128)(2,1)S(1)}, u32[]{:S(2)}, u32[]{:S(2)}) collective-permute-start(bf16[16,1024]{1,0:T(8,128)(2,1)S(1)} %slice_add_fusion.1.refs_1_), channel_id=1, source_target_pairs={{0,1},{1,0},{2,3},{3,2},{4,5},{5,4},{6,7},{7,6},{8,9},{9,8},{10,11... | collective-permute-start | bytes 98312 | tf_op jit(solution)/shard_map/ppermute | solution.py:418

commit v10 on v9

--- a/solution.py
+++ b/solution.py
@@ -22,9 +22,9 @@
 HINT = 10**10
 
 
-def piece_table():
+def piece_table(size):
     bins = F0 + np.arange(NF)
-    angle = (bins * np.arange(PIECE)[:, None] % NFFT) * (2.0 * np.pi / NFFT)
+    angle = (bins * np.arange(size)[:, None] % NFFT) * (2.0 * np.pi / NFFT)
     exact = np.concatenate([np.cos(angle), -np.sin(angle)], axis=1)
     high = exact.astype(ml_dtypes.bfloat16)
     low = (exact - high.astype(np.float64)).astype(ml_dtypes.bfloat16)
@@ -75,10 +75,25 @@
             ai + self.imag * jnp.where(self.odd, br, bi),
         )
 
+    def eighth(self, ar, ai, br, bi):
+        return ar + (br * self.cos - bi * self.sin), ai + (br * self.sin + bi * self.cos)
+
     def half(self, re, im):
-        ar, ai = self.quarter(re[0], im[0], re[2], im[2])
-        br, bi = self.quarter(re[1], im[1], re[3], im[3])
-        return ar + (br * self.cos - bi * self.sin), ai + (br * self.sin + bi * self.cos)
+        a = self.quarter(re[0], im[0], re[2], im[2])
+        b = self.quarter(re[1], im[1], re[3], im[3])
+        return self.eighth(*a, *b)
+
+    def half_of_eight(self, re, im):
+        quarters = [self.quarter(re[e], im[e], re[e + 4], im[e + 4]) for e in range(4)]
+        ar, ai = self.eighth(*quarters[0], *quarters[2])
+        br, bi = self.eighth(*quarters[1], *quarters[3])
+        lane = lax.broadcasted_iota(jnp.int32, (1, CHUNK), 1) % 16
+        cos, sin = jnp.zeros((1, CHUNK), F32), jnp.zeros((1, CHUNK), F32)
+        for k in range(16):
+            angle = 2.0 * np.pi * ((F0 + k) % 16) / 16
+            cos = jnp.where(lane == k, np.float32(np.cos(angle)), cos)
+            sin = jnp.where(lane == k, np.float32(-np.sin(angle)), sin)
+        return ar + (br * cos - bi * sin), ai + (br * sin + bi * cos)
 
 
 def half_spectra(x, table, channels, halves, turns, f):
@@ -132,7 +147,7 @@
     lax.fori_loop(0, count // ROWS, step, 0, unroll=4)
 
 
-def load_kernel(end, traces_in, table_in, ids_in, message, last_half, table, ids, traces, sems):
+def load_kernel(end, traces_in, table_in, ids_in, message, last_half, ids, traces, table, sems):
     channels, samples = traces.shape
     begin = traces_in.shape[1] - samples
     copies = [pltpu.make_async_copy(traces_in.at[:, begin:], traces, sems.at[0])]
@@ -147,15 +162,20 @@
     final = pltpu.roll(traces[:, samples - 128 :].astype(F32), 128 - end, 1)
     tile = jnp.where(lane < 128 - end, final, traces[:, :128].astype(F32))
     message[:, 2 * NF :] = tile.astype(BF16)
-    pieces = [samples - HALF + q * PIECE for q in range(HALF // PIECE)]
-    x = jnp.concatenate([traces[:, p : p + PIECE] for p in pieces], axis=0)
+    size = table.shape[1] // 2
+    starts = range(samples - HALF, samples, size)
+    x = jnp.concatenate([traces[:, p : p + size] for p in starts], axis=0)
+    both = jnp.concatenate([x, x], axis=1)
+    rows = [slice(e * channels, (e + 1) * channels) for e in range(HALF // size)]
     turns = Turns()
     for i, f in enumerate(range(0, NF, CHUNK)):
         re = slice(f, f + CHUNK)
         im = slice(NF + f, NF + f + CHUNK)
         copies[1 + 2 * i].wait()
         copies[2 + 2 * i].wait()
-        xr, xi = half_spectra(x, table, channels, 1, turns, f)[0]
+        dr = dot(both, table[2 * i])
+        di = dot(both, table[2 * i + 1])
+        xr, xi = turns.half_of_eight([dr[r] for r in rows], [di[r] for r in rows])
         last_half[:, re] = xr
         last_half[:, im] = xi
         message[:, re] = xr.astype(BF16)
@@ -423,25 +443,27 @@
     bits = [1 << b for b in range(chips.bit_length() - 1)]
 
     other = across(block_sources, "chan", 1)
-    inputs = (traces, jnp.asarray(piece_table()), block_sources)
-    message, last_half, table, ids = pl.pallas_call(
+    inputs = (traces, jnp.asarray(piece_table(PIECE // 2)), block_sources)
+    message, last_half, ids = pl.pallas_call(
         functools.partial(load_kernel, tap_count - 1),
         out_shape=[
             jax.ShapeDtypeStruct((channels, 2 * NF + 128), BF16),
             jax.ShapeDtypeStruct((channels, 2 * NF), F32),
-        ]
-        + [jax.ShapeDtypeStruct(a.shape, a.dtype) for a in inputs[1:]],
+            jax.ShapeDtypeStruct(block_sources.shape, jnp.int32),
+        ],
         in_specs=[hbm] * 3,
-        out_specs=[vmem] * 4,
+        out_specs=[vmem] * 3,
         scratch_shapes=[
             pltpu.VMEM((channels, HALF + 128), BF16),
+            pltpu.VMEM(inputs[1].shape, BF16),
             pltpu.SemaphoreType.DMA((2 + 2 * NF // CHUNK,)),
         ],
         compiler_params=params,
         name="load",
     )(*(pltpu.with_memory_space_constraint(a, pltpu.HBM) for a in inputs))
-    traces, taps = (
-        pltpu.with_memory_space_constraint(a, pltpu.VMEM) for a in (traces, filter_taps.T)
+    traces, taps, table = (
+        pltpu.with_memory_space_constraint(a, pltpu.VMEM)
+        for a in (traces, filter_taps.T, jnp.asarray(piece_table(PIECE)))
     )
     wanted = [
         pl.pallas_call(

time: 36.9 us -> 36.9 us (level)
  no operation moved by 1% of the time
where the time goes in v10:
time: 36.9 us; the launch traced here: 36.7 us
  starting transfers between devices  16.4 us (44%)
  waiting for transfers between devices  11.3 us (31%)
  Pallas kernels  8.44 us (23%)
    ppermute x11, starting transfers between devices, across(): return lax.ppermute(x, axis, [(i, i ^ distance) for i in range(size)])  12 us
    ppermute x11, waiting for transfers between devices, across(): return lax.ppermute(x, axis, [(i, i ^ distance) for i in range(size)])  11.3 us
    ppermute x1, starting transfers between devices, shards(): halo = lax.ppermute(message, 'tm', [(i - 1, i) for i in range(1, times)])  4.39 us
    pallas_call x4, Pallas kernels, correlate(): pl.pallas_call(functools.partial(correlate_kernel, spans, pairs, factor,...  2.58 us
    pallas_call x1, Pallas kernels, shards(): pl.pallas_call(functools.partial(load_kernel, tap_count - 1), out_shape=[...  2.16 us
    pallas_call x1, Pallas kernels, shards(): pl.pallas_call(functools.partial(rest_kernel, windows, times), out_shape=...  1.43 us
    pallas_call x1, Pallas kernels, shards(): pl.pallas_call(functools.partial(second_kernel, windows), out_shape=chunk...  1.03 us
    pallas_call x1, Pallas kernels, shards(): pl.pallas_call(functools.partial(first_kernel, windows), out_shape=chunk_...  0.89 us
  transfers between devices with their start and end apart: 12, of which 7 were waited for; matrix products, arithmetic and copies ran while one was open for 0% of the time, Pallas kernels for 16%

profile of v10, /device:TPU:0, one launch (start us, length us, event | category | flops | bytes accessed | tf_op | source)
XLA Modules:
  0.0 36.7 jit_solution(2194426019834786866)
XLA Ops:
  0.0 0.5 %collective-permute-start.1 = (s32[1,12]{1,0:T(1,128)}, s32[1,12]{1,0:T(1,128)S(1)}, u32[]{:S(2)}, u32[]{:S(2)}) collective-permute-start(s32[1,12]{1,0:T(1,128)} %ids_in.1), channel_id=1, source_target_pairs={{0,2},{2,0},{4,6},{6,4},{8,10},{10,8},{12,14},{14,12},{1,3},{3,1},... | collective-permute-start | bytes 152 | tf_op jit(solution)/shard_map/ppermute | solution.py:438
  0.5 2.2 %load.1 = (bf16[64,1152]{1,0:T(8,128)(2,1)S(1)}, f32[64,1024]{1,0:T(8,128)S(1)}, s32[1,12]{1,0:T(1,128)S(1)}) custom-call(bf16[64,6144]{1,0:T(8,128)(2,1)} %traces.3, bf16[4,512,256]{2,1,0:T(8,128)(2,1)} %constant.4.clone.table_in, s32[1,12]{1,0:T(1,128)} %ids_in.1), custom_call_target="tpu_custom_call" | custom-call | tf_op jit(solution)/shard_map/load/pallas_call | solution.py:447
  2.7 4.4 %collective-permute-start = (bf16[64,1152]{1,0:T(8,128)(2,1)S(1)}, bf16[64,1152]{1,0:T(8,128)(2,1)S(1)}, u32[]{:S(2)}, u32[]{:S(2)}) collective-permute-start(bf16[64,1152]{1,0:T(8,128)(2,1)S(1)} %get-tuple-element.25), channel_id=1, source_target_pairs={{0,1},{2,3},{4,5},{6,7},{8,9},{10,11},{12,13},{14,15},{16,17},{18,... | collective-permute-start | bytes 442376 | tf_op jit(solution)/shard_map/ppermute | solution.py:479
  7.1 0.0 collective-permute-done.1.other
  7.1 0.0 copy-start
  7.1 0.0 copy-start.1
  7.1 0.0 copy-start.2
  7.1 1.6 %collective-permute-start.2 = (s32[2,12]{1,0:T(2,128)S(1)}, s32[2,12]{1,0:T(2,128)S(1)}, u32[]{:S(2)}, u32[]{:S(2)}) collective-permute-start(s32[2,12]{1,0:T(2,128)S(1)} %pair.1), channel_id=1, source_target_pairs={{0,4},{2,6},{4,0},{6,2},{8,12},{10,14},{12,8},{14,10},{1,5},{3,7},... | collective-permute-start | bytes 296 | tf_op jit(solution)/shard_map/ppermute | solution.py:438
  8.8 0.0 copy-done
  8.8 0.1 copy-done.1
  8.8 0.0 copy-done.2
  8.8 0.9 %first.1 = (f32[128,512]{1,0:T(8,128)S(1)}, f32[64,512]{1,0:T(8,128)S(1)}, f32[64,512]{1,0:T(8,128)S(1)}, bf16[64,256]{1,0:T(8,128)(2,1)S(1)}, bf16[64,96]{1,0:T(8,128)(2,1)S(1)}, /*index=5*/bf16[64,144]{1,0:T(8,128)(2,1)S(1)}) custom-call(bf16[64,6144]{1,0:T(8,128)(2,1)S(1)} %copy-done.1, f32[33,64]{1,0:T(8,128)S(1)} %bitcast.9, ...), custom_call_target="tpu_custom_call" | custom-call | tf_op jit(solution)/shard_map/first/pallas_call | solution.py:491
  9.7 1.0 %collective-permute-done.2 = s32[2,12]{1,0:T(2,128)S(1)} collective-permute-done((s32[2,12]{1,0:T(2,128)S(1)}, s32[2,12]{1,0:T(2,128)S(1)}, u32[]{:S(2)}, u32[]{:S(2)}) %collective-permute-start.2) | collective-permute-done | bytes 128 | tf_op jit(solution)/shard_map/ppermute | solution.py:438
  10.8 2.6 %collective-permute-start.3 = (s32[4,12]{1,0:T(4,128)S(1)}, s32[4,12]{1,0:T(4,128)S(1)}, u32[]{:S(2)}, u32[]{:S(2)}) collective-permute-start(s32[4,12]{1,0:T(4,128)S(1)} %pad_add_fusion.refs_0_), channel_id=1, source_target_pairs={{0,8},{2,10},{4,12},{6,14},{8,0},{10,2},{12,4},{14,6},{1,9},{3,11}... | collective-permute-start | bytes 584 | tf_op jit(solution)/shard_map/ppermute | solution.py:438
  13.4 0.0 copy-start.3
  13.4 0.0 copy-start.4
  13.4 1.0 %second.1 = (f32[128,512]{1,0:T(8,128)S(1)}, f32[64,512]{1,0:T(8,128)S(1)}, bf16[64,1024]{1,0:T(8,128)(2,1)S(1)}) custom-call(bf16[64,6144]{1,0:T(8,128)(2,1)S(1)} %copy-done.1, bf16[4,1024,256]{2,1,0:T(8,128)(2,1)S(1)} %copy-done, f32[64,1024]{1,0:T(8,128)S(1)} %get-tuple-element.26.last_half, bf16[64,144]{1,0:T(8,128)(2,1)S(1)} %get-tuple-element.29.lines, ...), custom_call_target="tpu_custom_call" | custom-call | tf_op jit(solution)/shard_map/second/pallas_call | solution.py:509
  14.5 0.9 %collective-permute-done.3.refs_1_ = s32[4,12]{1,0:T(4,128)S(1)} collective-permute-done((s32[4,12]{1,0:T(4,128)S(1)}, s32[4,12]{1,0:T(4,128)S(1)}, u32[]{:S(2)}, u32[]{:S(2)}) %collective-permute-start.3) | collective-permute-done | bytes 224 | tf_op jit(solution)/shard_map/ppermute | solution.py:438
  15.3 0.0 copy-done.3
  15.3 0.0 copy-done.4
  15.3 0.3 picks.1.refs_1_
  15.7 0.0 collective-permute-done.halo
  15.7 1.4 %rest.1 = (bf16[160,1024]{1,0:T(8,128)(2,1)S(1)}, bf16[160,1024]{1,0:T(8,128)(2,1)S(1)}, bf16[96,1024]{1,0:T(8,128)(2,1)S(1)}, bf16[96,1024]{1,0:T(8,128)(2,1)S(1)}) custom-call(bf16[64,1152]{1,0:T(8,128)(2,1)S(1)} %collective-permute-done.halo, bf16[64,256]{1,0:T(8,128)(2,1)S(1)} %get-tuple-element.27.ends, f32[33,64]{1,0:T(8,128)S(1)} %bitcast.10, ...), custom_call_target="tpu_custom_call" | custom-call | tf_op jit(solution)/shard_map/rest/pallas_call | solution.py:530
  17.1 0.1 collective-permute-start.5
  17.2 1.6 %collective-permute-done.5 = bf16[160,1024]{1,0:T(8,128)(2,1)S(1)} collective-permute-done((bf16[160,1024]{1,0:T(8,128)(2,1)S(1)}, bf16[160,1024]{1,0:T(8,128)(2,1)S(1)}, u32[]{:S(2)}, u32[]{:S(2)}) %collective-permute-start.5) | collective-permute-done | bytes 327712 | tf_op jit(solution)/shard_map/ppermute | solution.py:438
  18.8 0.1 add.15
  18.9 1.6 %collective-permute-start.7 = (bf16[40,1024]{1,0:T(8,128)(2,1)S(1)}, bf16[40,1024]{1,0:T(8,128)(2,1)S(1)}, u32[]{:S(2)}, u32[]{:S(2)}) collective-permute-start(bf16[40,1024]{1,0:T(8,128)(2,1)S(1)} %get-tuple-element.43), channel_id=1, source_target_pairs={{0,4},{2,6},{4,0},{6,2},{8,12},{10,14},{12,8},{14,10},{1,5},{3,7},... | collective-permute-start | bytes 245768 | tf_op jit(solution)/shard_map/ppermute | solution.py:438
  20.6 0.5 %collective-permute-start.6 = (bf16[40,1024]{1,0:T(8,128)(2,1)S(1)}, bf16[40,1024]{1,0:T(8,128)(2,1)S(1)}, u32[]{:S(2)}, u32[]{:S(2)}) collective-permute-start(bf16[40,1024]{1,0:T(8,128)(2,1)S(1)} %get-tuple-element.41), channel_id=1, source_target_pairs={{0,4},{2,6},{4,0},{6,2},{8,12},{10,14},{12,8},{14,10},{1,5},{3,7},... | collective-permute-start | bytes 245768 | tf_op jit(solution)/shard_map/ppermute | solution.py:438
  21.0 2.9 %collective-permute-done.7 = bf16[40,1024]{1,0:T(8,128)(2,1)S(1)} collective-permute-done((bf16[40,1024]{1,0:T(8,128)(2,1)S(1)}, bf16[40,1024]{1,0:T(8,128)(2,1)S(1)}, u32[]{:S(2)}, u32[]{:S(2)}) %collective-permute-start.7) | collective-permute-done | bytes 81952 | tf_op jit(solution)/shard_map/ppermute | solution.py:438
  24.0 2.7 %collective-permute-start.10 = (bf16[24,1024]{1,0:T(8,128)(2,1)S(1)}, bf16[24,1024]{1,0:T(8,128)(2,1)S(1)}, u32[]{:S(2)}, u32[]{:S(2)}) collective-permute-start(bf16[24,1024]{1,0:T(8,128)(2,1)S(1)} %slice.39), channel_id=1, source_target_pairs={{0,8},{2,10},{4,12},{6,14},{8,0},{10,2},{12,4},{14,6},{1,9},{3,11}... | collective-permute-start | bytes 147464 | tf_op jit(solution)/shard_map/ppermute | solution.py:438
  26.6 0.0 collective-permute-start.4
  26.7 0.3 collective-permute-start.8
  27.0 0.0 collective-permute-done.6
  27.0 2.4 %collective-permute-done.10 = bf16[24,1024]{1,0:T(8,128)(2,1)S(1)} collective-permute-done((bf16[24,1024]{1,0:T(8,128)(2,1)S(1)}, bf16[24,1024]{1,0:T(8,128)(2,1)S(1)}, u32[]{:S(2)}, u32[]{:S(2)}) %collective-permute-start.10) | collective-permute-done | bytes 49184 | tf_op jit(solution)/shard_map/ppermute | solution.py:438
  29.4 0.1 collective-permute-start.11
  29.5 2.0 %collective-permute-done.8 = bf16[16,1024]{1,0:T(8,128)(2,1)S(1)} collective-permute-done((bf16[16,1024]{1,0:T(8,128)(2,1)S(1)}, bf16[16,1024]{1,0:T(8,128)(2,1)S(1)}, u32[]{:S(2)}, u32[]{:S(2)}) %collective-permute-start.8) | collective-permute-done | bytes 32800 | tf_op jit(solution)/shard_map/ppermute | solution.py:438
  31.5 2.0 %collective-permute-start.9 = (bf16[16,1024]{1,0:T(8,128)(2,1)S(1)}, bf16[16,1024]{1,0:T(8,128)(2,1)S(1)}, u32[]{:S(2)}, u32[]{:S(2)}) collective-permute-start(bf16[16,1024]{1,0:T(8,128)(2,1)S(1)} %slice_add_fusion.1.refs_1_), channel_id=1, source_target_pairs={{0,1},{1,0},{2,3},{3,2},{4,5},{5,4},{6,7},{7,6},{8,9},{9,8},{10,11... | collective-permute-start | bytes 98312 | tf_op jit(solution)/shard_map/ppermute | solution.py:438
  33.5 0.5 %correlate.4.refs_2_ = f32[12,32,1024]{2,1,0:T(8,128)S(1)} custom-call(bf16[3,32,1024]{2,1,0:T(8,128)(2,1)S(1)} %bitcast.5, bf16[24,1024]{1,0:T(8,128)(2,1)S(1)} %slice_add_fusion.refs_1_), custom_call_target="tpu_custom_call" | custom-call | tf_op jit(solution)/shard_map/correlate/pallas_call | solution.py:413
  34.0 0.3 correlate.5.refs_2_
  34.3 0.0 collective-permute-done.4
  34.3 0.0 collective-permute-done.11.refs_1_
  34.3 0.5 %correlate.6.refs_2_ = f32[12,32,1024]{2,1,0:T(8,128)S(1)} custom-call(bf16[3,32,1024]{2,1,0:T(8,128)(2,1)S(1)} %bitcast.7, bf16[24,1024]{1,0:T(8,128)(2,1)S(1)} %collective-permute-done.11.refs_1_, f32[12,32,1024]{2,1,0:T(8,128)S(1)} %correlate.5.refs_2_), custom_call_target="tpu_custom_call" | custom-call | tf_op jit(solution)/shard_map/correlate/pallas_call | solution.py:413
  34.8 0.6 %collective-permute-done.9.refs_1_ = bf16[16,1024]{1,0:T(8,128)(2,1)S(1)} collective-permute-done((bf16[16,1024]{1,0:T(8,128)(2,1)S(1)}, bf16[16,1024]{1,0:T(8,128)(2,1)S(1)}, u32[]{:S(2)}, u32[]{:S(2)}) %collective-permute-start.9) | collective-permute-done | bytes 32800 | tf_op jit(solution)/shard_map/ppermute | solution.py:438
  35.4 1.3 %correlate.7 = f32[12,32,1024]{2,1,0:T(8,128)} custom-call(bf16[3,32,1024]{2,1,0:T(8,128)(2,1)S(1)} %bitcast.8, bf16[16,1024]{1,0:T(8,128)(2,1)S(1)} %collective-permute-done.9.refs_1_, f32[12,32,1024]{2,1,0:T(8,128)S(1)} %correlate.6.refs_2_), custom_call_target="tpu_custom_call" | custom-call | tf_op jit(solution)/shard_map/correlate/pallas_call | solution.py:413
  (9 shorter events, 0.1 us)
Async XLA Ops:
  0.0 7.1 %collective-permute-start.1 = (s32[1,12]{1,0:T(1,128)}, s32[1,12]{1,0:T(1,128)S(1)}, u32[]{:S(2)}, u32[]{:S(2)}) collective-permute-start(s32[1,12]{1,0:T(1,128)} %ids_in.1), channel_id=1, source_target_pairs={{0,2},{2,0},{4,6},{6,4},{8,10},{10,8},{12,14},{14,12},{1,3},{3,1},... | collective-permute-start | bytes 152 | tf_op jit(solution)/shard_map/ppermute | solution.py:438
  2.7 13.0 %collective-permute-start = (bf16[64,1152]{1,0:T(8,128)(2,1)S(1)}, bf16[64,1152]{1,0:T(8,128)(2,1)S(1)}, u32[]{:S(2)}, u32[]{:S(2)}) collective-permute-start(bf16[64,1152]{1,0:T(8,128)(2,1)S(1)} %get-tuple-element.25), channel_id=1, source_target_pairs={{0,1},{2,3},{4,5},{6,7},{8,9},{10,11},{12,13},{14,15},{16,17},{18,... | collective-permute-start | bytes 442376 | tf_op jit(solution)/shard_map/ppermute | solution.py:479
  7.1 1.7 %copy-start = (bf16[4,1024,256]{2,1,0:T(8,128)(2,1)S(1)}, bf16[4,1024,256]{2,1,0:T(8,128)(2,1)}, u32[]{:S(2)}) copy-start(bf16[4,1024,256]{2,1,0:T(8,128)(2,1)} %constant.5.clone.table) | copy-start | bytes 6291460
  7.1 1.8 %copy-start.1 = (bf16[64,6144]{1,0:T(8,128)(2,1)S(1)}, bf16[64,6144]{1,0:T(8,128)(2,1)}, u32[]{:S(2)}) copy-start(bf16[64,6144]{1,0:T(8,128)(2,1)} %traces.3) | copy-start | bytes 2359300
  7.1 1.7 %copy-start.2 = (f32[64,33]{0,1:T(8,128)S(1)}, f32[64,33]{0,1:T(8,128)}, u32[]{:S(2)}) copy-start(f32[64,33]{0,1:T(8,128)} %param.8) | copy-start | bytes 25348
  7.1 3.6 %collective-permute-start.2 = (s32[2,12]{1,0:T(2,128)S(1)}, s32[2,12]{1,0:T(2,128)S(1)}, u32[]{:S(2)}, u32[]{:S(2)}) collective-permute-start(s32[2,12]{1,0:T(2,128)S(1)} %pair.1), channel_id=1, source_target_pairs={{0,4},{2,6},{4,0},{6,2},{8,12},{10,14},{12,8},{14,10},{1,5},{3,7},... | collective-permute-start | bytes 296 | tf_op jit(solution)/shard_map/ppermute | solution.py:438
  10.8 4.5 %collective-permute-start.3 = (s32[4,12]{1,0:T(4,128)S(1)}, s32[4,12]{1,0:T(4,128)S(1)}, u32[]{:S(2)}, u32[]{:S(2)}) collective-permute-start(s32[4,12]{1,0:T(4,128)S(1)} %pad_add_fusion.refs_0_), channel_id=1, source_target_pairs={{0,8},{2,10},{4,12},{6,14},{8,0},{10,2},{12,4},{14,6},{1,9},{3,11}... | collective-permute-start | bytes 584 | tf_op jit(solution)/shard_map/ppermute | solution.py:438
  13.4 1.9 %copy-start.3 = (s32[8,36]{1,0:T(8,128)S(1)}, s32[8,36]{1,0:T(8,128)}, u32[]{:S(2)}) copy-start(s32[8,36]{1,0:T(8,128)} %slots.1) | copy-start | bytes 3460
  13.4 1.9 %copy-start.4 = (s32[8]{0:T(128)S(1)}, s32[8]{0:T(128)}, u32[]{:S(2)}) copy-start(s32[8]{0:T(128)} %param.9) | copy-start | bytes 100
  17.1 1.7 %collective-permute-start.5 = (bf16[160,1024]{1,0:T(8,128)(2,1)S(1)}, bf16[160,1024]{1,0:T(8,128)(2,1)S(1)}, u32[]{:S(2)}, u32[]{:S(2)}) collective-permute-start(bf16[160,1024]{1,0:T(8,128)(2,1)S(1)} %get-tuple-element.39), channel_id=1, source_target_pairs={{0,2},{2,0},{4,6},{6,4},{8,10},{10,8},{12,14},{14,12},{1,3},{3,1},... | collective-permute-start | bytes 983048 | tf_op jit(solution)/shard_map/ppermute | solution.py:438
  18.9 5.0 %collective-permute-start.7 = (bf16[40,1024]{1,0:T(8,128)(2,1)S(1)}, bf16[40,1024]{1,0:T(8,128)(2,1)S(1)}, u32[]{:S(2)}, u32[]{:S(2)}) collective-permute-start(bf16[40,1024]{1,0:T(8,128)(2,1)S(1)} %get-tuple-element.43), channel_id=1, source_target_pairs={{0,4},{2,6},{4,0},{6,2},{8,12},{10,14},{12,8},{14,10},{1,5},{3,7},... | collective-permute-start | bytes 245768 | tf_op jit(solution)/shard_map/ppermute | solution.py:438
  20.6 6.4 %collective-permute-start.6 = (bf16[40,1024]{1,0:T(8,128)(2,1)S(1)}, bf16[40,1024]{1,0:T(8,128)(2,1)S(1)}, u32[]{:S(2)}, u32[]{:S(2)}) collective-permute-start(bf16[40,1024]{1,0:T(8,128)(2,1)S(1)} %get-tuple-element.41), channel_id=1, source_target_pairs={{0,4},{2,6},{4,0},{6,2},{8,12},{10,14},{12,8},{14,10},{1,5},{3,7},... | collective-permute-start | bytes 245768 | tf_op jit(solution)/shard_map/ppermute | solution.py:438
  24.0 5.4 %collective-permute-start.10 = (bf16[24,1024]{1,0:T(8,128)(2,1)S(1)}, bf16[24,1024]{1,0:T(8,128)(2,1)S(1)}, u32[]{:S(2)}, u32[]{:S(2)}) collective-permute-start(bf16[24,1024]{1,0:T(8,128)(2,1)S(1)} %slice.39), channel_id=1, source_target_pairs={{0,8},{2,10},{4,12},{6,14},{8,0},{10,2},{12,4},{14,6},{1,9},{3,11}... | collective-permute-start | bytes 147464 | tf_op jit(solution)/shard_map/ppermute | solution.py:438
  26.6 7.6 %collective-permute-start.4 = (bf16[96,1024]{1,0:T(8,128)(2,1)S(1)}, bf16[96,1024]{1,0:T(8,128)(2,1)S(1)}, u32[]{:S(2)}, u32[]{:S(2)}) collective-permute-start(bf16[96,1024]{1,0:T(8,128)(2,1)S(1)} %get-tuple-element.37), channel_id=1, source_target_pairs={{0,1},{1,0},{2,3},{3,2},{4,5},{5,4},{6,7},{7,6},{8,9},{9,8},{10,11... | collective-permute-start | bytes 589832 | tf_op jit(solution)/shard_map/ppermute | solution.py:438
  26.7 4.8 %collective-permute-start.8 = (bf16[16,1024]{1,0:T(8,128)(2,1)S(1)}, bf16[16,1024]{1,0:T(8,128)(2,1)S(1)}, u32[]{:S(2)}, u32[]{:S(2)}) collective-permute-start(bf16[16,1024]{1,0:T(8,128)(2,1)S(1)} %slice.37), channel_id=1, source_target_pairs={{0,8},{2,10},{4,12},{6,14},{8,0},{10,2},{12,4},{14,6},{1,9},{3,11}... | collective-permute-start | bytes 98312 | tf_op jit(solution)/shard_map/ppermute | solution.py:438
  29.4 4.9 %collective-permute-start.11 = (bf16[24,1024]{1,0:T(8,128)(2,1)S(1)}, bf16[24,1024]{1,0:T(8,128)(2,1)S(1)}, u32[]{:S(2)}, u32[]{:S(2)}) collective-permute-start(bf16[24,1024]{1,0:T(8,128)(2,1)S(1)} %slice_add_fusion.refs_1_), channel_id=1, source_target_pairs={{0,1},{1,0},{2,3},{3,2},{4,5},{5,4},{6,7},{7,6},{8,9},{9,8},{10,11... | collective-permute-start | bytes 147464 | tf_op jit(solution)/shard_map/ppermute | solution.py:438
  31.5 3.9 %collective-permute-start.9 = (bf16[16,1024]{1,0:T(8,128)(2,1)S(1)}, bf16[16,1024]{1,0:T(8,128)(2,1)S(1)}, u32[]{:S(2)}, u32[]{:S(2)}) collective-permute-start(bf16[16,1024]{1,0:T(8,128)(2,1)S(1)} %slice_add_fusion.1.refs_1_), channel_id=1, source_target_pairs={{0,1},{1,0},{2,3},{3,2},{4,5},{5,4},{6,7},{7,6},{8,9},{9,8},{10,11... | collective-permute-start | bytes 98312 | tf_op jit(solution)/shard_map/ppermute | solution.py:438

commit v11 on v9

--- a/solution.py
+++ b/solution.py
@@ -276,7 +276,7 @@
 
 
 def rest_kernel(
-    windows, times, halo, ends, taps, table, part_a, part_b, response_a, response_b, *refs
+    windows, pairs, times, halo, ends, taps, table, part_a, part_b, response_a, response_b, *refs
 ):
     own_white, picks, keep, send = refs[:4]
     blocks = refs[4 : 4 + times]
@@ -309,26 +309,35 @@
     count = rest * channels
     whiten_all(spectra, white, count)
     white[count:, :] = own_white[...]
-    base = keep.shape[0]
-    size = channels // times
+    base = picks.shape[0] // 2
+    sizes = part_rows(windows, pairs)
+    used = [(windows - 1) * pairs, pairs]
+    part = channels // times
     choose = picks[...]
     for f in range(0, 2 * NF, CHUNK):
         cols = slice(f, f + CHUNK)
         out = dot(choose, white[:, cols]).astype(BF16)
-        keep[:, cols] = out[:base]
-        send[:, cols] = out[base:]
+        imag = f >= NF
+        place = slice(f - NF * imag, f - NF * imag + CHUNK)
+        for target, first in ((keep, 0), (send, base)):
+            for d in range(base // sum(sizes)):
+                at, row = first + d * sum(sizes), d * 2 * sum(used)
+                for size, n in zip(sizes, used):
+                    put = row + imag * n
+                    target[put : put + n, place] = out[at : at + n]
+                    at, row = at + size, row + 2 * n
     for d in range(times):
-        line = (lax.axis_index("tm") ^ d) * size
+        line = (lax.axis_index("tm") ^ d) * part
         for w in range(windows):
-            if size % ROWS == 0:
+            if part % ROWS == 0:
                 at = pl.multiple_of(w * channels + line, ROWS)
-                blocks[d][w * size : (w + 1) * size, :] = white[pl.ds(at, size), :]
+                blocks[d][w * part : (w + 1) * part, :] = white[pl.ds(at, part), :]
             else:
-                row = lax.broadcasted_iota(jnp.int32, (size, channels), 0)
-                col = lax.broadcasted_iota(jnp.int32, (size, channels), 1)
+                row = lax.broadcasted_iota(jnp.int32, (part, channels), 0)
+                col = lax.broadcasted_iota(jnp.int32, (part, channels), 1)
                 move = (col == row + line).astype(F32).astype(BF16)
                 moved = dot(move, white[w * channels : (w + 1) * channels, :])
-                blocks[d][w * size : (w + 1) * size, :] = moved.astype(BF16)
+                blocks[d][w * part : (w + 1) * part, :] = moved.astype(BF16)
 
 
 def correlate_kernel(spans, pairs, factor, has_total, last, *refs):
@@ -342,9 +351,12 @@
     for receiver, source, span in zip(receivers, sources, spans):
         for i, w in enumerate(span):
             line_r[windows] = receiver[w].astype(F32) * factor
-            rows = source[i * pairs : (i + 1) * pairs, :].astype(F32)
-            for p in range(pairs):
-                line_s[p, windows : windows + 1, :] = rows[p : p + 1, :]
+            for c in range(2):
+                at = (c * len(span) + i) * pairs
+                rows = source[at : at + pairs, :].astype(F32)
+                cols = slice(c * NF, (c + 1) * NF)
+                for p in range(pairs):
+                    line_s[p, windows : windows + 1, cols] = rows[p : p + 1, :]
             windows += 1
 
     def copy(p):
@@ -412,6 +424,7 @@
     part = channels // times
     sizes = part_rows(windows, pairs)
     rows_out = chips * sum(sizes)
+    rows, cut = 2 * windows * pairs, 2 * (windows - 1) * pairs
 
     def across(x, axis, distance):
         size = lax.axis_size(axis)
@@ -506,8 +519,8 @@
         name="picks",
     )(source_counts[None], source_channel, *wanted)
     outs = pl.pallas_call(
-        functools.partial(rest_kernel, windows, times),
-        out_shape=[jax.ShapeDtypeStruct((rows_out, 2 * NF), BF16)] * 2
+        functools.partial(rest_kernel, windows, pairs, times),
+        out_shape=[jax.ShapeDtypeStruct((chips * rows, NF), BF16)] * 2
         + [jax.ShapeDtypeStruct((windows * part, 2 * NF), BF16)] * times,
         in_specs=[vmem] * 10,
         out_specs=[vmem] * (2 + times),
@@ -532,7 +545,6 @@
     )
     keep, send, blocks = outs[0], outs[1], outs[2:]
     gathered = keep + across(send, "chan", 1)
-    rows = sum(sizes)
     pieces = [gathered[d * rows : (d + 1) * rows] for d in range(chips)]
     pieces = list(lax.optimization_barrier(tuple(pieces)))
     for bit in bits:
@@ -545,10 +557,10 @@
     mine = pieces[0]
     for bit in bits[:-1]:
         mine = mine + across(pieces[bit], "chan", 2 * bit)
-    mine = [mine[: sizes[0]], mine[sizes[0] :]]
+    mine = [mine[:cut], mine[cut:]]
     if bits:
         last = pieces[bits[-1]]
-        for i, x in enumerate((last[: sizes[0]], last[sizes[0] :])):
+        for i, x in enumerate((last[:cut], last[cut:])):
             mine[i] = mine[i] + across(x, "chan", 2 * bits[-1])
     receivers = [blocks[0]]
     for d in range(1, times):

time: 36.9 us -> 36.4 us (0.986)
  waiting for transfers between devices: 11.4 us -> 10.9 us
    ppermute x11, waiting for transfers between devices: 11.4 us -> 10.9 us  [across(): return lax.ppermute(x, axis, [(i, i ^ distance) for i in range(size)])]
where the time goes in v11:
time: 36.4 us; the launch traced here: 36.3 us
  starting transfers between devices  16.4 us (45%)
  waiting for transfers between devices  10.9 us (30%)
  Pallas kernels  8.56 us (24%)
    ppermute x11, starting transfers between devices, across(): return lax.ppermute(x, axis, [(i, i ^ distance) for i in range(size)])  12 us
    ppermute x11, waiting for transfers between devices, across(): return lax.ppermute(x, axis, [(i, i ^ distance) for i in range(size)])  10.9 us
    ppermute x1, starting transfers between devices, shards(): halo = lax.ppermute(message, 'tm', [(i - 1, i) for i in range(1, times)])  4.39 us
    pallas_call x4, Pallas kernels, correlate(): pl.pallas_call(functools.partial(correlate_kernel, spans, pairs, factor,...  2.59 us
    pallas_call x1, Pallas kernels, shards(): pl.pallas_call(functools.partial(load_kernel, tap_count - 1), out_shape=[...  2.26 us
    pallas_call x1, Pallas kernels, shards(): pl.pallas_call(functools.partial(rest_kernel, windows, pairs, times), out...  1.44 us
    pallas_call x1, Pallas kernels, shards(): pl.pallas_call(functools.partial(second_kernel, windows), out_shape=chunk...  1.03 us
    pallas_call x1, Pallas kernels, shards(): pl.pallas_call(functools.partial(first_kernel, windows), out_shape=chunk_...  0.89 us
  transfers between devices with their start and end apart: 12, of which 7 were waited for; matrix products, arithmetic and copies ran while one was open for 0% of the time, Pallas kernels for 16%

profile of v11, /device:TPU:0, one launch (start us, length us, event | category | flops | bytes accessed | tf_op | source)
XLA Modules:
  0.0 36.3 jit_solution(8517297953189881148)
XLA Ops:
  0.0 0.5 %collective-permute-start.1 = (s32[1,12]{1,0:T(1,128)}, s32[1,12]{1,0:T(1,128)S(1)}, u32[]{:S(2)}, u32[]{:S(2)}) collective-permute-start(s32[1,12]{1,0:T(1,128)} %ids_in.1), channel_id=1, source_target_pairs={{0,2},{2,0},{4,6},{6,4},{8,10},{10,8},{12,14},{14,12},{1,3},{3,1},... | collective-permute-start | bytes 152 | tf_op jit(solution)/shard_map/ppermute | solution.py:431
  0.5 2.3 %load.1 = (bf16[64,1152]{1,0:T(8,128)(2,1)S(1)}, f32[64,1024]{1,0:T(8,128)S(1)}, bf16[4,1024,256]{2,1,0:T(8,128)(2,1)S(1)}, s32[1,12]{1,0:T(1,128)S(1)}) custom-call(bf16[64,6144]{1,0:T(8,128)(2,1)} %traces.3, bf16[4,1024,256]{2,1,0:T(8,128)(2,1)} %constant.2.clone.table_in, s32[1,12]{1,0:T(1,128)} %ids_in.1), custom_call_target="tpu_custom_call" | custom-call | tf_op jit(solution)/shard_map/load/pallas_call | solution.py:440
  2.8 4.4 %collective-permute-start = (bf16[64,1152]{1,0:T(8,128)(2,1)S(1)}, bf16[64,1152]{1,0:T(8,128)(2,1)S(1)}, u32[]{:S(2)}, u32[]{:S(2)}) collective-permute-start(bf16[64,1152]{1,0:T(8,128)(2,1)S(1)} %get-tuple-element.26), channel_id=1, source_target_pairs={{0,1},{2,3},{4,5},{6,7},{8,9},{10,11},{12,13},{14,15},{16,17},{18,... | collective-permute-start | bytes 442376 | tf_op jit(solution)/shard_map/ppermute | solution.py:470
  7.2 0.0 collective-permute-done.1.other
  7.2 0.0 copy-start
  7.2 0.0 copy-start.1
  7.2 1.6 %collective-permute-start.2 = (s32[2,12]{1,0:T(2,128)S(1)}, s32[2,12]{1,0:T(2,128)S(1)}, u32[]{:S(2)}, u32[]{:S(2)}) collective-permute-start(s32[2,12]{1,0:T(2,128)S(1)} %pair.1), channel_id=1, source_target_pairs={{0,4},{2,6},{4,0},{6,2},{8,12},{10,14},{12,8},{14,10},{1,5},{3,7},... | collective-permute-start | bytes 296 | tf_op jit(solution)/shard_map/ppermute | solution.py:431
  8.9 0.0 copy-done
  8.9 0.0 copy-done.1
  8.9 0.9 %first.1 = (f32[128,512]{1,0:T(8,128)S(1)}, f32[64,512]{1,0:T(8,128)S(1)}, f32[64,512]{1,0:T(8,128)S(1)}, bf16[64,256]{1,0:T(8,128)(2,1)S(1)}, bf16[64,96]{1,0:T(8,128)(2,1)S(1)}, /*index=5*/bf16[64,144]{1,0:T(8,128)(2,1)S(1)}) custom-call(bf16[64,6144]{1,0:T(8,128)(2,1)S(1)} %copy-done, f32[33,64]{1,0:T(8,128)S(1)} %bitcast.9, ...), custom_call_target="tpu_custom_call" | custom-call | tf_op jit(solution)/shard_map/first/pallas_call | solution.py:482
  9.8 1.1 %collective-permute-done.2 = s32[2,12]{1,0:T(2,128)S(1)} collective-permute-done((s32[2,12]{1,0:T(2,128)S(1)}, s32[2,12]{1,0:T(2,128)S(1)}, u32[]{:S(2)}, u32[]{:S(2)}) %collective-permute-start.2) | collective-permute-done | bytes 128 | tf_op jit(solution)/shard_map/ppermute | solution.py:431
  10.9 2.6 %collective-permute-start.3 = (s32[4,12]{1,0:T(4,128)S(1)}, s32[4,12]{1,0:T(4,128)S(1)}, u32[]{:S(2)}, u32[]{:S(2)}) collective-permute-start(s32[4,12]{1,0:T(4,128)S(1)} %pad_add_fusion.refs_0_), channel_id=1, source_target_pairs={{0,8},{2,10},{4,12},{6,14},{8,0},{10,2},{12,4},{14,6},{1,9},{3,11}... | collective-permute-start | bytes 584 | tf_op jit(solution)/shard_map/ppermute | solution.py:431
  13.5 0.0 copy-start.2
  13.5 0.0 copy-start.3
  13.5 1.0 %second.1 = (f32[128,512]{1,0:T(8,128)S(1)}, f32[64,512]{1,0:T(8,128)S(1)}, bf16[64,1024]{1,0:T(8,128)(2,1)S(1)}) custom-call(bf16[64,6144]{1,0:T(8,128)(2,1)S(1)} %copy-done, bf16[4,1024,256]{2,1,0:T(8,128)(2,1)S(1)} %get-tuple-element.27.table, f32[64,1024]{1,0:T(8,128)S(1)} %get-tuple-element.28.last_half, bf16[64,144]{1,0:T(8,128)(2,1)S(1)} %get-tuple-element.31.lines, ...), custom_call_target="tpu_custom_call" | custom-call | tf_op jit(solution)/shard_map/second/pallas_call | solution.py:500
  14.5 0.9 %collective-permute-done.3.refs_1_ = s32[4,12]{1,0:T(4,128)S(1)} collective-permute-done((s32[4,12]{1,0:T(4,128)S(1)}, s32[4,12]{1,0:T(4,128)S(1)}, u32[]{:S(2)}, u32[]{:S(2)}) %collective-permute-start.3) | collective-permute-done | bytes 224 | tf_op jit(solution)/shard_map/ppermute | solution.py:431
  15.4 0.0 copy-done.2
  15.4 0.0 copy-done.3
  15.4 0.3 picks.1.refs_1_
  15.8 0.0 collective-permute-done.halo
  15.8 1.4 %rest.1 = (bf16[288,512]{1,0:T(8,128)(2,1)S(1)}, bf16[288,512]{1,0:T(8,128)(2,1)S(1)}, bf16[96,1024]{1,0:T(8,128)(2,1)S(1)}, bf16[96,1024]{1,0:T(8,128)(2,1)S(1)}) custom-call(bf16[64,1152]{1,0:T(8,128)(2,1)S(1)} %collective-permute-done.halo, bf16[64,256]{1,0:T(8,128)(2,1)S(1)} %get-tuple-element.29.ends, f32[33,64]{1,0:T(8,128)S(1)} %bitcast.10, ...), custom_call_target="tpu_custom_call" | custom-call | tf_op jit(solution)/shard_map/rest/pallas_call | solution.py:521
  17.2 0.1 collective-permute-start.5
  17.3 1.6 %collective-permute-done.5 = bf16[288,512]{1,0:T(8,128)(2,1)S(1)} collective-permute-done((bf16[288,512]{1,0:T(8,128)(2,1)S(1)}, bf16[288,512]{1,0:T(8,128)(2,1)S(1)}, u32[]{:S(2)}, u32[]{:S(2)}) %collective-permute-start.5) | collective-permute-done | bytes 294944 | tf_op jit(solution)/shard_map/ppermute | solution.py:431
  18.9 0.1 add.15
  19.0 1.6 %collective-permute-start.7 = (bf16[72,512]{1,0:T(8,128)(2,1)S(1)}, bf16[72,512]{1,0:T(8,128)(2,1)S(1)}, u32[]{:S(2)}, u32[]{:S(2)}) collective-permute-start(bf16[72,512]{1,0:T(8,128)(2,1)S(1)} %get-tuple-element.45), channel_id=1, source_target_pairs={{0,4},{2,6},{4,0},{6,2},{8,12},{10,14},{12,8},{14,10},{1,5},{3,7},... | collective-permute-start | bytes 221192 | tf_op jit(solution)/shard_map/ppermute | solution.py:431
  20.6 0.4 %collective-permute-start.6 = (bf16[72,512]{1,0:T(8,128)(2,1)S(1)}, bf16[72,512]{1,0:T(8,128)(2,1)S(1)}, u32[]{:S(2)}, u32[]{:S(2)}) collective-permute-start(bf16[72,512]{1,0:T(8,128)(2,1)S(1)} %get-tuple-element.43), channel_id=1, source_target_pairs={{0,4},{2,6},{4,0},{6,2},{8,12},{10,14},{12,8},{14,10},{1,5},{3,7},... | collective-permute-start | bytes 221192 | tf_op jit(solution)/shard_map/ppermute | solution.py:431
  21.1 2.6 %collective-permute-done.7 = bf16[72,512]{1,0:T(8,128)(2,1)S(1)} collective-permute-done((bf16[72,512]{1,0:T(8,128)(2,1)S(1)}, bf16[72,512]{1,0:T(8,128)(2,1)S(1)}, u32[]{:S(2)}, u32[]{:S(2)}) %collective-permute-start.7) | collective-permute-done | bytes 73760 | tf_op jit(solution)/shard_map/ppermute | solution.py:431
  23.8 2.6 %collective-permute-start.10 = (bf16[48,512]{1,0:T(8,128)(2,1)S(1)}, bf16[48,512]{1,0:T(8,128)(2,1)S(1)}, u32[]{:S(2)}, u32[]{:S(2)}) collective-permute-start(bf16[48,512]{1,0:T(8,128)(2,1)S(1)} %slice.39), channel_id=1, source_target_pairs={{0,8},{2,10},{4,12},{6,14},{8,0},{10,2},{12,4},{14,6},{1,9},{3,11}... | collective-permute-start | bytes 147464 | tf_op jit(solution)/shard_map/ppermute | solution.py:431
  26.4 0.0 collective-permute-start.4
  26.4 0.3 collective-permute-start.8
  26.8 0.0 collective-permute-done.6
  26.8 2.3 %collective-permute-done.10 = bf16[48,512]{1,0:T(8,128)(2,1)S(1)} collective-permute-done((bf16[48,512]{1,0:T(8,128)(2,1)S(1)}, bf16[48,512]{1,0:T(8,128)(2,1)S(1)}, u32[]{:S(2)}, u32[]{:S(2)}) %collective-permute-start.10) | collective-permute-done | bytes 49184 | tf_op jit(solution)/shard_map/ppermute | solution.py:431
  29.1 0.1 collective-permute-start.11
  29.2 2.0 %collective-permute-done.8 = bf16[24,512]{1,0:T(8,128)(2,1)S(1)} collective-permute-done((bf16[24,512]{1,0:T(8,128)(2,1)S(1)}, bf16[24,512]{1,0:T(8,128)(2,1)S(1)}, u32[]{:S(2)}, u32[]{:S(2)}) %collective-permute-start.8) | collective-permute-done | bytes 24608 | tf_op jit(solution)/shard_map/ppermute | solution.py:431
  31.1 2.0 %collective-permute-start.9 = (bf16[24,512]{1,0:T(8,128)(2,1)S(1)}, bf16[24,512]{1,0:T(8,128)(2,1)S(1)}, u32[]{:S(2)}, u32[]{:S(2)}) collective-permute-start(bf16[24,512]{1,0:T(8,128)(2,1)S(1)} %slice_add_fusion.1.refs_1_), channel_id=1, source_target_pairs={{0,1},{1,0},{2,3},{3,2},{4,5},{5,4},{6,7},{7,6},{8,9},{9,8},{10,11... | collective-permute-start | bytes 73736 | tf_op jit(solution)/shard_map/ppermute | solution.py:431
  33.2 0.5 %correlate.4.refs_2_ = f32[12,32,1024]{2,1,0:T(8,128)S(1)} custom-call(bf16[3,32,1024]{2,1,0:T(8,128)(2,1)S(1)} %bitcast.5, bf16[48,512]{1,0:T(8,128)(2,1)S(1)} %slice_add_fusion.refs_1_), custom_call_target="tpu_custom_call" | custom-call | tf_op jit(solution)/shard_map/correlate/pallas_call | solution.py:405
  33.7 0.3 correlate.5.refs_2_
  34.0 0.0 collective-permute-done.4
  34.0 0.0 collective-permute-done.11.refs_1_
  34.0 0.5 %correlate.6.refs_2_ = f32[12,32,1024]{2,1,0:T(8,128)S(1)} custom-call(bf16[3,32,1024]{2,1,0:T(8,128)(2,1)S(1)} %bitcast.7, bf16[48,512]{1,0:T(8,128)(2,1)S(1)} %collective-permute-done.11.refs_1_, f32[12,32,1024]{2,1,0:T(8,128)S(1)} %correlate.5.refs_2_), custom_call_target="tpu_custom_call" | custom-call | tf_op jit(solution)/shard_map/correlate/pallas_call | solution.py:405
  34.5 0.5 %collective-permute-done.9.refs_1_ = bf16[24,512]{1,0:T(8,128)(2,1)S(1)} collective-permute-done((bf16[24,512]{1,0:T(8,128)(2,1)S(1)}, bf16[24,512]{1,0:T(8,128)(2,1)S(1)}, u32[]{:S(2)}, u32[]{:S(2)}) %collective-permute-start.9) | collective-permute-done | bytes 24608 | tf_op jit(solution)/shard_map/ppermute | solution.py:431
  35.0 1.3 %correlate.7 = f32[12,32,1024]{2,1,0:T(8,128)} custom-call(bf16[3,32,1024]{2,1,0:T(8,128)(2,1)S(1)} %bitcast.8, bf16[24,512]{1,0:T(8,128)(2,1)S(1)} %collective-permute-done.9.refs_1_, f32[12,32,1024]{2,1,0:T(8,128)S(1)} %correlate.6.refs_2_), custom_call_target="tpu_custom_call" | custom-call | tf_op jit(solution)/shard_map/correlate/pallas_call | solution.py:405
  (9 shorter events, 0.1 us)
Async XLA Ops:
  0.0 7.2 %collective-permute-start.1 = (s32[1,12]{1,0:T(1,128)}, s32[1,12]{1,0:T(1,128)S(1)}, u32[]{:S(2)}, u32[]{:S(2)}) collective-permute-start(s32[1,12]{1,0:T(1,128)} %ids_in.1), channel_id=1, source_target_pairs={{0,2},{2,0},{4,6},{6,4},{8,10},{10,8},{12,14},{14,12},{1,3},{3,1},... | collective-permute-start | bytes 152 | tf_op jit(solution)/shard_map/ppermute | solution.py:431
  2.8 13.0 %collective-permute-start = (bf16[64,1152]{1,0:T(8,128)(2,1)S(1)}, bf16[64,1152]{1,0:T(8,128)(2,1)S(1)}, u32[]{:S(2)}, u32[]{:S(2)}) collective-permute-start(bf16[64,1152]{1,0:T(8,128)(2,1)S(1)} %get-tuple-element.26), channel_id=1, source_target_pairs={{0,1},{2,3},{4,5},{6,7},{8,9},{10,11},{12,13},{14,15},{16,17},{18,... | collective-permute-start | bytes 442376 | tf_op jit(solution)/shard_map/ppermute | solution.py:470
  7.2 1.7 %copy-start = (bf16[64,6144]{1,0:T(8,128)(2,1)S(1)}, bf16[64,6144]{1,0:T(8,128)(2,1)}, u32[]{:S(2)}) copy-start(bf16[64,6144]{1,0:T(8,128)(2,1)} %traces.3) | copy-start | bytes 2359300
  7.2 1.7 %copy-start.1 = (f32[64,33]{0,1:T(8,128)S(1)}, f32[64,33]{0,1:T(8,128)}, u32[]{:S(2)}) copy-start(f32[64,33]{0,1:T(8,128)} %param.7) | copy-start | bytes 25348
  7.2 3.6 %collective-permute-start.2 = (s32[2,12]{1,0:T(2,128)S(1)}, s32[2,12]{1,0:T(2,128)S(1)}, u32[]{:S(2)}, u32[]{:S(2)}) collective-permute-start(s32[2,12]{1,0:T(2,128)S(1)} %pair.1), channel_id=1, source_target_pairs={{0,4},{2,6},{4,0},{6,2},{8,12},{10,14},{12,8},{14,10},{1,5},{3,7},... | collective-permute-start | bytes 296 | tf_op jit(solution)/shard_map/ppermute | solution.py:431
  10.9 4.5 %collective-permute-start.3 = (s32[4,12]{1,0:T(4,128)S(1)}, s32[4,12]{1,0:T(4,128)S(1)}, u32[]{:S(2)}, u32[]{:S(2)}) collective-permute-start(s32[4,12]{1,0:T(4,128)S(1)} %pad_add_fusion.refs_0_), channel_id=1, source_target_pairs={{0,8},{2,10},{4,12},{6,14},{8,0},{10,2},{12,4},{14,6},{1,9},{3,11}... | collective-permute-start | bytes 584 | tf_op jit(solution)/shard_map/ppermute | solution.py:431
  13.5 1.9 %copy-start.2 = (s32[8,36]{1,0:T(8,128)S(1)}, s32[8,36]{1,0:T(8,128)}, u32[]{:S(2)}) copy-start(s32[8,36]{1,0:T(8,128)} %slots.1) | copy-start | bytes 3460
  13.5 1.9 %copy-start.3 = (s32[8]{0:T(128)S(1)}, s32[8]{0:T(128)}, u32[]{:S(2)}) copy-start(s32[8]{0:T(128)} %param.8) | copy-start | bytes 100
  17.2 1.6 %collective-permute-start.5 = (bf16[288,512]{1,0:T(8,128)(2,1)S(1)}, bf16[288,512]{1,0:T(8,128)(2,1)S(1)}, u32[]{:S(2)}, u32[]{:S(2)}) collective-permute-start(bf16[288,512]{1,0:T(8,128)(2,1)S(1)} %get-tuple-element.41), channel_id=1, source_target_pairs={{0,2},{2,0},{4,6},{6,4},{8,10},{10,8},{12,14},{14,12},{1,3},{3,1},... | collective-permute-start | bytes 884744 | tf_op jit(solution)/shard_map/ppermute | solution.py:431
  19.0 4.7 %collective-permute-start.7 = (bf16[72,512]{1,0:T(8,128)(2,1)S(1)}, bf16[72,512]{1,0:T(8,128)(2,1)S(1)}, u32[]{:S(2)}, u32[]{:S(2)}) collective-permute-start(bf16[72,512]{1,0:T(8,128)(2,1)S(1)} %get-tuple-element.45), channel_id=1, source_target_pairs={{0,4},{2,6},{4,0},{6,2},{8,12},{10,14},{12,8},{14,10},{1,5},{3,7},... | collective-permute-start | bytes 221192 | tf_op jit(solution)/shard_map/ppermute | solution.py:431
  20.6 6.1 %collective-permute-start.6 = (bf16[72,512]{1,0:T(8,128)(2,1)S(1)}, bf16[72,512]{1,0:T(8,128)(2,1)S(1)}, u32[]{:S(2)}, u32[]{:S(2)}) collective-permute-start(bf16[72,512]{1,0:T(8,128)(2,1)S(1)} %get-tuple-element.43), channel_id=1, source_target_pairs={{0,4},{2,6},{4,0},{6,2},{8,12},{10,14},{12,8},{14,10},{1,5},{3,7},... | collective-permute-start | bytes 221192 | tf_op jit(solution)/shard_map/ppermute | solution.py:431
  23.8 5.3 %collective-permute-start.10 = (bf16[48,512]{1,0:T(8,128)(2,1)S(1)}, bf16[48,512]{1,0:T(8,128)(2,1)S(1)}, u32[]{:S(2)}, u32[]{:S(2)}) collective-permute-start(bf16[48,512]{1,0:T(8,128)(2,1)S(1)} %slice.39), channel_id=1, source_target_pairs={{0,8},{2,10},{4,12},{6,14},{8,0},{10,2},{12,4},{14,6},{1,9},{3,11}... | collective-permute-start | bytes 147464 | tf_op jit(solution)/shard_map/ppermute | solution.py:431
  26.4 7.5 %collective-permute-start.4 = (bf16[96,1024]{1,0:T(8,128)(2,1)S(1)}, bf16[96,1024]{1,0:T(8,128)(2,1)S(1)}, u32[]{:S(2)}, u32[]{:S(2)}) collective-permute-start(bf16[96,1024]{1,0:T(8,128)(2,1)S(1)} %get-tuple-element.39), channel_id=1, source_target_pairs={{0,1},{1,0},{2,3},{3,2},{4,5},{5,4},{6,7},{7,6},{8,9},{9,8},{10,11... | collective-permute-start | bytes 589832 | tf_op jit(solution)/shard_map/ppermute | solution.py:431
  26.4 4.7 %collective-permute-start.8 = (bf16[24,512]{1,0:T(8,128)(2,1)S(1)}, bf16[24,512]{1,0:T(8,128)(2,1)S(1)}, u32[]{:S(2)}, u32[]{:S(2)}) collective-permute-start(bf16[24,512]{1,0:T(8,128)(2,1)S(1)} %slice.37), channel_id=1, source_target_pairs={{0,8},{2,10},{4,12},{6,14},{8,0},{10,2},{12,4},{14,6},{1,9},{3,11}... | collective-permute-start | bytes 73736 | tf_op jit(solution)/shard_map/ppermute | solution.py:431
  29.1 4.9 %collective-permute-start.11 = (bf16[48,512]{1,0:T(8,128)(2,1)S(1)}, bf16[48,512]{1,0:T(8,128)(2,1)S(1)}, u32[]{:S(2)}, u32[]{:S(2)}) collective-permute-start(bf16[48,512]{1,0:T(8,128)(2,1)S(1)} %slice_add_fusion.refs_1_), channel_id=1, source_target_pairs={{0,1},{1,0},{2,3},{3,2},{4,5},{5,4},{6,7},{7,6},{8,9},{9,8},{10,11... | collective-permute-start | bytes 147464 | tf_op jit(solution)/shard_map/ppermute | solution.py:431
  31.1 3.8 %collective-permute-start.9 = (bf16[24,512]{1,0:T(8,128)(2,1)S(1)}, bf16[24,512]{1,0:T(8,128)(2,1)S(1)}, u32[]{:S(2)}, u32[]{:S(2)}) collective-permute-start(bf16[24,512]{1,0:T(8,128)(2,1)S(1)} %slice_add_fusion.1.refs_1_), channel_id=1, source_target_pairs={{0,1},{1,0},{2,3},{3,2},{4,5},{5,4},{6,7},{7,6},{8,9},{9,8},{10,11... | collective-permute-start | bytes 73736 | tf_op jit(solution)/shard_map/ppermute | solution.py:431

commit v12 on v11

--- a/solution.py
+++ b/solution.py
@@ -136,9 +136,14 @@
     channels, samples = traces.shape
     begin = traces_in.shape[1] - samples
     copies = [pltpu.make_async_copy(traces_in.at[:, begin:], traces, sems.at[0])]
-    at = 1 + table.shape[0]
-    for i in range(table.shape[0]):
-        copies.append(pltpu.make_async_copy(table_in.at[i], table.at[i], sems.at[1 + i]))
+    at = 1 + 2 * table.shape[0]
+    for k in range(0, table.shape[0], 2):
+        for part in (slice(0, PIECE), slice(PIECE, 2 * PIECE)):
+            for i in (k, k + 1):
+                sem = sems.at[len(copies)]
+                copies.append(
+                    pltpu.make_async_copy(table_in.at[i, part], table.at[i, part], sem)
+                )
     copies.append(pltpu.make_async_copy(ids_in, ids, sems.at[at]))
     for copy in copies:
         copy.start()
@@ -150,12 +155,20 @@
     pieces = [samples - HALF + q * PIECE for q in range(HALF // PIECE)]
     x = jnp.concatenate([traces[:, p : p + PIECE] for p in pieces], axis=0)
     turns = Turns()
+    rows = [slice(e * channels, (e + 1) * channels) for e in range(HALF // PIECE)]
     for i, f in enumerate(range(0, NF, CHUNK)):
         re = slice(f, f + CHUNK)
         im = slice(NF + f, NF + f + CHUNK)
-        copies[1 + 2 * i].wait()
-        copies[2 + 2 * i].wait()
-        xr, xi = half_spectra(x, table, channels, 1, turns, f)[0]
+        sums = []
+        for j, part in enumerate((slice(0, PIECE), slice(PIECE, 2 * PIECE))):
+            for c in range(2):
+                copies[1 + 4 * i + 2 * j + c].wait()
+                term = dot(x, table[2 * i + c, part, :])
+                if j:
+                    sums[c] = sums[c] + term
+                else:
+                    sums.append(term)
+        xr, xi = turns.half(*([total[r] for r in rows] for total in sums))
         last_half[:, re] = xr
         last_half[:, im] = xi
         message[:, re] = xr.astype(BF16)
@@ -448,7 +461,7 @@
         out_specs=[vmem] * 4,
         scratch_shapes=[
             pltpu.VMEM((channels, HALF + 128), BF16),
-            pltpu.SemaphoreType.DMA((2 + 2 * NF // CHUNK,)),
+            pltpu.SemaphoreType.DMA((2 + 4 * NF // CHUNK,)),
         ],
         compiler_params=params,
         name="load",

time: 36.4 us -> 37.2 us (1.022)
  Pallas kernels: 8.56 us -> 9.33 us
    pallas_call x1, Pallas kernels: 2.26 us -> 3.04 us  [shards(): pl.pallas_call(functools.partial(load_kernel, tap_count - 1), out_shape=[...]
  transfers between devices with their start and end apart: 12 -> 12, of which waited for: 7 -> 7; matrix products, arithmetic and copies ran while one was open for 0% -> 0% of each run, Pallas kernels for 16% -> 18%
where the time goes in v12:
time: 37.2 us; the launch traced here: 37 us
  starting transfers between devices  16.4 us (44%)
  waiting for transfers between devices  10.9 us (29%)
  Pallas kernels  9.33 us (25%)
    ppermute x11, starting transfers between devices, across(): return lax.ppermute(x, axis, [(i, i ^ distance) for i in range(size)])  12 us
    ppermute x11, waiting for transfers between devices, across(): return lax.ppermute(x, axis, [(i, i ^ distance) for i in range(size)])  10.9 us
    ppermute x1, starting transfers between devices, shards(): halo = lax.ppermute(message, 'tm', [(i - 1, i) for i in range(1, times)])  4.39 us
    pallas_call x1, Pallas kernels, shards(): pl.pallas_call(functools.partial(load_kernel, tap_count - 1), out_shape=[...  3.04 us
    pallas_call x4, Pallas kernels, correlate(): pl.pallas_call(functools.partial(correlate_kernel, spans, pairs, factor,...  2.59 us
    pallas_call x1, Pallas kernels, shards(): pl.pallas_call(functools.partial(rest_kernel, windows, pairs, times), out...  1.43 us
    pallas_call x1, Pallas kernels, shards(): pl.pallas_call(functools.partial(second_kernel, windows), out_shape=chunk...  1.03 us
    pallas_call x1, Pallas kernels, shards(): pl.pallas_call(functools.partial(first_kernel, windows), out_shape=chunk_...  0.89 us
  transfers between devices with their start and end apart: 12, of which 7 were waited for; matrix products, arithmetic and copies ran while one was open for 0% of the time, Pallas kernels for 18%

profile of v12, /device:TPU:0, one launch (start us, length us, event | category | flops | bytes accessed | tf_op | source)
XLA Modules:
  0.0 37.0 jit_solution(15603813841810042222)
XLA Ops:
  0.0 0.5 %collective-permute-start.1 = (s32[1,12]{1,0:T(1,128)}, s32[1,12]{1,0:T(1,128)S(1)}, u32[]{:S(2)}, u32[]{:S(2)}) collective-permute-start(s32[1,12]{1,0:T(1,128)} %ids_in.1), channel_id=1, source_target_pairs={{0,2},{2,0},{4,6},{6,4},{8,10},{10,8},{12,14},{14,12},{1,3},{3,1},... | collective-permute-start | bytes 152 | tf_op jit(solution)/shard_map/ppermute | solution.py:444
  0.5 3.0 %load.1 = (bf16[64,1152]{1,0:T(8,128)(2,1)S(1)}, f32[64,1024]{1,0:T(8,128)S(1)}, bf16[4,1024,256]{2,1,0:T(8,128)(2,1)S(1)}, s32[1,12]{1,0:T(1,128)S(1)}) custom-call(bf16[64,6144]{1,0:T(8,128)(2,1)} %traces.3, bf16[4,1024,256]{2,1,0:T(8,128)(2,1)} %constant.2.clone.table_in, s32[1,12]{1,0:T(1,128)} %ids_in.1), custom_call_target="tpu_custom_call" | custom-call | tf_op jit(solution)/shard_map/load/pallas_call | solution.py:453
  3.5 4.4 %collective-permute-start = (bf16[64,1152]{1,0:T(8,128)(2,1)S(1)}, bf16[64,1152]{1,0:T(8,128)(2,1)S(1)}, u32[]{:S(2)}, u32[]{:S(2)}) collective-permute-start(bf16[64,1152]{1,0:T(8,128)(2,1)S(1)} %get-tuple-element.26), channel_id=1, source_target_pairs={{0,1},{2,3},{4,5},{6,7},{8,9},{10,11},{12,13},{14,15},{16,17},{18,... | collective-permute-start | bytes 442376 | tf_op jit(solution)/shard_map/ppermute | solution.py:483
  7.9 0.0 collective-permute-done.1.other
  7.9 0.0 copy-start
  8.0 0.0 copy-start.1
  8.0 1.6 %collective-permute-start.2 = (s32[2,12]{1,0:T(2,128)S(1)}, s32[2,12]{1,0:T(2,128)S(1)}, u32[]{:S(2)}, u32[]{:S(2)}) collective-permute-start(s32[2,12]{1,0:T(2,128)S(1)} %pair.1), channel_id=1, source_target_pairs={{0,4},{2,6},{4,0},{6,2},{8,12},{10,14},{12,8},{14,10},{1,5},{3,7},... | collective-permute-start | bytes 296 | tf_op jit(solution)/shard_map/ppermute | solution.py:444
  9.6 0.0 copy-done
  9.6 0.0 copy-done.1
  9.6 0.9 %first.1 = (f32[128,512]{1,0:T(8,128)S(1)}, f32[64,512]{1,0:T(8,128)S(1)}, f32[64,512]{1,0:T(8,128)S(1)}, bf16[64,256]{1,0:T(8,128)(2,1)S(1)}, bf16[64,96]{1,0:T(8,128)(2,1)S(1)}, /*index=5*/bf16[64,144]{1,0:T(8,128)(2,1)S(1)}) custom-call(bf16[64,6144]{1,0:T(8,128)(2,1)S(1)} %copy-done, f32[33,64]{1,0:T(8,128)S(1)} %bitcast.9, ...), custom_call_target="tpu_custom_call" | custom-call | tf_op jit(solution)/shard_map/first/pallas_call | solution.py:495
  10.5 1.1 %collective-permute-done.2 = s32[2,12]{1,0:T(2,128)S(1)} collective-permute-done((s32[2,12]{1,0:T(2,128)S(1)}, s32[2,12]{1,0:T(2,128)S(1)}, u32[]{:S(2)}, u32[]{:S(2)}) %collective-permute-start.2) | collective-permute-done | bytes 128 | tf_op jit(solution)/shard_map/ppermute | solution.py:444
  11.6 2.6 %collective-permute-start.3 = (s32[4,12]{1,0:T(4,128)S(1)}, s32[4,12]{1,0:T(4,128)S(1)}, u32[]{:S(2)}, u32[]{:S(2)}) collective-permute-start(s32[4,12]{1,0:T(4,128)S(1)} %pad_add_fusion.refs_0_), channel_id=1, source_target_pairs={{0,8},{2,10},{4,12},{6,14},{8,0},{10,2},{12,4},{14,6},{1,9},{3,11}... | collective-permute-start | bytes 584 | tf_op jit(solution)/shard_map/ppermute | solution.py:444
  14.3 0.0 copy-start.2
  14.3 0.0 copy-start.3
  14.3 1.0 %second.1 = (f32[128,512]{1,0:T(8,128)S(1)}, f32[64,512]{1,0:T(8,128)S(1)}, bf16[64,1024]{1,0:T(8,128)(2,1)S(1)}) custom-call(bf16[64,6144]{1,0:T(8,128)(2,1)S(1)} %copy-done, bf16[4,1024,256]{2,1,0:T(8,128)(2,1)S(1)} %get-tuple-element.27.table, f32[64,1024]{1,0:T(8,128)S(1)} %get-tuple-element.28.last_half, bf16[64,144]{1,0:T(8,128)(2,1)S(1)} %get-tuple-element.31.lines, ...), custom_call_target="tpu_custom_call" | custom-call | tf_op jit(solution)/shard_map/second/pallas_call | solution.py:513
  15.3 0.9 %collective-permute-done.3.refs_1_ = s32[4,12]{1,0:T(4,128)S(1)} collective-permute-done((s32[4,12]{1,0:T(4,128)S(1)}, s32[4,12]{1,0:T(4,128)S(1)}, u32[]{:S(2)}, u32[]{:S(2)}) %collective-permute-start.3) | collective-permute-done | bytes 224 | tf_op jit(solution)/shard_map/ppermute | solution.py:444
  16.2 0.0 copy-done.2
  16.2 0.0 copy-done.3
  16.2 0.3 picks.1.refs_1_
  16.5 0.0 collective-permute-done.halo
  16.5 1.4 %rest.1 = (bf16[288,512]{1,0:T(8,128)(2,1)S(1)}, bf16[288,512]{1,0:T(8,128)(2,1)S(1)}, bf16[96,1024]{1,0:T(8,128)(2,1)S(1)}, bf16[96,1024]{1,0:T(8,128)(2,1)S(1)}) custom-call(bf16[64,1152]{1,0:T(8,128)(2,1)S(1)} %collective-permute-done.halo, bf16[64,256]{1,0:T(8,128)(2,1)S(1)} %get-tuple-element.29.ends, f32[33,64]{1,0:T(8,128)S(1)} %bitcast.10, ...), custom_call_target="tpu_custom_call" | custom-call | tf_op jit(solution)/shard_map/rest/pallas_call | solution.py:534
  18.0 0.1 collective-permute-start.5
  18.1 1.6 %collective-permute-done.5 = bf16[288,512]{1,0:T(8,128)(2,1)S(1)} collective-permute-done((bf16[288,512]{1,0:T(8,128)(2,1)S(1)}, bf16[288,512]{1,0:T(8,128)(2,1)S(1)}, u32[]{:S(2)}, u32[]{:S(2)}) %collective-permute-start.5) | collective-permute-done | bytes 294944 | tf_op jit(solution)/shard_map/ppermute | solution.py:444
  19.6 0.1 add.15
  19.7 1.6 %collective-permute-start.7 = (bf16[72,512]{1,0:T(8,128)(2,1)S(1)}, bf16[72,512]{1,0:T(8,128)(2,1)S(1)}, u32[]{:S(2)}, u32[]{:S(2)}) collective-permute-start(bf16[72,512]{1,0:T(8,128)(2,1)S(1)} %get-tuple-element.45), channel_id=1, source_target_pairs={{0,4},{2,6},{4,0},{6,2},{8,12},{10,14},{12,8},{14,10},{1,5},{3,7},... | collective-permute-start | bytes 221192 | tf_op jit(solution)/shard_map/ppermute | solution.py:444
  21.4 0.4 %collective-permute-start.6 = (bf16[72,512]{1,0:T(8,128)(2,1)S(1)}, bf16[72,512]{1,0:T(8,128)(2,1)S(1)}, u32[]{:S(2)}, u32[]{:S(2)}) collective-permute-start(bf16[72,512]{1,0:T(8,128)(2,1)S(1)} %get-tuple-element.43), channel_id=1, source_target_pairs={{0,4},{2,6},{4,0},{6,2},{8,12},{10,14},{12,8},{14,10},{1,5},{3,7},... | collective-permute-start | bytes 221192 | tf_op jit(solution)/shard_map/ppermute | solution.py:444
  21.8 2.6 %collective-permute-done.7 = bf16[72,512]{1,0:T(8,128)(2,1)S(1)} collective-permute-done((bf16[72,512]{1,0:T(8,128)(2,1)S(1)}, bf16[72,512]{1,0:T(8,128)(2,1)S(1)}, u32[]{:S(2)}, u32[]{:S(2)}) %collective-permute-start.7) | collective-permute-done | bytes 73760 | tf_op jit(solution)/shard_map/ppermute | solution.py:444
  24.5 2.7 %collective-permute-start.10 = (bf16[48,512]{1,0:T(8,128)(2,1)S(1)}, bf16[48,512]{1,0:T(8,128)(2,1)S(1)}, u32[]{:S(2)}, u32[]{:S(2)}) collective-permute-start(bf16[48,512]{1,0:T(8,128)(2,1)S(1)} %slice.39), channel_id=1, source_target_pairs={{0,8},{2,10},{4,12},{6,14},{8,0},{10,2},{12,4},{14,6},{1,9},{3,11}... | collective-permute-start | bytes 147464 | tf_op jit(solution)/shard_map/ppermute | solution.py:444
  27.2 0.0 collective-permute-start.4
  27.2 0.3 collective-permute-start.8
  27.5 0.0 collective-permute-done.6
  27.6 2.3 %collective-permute-done.10 = bf16[48,512]{1,0:T(8,128)(2,1)S(1)} collective-permute-done((bf16[48,512]{1,0:T(8,128)(2,1)S(1)}, bf16[48,512]{1,0:T(8,128)(2,1)S(1)}, u32[]{:S(2)}, u32[]{:S(2)}) %collective-permute-start.10) | collective-permute-done | bytes 49184 | tf_op jit(solution)/shard_map/ppermute | solution.py:444
  29.9 0.1 collective-permute-start.11
  29.9 2.0 %collective-permute-done.8 = bf16[24,512]{1,0:T(8,128)(2,1)S(1)} collective-permute-done((bf16[24,512]{1,0:T(8,128)(2,1)S(1)}, bf16[24,512]{1,0:T(8,128)(2,1)S(1)}, u32[]{:S(2)}, u32[]{:S(2)}) %collective-permute-start.8) | collective-permute-done | bytes 24608 | tf_op jit(solution)/shard_map/ppermute | solution.py:444
  31.9 2.0 %collective-permute-start.9 = (bf16[24,512]{1,0:T(8,128)(2,1)S(1)}, bf16[24,512]{1,0:T(8,128)(2,1)S(1)}, u32[]{:S(2)}, u32[]{:S(2)}) collective-permute-start(bf16[24,512]{1,0:T(8,128)(2,1)S(1)} %slice_add_fusion.1.refs_1_), channel_id=1, source_target_pairs={{0,1},{1,0},{2,3},{3,2},{4,5},{5,4},{6,7},{7,6},{8,9},{9,8},{10,11... | collective-permute-start | bytes 73736 | tf_op jit(solution)/shard_map/ppermute | solution.py:444
  33.9 0.5 %correlate.4.refs_2_ = f32[12,32,1024]{2,1,0:T(8,128)S(1)} custom-call(bf16[3,32,1024]{2,1,0:T(8,128)(2,1)S(1)} %bitcast.5, bf16[48,512]{1,0:T(8,128)(2,1)S(1)} %slice_add_fusion.refs_1_), custom_call_target="tpu_custom_call" | custom-call | tf_op jit(solution)/shard_map/correlate/pallas_call | solution.py:418
  34.4 0.3 correlate.5.refs_2_
  34.7 0.0 collective-permute-done.4
  34.7 0.0 collective-permute-done.11.refs_1_
  34.7 0.5 %correlate.6.refs_2_ = f32[12,32,1024]{2,1,0:T(8,128)S(1)} custom-call(bf16[3,32,1024]{2,1,0:T(8,128)(2,1)S(1)} %bitcast.7, bf16[48,512]{1,0:T(8,128)(2,1)S(1)} %collective-permute-done.11.refs_1_, f32[12,32,1024]{2,1,0:T(8,128)S(1)} %correlate.5.refs_2_), custom_call_target="tpu_custom_call" | custom-call | tf_op jit(solution)/shard_map/correlate/pallas_call | solution.py:418
  35.3 0.5 %collective-permute-done.9.refs_1_ = bf16[24,512]{1,0:T(8,128)(2,1)S(1)} collective-permute-done((bf16[24,512]{1,0:T(8,128)(2,1)S(1)}, bf16[24,512]{1,0:T(8,128)(2,1)S(1)}, u32[]{:S(2)}, u32[]{:S(2)}) %collective-permute-start.9) | collective-permute-done | bytes 24608 | tf_op jit(solution)/shard_map/ppermute | solution.py:444
  35.7 1.3 %correlate.7 = f32[12,32,1024]{2,1,0:T(8,128)} custom-call(bf16[3,32,1024]{2,1,0:T(8,128)(2,1)S(1)} %bitcast.8, bf16[24,512]{1,0:T(8,128)(2,1)S(1)} %collective-permute-done.9.refs_1_, f32[12,32,1024]{2,1,0:T(8,128)S(1)} %correlate.6.refs_2_), custom_call_target="tpu_custom_call" | custom-call | tf_op jit(solution)/shard_map/correlate/pallas_call | solution.py:418
  (9 shorter events, 0.1 us)
Async XLA Ops:
  0.0 7.9 %collective-permute-start.1 = (s32[1,12]{1,0:T(1,128)}, s32[1,12]{1,0:T(1,128)S(1)}, u32[]{:S(2)}, u32[]{:S(2)}) collective-permute-start(s32[1,12]{1,0:T(1,128)} %ids_in.1), channel_id=1, source_target_pairs={{0,2},{2,0},{4,6},{6,4},{8,10},{10,8},{12,14},{14,12},{1,3},{3,1},... | collective-permute-start | bytes 152 | tf_op jit(solution)/shard_map/ppermute | solution.py:444
  3.5 13.0 %collective-permute-start = (bf16[64,1152]{1,0:T(8,128)(2,1)S(1)}, bf16[64,1152]{1,0:T(8,128)(2,1)S(1)}, u32[]{:S(2)}, u32[]{:S(2)}) collective-permute-start(bf16[64,1152]{1,0:T(8,128)(2,1)S(1)} %get-tuple-element.26), channel_id=1, source_target_pairs={{0,1},{2,3},{4,5},{6,7},{8,9},{10,11},{12,13},{14,15},{16,17},{18,... | collective-permute-start | bytes 442376 | tf_op jit(solution)/shard_map/ppermute | solution.py:483
  7.9 1.7 %copy-start = (bf16[64,6144]{1,0:T(8,128)(2,1)S(1)}, bf16[64,6144]{1,0:T(8,128)(2,1)}, u32[]{:S(2)}) copy-start(bf16[64,6144]{1,0:T(8,128)(2,1)} %traces.3) | copy-start | bytes 2359300
  8.0 1.7 %copy-start.1 = (f32[64,33]{0,1:T(8,128)S(1)}, f32[64,33]{0,1:T(8,128)}, u32[]{:S(2)}) copy-start(f32[64,33]{0,1:T(8,128)} %param.7) | copy-start | bytes 25348
  8.0 3.6 %collective-permute-start.2 = (s32[2,12]{1,0:T(2,128)S(1)}, s32[2,12]{1,0:T(2,128)S(1)}, u32[]{:S(2)}, u32[]{:S(2)}) collective-permute-start(s32[2,12]{1,0:T(2,128)S(1)} %pair.1), channel_id=1, source_target_pairs={{0,4},{2,6},{4,0},{6,2},{8,12},{10,14},{12,8},{14,10},{1,5},{3,7},... | collective-permute-start | bytes 296 | tf_op jit(solution)/shard_map/ppermute | solution.py:444
  11.6 4.5 %collective-permute-start.3 = (s32[4,12]{1,0:T(4,128)S(1)}, s32[4,12]{1,0:T(4,128)S(1)}, u32[]{:S(2)}, u32[]{:S(2)}) collective-permute-start(s32[4,12]{1,0:T(4,128)S(1)} %pad_add_fusion.refs_0_), channel_id=1, source_target_pairs={{0,8},{2,10},{4,12},{6,14},{8,0},{10,2},{12,4},{14,6},{1,9},{3,11}... | collective-permute-start | bytes 584 | tf_op jit(solution)/shard_map/ppermute | solution.py:444
  14.3 1.9 %copy-start.2 = (s32[8,36]{1,0:T(8,128)S(1)}, s32[8,36]{1,0:T(8,128)}, u32[]{:S(2)}) copy-start(s32[8,36]{1,0:T(8,128)} %slots.1) | copy-start | bytes 3460
  14.3 1.9 %copy-start.3 = (s32[8]{0:T(128)S(1)}, s32[8]{0:T(128)}, u32[]{:S(2)}) copy-start(s32[8]{0:T(128)} %param.8) | copy-start | bytes 100
  18.0 1.6 %collective-permute-start.5 = (bf16[288,512]{1,0:T(8,128)(2,1)S(1)}, bf16[288,512]{1,0:T(8,128)(2,1)S(1)}, u32[]{:S(2)}, u32[]{:S(2)}) collective-permute-start(bf16[288,512]{1,0:T(8,128)(2,1)S(1)} %get-tuple-element.41), channel_id=1, source_target_pairs={{0,2},{2,0},{4,6},{6,4},{8,10},{10,8},{12,14},{14,12},{1,3},{3,1},... | collective-permute-start | bytes 884744 | tf_op jit(solution)/shard_map/ppermute | solution.py:444
  19.7 4.7 %collective-permute-start.7 = (bf16[72,512]{1,0:T(8,128)(2,1)S(1)}, bf16[72,512]{1,0:T(8,128)(2,1)S(1)}, u32[]{:S(2)}, u32[]{:S(2)}) collective-permute-start(bf16[72,512]{1,0:T(8,128)(2,1)S(1)} %get-tuple-element.45), channel_id=1, source_target_pairs={{0,4},{2,6},{4,0},{6,2},{8,12},{10,14},{12,8},{14,10},{1,5},{3,7},... | collective-permute-start | bytes 221192 | tf_op jit(solution)/shard_map/ppermute | solution.py:444
  21.4 6.1 %collective-permute-start.6 = (bf16[72,512]{1,0:T(8,128)(2,1)S(1)}, bf16[72,512]{1,0:T(8,128)(2,1)S(1)}, u32[]{:S(2)}, u32[]{:S(2)}) collective-permute-start(bf16[72,512]{1,0:T(8,128)(2,1)S(1)} %get-tuple-element.43), channel_id=1, source_target_pairs={{0,4},{2,6},{4,0},{6,2},{8,12},{10,14},{12,8},{14,10},{1,5},{3,7},... | collective-permute-start | bytes 221192 | tf_op jit(solution)/shard_map/ppermute | solution.py:444
  24.5 5.3 %collective-permute-start.10 = (bf16[48,512]{1,0:T(8,128)(2,1)S(1)}, bf16[48,512]{1,0:T(8,128)(2,1)S(1)}, u32[]{:S(2)}, u32[]{:S(2)}) collective-permute-start(bf16[48,512]{1,0:T(8,128)(2,1)S(1)} %slice.39), channel_id=1, source_target_pairs={{0,8},{2,10},{4,12},{6,14},{8,0},{10,2},{12,4},{14,6},{1,9},{3,11}... | collective-permute-start | bytes 147464 | tf_op jit(solution)/shard_map/ppermute | solution.py:444
  27.2 7.5 %collective-permute-start.4 = (bf16[96,1024]{1,0:T(8,128)(2,1)S(1)}, bf16[96,1024]{1,0:T(8,128)(2,1)S(1)}, u32[]{:S(2)}, u32[]{:S(2)}) collective-permute-start(bf16[96,1024]{1,0:T(8,128)(2,1)S(1)} %get-tuple-element.39), channel_id=1, source_target_pairs={{0,1},{1,0},{2,3},{3,2},{4,5},{5,4},{6,7},{7,6},{8,9},{9,8},{10,11... | collective-permute-start | bytes 589832 | tf_op jit(solution)/shard_map/ppermute | solution.py:444
  27.2 4.7 %collective-permute-start.8 = (bf16[24,512]{1,0:T(8,128)(2,1)S(1)}, bf16[24,512]{1,0:T(8,128)(2,1)S(1)}, u32[]{:S(2)}, u32[]{:S(2)}) collective-permute-start(bf16[24,512]{1,0:T(8,128)(2,1)S(1)} %slice.37), channel_id=1, source_target_pairs={{0,8},{2,10},{4,12},{6,14},{8,0},{10,2},{12,4},{14,6},{1,9},{3,11}... | collective-permute-start | bytes 73736 | tf_op jit(solution)/shard_map/ppermute | solution.py:444
  29.9 4.9 %collective-permute-start.11 = (bf16[48,512]{1,0:T(8,128)(2,1)S(1)}, bf16[48,512]{1,0:T(8,128)(2,1)S(1)}, u32[]{:S(2)}, u32[]{:S(2)}) collective-permute-start(bf16[48,512]{1,0:T(8,128)(2,1)S(1)} %slice_add_fusion.refs_1_), channel_id=1, source_target_pairs={{0,1},{1,0},{2,3},{3,2},{4,5},{5,4},{6,7},{7,6},{8,9},{9,8},{10,11... | collective-permute-start | bytes 147464 | tf_op jit(solution)/shard_map/ppermute | solution.py:444
  31.9 3.8 %collective-permute-start.9 = (bf16[24,512]{1,0:T(8,128)(2,1)S(1)}, bf16[24,512]{1,0:T(8,128)(2,1)S(1)}, u32[]{:S(2)}, u32[]{:S(2)}) collective-permute-start(bf16[24,512]{1,0:T(8,128)(2,1)S(1)} %slice_add_fusion.1.refs_1_), channel_id=1, source_target_pairs={{0,1},{1,0},{2,3},{3,2},{4,5},{5,4},{6,7},{7,6},{8,9},{9,8},{10,11... | collective-permute-start | bytes 73736 | tf_op jit(solution)/shard_map/ppermute | solution.py:444

commit v13 on v11

--- a/solution.py
+++ b/solution.py
@@ -129,7 +129,7 @@
         white[rows, NF:] = im
         return carry
 
-    lax.fori_loop(0, count // ROWS, step, 0, unroll=4)
+    lax.fori_loop(0, count // ROWS, step, 0, unroll=min(8, count // ROWS))
 
 
 def load_kernel(end, traces_in, table_in, ids_in, message, last_half, table, ids, traces, sems):
@@ -276,11 +276,9 @@
 
 
 def rest_kernel(
-    windows, pairs, times, halo, ends, taps, table, part_a, part_b, response_a, response_b, *refs
+    windows, pairs, halo, ends, taps, table, part_a, part_b, response_a, response_b, *refs
 ):
-    own_white, picks, keep, send = refs[:4]
-    blocks = refs[4 : 4 + times]
-    shifted, spectra, white = refs[4 + times :]
+    own_white, picks, send, white, shifted, spectra = refs
     channels = response_a.shape[0]
     tap_count = taps.shape[0]
     tile = 128
@@ -309,23 +307,31 @@
     count = rest * channels
     whiten_all(spectra, white, count)
     white[count:, :] = own_white[...]
-    base = picks.shape[0] // 2
+    spread(windows, pairs, white, picks, send, picks.shape[0] // 2)
+
+
+def spread(windows, pairs, white, picks, target, first):
+    count = picks.shape[0] // 2
     sizes = part_rows(windows, pairs)
     used = [(windows - 1) * pairs, pairs]
-    part = channels // times
-    choose = picks[...]
+    choose = picks[first : first + count, :]
     for f in range(0, 2 * NF, CHUNK):
-        cols = slice(f, f + CHUNK)
-        out = dot(choose, white[:, cols]).astype(BF16)
+        out = dot(choose, white[:, f : f + CHUNK]).astype(BF16)
         imag = f >= NF
         place = slice(f - NF * imag, f - NF * imag + CHUNK)
-        for target, first in ((keep, 0), (send, base)):
-            for d in range(base // sum(sizes)):
-                at, row = first + d * sum(sizes), d * 2 * sum(used)
-                for size, n in zip(sizes, used):
-                    put = row + imag * n
-                    target[put : put + n, place] = out[at : at + n]
-                    at, row = at + size, row + 2 * n
+        for d in range(count // sum(sizes)):
+            at, row = d * sum(sizes), d * 2 * sum(used)
+            for size, n in zip(sizes, used):
+                put = row + imag * n
+                target[put : put + n, place] = out[at : at + n]
+                at, row = at + size, row + 2 * n
+
+
+def keep_kernel(windows, pairs, white, picks, keep, *blocks):
+    times = len(blocks)
+    channels = white.shape[0] // windows
+    part = channels // times
+    spread(windows, pairs, white, picks, keep, 0)
     for d in range(times):
         line = (lax.axis_index("tm") ^ d) * part
         for w in range(windows):
@@ -384,7 +390,7 @@
             copy(p).start()
         return carry
 
-    lax.fori_loop(0, pairs, one, 0, unroll=2 if pairs % 2 == 0 else 1)
+    lax.fori_loop(0, pairs, one, 0, unroll=4 if pairs % 4 == 0 else 1)
     if last:
         for p in range(pairs):
             copy(p).wait()
@@ -518,16 +524,17 @@
         compiler_params=params,
         name="picks",
     )(source_counts[None], source_channel, *wanted)
-    outs = pl.pallas_call(
-        functools.partial(rest_kernel, windows, pairs, times),
-        out_shape=[jax.ShapeDtypeStruct((chips * rows, NF), BF16)] * 2
-        + [jax.ShapeDtypeStruct((windows * part, 2 * NF), BF16)] * times,
+    send, white = pl.pallas_call(
+        functools.partial(rest_kernel, windows, pairs),
+        out_shape=[
+            jax.ShapeDtypeStruct((chips * rows, NF), BF16),
+            jax.ShapeDtypeStruct((width, 2 * NF), BF16),
+        ],
         in_specs=[vmem] * 10,
-        out_specs=[vmem] * (2 + times),
+        out_specs=[vmem] * 2,
         scratch_shapes=[
             pltpu.VMEM((2 * tap_count + 6, width - channels), F32),
             pltpu.VMEM((width - channels, 2 * NF), F32),
-            pltpu.VMEM((width, 2 * NF), BF16),
         ],
         compiler_params=params,
         name="rest",
@@ -543,7 +550,15 @@
         own_white,
         picks,
     )
-    keep, send, blocks = outs[0], outs[1], outs[2:]
+    keep, *blocks = pl.pallas_call(
+        functools.partial(keep_kernel, windows, pairs),
+        out_shape=[jax.ShapeDtypeStruct((chips * rows, NF), BF16)]
+        + [jax.ShapeDtypeStruct((windows * part, 2 * NF), BF16)] * times,
+        in_specs=[vmem] * 2,
+        out_specs=[vmem] * (1 + times),
+        compiler_params=params,
+        name="keep",
+    )(white, picks)
     gathered = keep + across(send, "chan", 1)
     pieces = [gathered[d * rows : (d + 1) * rows] for d in range(chips)]
     pieces = list(lax.optimization_barrier(tuple(pieces)))

time: 36.4 us -> 36.2 us (level)
    pallas_call x1 -> x2, Pallas kernels: 1.44 us -> 1.43 us  [the longest x1 1.19 us: shards(): pl.pallas_call(functools.partial(rest_kernel, windows, pairs), out_shape=...]
  transfers between devices with their start and end apart: 12 -> 12, of which waited for: 7 -> 7; matrix products, arithmetic and copies ran while one was open for 0% -> 0% of each run, Pallas kernels for 16% -> 17%
where the time goes in v13:
time: 36.2 us; the launch traced here: 36 us
  starting transfers between devices  16.4 us (45%)
  waiting for transfers between devices  10.7 us (30%)
  Pallas kernels  8.47 us (23%)
    ppermute x11, starting transfers between devices, across(): return lax.ppermute(x, axis, [(i, i ^ distance) for i in range(size)])  12 us
    ppermute x11, waiting for transfers between devices, across(): return lax.ppermute(x, axis, [(i, i ^ distance) for i in range(size)])  10.7 us
    ppermute x1, starting transfers between devices, shards(): halo = lax.ppermute(message, 'tm', [(i - 1, i) for i in range(1, times)])  4.39 us
    pallas_call x4, Pallas kernels, correlate(): pl.pallas_call(functools.partial(correlate_kernel, spans, pairs, factor,...  2.51 us
    pallas_call x1, Pallas kernels, shards(): pl.pallas_call(functools.partial(load_kernel, tap_count - 1), out_shape=[...  2.26 us
    pallas_call x1, Pallas kernels, shards(): pl.pallas_call(functools.partial(rest_kernel, windows, pairs), out_shape=...  1.19 us
    pallas_call x1, Pallas kernels, shards(): pl.pallas_call(functools.partial(second_kernel, windows), out_shape=chunk...  1.03 us
    pallas_call x1, Pallas kernels, shards(): pl.pallas_call(functools.partial(first_kernel, windows), out_shape=chunk_...  0.89 us
  transfers between devices with their start and end apart: 12, of which 7 were waited for; matrix products, arithmetic and copies ran while one was open for 0% of the time, Pallas kernels for 17%

profile of v13, /device:TPU:0, one launch (start us, length us, event | category | flops | bytes accessed | tf_op | source)
XLA Modules:
  0.0 36.0 jit_solution(13883577155710984320)
XLA Ops:
  0.0 0.5 %collective-permute-start.1 = (s32[1,12]{1,0:T(1,128)}, s32[1,12]{1,0:T(1,128)S(1)}, u32[]{:S(2)}, u32[]{:S(2)}) collective-permute-start(s32[1,12]{1,0:T(1,128)} %ids_in.1), channel_id=1, source_target_pairs={{0,2},{2,0},{4,6},{6,4},{8,10},{10,8},{12,14},{14,12},{1,3},{3,1},... | collective-permute-start | bytes 152 | tf_op jit(solution)/shard_map/ppermute | solution.py:437
  0.5 2.3 %load.1 = (bf16[64,1152]{1,0:T(8,128)(2,1)S(1)}, f32[64,1024]{1,0:T(8,128)S(1)}, bf16[4,1024,256]{2,1,0:T(8,128)(2,1)S(1)}, s32[1,12]{1,0:T(1,128)S(1)}) custom-call(bf16[64,6144]{1,0:T(8,128)(2,1)} %traces.3, bf16[4,1024,256]{2,1,0:T(8,128)(2,1)} %constant.2.clone.table_in, s32[1,12]{1,0:T(1,128)} %ids_in.1), custom_call_target="tpu_custom_call" | custom-call | tf_op jit(solution)/shard_map/load/pallas_call | solution.py:446
  2.8 4.4 %collective-permute-start = (bf16[64,1152]{1,0:T(8,128)(2,1)S(1)}, bf16[64,1152]{1,0:T(8,128)(2,1)S(1)}, u32[]{:S(2)}, u32[]{:S(2)}) collective-permute-start(bf16[64,1152]{1,0:T(8,128)(2,1)S(1)} %get-tuple-element.27), channel_id=1, source_target_pairs={{0,1},{2,3},{4,5},{6,7},{8,9},{10,11},{12,13},{14,15},{16,17},{18,... | collective-permute-start | bytes 442376 | tf_op jit(solution)/shard_map/ppermute | solution.py:476
  7.2 0.0 collective-permute-done.1.other
  7.2 0.0 copy-start
  7.2 0.0 copy-start.1
  7.2 1.6 %collective-permute-start.2 = (s32[2,12]{1,0:T(2,128)S(1)}, s32[2,12]{1,0:T(2,128)S(1)}, u32[]{:S(2)}, u32[]{:S(2)}) collective-permute-start(s32[2,12]{1,0:T(2,128)S(1)} %pair.1), channel_id=1, source_target_pairs={{0,4},{2,6},{4,0},{6,2},{8,12},{10,14},{12,8},{14,10},{1,5},{3,7},... | collective-permute-start | bytes 296 | tf_op jit(solution)/shard_map/ppermute | solution.py:437
  8.9 0.0 copy-done
  8.9 0.0 copy-done.1
  8.9 0.9 %first.1 = (f32[128,512]{1,0:T(8,128)S(1)}, f32[64,512]{1,0:T(8,128)S(1)}, f32[64,512]{1,0:T(8,128)S(1)}, bf16[64,256]{1,0:T(8,128)(2,1)S(1)}, bf16[64,96]{1,0:T(8,128)(2,1)S(1)}, /*index=5*/bf16[64,144]{1,0:T(8,128)(2,1)S(1)}) custom-call(bf16[64,6144]{1,0:T(8,128)(2,1)S(1)} %copy-done, f32[33,64]{1,0:T(8,128)S(1)} %bitcast.9, ...), custom_call_target="tpu_custom_call" | custom-call | tf_op jit(solution)/shard_map/first/pallas_call | solution.py:488
  9.8 1.1 %collective-permute-done.2 = s32[2,12]{1,0:T(2,128)S(1)} collective-permute-done((s32[2,12]{1,0:T(2,128)S(1)}, s32[2,12]{1,0:T(2,128)S(1)}, u32[]{:S(2)}, u32[]{:S(2)}) %collective-permute-start.2) | collective-permute-done | bytes 128 | tf_op jit(solution)/shard_map/ppermute | solution.py:437
  10.9 2.6 %collective-permute-start.3 = (s32[4,12]{1,0:T(4,128)S(1)}, s32[4,12]{1,0:T(4,128)S(1)}, u32[]{:S(2)}, u32[]{:S(2)}) collective-permute-start(s32[4,12]{1,0:T(4,128)S(1)} %pad_add_fusion.refs_0_), channel_id=1, source_target_pairs={{0,8},{2,10},{4,12},{6,14},{8,0},{10,2},{12,4},{14,6},{1,9},{3,11}... | collective-permute-start | bytes 584 | tf_op jit(solution)/shard_map/ppermute | solution.py:437
  13.5 0.0 copy-start.2
  13.5 0.0 copy-start.3
  13.5 1.0 %second.1 = (f32[128,512]{1,0:T(8,128)S(1)}, f32[64,512]{1,0:T(8,128)S(1)}, bf16[64,1024]{1,0:T(8,128)(2,1)S(1)}) custom-call(bf16[64,6144]{1,0:T(8,128)(2,1)S(1)} %copy-done, bf16[4,1024,256]{2,1,0:T(8,128)(2,1)S(1)} %get-tuple-element.28.table, f32[64,1024]{1,0:T(8,128)S(1)} %get-tuple-element.29.last_half, bf16[64,144]{1,0:T(8,128)(2,1)S(1)} %get-tuple-element.32.lines, ...), custom_call_target="tpu_custom_call" | custom-call | tf_op jit(solution)/shard_map/second/pallas_call | solution.py:506
  14.6 0.9 %collective-permute-done.3.refs_1_ = s32[4,12]{1,0:T(4,128)S(1)} collective-permute-done((s32[4,12]{1,0:T(4,128)S(1)}, s32[4,12]{1,0:T(4,128)S(1)}, u32[]{:S(2)}, u32[]{:S(2)}) %collective-permute-start.3) | collective-permute-done | bytes 224 | tf_op jit(solution)/shard_map/ppermute | solution.py:437
  15.4 0.0 copy-done.2
  15.4 0.0 copy-done.3
  15.4 0.3 picks.1.refs_1_
  15.8 0.0 collective-permute-done.halo
  15.8 1.2 %rest.1 = (bf16[288,512]{1,0:T(8,128)(2,1)S(1)}, bf16[192,1024]{1,0:T(8,128)(2,1)S(1)}) custom-call(bf16[64,1152]{1,0:T(8,128)(2,1)S(1)} %collective-permute-done.halo, bf16[64,256]{1,0:T(8,128)(2,1)S(1)} %get-tuple-element.30.ends, f32[33,64]{1,0:T(8,128)S(1)} %bitcast.10, bf16[4,1024,256]{2,1,0:T(8,128)(2,1)S(1)} %get-tuple-element.28.table, ...), custom_call_target="tpu_custom_call" | custom-call | tf_op jit(solution)/shard_map/rest/pallas_call | solution.py:527
  17.0 0.1 collective-permute-start.5
  17.0 0.2 keep.1
  17.3 1.3 %collective-permute-done.5 = bf16[288,512]{1,0:T(8,128)(2,1)S(1)} collective-permute-done((bf16[288,512]{1,0:T(8,128)(2,1)S(1)}, bf16[288,512]{1,0:T(8,128)(2,1)S(1)}, u32[]{:S(2)}, u32[]{:S(2)}) %collective-permute-start.5) | collective-permute-done | bytes 294944 | tf_op jit(solution)/shard_map/ppermute | solution.py:437
  18.6 0.1 add.15
  18.7 1.6 %collective-permute-start.7 = (bf16[72,512]{1,0:T(8,128)(2,1)S(1)}, bf16[72,512]{1,0:T(8,128)(2,1)S(1)}, u32[]{:S(2)}, u32[]{:S(2)}) collective-permute-start(bf16[72,512]{1,0:T(8,128)(2,1)S(1)} %get-tuple-element.47), channel_id=1, source_target_pairs={{0,4},{2,6},{4,0},{6,2},{8,12},{10,14},{12,8},{14,10},{1,5},{3,7},... | collective-permute-start | bytes 221192 | tf_op jit(solution)/shard_map/ppermute | solution.py:437
  20.4 0.4 %collective-permute-start.6 = (bf16[72,512]{1,0:T(8,128)(2,1)S(1)}, bf16[72,512]{1,0:T(8,128)(2,1)S(1)}, u32[]{:S(2)}, u32[]{:S(2)}) collective-permute-start(bf16[72,512]{1,0:T(8,128)(2,1)S(1)} %get-tuple-element.45), channel_id=1, source_target_pairs={{0,4},{2,6},{4,0},{6,2},{8,12},{10,14},{12,8},{14,10},{1,5},{3,7},... | collective-permute-start | bytes 221192 | tf_op jit(solution)/shard_map/ppermute | solution.py:437
  20.8 2.6 %collective-permute-done.7 = bf16[72,512]{1,0:T(8,128)(2,1)S(1)} collective-permute-done((bf16[72,512]{1,0:T(8,128)(2,1)S(1)}, bf16[72,512]{1,0:T(8,128)(2,1)S(1)}, u32[]{:S(2)}, u32[]{:S(2)}) %collective-permute-start.7) | collective-permute-done | bytes 73760 | tf_op jit(solution)/shard_map/ppermute | solution.py:437
  23.5 2.7 %collective-permute-start.10 = (bf16[48,512]{1,0:T(8,128)(2,1)S(1)}, bf16[48,512]{1,0:T(8,128)(2,1)S(1)}, u32[]{:S(2)}, u32[]{:S(2)}) collective-permute-start(bf16[48,512]{1,0:T(8,128)(2,1)S(1)} %slice.39), channel_id=1, source_target_pairs={{0,8},{2,10},{4,12},{6,14},{8,0},{10,2},{12,4},{14,6},{1,9},{3,11}... | collective-permute-start | bytes 147464 | tf_op jit(solution)/shard_map/ppermute | solution.py:437
  26.2 0.0 collective-permute-start.4
  26.2 0.3 collective-permute-start.8
  26.5 0.0 collective-permute-done.6
  26.5 2.3 %collective-permute-done.10 = bf16[48,512]{1,0:T(8,128)(2,1)S(1)} collective-permute-done((bf16[48,512]{1,0:T(8,128)(2,1)S(1)}, bf16[48,512]{1,0:T(8,128)(2,1)S(1)}, u32[]{:S(2)}, u32[]{:S(2)}) %collective-permute-start.10) | collective-permute-done | bytes 49184 | tf_op jit(solution)/shard_map/ppermute | solution.py:437
  28.8 0.1 collective-permute-start.11
  28.9 2.0 %collective-permute-done.8 = bf16[24,512]{1,0:T(8,128)(2,1)S(1)} collective-permute-done((bf16[24,512]{1,0:T(8,128)(2,1)S(1)}, bf16[24,512]{1,0:T(8,128)(2,1)S(1)}, u32[]{:S(2)}, u32[]{:S(2)}) %collective-permute-start.8) | collective-permute-done | bytes 24608 | tf_op jit(solution)/shard_map/ppermute | solution.py:437
  30.9 2.0 %collective-permute-start.9 = (bf16[24,512]{1,0:T(8,128)(2,1)S(1)}, bf16[24,512]{1,0:T(8,128)(2,1)S(1)}, u32[]{:S(2)}, u32[]{:S(2)}) collective-permute-start(bf16[24,512]{1,0:T(8,128)(2,1)S(1)} %slice_add_fusion.1.refs_1_), channel_id=1, source_target_pairs={{0,1},{1,0},{2,3},{3,2},{4,5},{5,4},{6,7},{7,6},{8,9},{9,8},{10,11... | collective-permute-start | bytes 73736 | tf_op jit(solution)/shard_map/ppermute | solution.py:437
  32.9 0.4 %correlate.4.refs_2_ = f32[12,32,1024]{2,1,0:T(8,128)S(1)} custom-call(bf16[3,32,1024]{2,1,0:T(8,128)(2,1)S(1)} %bitcast.5, bf16[48,512]{1,0:T(8,128)(2,1)S(1)} %slice_add_fusion.refs_1_), custom_call_target="tpu_custom_call" | custom-call | tf_op jit(solution)/shard_map/correlate/pallas_call | solution.py:411
  33.4 0.3 correlate.5.refs_2_
  33.7 0.0 collective-permute-done.4
  33.7 0.0 collective-permute-done.11.refs_1_
  33.7 0.5 %correlate.6.refs_2_ = f32[12,32,1024]{2,1,0:T(8,128)S(1)} custom-call(bf16[3,32,1024]{2,1,0:T(8,128)(2,1)S(1)} %bitcast.7, bf16[48,512]{1,0:T(8,128)(2,1)S(1)} %collective-permute-done.11.refs_1_, f32[12,32,1024]{2,1,0:T(8,128)S(1)} %correlate.5.refs_2_), custom_call_target="tpu_custom_call" | custom-call | tf_op jit(solution)/shard_map/correlate/pallas_call | solution.py:411
  34.2 0.5 %collective-permute-done.9.refs_1_ = bf16[24,512]{1,0:T(8,128)(2,1)S(1)} collective-permute-done((bf16[24,512]{1,0:T(8,128)(2,1)S(1)}, bf16[24,512]{1,0:T(8,128)(2,1)S(1)}, u32[]{:S(2)}, u32[]{:S(2)}) %collective-permute-start.9) | collective-permute-done | bytes 24608 | tf_op jit(solution)/shard_map/ppermute | solution.py:437
  34.7 1.3 %correlate.7 = f32[12,32,1024]{2,1,0:T(8,128)} custom-call(bf16[3,32,1024]{2,1,0:T(8,128)(2,1)S(1)} %bitcast.8, bf16[24,512]{1,0:T(8,128)(2,1)S(1)} %collective-permute-done.9.refs_1_, f32[12,32,1024]{2,1,0:T(8,128)S(1)} %correlate.6.refs_2_), custom_call_target="tpu_custom_call" | custom-call | tf_op jit(solution)/shard_map/correlate/pallas_call | solution.py:411
  (9 shorter events, 0.1 us)
Async XLA Ops:
  0.0 7.2 %collective-permute-start.1 = (s32[1,12]{1,0:T(1,128)}, s32[1,12]{1,0:T(1,128)S(1)}, u32[]{:S(2)}, u32[]{:S(2)}) collective-permute-start(s32[1,12]{1,0:T(1,128)} %ids_in.1), channel_id=1, source_target_pairs={{0,2},{2,0},{4,6},{6,4},{8,10},{10,8},{12,14},{14,12},{1,3},{3,1},... | collective-permute-start | bytes 152 | tf_op jit(solution)/shard_map/ppermute | solution.py:437
  2.8 13.0 %collective-permute-start = (bf16[64,1152]{1,0:T(8,128)(2,1)S(1)}, bf16[64,1152]{1,0:T(8,128)(2,1)S(1)}, u32[]{:S(2)}, u32[]{:S(2)}) collective-permute-start(bf16[64,1152]{1,0:T(8,128)(2,1)S(1)} %get-tuple-element.27), channel_id=1, source_target_pairs={{0,1},{2,3},{4,5},{6,7},{8,9},{10,11},{12,13},{14,15},{16,17},{18,... | collective-permute-start | bytes 442376 | tf_op jit(solution)/shard_map/ppermute | solution.py:476
  7.2 1.7 %copy-start = (bf16[64,6144]{1,0:T(8,128)(2,1)S(1)}, bf16[64,6144]{1,0:T(8,128)(2,1)}, u32[]{:S(2)}) copy-start(bf16[64,6144]{1,0:T(8,128)(2,1)} %traces.3) | copy-start | bytes 2359300
  7.2 1.7 %copy-start.1 = (f32[64,33]{0,1:T(8,128)S(1)}, f32[64,33]{0,1:T(8,128)}, u32[]{:S(2)}) copy-start(f32[64,33]{0,1:T(8,128)} %param.7) | copy-start | bytes 25348
  7.2 3.6 %collective-permute-start.2 = (s32[2,12]{1,0:T(2,128)S(1)}, s32[2,12]{1,0:T(2,128)S(1)}, u32[]{:S(2)}, u32[]{:S(2)}) collective-permute-start(s32[2,12]{1,0:T(2,128)S(1)} %pair.1), channel_id=1, source_target_pairs={{0,4},{2,6},{4,0},{6,2},{8,12},{10,14},{12,8},{14,10},{1,5},{3,7},... | collective-permute-start | bytes 296 | tf_op jit(solution)/shard_map/ppermute | solution.py:437
  10.9 4.5 %collective-permute-start.3 = (s32[4,12]{1,0:T(4,128)S(1)}, s32[4,12]{1,0:T(4,128)S(1)}, u32[]{:S(2)}, u32[]{:S(2)}) collective-permute-start(s32[4,12]{1,0:T(4,128)S(1)} %pad_add_fusion.refs_0_), channel_id=1, source_target_pairs={{0,8},{2,10},{4,12},{6,14},{8,0},{10,2},{12,4},{14,6},{1,9},{3,11}... | collective-permute-start | bytes 584 | tf_op jit(solution)/shard_map/ppermute | solution.py:437
  13.5 1.9 %copy-start.2 = (s32[8,36]{1,0:T(8,128)S(1)}, s32[8,36]{1,0:T(8,128)}, u32[]{:S(2)}) copy-start(s32[8,36]{1,0:T(8,128)} %slots.1) | copy-start | bytes 3460
  13.5 1.9 %copy-start.3 = (s32[8]{0:T(128)S(1)}, s32[8]{0:T(128)}, u32[]{:S(2)}) copy-start(s32[8]{0:T(128)} %param.8) | copy-start | bytes 100
  17.0 1.6 %collective-permute-start.5 = (bf16[288,512]{1,0:T(8,128)(2,1)S(1)}, bf16[288,512]{1,0:T(8,128)(2,1)S(1)}, u32[]{:S(2)}, u32[]{:S(2)}) collective-permute-start(bf16[288,512]{1,0:T(8,128)(2,1)S(1)} %get-tuple-element.43), channel_id=1, source_target_pairs={{0,2},{2,0},{4,6},{6,4},{8,10},{10,8},{12,14},{14,12},{1,3},{3,1},... | collective-permute-start | bytes 884744 | tf_op jit(solution)/shard_map/ppermute | solution.py:437
  18.7 4.7 %collective-permute-start.7 = (bf16[72,512]{1,0:T(8,128)(2,1)S(1)}, bf16[72,512]{1,0:T(8,128)(2,1)S(1)}, u32[]{:S(2)}, u32[]{:S(2)}) collective-permute-start(bf16[72,512]{1,0:T(8,128)(2,1)S(1)} %get-tuple-element.47), channel_id=1, source_target_pairs={{0,4},{2,6},{4,0},{6,2},{8,12},{10,14},{12,8},{14,10},{1,5},{3,7},... | collective-permute-start | bytes 221192 | tf_op jit(solution)/shard_map/ppermute | solution.py:437
  20.4 6.1 %collective-permute-start.6 = (bf16[72,512]{1,0:T(8,128)(2,1)S(1)}, bf16[72,512]{1,0:T(8,128)(2,1)S(1)}, u32[]{:S(2)}, u32[]{:S(2)}) collective-permute-start(bf16[72,512]{1,0:T(8,128)(2,1)S(1)} %get-tuple-element.45), channel_id=1, source_target_pairs={{0,4},{2,6},{4,0},{6,2},{8,12},{10,14},{12,8},{14,10},{1,5},{3,7},... | collective-permute-start | bytes 221192 | tf_op jit(solution)/shard_map/ppermute | solution.py:437
  23.5 5.3 %collective-permute-start.10 = (bf16[48,512]{1,0:T(8,128)(2,1)S(1)}, bf16[48,512]{1,0:T(8,128)(2,1)S(1)}, u32[]{:S(2)}, u32[]{:S(2)}) collective-permute-start(bf16[48,512]{1,0:T(8,128)(2,1)S(1)} %slice.39), channel_id=1, source_target_pairs={{0,8},{2,10},{4,12},{6,14},{8,0},{10,2},{12,4},{14,6},{1,9},{3,11}... | collective-permute-start | bytes 147464 | tf_op jit(solution)/shard_map/ppermute | solution.py:437
  26.2 7.5 %collective-permute-start.4 = (bf16[96,1024]{1,0:T(8,128)(2,1)S(1)}, bf16[96,1024]{1,0:T(8,128)(2,1)S(1)}, u32[]{:S(2)}, u32[]{:S(2)}) collective-permute-start(bf16[96,1024]{1,0:T(8,128)(2,1)S(1)} %get-tuple-element.41), channel_id=1, source_target_pairs={{0,1},{1,0},{2,3},{3,2},{4,5},{5,4},{6,7},{7,6},{8,9},{9,8},{10,11... | collective-permute-start | bytes 589832 | tf_op jit(solution)/shard_map/ppermute | solution.py:437
  26.2 4.7 %collective-permute-start.8 = (bf16[24,512]{1,0:T(8,128)(2,1)S(1)}, bf16[24,512]{1,0:T(8,128)(2,1)S(1)}, u32[]{:S(2)}, u32[]{:S(2)}) collective-permute-start(bf16[24,512]{1,0:T(8,128)(2,1)S(1)} %slice.37), channel_id=1, source_target_pairs={{0,8},{2,10},{4,12},{6,14},{8,0},{10,2},{12,4},{14,6},{1,9},{3,11}... | collective-permute-start | bytes 73736 | tf_op jit(solution)/shard_map/ppermute | solution.py:437
  28.8 4.8 %collective-permute-start.11 = (bf16[48,512]{1,0:T(8,128)(2,1)S(1)}, bf16[48,512]{1,0:T(8,128)(2,1)S(1)}, u32[]{:S(2)}, u32[]{:S(2)}) collective-permute-start(bf16[48,512]{1,0:T(8,128)(2,1)S(1)} %slice_add_fusion.refs_1_), channel_id=1, source_target_pairs={{0,1},{1,0},{2,3},{3,2},{4,5},{5,4},{6,7},{7,6},{8,9},{9,8},{10,11... | collective-permute-start | bytes 147464 | tf_op jit(solution)/shard_map/ppermute | solution.py:437
  30.9 3.8 %collective-permute-start.9 = (bf16[24,512]{1,0:T(8,128)(2,1)S(1)}, bf16[24,512]{1,0:T(8,128)(2,1)S(1)}, u32[]{:S(2)}, u32[]{:S(2)}) collective-permute-start(bf16[24,512]{1,0:T(8,128)(2,1)S(1)} %slice_add_fusion.1.refs_1_), channel_id=1, source_target_pairs={{0,1},{1,0},{2,3},{3,2},{4,5},{5,4},{6,7},{7,6},{8,9},{9,8},{10,11... | collective-permute-start | bytes 73736 | tf_op jit(solution)/shard_map/ppermute | solution.py:437
